TPU v7x, 32 devices: a whole 2x2x4 slice. The times are simulated.
32 devices in a mesh: dp: 4 (over x, core), fsdp: 8 (over z, y).
Axes of the slice: x: 2, y: 2, z: 4, core: 2. Of those that a mesh axis runs over, the one named last changes fastest.
Arguments:
- tokens: bfloat16 [3, 32768, 512], P(None, ('dp', 'fsdp')), may hold values from -6 to 6
- cotangent: bfloat16 [3, 32768, 512], P(None, ('dp', 'fsdp')), may hold values from -6 to 6
- lengths: int32 [3, 16], replicated, may hold values from 16 to 48, as said below
- stretch_order: int32 [3, 512], replicated, may hold values from 0 to 511, as said below
- ln1_gain: bfloat16 [512], P(('dp', 'fsdp')), may hold values from 0.099609375 to 1.8984375
- ln1_bias: bfloat16 [512], P(('dp', 'fsdp')), may hold values from -3 to 3
- w_qkv: bfloat16 [512, 1536], P(('dp', 'fsdp')), may hold values from -0.25 to 0.25
- b_qkv: bfloat16 [1536], P(('dp', 'fsdp')), may hold values from -2 to 2
- w_out: bfloat16 [512, 512], P(('dp', 'fsdp')), may hold values from -1 to 1
- b_out: bfloat16 [512], P(('dp', 'fsdp')), may hold values from -3 to 3
- ln2_gain: bfloat16 [512], P(('dp', 'fsdp')), may hold values from 0.099609375 to 1.8984375
- ln2_bias: bfloat16 [512], P(('dp', 'fsdp')), may hold values from -3 to 3
- w_up: bfloat16 [512, 2048], P(('dp', 'fsdp')), may hold values from -0.25 to 0.25
- b_up: bfloat16 [2048], P(('dp', 'fsdp')), may hold values from -3 to 3
- w_down: bfloat16 [2048, 512], P(('dp', 'fsdp')), may hold values from -0.125 to 0.125
- b_down: bfloat16 [512], P(('dp', 'fsdp')), may hold values from -3 to 3
Outputs:
- result: bfloat16 [3, 32768, 512], P(None, ('dp', 'fsdp'))
- input_grad: bfloat16 [3, 32768, 512], P(None, ('dp', 'fsdp'))
- grad_ln1_gain: float32 [512], P(('dp', 'fsdp'))
- grad_ln1_bias: float32 [512], P(('dp', 'fsdp'))
- grad_w_qkv: float32 [512, 1536], P(('dp', 'fsdp'))
- grad_b_qk: float32 [1024], P(('dp', 'fsdp'))
- grad_b_value: float32 [512], P(('dp', 'fsdp'))
- grad_w_out: float32 [512, 512], P(('dp', 'fsdp'))
- grad_b_out: float32 [512], P(('dp', 'fsdp'))
- grad_ln2_gain: float32 [512], P(('dp', 'fsdp'))
- grad_ln2_bias: float32 [512], P(('dp', 'fsdp'))
- grad_w_up: float32 [512, 2048], P(('dp', 'fsdp'))
- grad_b_up: float32 [2048], P(('dp', 'fsdp'))
- grad_w_down: float32 [2048, 512], P(('dp', 'fsdp'))
- grad_b_down: float32 [512], P(('dp', 'fsdp'))
Inputs may be any that keep to these rules, and one draw needn't show every extreme that they name: `lengths`: each row sums to 512: the sequences of a micro-batch lie end to end from its first layout row and fill it. No sequence crosses from the layout stretches of one dp index to those of the next: each aligned block of 1024 / 64 * 8 layout stretches holds whole sequences. `stretch_order`: each row is a permutation of the stretches. Layout position p belongs to the device p // 16 of dp+fsdp; the stretch placed there arrives on a device with the same fsdp index, and every device receives exactly 1024 / 64 / 4 stretches from each device of the same fsdp index.
All inputs are finite; a program needn't handle non-finite values.
Results may differ from a plain program's by a relative error of at most 0.0085.
Values may be sent and summed in bfloat16 or wider, within the bound.
No kernel may reach another device: no remote copies, remote signals or barrier semaphores. Data moves between devices by JAX's collectives and lax.ppermute only.
A program may use at most 384 MiB of HBM per device.

v0:
```python
import jax
import jax.numpy as jnp
from jax import lax
from jax.sharding import PartitionSpec as P

HEADS = 8
HEAD_DIM = 64
STRETCH = 64


highest = lax.Precision.HIGHEST
eps_norm = 1e-05


def carried_in(part, axis, combine, identity, reverse):
    count = lax.axis_size(axis)
    place = lax.axis_index(axis)
    ahead = count - 1 - place if reverse else place
    gathered = jax.tree.map(lambda a: lax.all_gather(a, axis), part)
    state = jax.tree.map(lambda a, e: jnp.zeros_like(a) + jnp.asarray(e, a.dtype), part, identity)

    def one(step, state):
        source = count - 1 - step if reverse else step
        return combine(
            state, jax.tree.map(lambda a: lax.dynamic_index_in_dim(a, source, 0, False), gathered)
        )

    return lax.fori_loop(0, ahead, one, state)


def layer_norm(values, gain_vec, shift_vec):
    centre = jnp.mean(values, axis=-1, keepdims=True)
    centred = values - centre
    spread = jnp.mean(centred * centred, axis=-1, keepdims=True)
    return centred * lax.rsqrt(spread + eps_norm) * gain_vec + shift_vec


def feature(values):
    return jax.nn.elu(values) + 1.0


def split_heads(matrix):
    return matrix.astype(jnp.float32).reshape(-1, STRETCH, HEADS, HEAD_DIM).transpose(0, 2, 1, 3)


def merge_heads(blocked):
    return blocked.transpose(0, 2, 1, 3).reshape(-1, HEADS * HEAD_DIM)


def matmul(left, right):
    return jnp.dot(left, right, preferred_element_type=jnp.float32)


def inner_left(left, right):
    return lax.dot_general(
        left, right, (((0,), (0,)), ((), ())), preferred_element_type=jnp.float32
    )


def inner_right(left, right):
    return lax.dot_general(
        left, right, (((1,), (1,)), ((), ())), preferred_element_type=jnp.float32
    )


def combine_states(earlier, later):
    carry_on = 1.0 - later[2]
    return (
        later[0] + carry_on * earlier[0],
        later[1] + carry_on * earlier[1],
        jnp.maximum(earlier[2], later[2]),
    )


def layer_pass(rows_bf, grad_bf, restart_int, forward_set, shard_set):
    (
        gain_one,
        shift_one,
        qkv_weight,
        qkv_bias,
        out_weight,
        out_bias,
        gain_two,
        shift_two,
        up_weight,
        up_bias,
        down_weight,
        down_bias,
    ) = forward_set
    model_width = HEADS * HEAD_DIM
    stretch_count = restart_int.shape[0]
    segment = jnp.cumsum(restart_int)
    order = jnp.arange(stretch_count, dtype=jnp.int32)
    same_part = (segment[:, None] == segment[None, :]) & (order[None, :] < order[:, None])
    earlier = same_part.astype(jnp.float32)
    opened = (segment == 0).astype(jnp.float32)
    closing = (segment == segment[-1]).astype(jnp.float32)
    cut = jnp.max(restart_int).astype(jnp.float32)
    identity = (
        jnp.zeros((HEADS, HEAD_DIM, HEAD_DIM), jnp.float32),
        jnp.zeros((HEADS, HEAD_DIM), jnp.float32),
        jnp.zeros((), jnp.float32),
    )
    gain_one_f = gain_one.astype(jnp.float32)
    shift_one_f = shift_one.astype(jnp.float32)
    gain_two_f = gain_two.astype(jnp.float32)
    shift_two_f = shift_two.astype(jnp.float32)
    rows_in = rows_bf.astype(jnp.float32)
    normed = layer_norm(rows_in, gain_one_f, shift_one_f).astype(jnp.bfloat16)
    mixed = matmul(normed, qkv_weight) + qkv_bias.astype(jnp.float32)
    query_pre = mixed[:, :model_width]
    key_pre = mixed[:, model_width : 2 * model_width]
    queries = split_heads(feature(query_pre).astype(jnp.bfloat16))
    key_rows = split_heads(feature(key_pre).astype(jnp.bfloat16))
    value_rows = split_heads(mixed[:, 2 * model_width :].astype(jnp.bfloat16))
    kv_blocks = jnp.einsum("chjd,chje->chde", key_rows, value_rows, precision=highest)
    key_totals = jnp.sum(key_rows, axis=2)
    state_before = jnp.einsum("cz,zhde->chde", earlier, kv_blocks, precision=highest)
    sum_before = jnp.einsum("cz,zhd->chd", earlier, key_totals, precision=highest)
    local_state = jnp.einsum("z,zhde->hde", closing, kv_blocks, precision=highest)
    local_sum = jnp.einsum("z,zhd->hd", closing, key_totals, precision=highest)
    incoming = carried_in((local_state, local_sum, cut), "fsdp", combine_states, identity, False)
    state_prev = state_before + opened[:, None, None, None] * incoming[0][None]
    sum_prev = sum_before + opened[:, None, None] * incoming[1][None]
    causal = jnp.tril(jnp.ones((STRETCH, STRETCH), jnp.float32))
    mixing = jnp.einsum("chid,chjd->chij", queries, key_rows, precision=highest) * causal
    numerator = jnp.einsum("chij,chje->chie", mixing, value_rows, precision=highest)
    numerator = numerator + jnp.einsum("chid,chde->chie", queries, state_prev, precision=highest)
    denominator = jnp.sum(mixing, axis=-1) + jnp.einsum(
        "chid,chd->chi", queries, sum_prev, precision=highest
    )
    attended_heads = numerator / denominator[..., None]
    attended = merge_heads(attended_heads).astype(jnp.bfloat16)
    middle = rows_in + matmul(attended, out_weight) + out_bias.astype(jnp.float32)
    normed_two = layer_norm(middle, gain_two_f, shift_two_f).astype(jnp.bfloat16)
    hidden = matmul(normed_two, up_weight) + up_bias.astype(jnp.float32)
    active = jax.nn.gelu(hidden).astype(jnp.bfloat16)
    output = (middle + matmul(active, down_weight) + down_bias.astype(jnp.float32)).astype(
        jnp.bfloat16
    )
    (
        shard_g1,
        shard_s1,
        shard_qkv,
        shard_qb,
        shard_out,
        shard_ob,
        shard_g2,
        shard_s2,
        shard_up,
        shard_ub,
        shard_down,
        shard_db,
    ) = shard_set
    backward_set = (
        lax.all_gather(shard_g1, ("dp", "fsdp"), axis=0, tiled=True),
        lax.all_gather(shard_s1, ("dp", "fsdp"), axis=0, tiled=True),
        lax.all_gather(shard_qkv, ("dp", "fsdp"), axis=0, tiled=True),
        lax.all_gather(shard_qb, ("dp", "fsdp"), axis=0, tiled=True),
        lax.all_gather(shard_out, ("dp", "fsdp"), axis=0, tiled=True),
        lax.all_gather(shard_ob, ("dp", "fsdp"), axis=0, tiled=True),
        lax.all_gather(shard_g2, ("dp", "fsdp"), axis=0, tiled=True),
        lax.all_gather(shard_s2, ("dp", "fsdp"), axis=0, tiled=True),
        lax.all_gather(shard_up, ("dp", "fsdp"), axis=0, tiled=True),
        lax.all_gather(shard_ub, ("dp", "fsdp"), axis=0, tiled=True),
        lax.all_gather(shard_down, ("dp", "fsdp"), axis=0, tiled=True),
        lax.all_gather(shard_db, ("dp", "fsdp"), axis=0, tiled=True),
    )
    qkv_back = backward_set[2]
    out_back = backward_set[4]
    up_back = backward_set[8]
    down_back = backward_set[10]
    grad_out = grad_bf.astype(jnp.float32)
    grad_down = inner_left(active, grad_bf)
    grad_down_bias = jnp.sum(grad_out, axis=0)
    _, gelu_back = jax.vjp(jax.nn.gelu, hidden)
    grad_hidden = gelu_back(inner_right(grad_bf, down_back))[0].astype(jnp.bfloat16)
    grad_up = inner_left(normed_two, grad_hidden)
    grad_up_bias = jnp.sum(grad_hidden.astype(jnp.float32), axis=0)
    _, norm_back_two = jax.vjp(layer_norm, middle, gain_two_f, shift_two_f)
    grad_middle_part, grad_gain_two, grad_shift_two = norm_back_two(
        inner_right(grad_hidden, up_back)
    )
    grad_middle = grad_out + grad_middle_part
    grad_branch = grad_middle.astype(jnp.bfloat16)
    grad_out_weight = inner_left(attended, grad_branch)
    grad_out_bias = jnp.sum(grad_branch.astype(jnp.float32), axis=0)
    grad_heads = split_heads(inner_right(grad_branch, out_back).astype(jnp.bfloat16))
    grad_numer = grad_heads / denominator[..., None]
    grad_denom = -jnp.sum(grad_heads * attended_heads, axis=-1) / denominator
    grad_mixing = (
        jnp.einsum("chie,chje->chij", grad_numer, value_rows, precision=highest)
        + grad_denom[..., None]
    ) * causal
    grad_value = jnp.einsum("chij,chie->chje", mixing, grad_numer, precision=highest)
    grad_query = jnp.einsum("chij,chjd->chid", grad_mixing, key_rows, precision=highest)
    grad_query = grad_query + jnp.einsum(
        "chie,chde->chid", grad_numer, state_prev, precision=highest
    )
    grad_query = grad_query + grad_denom[..., None] * sum_prev[:, :, None, :]
    grad_key = jnp.einsum("chij,chid->chjd", grad_mixing, queries, precision=highest)
    grad_state = jnp.einsum("chid,chie->chde", queries, grad_numer, precision=highest)
    grad_ksum = jnp.einsum("chid,chi->chd", queries, grad_denom, precision=highest)
    after_state = jnp.einsum("zc,zhde->chde", earlier, grad_state, precision=highest)
    after_sum = jnp.einsum("zc,zhd->chd", earlier, grad_ksum, precision=highest)
    back_state = jnp.einsum("z,zhde->hde", opened, grad_state, precision=highest)
    back_sum = jnp.einsum("z,zhd->hd", opened, grad_ksum, precision=highest)
    outgoing = carried_in((back_state, back_sum, cut), "fsdp", combine_states, identity, True)
    grad_blocks = after_state + closing[:, None, None, None] * outgoing[0][None]
    grad_totals = after_sum + closing[:, None, None] * outgoing[1][None]
    grad_key = grad_key + jnp.einsum("chje,chde->chjd", value_rows, grad_blocks, precision=highest)
    grad_key = grad_key + grad_totals[:, :, None, :]
    grad_value = grad_value + jnp.einsum(
        "chjd,chde->chje", key_rows, grad_blocks, precision=highest
    )
    _, query_back = jax.vjp(feature, query_pre)
    _, key_back = jax.vjp(feature, key_pre)
    grad_mixed = jnp.concatenate(
        [
            query_back(merge_heads(grad_query))[0],
            key_back(merge_heads(grad_key))[0],
            merge_heads(grad_value),
        ],
        axis=1,
    ).astype(jnp.bfloat16)
    grad_qkv = inner_left(normed, grad_mixed)
    grad_qkv_bias = jnp.sum(grad_mixed.astype(jnp.float32), axis=0)
    _, norm_back_one = jax.vjp(layer_norm, rows_in, gain_one_f, shift_one_f)
    grad_rows_part, grad_gain_one, grad_shift_one = norm_back_one(inner_right(grad_mixed, qkv_back))
    input_grad = (grad_middle + grad_rows_part).astype(jnp.bfloat16)
    grads = (
        grad_gain_one,
        grad_shift_one,
        grad_qkv,
        grad_qkv_bias[: 2 * model_width],
        grad_qkv_bias[2 * model_width :],
        grad_out_weight,
        grad_out_bias,
        grad_gain_two,
        grad_shift_two,
        grad_up,
        grad_up_bias,
        grad_down,
        grad_down_bias,
    )
    return (output, input_grad, grads)


def body(
    tokens,
    cotangent,
    lengths,
    stretch_order,
    ln1_gain,
    ln1_bias,
    w_qkv,
    b_qkv,
    w_out,
    b_out,
    ln2_gain,
    ln2_bias,
    w_up,
    b_up,
    w_down,
    b_down,
):
    micro_count = tokens.shape[0]
    width = tokens.shape[2]
    stretch_count = tokens.shape[1] // STRETCH
    fsdp_size = lax.axis_size("fsdp")
    device = lax.axis_index(("dp", "fsdp"))
    within = jnp.arange(stretch_count, dtype=jnp.int32)
    global_index = device * stretch_count + within
    shard_set = (
        ln1_gain,
        ln1_bias,
        w_qkv,
        b_qkv,
        w_out,
        b_out,
        ln2_gain,
        ln2_bias,
        w_up,
        b_up,
        w_down,
        b_down,
    )
    totals = None
    shards = None
    results = []
    input_grads = []
    for micro_idx in range(micro_count):
        seq_lengths = lengths[micro_idx]
        starts = jnp.cumsum(seq_lengths) - seq_lengths
        restart_int = jnp.any(global_index[:, None] == starts[None, :], axis=1).astype(jnp.int32)
        order_row = stretch_order[micro_idx]
        inverse = jnp.argsort(order_row)
        landing = inverse[global_index]
        send_order = jnp.argsort(landing)
        source_dev = order_row[global_index] // stretch_count
        recv_key = source_dev // fsdp_size * stretch_count + within
        recv_order = jnp.argsort(recv_key)
        placing = jnp.argsort(recv_order)
        restore = jnp.argsort(send_order)
        row_blocks = tokens[micro_idx].reshape(stretch_count, STRETCH, width)
        grad_blocks = cotangent[micro_idx].reshape(stretch_count, STRETCH, width)
        moved_rows, moved_grads = (
            lax.all_to_all(row_blocks[send_order], "dp", split_axis=0, concat_axis=0, tiled=True),
            lax.all_to_all(grad_blocks[send_order], "dp", split_axis=0, concat_axis=0, tiled=True),
        )
        layout_rows = moved_rows[placing].reshape(-1, width)
        layout_grads = moved_grads[placing].reshape(-1, width)
        forward_set = (
            lax.all_gather(ln1_gain, ("dp", "fsdp"), axis=0, tiled=True),
            lax.all_gather(ln1_bias, ("dp", "fsdp"), axis=0, tiled=True),
            lax.all_gather(w_qkv, ("dp", "fsdp"), axis=0, tiled=True),
            lax.all_gather(b_qkv, ("dp", "fsdp"), axis=0, tiled=True),
            lax.all_gather(w_out, ("dp", "fsdp"), axis=0, tiled=True),
            lax.all_gather(b_out, ("dp", "fsdp"), axis=0, tiled=True),
            lax.all_gather(ln2_gain, ("dp", "fsdp"), axis=0, tiled=True),
            lax.all_gather(ln2_bias, ("dp", "fsdp"), axis=0, tiled=True),
            lax.all_gather(w_up, ("dp", "fsdp"), axis=0, tiled=True),
            lax.all_gather(b_up, ("dp", "fsdp"), axis=0, tiled=True),
            lax.all_gather(w_down, ("dp", "fsdp"), axis=0, tiled=True),
            lax.all_gather(b_down, ("dp", "fsdp"), axis=0, tiled=True),
        )
        output, input_grad, grads = layer_pass(
            layout_rows, layout_grads, restart_int, forward_set, shard_set
        )
        out_blocks = output.reshape(stretch_count, STRETCH, width)[recv_order]
        back_blocks = input_grad.reshape(stretch_count, STRETCH, width)[recv_order]
        home_out, home_grad = (
            lax.all_to_all(out_blocks, "dp", split_axis=0, concat_axis=0, tiled=True),
            lax.all_to_all(back_blocks, "dp", split_axis=0, concat_axis=0, tiled=True),
        )
        results.append(home_out[restore].reshape(-1, width))
        input_grads.append(home_grad[restore].reshape(-1, width))
        totals = grads if totals is None else jax.tree.map(jnp.add, totals, grads)
    shards = (
        lax.psum_scatter(totals[0], ("dp", "fsdp"), scatter_dimension=0, tiled=True),
        lax.psum_scatter(totals[1], ("dp", "fsdp"), scatter_dimension=0, tiled=True),
        lax.psum_scatter(totals[2], ("dp", "fsdp"), scatter_dimension=0, tiled=True),
        lax.psum_scatter(totals[3], ("dp", "fsdp"), scatter_dimension=0, tiled=True),
        lax.psum_scatter(totals[4], ("dp", "fsdp"), scatter_dimension=0, tiled=True),
        lax.psum_scatter(totals[5], ("dp", "fsdp"), scatter_dimension=0, tiled=True),
        lax.psum_scatter(totals[6], ("dp", "fsdp"), scatter_dimension=0, tiled=True),
        lax.psum_scatter(totals[7], ("dp", "fsdp"), scatter_dimension=0, tiled=True),
        lax.psum_scatter(totals[8], ("dp", "fsdp"), scatter_dimension=0, tiled=True),
        lax.psum_scatter(totals[9], ("dp", "fsdp"), scatter_dimension=0, tiled=True),
        lax.psum_scatter(totals[10], ("dp", "fsdp"), scatter_dimension=0, tiled=True),
        lax.psum_scatter(totals[11], ("dp", "fsdp"), scatter_dimension=0, tiled=True),
        lax.psum_scatter(totals[12], ("dp", "fsdp"), scatter_dimension=0, tiled=True),
    )
    return (
        jnp.stack(results),
        jnp.stack(input_grads),
        shards[0],
        shards[1],
        shards[2],
        shards[3],
        shards[4],
        shards[5],
        shards[6],
        shards[7],
        shards[8],
        shards[9],
        shards[10],
        shards[11],
        shards[12],
    )


def solution(mesh):
    in_specs = (
        P(None, ("dp", "fsdp"), None),
        P(None, ("dp", "fsdp"), None),
        P(),
        P(),
        P(("dp", "fsdp")),
        P(("dp", "fsdp")),
        P(("dp", "fsdp"), None),
        P(("dp", "fsdp")),
        P(("dp", "fsdp"), None),
        P(("dp", "fsdp")),
        P(("dp", "fsdp")),
        P(("dp", "fsdp")),
        P(("dp", "fsdp"), None),
        P(("dp", "fsdp")),
        P(("dp", "fsdp"), None),
        P(("dp", "fsdp")),
    )
    out_specs = (
        P(None, ("dp", "fsdp"), None),
        P(None, ("dp", "fsdp"), None),
        P(("dp", "fsdp")),
        P(("dp", "fsdp")),
        P(("dp", "fsdp"), None),
        P(("dp", "fsdp")),
        P(("dp", "fsdp")),
        P(("dp", "fsdp"), None),
        P(("dp", "fsdp")),
        P(("dp", "fsdp")),
        P(("dp", "fsdp")),
        P(("dp", "fsdp"), None),
        P(("dp", "fsdp")),
        P(("dp", "fsdp"), None),
        P(("dp", "fsdp")),
    )
    return jax.shard_map(body, mesh=mesh, in_specs=in_specs, out_specs=out_specs, check_vma=False)
```

profile of v0, /device:TPU:0, one launch (start us, length us, event | category | flops | bytes accessed | tf_op | source)
XLA Modules:
  0.0 1700.6 jit_solution(14570166735527686970)
XLA Ops:
  49.6 42.1 %all-reduce.22 = (bf16[512]{0:T(512)(128)(2,1)S(1)}, bf16[512]{0:T(512)(128)(2,1)S(1)}, bf16[1536]{0:T(1024)(128)(2,1)S(1)}, bf16[512]{0:T(512)(128)(2,1)S(1)}, ...) all-reduce(bf16[512]{0:T(512)(128)(2,1)S(1)} %dynamic-update-slice., ...), channel_id=1, replica_groups=mesh['dp'=4,'fsdp'=8] {'dp','fsdp'}, use_global_device_ids=true, to_apply=%add.1 | all-reduce | flops 6656 | bytes 26624
  101.2 13.0 all-to-all-done.4
  121.2 11.7 all-to-all-done.2
  241.7 11.7 all-to-all-done.6
  264.3 22.1 %all-reduce.21 = (f32[8]{0:T(128)}, f32[8]{0:T(128)}, f32[8]{0:T(128)S(1)}) all-reduce(f32[8]{0:T(128)S(1)} %dynamic-update-slice.10, f32[8]{0:T(128)S(1)} %dynamic-update-slice.9, f32[8]{0:T(128)S(1)} %dynamic-update-slice.3), channel_id=1, replica_groups=mesh['dp'=4,'fsdp'=8] {'fsdp'}, use_global_device_ids=true, to_apply=%add.10 | all-reduce | flops 24 | bytes 192
  298.9 73.5 %all_gather.178 = bf16[512,512]{1,0:T(8,128)(2,1)} all-gather(bf16[16,512]{1,0:T(8,128)(2,1)S(1)} %copy-done.212), channel_id=1, replica_groups=mesh['dp'=4,'fsdp'=8] {'dp','fsdp'}, dimensions={0}, use_global_device_ids=true | all-gather | bytes 540672 | tf_op jit(solution)/shard_map/all_gather | solution.py:318
  398.6 30.5 %all-gather.1 = f32[64,64]{1,0:T(8,128)S(1)} all-gather(f32[8,64]{1,0:T(8,128)S(1)} %bitcast.680), channel_id=3, replica_groups=mesh['dp'=4,'fsdp'=8] {'fsdp'}, dimensions={0}, use_global_device_ids=true | all-gather | bytes 18432 | tf_op jit(solution)/shard_map/all_gather | solution.py:19
  475.7 32.0 %all-gather.3 = f32[64,64]{1,0:T(8,128)} all-gather(f32[8,64]{1,0:T(8,128)S(1)} %bitcast.681), channel_id=5, replica_groups=mesh['dp'=4,'fsdp'=8] {'fsdp'}, dimensions={0}, use_global_device_ids=true | all-gather | bytes 18432 | tf_op jit(solution)/shard_map/all_gather | solution.py:19
  508.6 30.4 %all-gather.5 = f32[64,64]{1,0:T(8,128)S(1)} all-gather(f32[8,64]{1,0:T(8,128)S(1)} %bitcast.682), channel_id=7, replica_groups=mesh['dp'=4,'fsdp'=8] {'fsdp'}, dimensions={0}, use_global_device_ids=true | all-gather | bytes 18432 | tf_op jit(solution)/shard_map/all_gather | solution.py:19
  539.0 8.6 multiply_reduce_fusion.2
  548.2 7.2 multiply_add_fusion.5
  575.0 7.7 multiply_add_fusion.4
  606.7 7.2 multiply_add_fusion.3
  642.7 5.9 fusion.346
  648.6 9.0 multiply_convert_fusion.2
  657.6 11.1 convert_reduce_fusion.1
  674.5 8.6 convert_reduce_fusion
  685.6 8.6 convert_reduce_fusion.2
  715.3 8.0 fusion.170
  737.0 7.9 fusion.151
  753.0 5.9 copy.418
  759.0 8.0 fusion.132
  782.3 6.8 fusion.43
  810.8 7.9 fusion.78
  827.6 15.8 bitcast_add_fusion.14
  843.4 12.4 bitcast_add_fusion.13
  855.9 12.5 bitcast_add_fusion.12
  878.6 7.5 copy.406
  890.8 7.5 copy.427
  903.5 90.0 %all-gather.7 = f32[64,64]{1,0:T(8,128)S(1)} all-gather(f32[8,64]{1,0:T(8,128)S(1)} %bitcast.677), channel_id=9, replica_groups=mesh['dp'=4,'fsdp'=8] {'fsdp'}, dimensions={0}, use_global_device_ids=true | all-gather | bytes 18432 | tf_op jit(solution)/shard_map/all_gather | solution.py:19
  993.5 31.8 %all-gather.9 = f32[64,64]{1,0:T(8,128)} all-gather(f32[8,64]{1,0:T(8,128)S(1)} %bitcast.678), channel_id=11, replica_groups=mesh['dp'=4,'fsdp'=8] {'fsdp'}, dimensions={0}, use_global_device_ids=true | all-gather | bytes 18432 | tf_op jit(solution)/shard_map/all_gather | solution.py:19
  1025.3 30.4 %all-gather.11 = f32[64,64]{1,0:T(8,128)S(1)} all-gather(f32[8,64]{1,0:T(8,128)S(1)} %bitcast.679), channel_id=13, replica_groups=mesh['dp'=4,'fsdp'=8] {'fsdp'}, dimensions={0}, use_global_device_ids=true | all-gather | bytes 18432 | tf_op jit(solution)/shard_map/all_gather | solution.py:19
  1059.0 8.4 fusion.75
  1077.6 16.4 while.93
  1094.3 7.1 multiply_add_fusion.2
  1122.3 11.7 fusion.126
  1140.4 25.5 %while.94 = (s32[]{:T(128)}, f32[8,64,64]{2,1,0:T(8,128)S(1)}, f32[8,64]{1,0:T(8,128)S(1)}, s32[]{:T(128)}, f32[8,8,64,64]{3,2,1,0:T(8,128)}, /*index=5*/f32[8]{...) while((s32[]{:T(128)}, f32[8,64,64]{2,1,0:T(8,128)S(1)}, ...), condition=%wide.region_62.63_spmd, body=%wide.region_61.62_spmd.sunk | while | flops 66567 | bytes 399563 | solution.py:28
  1167.0 7.1 multiply_add_fusion.1
  1195.2 11.7 fusion.127
  1214.2 16.4 while.95
  1231.7 6.9 multiply_add_fusion
  1259.3 11.8 fusion.128
  1348.0 8.3 add_convert_fusion.12
  1377.4 7.2 fusion.181
  1396.2 6.3 add_convert_fusion.9
  1453.3 45.7 %all-reduce.20 = (f32[512]{0:T(512)S(1)}, f32[512]{0:T(512)S(1)}, f32[1024]{0:T(1024)S(1)}, f32[512]{0:T(512)S(1)}, f32[512]{0:T(512)S(1)}, /*index=5*/f32[512]{...) all-reduce(f32[512]{0:T(512)S(1)} %add_add_fusion.17, ...), channel_id=14, replica_groups=mesh['dp'=4,'fsdp'=8] {'dp','fsdp'}, use_global_device_ids=true, to_apply=%region_75.76.clone | all-reduce | flops 6656 | bytes 53248
  1510.6 39.0 %reduce-scatter.11.cloned.1.call-done = f32[64,512]{1,0:T(8,128)} async-done(((f32[2048,512]{1,0:T(8,128)}), f32[64,512]{1,0:T(8,128)}) %reduce-scatter.11.cloned.1.call-update) | async-done | bytes 131088 | tf_op jit(solution)/shard_map/reduce_scatter | solution.py:351
  1549.6 144.1 %reduce-scatter.9.cloned.1.call-done = f32[16,2048]{1,0:T(8,128)} async-done(((f32[512,2048]{1,0:T(8,128)}), f32[16,2048]{1,0:T(8,128)}) %reduce-scatter.9.cloned.1.call-update) | async-done | bytes 131088 | tf_op jit(solution)/shard_map/reduce_scatter | solution.py:349
  (1096 shorter events, 757.2 us)
Async XLA Ops:
  19.0 77.1 %all-to-all-start = ((bf16[16,64,512]{2,1,0:T(8,128)(2,1)}), bf16[16,64,512]{2,1,0:T(8,128)(2,1)S(1)}, u32[]{:S(2)}, u32[]{:S(2)}) async-start(bf16[16,64,512]{2,1,0:T(8,128)(2,1)} %gather_fusion.1), calls=%async_computation | async-start | bytes 2097152 | tf_op jit(solution)/shard_map/all_to_all | solution.py:308
  23.2 115.3 %all-gather.22.cloned.1.call-start = ((), (), s32[]{:S(2)}) async-start(), calls=%async_computation.16 | async-start | bytes 1622016 | tf_op jit(solution)/shard_map/all_gather | solution.py:316
  47.1 501.1 %copy-start.174 = (s32[16]{0:T(128)}, s32[16]{0:T(128)S(1)}, u32[]{:S(2)}) copy-start(s32[16]{0:T(128)S(1)} %reduce.12) | copy-start | bytes 196
  91.7 44.0 %copy-start.208 = (f32[512]{0:T(512)}, f32[512]{0:T(512)S(1)}, u32[]{:S(2)}) copy-start(f32[512]{0:T(512)S(1)} %convert_element_type.367) | copy-start | bytes 6148
  96.1 18.0 %all-to-all-start.4 = ((bf16[16,64,512]{2,1,0:T(8,128)(2,1)}), bf16[16,64,512]{2,1,0:T(8,128)(2,1)S(1)}, u32[]{:S(2)}, u32[]{:S(2)}) async-start(bf16[16,64,512]{2,1,0:T(8,128)(2,1)} %gather_fusion.13), calls=%async_computation.4 | async-start | bytes 2097152 | tf_op jit(solution)/shard_map/all_to_all | solution.py:308
  114.1 18.8 %all-to-all-start.2 = ((bf16[16,64,512]{2,1,0:T(8,128)(2,1)}), bf16[16,64,512]{2,1,0:T(8,128)(2,1)}, u32[]{:S(2)}, u32[]{:S(2)}) async-start(bf16[16,64,512]{2,1,0:T(8,128)(2,1)} %gather_fusion.7), calls=%async_computation.2 | async-start | bytes 2097152 | tf_op jit(solution)/shard_map/all_to_all | solution.py:308
  118.4 429.2 %all-gather.28.cloned.1.call-start = ((), (), s32[]{:S(2)}) async-start(), calls=%async_computation.23 | async-start | bytes 2359296 | tf_op jit(solution)/shard_map/all_gather | solution.py:19
  120.3 513.8 %copy-start.12 = (bf16[16,64,512]{2,1,0:T(8,128)(2,1)}, bf16[16,64,512]{2,1,0:T(8,128)(2,1)S(1)}, u32[]{:S(2)}) copy-start(bf16[16,64,512]{2,1,0:T(8,128)(2,1)S(1)} %gather_fusion.15) | copy-start | bytes 3145732
  167.5 407.4 %all-gather.30.cloned.1.call-start = ((), (), s32[]{:S(2)}) async-start(), calls=%async_computation.24 | async-start | bytes 2359296 | tf_op jit(solution)/shard_map/all_gather | solution.py:19
  168.2 419.3 %copy-start.178 = (s32[16]{0:T(128)}, s32[16]{0:T(128)S(1)}, u32[]{:S(2)}) copy-start(s32[16]{0:T(128)S(1)} %reduce.13) | copy-start | bytes 196
  197.7 408.9 %all-gather.32.cloned.1.call-start = ((), (), s32[]{:S(2)}) async-start(), calls=%async_computation.25 | async-start | bytes 2359296 | tf_op jit(solution)/shard_map/all_gather | solution.py:19
  198.2 420.6 %copy-start.176 = (s32[16]{0:T(128)}, s32[16]{0:T(128)S(1)}, u32[]{:S(2)}) copy-start(s32[16]{0:T(128)S(1)} %reduce.14) | copy-start | bytes 196
  209.0 257.3 %copy-start = (bf16[16,64,8,64]{3,2,1,0:T(8,128)(2,1)}, bf16[16,64,8,64]{3,2,1,0:T(8,128)(2,1)S(1)}, u32[]{:S(2)}) copy-start(bf16[16,64,8,64]{3,2,1,0:T(8,128)(2,1)S(1)} %reshape.606) | copy-start | bytes 3145732
  227.5 410.4 %all-gather.24.cloned.1.call-start = ((), (), s32[]{:S(2)}) async-start(), calls=%async_computation.17 | async-start | bytes 2162688 | tf_op jit(solution)/shard_map/all_gather | solution.py:322
  234.5 18.9 %all-to-all-start.6 = ((bf16[16,64,512]{2,1,0:T(8,128)(2,1)}), bf16[16,64,512]{2,1,0:T(8,128)(2,1)}, u32[]{:S(2)}, u32[]{:S(2)}) async-start(bf16[16,64,512]{2,1,0:T(8,128)(2,1)} %gather_fusion.18), calls=%async_computation.6 | async-start | bytes 2097152 | tf_op jit(solution)/shard_map/all_to_all | solution.py:309
  241.7 57.1 %copy-start.212 = (bf16[16,512]{1,0:T(8,128)(2,1)S(1)}, bf16[16,512]{1,0:T(8,128)(2,1)}, u32[]{:S(2)}) copy-start(bf16[16,512]{1,0:T(8,128)(2,1)} %param.36) | copy-start | bytes 49156
  253.4 38.6 %all-to-all-start.8 = ((bf16[16,64,512]{2,1,0:T(8,128)(2,1)}), bf16[16,64,512]{2,1,0:T(8,128)(2,1)}, u32[]{:S(2)}, u32[]{:S(2)}) async-start(bf16[16,64,512]{2,1,0:T(8,128)(2,1)} %gather_fusion.22), calls=%async_computation.8 | async-start | bytes 2097152 | tf_op jit(solution)/shard_map/all_to_all | solution.py:309
  257.7 399.9 %all-gather.26.cloned.1.call-start = ((), (), s32[]{:S(2)}) async-start(), calls=%async_computation.18 | async-start | bytes 2162688 | tf_op jit(solution)/shard_map/all_gather | solution.py:324
  286.4 286.0 %copy-start.233 = (f32[512]{0:T(512)}, f32[512]{0:T(512)S(1)}, u32[]{:S(2)}) copy-start(f32[512]{0:T(512)S(1)} %convert_element_type.380) | copy-start | bytes 6148
  292.0 86.0 %all-to-all-start.10 = ((bf16[16,64,512]{2,1,0:T(8,128)(2,1)}), bf16[16,64,512]{2,1,0:T(8,128)(2,1)}, u32[]{:S(2)}, u32[]{:S(2)}) async-start(bf16[16,64,512]{2,1,0:T(8,128)(2,1)} %gather_fusion.26), calls=%async_computation.10 | async-start | bytes 2097152 | tf_op jit(solution)/shard_map/all_to_all | solution.py:309
  296.4 781.2 %all-gather.34.cloned.1.call-start = ((), (), s32[]{:S(2)}) async-start(), calls=%async_computation.26 | async-start | bytes 2359296 | tf_op jit(solution)/shard_map/all_gather | solution.py:19
  296.4 324.5 %copy-start.121 = (f32[64,64]{0,1:T(8,128)}, f32[64,64]{0,1:T(8,128)S(1)}, u32[]{:S(2)}) copy-start(f32[64,64]{0,1:T(8,128)S(1)} %fusion.279) | copy-start | bytes 49156
  389.1 85.9 %copy-start.152 = (f32[16,8,64]{2,1,0:T(8,128)}, f32[16,8,64]{2,1,0:T(8,128)S(1)}, u32[]{:S(2)}) copy-start(f32[16,8,64]{2,1,0:T(8,128)S(1)} %convert_reduce_fusion.7) | copy-start | bytes 98308
  470.7 68.3 %copy-start.6 = (bf16[16,64,8,64]{3,2,1,0:T(8,128)(2,1)S(1)}, bf16[16,64,8,64]{3,2,1,0:T(8,128)(2,1)}, u32[]{:S(2)}) copy-start(bf16[16,64,8,64]{3,2,1,0:T(8,128)(2,1)} %copy-done.5) | copy-start | bytes 3145732
  574.9 123.8 %copy-start.19 = (f32[1024,512]{1,0:T(8,128)}, f32[1024,512]{1,0:T(8,128)S(1)}, u32[]{:S(2)}) copy-start(f32[1024,512]{1,0:T(8,128)S(1)} %get-tuple-element.781) | copy-start | bytes 6291460
  574.9 123.8 %copy-start.166 = (f32[1024]{0:T(1024)}, f32[1024]{0:T(1024)S(1)}, u32[]{:S(2)}) copy-start(f32[1024]{0:T(1024)S(1)} %broadcast_multiply_fusion.5) | copy-start | bytes 12292
  606.6 92.1 %copy-start.168 = (f32[1024]{0:T(1024)}, f32[1024]{0:T(1024)S(1)}, u32[]{:S(2)}) copy-start(f32[1024]{0:T(1024)S(1)} %broadcast_multiply_fusion.4) | copy-start | bytes 12292
  637.3 61.4 %copy-start.206 = (f32[1024]{0:T(1024)}, f32[1024]{0:T(1024)S(1)}, u32[]{:S(2)}) copy-start(f32[1024]{0:T(1024)S(1)} %broadcast_multiply_fusion.3) | copy-start | bytes 12292
  637.8 60.9 %copy-start.170 = (f32[1024]{0:T(1024)}, f32[1024]{0:T(1024)S(1)}, u32[]{:S(2)}) copy-start(f32[1024]{0:T(1024)S(1)} %fusion.307) | copy-start | bytes 12292
  637.8 60.9 %copy-start.172 = (f32[1024]{0:T(1024)}, f32[1024]{0:T(1024)S(1)}, u32[]{:S(2)}) copy-start(f32[1024]{0:T(1024)S(1)} %fusion.308) | copy-start | bytes 12292
  637.8 60.9 %copy-start.217 = (f32[1024]{0:T(1024)}, f32[1024]{0:T(1024)S(1)}, u32[]{:S(2)}) copy-start(f32[1024]{0:T(1024)S(1)} %fusion.309) | copy-start | bytes 12292
  768.6 53.4 %copy-start.150 = (f32[16,8,64]{2,1,0:T(8,128)}, f32[16,8,64]{2,1,0:T(8,128)S(1)}, u32[]{:S(2)}) copy-start(f32[16,8,64]{2,1,0:T(8,128)S(1)} %negate_divide_fusion) | copy-start | bytes 98308
  778.7 361.6 %all-gather.36.cloned.1.call-start = ((), (), s32[]{:S(2)}) async-start(), calls=%async_computation.27 | async-start | bytes 2359296 | tf_op jit(solution)/shard_map/all_gather | solution.py:19
  792.5 75.9 %copy-start.156 = (f32[16,8,1,64]{3,2,1,0:T(1,128)}, f32[16,8,1,64]{3,2,1,0:T(1,128)S(1)}, u32[]{:S(2)}) copy-start(f32[16,8,1,64]{3,2,1,0:T(1,128)S(1)} %fusion.134) | copy-start | bytes 98308
  810.6 403.5 %all-gather.38.cloned.1.call-start = ((), (), s32[]{:S(2)}) async-start(), calls=%async_computation.28 | async-start | bytes 2359296 | tf_op jit(solution)/shard_map/all_gather | solution.py:19
  827.1 683.5 %reduce-scatter.7.cloned.1.call-start = ((), (), s32[]{:S(2)}) async-start(), calls=%async_computation.20 | async-start | bytes 1081344 | tf_op jit(solution)/shard_map/reduce_scatter | solution.py:345
  898.3 157.4 %copy-start.109 = (bf16[1024,512]{1,0:T(8,128)(2,1)S(1)}, bf16[1024,512]{1,0:T(8,128)(2,1)}, u32[]{:S(2)}) copy-start(bf16[1024,512]{1,0:T(8,128)(2,1)} %copy-done.108) | copy-start | bytes 3145732
  1077.5 433.1 %reduce-scatter.5.cloned.1.call-start = ((), (), s32[]{:S(2)}) async-start(), calls=%async_computation.19 | async-start | bytes 3244032 | tf_op jit(solution)/shard_map/reduce_scatter | solution.py:342
  1140.3 145.6 %copy-start.89 = (bf16[1024,512]{1,0:T(8,128)(2,1)}, bf16[1024,512]{1,0:T(8,128)(2,1)S(1)}, u32[]{:S(2)}) copy-start(bf16[1024,512]{1,0:T(8,128)(2,1)S(1)} %reshape.614) | copy-start | bytes 3145732
  1297.9 251.7 %reduce-scatter.11.cloned.1.call-start = ((), (), s32[]{:S(2)}) async-start(), calls=%async_computation.22 | async-start | bytes 4325376 | tf_op jit(solution)/shard_map/reduce_scatter | solution.py:351
  1328.3 44.8 %all-to-all-start.1 = ((bf16[16,64,512]{2,1,0:T(8,128)(2,1)}), bf16[16,64,512]{2,1,0:T(8,128)(2,1)}, u32[]{:S(2)}, u32[]{:S(2)}) async-start(bf16[16,64,512]{2,1,0:T(8,128)(2,1)} %gather_fusion.4), calls=%async_computation.1 | async-start | bytes 2097152 | tf_op jit(solution)/shard_map/all_to_all | solution.py:333
  1332.6 361.1 %reduce-scatter.9.cloned.1.call-start = ((), (), s32[]{:S(2)}) async-start(), calls=%async_computation.21 | async-start | bytes 4325376 | tf_op jit(solution)/shard_map/reduce_scatter | solution.py:349
  1373.1 18.8 %all-to-all-start.3 = ((bf16[16,64,512]{2,1,0:T(8,128)(2,1)}), bf16[16,64,512]{2,1,0:T(8,128)(2,1)}, u32[]{:S(2)}, u32[]{:S(2)}) async-start(bf16[16,64,512]{2,1,0:T(8,128)(2,1)} %gather_fusion.10), calls=%async_computation.3 | async-start | bytes 2097152 | tf_op jit(solution)/shard_map/all_to_all | solution.py:333
  1391.9 18.8 %all-to-all-start.5 = ((bf16[16,64,512]{2,1,0:T(8,128)(2,1)}), bf16[16,64,512]{2,1,0:T(8,128)(2,1)}, u32[]{:S(2)}, u32[]{:S(2)}) async-start(bf16[16,64,512]{2,1,0:T(8,128)(2,1)} %gather_fusion.16), calls=%async_computation.5 | async-start | bytes 2097152 | tf_op jit(solution)/shard_map/all_to_all | solution.py:333
  1410.7 18.0 %all-to-all-start.7 = ((bf16[16,64,512]{2,1,0:T(8,128)(2,1)}), bf16[16,64,512]{2,1,0:T(8,128)(2,1)S(1)}, u32[]{:S(2)}, u32[]{:S(2)}) async-start(bf16[16,64,512]{2,1,0:T(8,128)(2,1)} %gather_fusion.20), calls=%async_computation.7 | async-start | bytes 2097152 | tf_op jit(solution)/shard_map/all_to_all | solution.py:334
  1428.6 18.8 %all-to-all-start.11 = ((bf16[16,64,512]{2,1,0:T(8,128)(2,1)}), bf16[16,64,512]{2,1,0:T(8,128)(2,1)}, u32[]{:S(2)}, u32[]{:S(2)}) async-start(bf16[16,64,512]{2,1,0:T(8,128)(2,1)} %gather_fusion.28), calls=%async_computation.11 | async-start | bytes 2097152 | tf_op jit(solution)/shard_map/all_to_all | solution.py:334
  1442.2 62.0 %copy-start.114 = (bf16[16,64,512]{2,1,0:T(8,128)(2,1)S(1)}, bf16[16,64,512]{2,1,0:T(8,128)(2,1)}, u32[]{:S(2)}) copy-start(bf16[16,64,512]{2,1,0:T(8,128)(2,1)} %copy-done.113) | copy-start | bytes 3145732
  1447.4 59.3 %all-to-all-start.9 = ((bf16[16,64,512]{2,1,0:T(8,128)(2,1)}), bf16[16,64,512]{2,1,0:T(8,128)(2,1)}, u32[]{:S(2)}, u32[]{:S(2)}) async-start(bf16[16,64,512]{2,1,0:T(8,128)(2,1)} %gather_fusion.24), calls=%async_computation.9 | async-start | bytes 2097152 | tf_op jit(solution)/shard_map/all_to_all | solution.py:334
  (266 other events, 2009.9 us)
Sparse Core Ops, SparseCore 0:
  26.9 58.8 all-gather.21
  167.7 49.7 all-gather.27
  219.6 47.7 all-gather.29
  269.4 50.1 all-gather.31
  322.4 55.2 all-gather.23
  380.5 55.4 all-gather.25
  778.8 110.5 all-gather.33
  891.5 47.7 all-gather.35
  941.5 48.2 all-gather.37
  1077.6 136.8 reduce-scatter.6
  1298.0 105.1 reduce-scatter.4
  1406.0 143.5 reduce-scatter.10
  1552.5 141.0 reduce-scatter.8
where the time goes:
time: 1710 us; the launch traced here: 1700 us
  matrix products  481 us (28%)
  blocking collectives  429 us (25%)
  local copies, waits for them, and re-layouts  341 us (20%)
  waiting for transfers between devices  240 us (14%)
  other arithmetic  123 us (7%)
  starting transfers between devices  51.8 us (3%)
  between operations  20.7 us (1%)
    all_gather x6, blocking collectives, carried_in(): gathered = jax.tree.map(lambda a: lax.all_gather(a, axis), part)  245 us
    reduce_scatter x1, waiting for transfers between devices, body(): lax.psum_scatter(totals[9], ('dp', 'fsdp'), scatter_dimension=0, tiled=True)  144 us
    unnamed x3, blocking collectives  110 us
    all_gather x1, blocking collectives, body(): lax.all_gather(w_out, ('dp', 'fsdp'), axis=0, tiled=True)  73.5 us
    reshape x15, local copies, waits for them, and re-layouts, split_heads(): matrix.astype(jnp.float32).reshape(-1, STRETCH, HEADS, HEAD_DIM)  56 us
    dot_general x12, matrix products, matmul(): return jnp.dot(left, right, preferred_element_type=jnp.float32)  55.3 us
    dot_general x12, matrix products, inner_right(): lax.dot_general(left, right, (((1,), (1,)), ((), ())), preferred_element_...  55.2 us
    transpose x12, local copies, waits for them, and re-layouts, split_heads(): matrix.astype(jnp.float32).reshape(-1, STRETCH, HEADS, HEAD_DIM)  47.9 us
  transfers between devices with their start and end apart: 25, of which 9 were waited for; matrix products, arithmetic and copies ran while one was open for 45% of the time, Pallas kernels for 0%

commit v1 on v0

v1 whole, which is shorter than its diff:
```python
import functools

import jax
import jax.numpy as jnp
from jax import lax
from jax.experimental import pallas as pl
from jax.experimental.pallas import tpu as pltpu
from jax.sharding import PartitionSpec as P

HEADS = 8
HEAD_DIM = 64
STRETCH = 64
LONGEST = 48
CHUNK = 2 * STRETCH
TILE = 2 * CHUNK
PAIRS = HEADS // 2
PAIR = 2 * HEAD_DIM
MODEL = HEADS * HEAD_DIM
BOTH = ("dp", "fsdp")
EPS = 1e-05
VMEM_LIMIT = 60 * 1024 * 1024

f32 = jnp.float32
bf16 = jnp.bfloat16


def nn(a, b):
    return lax.dot_general(a, b, (((1,), (0,)), ((), ())), preferred_element_type=f32)


def nt(a, b):
    return lax.dot_general(a, b, (((1,), (1,)), ((), ())), preferred_element_type=f32)


def tn(a, b):
    return lax.dot_general(a, b, (((0,), (0,)), ((), ())), preferred_element_type=f32)


def lanes(rows, width):
    return lax.broadcasted_iota(jnp.int32, (rows, width), 1)


def sublanes(rows, width):
    return lax.broadcasted_iota(jnp.int32, (rows, width), 0)


def first_head(rows):
    return lanes(rows, PAIR) < HEAD_DIM


def same_head():
    return (sublanes(PAIR, PAIR) // HEAD_DIM) == (lanes(PAIR, PAIR) // HEAD_DIM)


def by_head(x, rows):
    low = first_head(rows)
    zero = jnp.zeros_like(x)
    return jnp.concatenate([jnp.where(low, x, zero), jnp.where(low, zero, x)], axis=0)


def flag(value):
    return value.astype(f32)


def col(pair):
    return slice(pair * PAIR, (pair + 1) * PAIR)


def standardize(x):
    centre = jnp.mean(x, axis=-1, keepdims=True)
    centred = x - centre
    spread = jnp.mean(centred * centred, axis=-1, keepdims=True)
    scale = lax.rsqrt(spread + EPS)
    return centred * scale, scale


def norm_back(upstream, gain, n, scale):
    ug = upstream * gain
    return scale * (
        ug
        - jnp.mean(ug, axis=-1, keepdims=True)
        - n * jnp.mean(ug * n, axis=-1, keepdims=True)
    )


def unpack_state(block, pair):
    part = block[:HEAD_DIM, col(pair)]
    low = first_head(HEAD_DIM)
    zero = jnp.zeros_like(part)
    state = jnp.concatenate([jnp.where(low, part, zero), jnp.where(low, zero, part)], axis=0)
    row = block[HEAD_DIM : HEAD_DIM + 1, col(pair)]
    eye = sublanes(PAIR, PAIR) == lanes(PAIR, PAIR)
    diagonal = jnp.where(eye, row, 0.0)
    ones = jnp.where(same_head(), 1.0, 0.0).astype(bf16)
    high = diagonal.astype(bf16)
    low_part = (diagonal - high.astype(f32)).astype(bf16)
    sums = nn(high, ones) + nn(low_part, ones)
    return jnp.concatenate([state, sums], axis=1)


def pack_state(ref, pair, state, row):
    low = first_head(HEAD_DIM)
    ref[:HEAD_DIM, col(pair)] = jnp.where(low, state[:HEAD_DIM], state[HEAD_DIM:])
    ref[HEAD_DIM : HEAD_DIM + 1, col(pair)] = row
    ref[HEAD_DIM + 1 :, col(pair)] = jnp.zeros((7, PAIR), f32)


def qkv_kernel(
    placing, closing, rows, weight, bias, gain, shift, x_out, normed_out, qkv_out, state_out, acc, sums
):
    step = pl.program_id(0)
    per = TILE // STRETCH

    @pl.when(step == 0)
    def _():
        acc[...] = jnp.zeros_like(acc)
        sums[...] = jnp.zeros_like(sums)

    for i in range(per):
        x_out[i * STRETCH : (i + 1) * STRETCH, :] = rows[placing[step * per + i]]
    x = x_out[...].astype(f32)
    n, _ = standardize(x)
    normed = (n * gain[...] + shift[...]).astype(bf16)
    normed_out[...] = normed
    for part in range(2):
        at = slice(part * MODEL, (part + 1) * MODEL)
        mixed = nn(normed, weight[:, at]) + bias[:, at]
        feature = jnp.where(mixed > 0, mixed + 1.0, jnp.exp(jnp.minimum(mixed, 0.0)))
        qkv_out[:, at] = feature.astype(bf16)
    at = slice(2 * MODEL, 3 * MODEL)
    qkv_out[:, at] = (nn(normed, weight[:, at]) + bias[:, at]).astype(bf16)
    keep = jnp.concatenate(
        [jnp.full((STRETCH, 1), flag(closing[step * per + i]), f32) for i in range(per)], axis=0
    )
    for pair in range(PAIRS):
        k = qkv_out[:, MODEL + pair * PAIR : MODEL + (pair + 1) * PAIR].astype(f32) * keep
        v = qkv_out[:, 2 * MODEL + pair * PAIR : 2 * MODEL + (pair + 1) * PAIR]
        acc[pair] += tn(k.astype(bf16), v)
        sums[:, col(pair)] += jnp.sum(k, axis=0, keepdims=True)

    @pl.when(step == pl.num_programs(0) - 1)
    def _():
        for pair in range(PAIRS):
            pack_state(state_out, pair, acc[pair], sums[:, col(pair)])


def whole(shape):
    zeros = (0,) * len(shape)
    return pl.BlockSpec(shape, lambda i, *_: zeros)


def fixed(shape):
    zeros = (0,) * len(shape)
    return pl.BlockSpec(shape, lambda i, *_: zeros, pipeline_mode=pl.Buffered(1))


def tiled(width, flip=0):
    if flip:
        return pl.BlockSpec((TILE, width), lambda i, *_: (flip - 1 - i, 0))
    return pl.BlockSpec((TILE, width), lambda i, *_: (i, 0))


def params(steps=1):
    return pltpu.CompilerParams(
        dimension_semantics=("arbitrary",) * steps, vmem_limit_bytes=VMEM_LIMIT
    )


def run_qkv(placing, closing, rows, weight, bias, gain, shift):
    stretches, _, width = rows.shape
    count = stretches * STRETCH
    return pl.pallas_call(
        qkv_kernel,
        name="qkv",
        grid_spec=pltpu.PrefetchScalarGridSpec(
            num_scalar_prefetch=2,
            grid=(count // TILE,),
            in_specs=[
                fixed(rows.shape),
                fixed(weight.shape),
                fixed(bias.shape),
                fixed(gain.shape),
                fixed(shift.shape),
            ],
            out_specs=[
                tiled(width),
                tiled(width),
                tiled(3 * MODEL),
                whole((HEAD_DIM + 8, MODEL)),
            ],
            scratch_shapes=[
                pltpu.VMEM((PAIRS, PAIR, PAIR), f32),
                pltpu.VMEM((1, MODEL), f32),
            ],
        ),
        out_shape=[
            jax.ShapeDtypeStruct((count, width), bf16),
            jax.ShapeDtypeStruct((count, width), bf16),
            jax.ShapeDtypeStruct((count, 3 * MODEL), bf16),
            jax.ShapeDtypeStruct((HEAD_DIM + 8, MODEL), f32),
        ],
        compiler_params=params(),
        cost_estimate=pl.CostEstimate(
            flops=2 * count * width * 3 * MODEL, bytes_accessed=8 << 20, transcendentals=count * 1024
        ),
    )(placing, closing, rows, weight, bias, gain, shift)


def causal(second, transposed):
    i = sublanes(CHUNK, 2 * CHUNK)
    j = lanes(CHUNK, 2 * CHUNK) % CHUNK
    if transposed:
        i, j = j, i
    crosses = (i >= STRETCH) & (j < STRETCH)
    return jnp.where(crosses, 1.0 - second, jnp.where(j <= i, 1.0, 0.0))


def mid_kernel(
    placing,
    restart,
    opened,
    x_ref,
    qkv_ref,
    cot_ref,
    inc_ref,
    w_out,
    w_up,
    w_down,
    b_out,
    gain,
    shift,
    b_up,
    b_down,
    result,
    active_out,
    hidden_out,
    normed_out,
    att_out,
    branch_out,
    gn_out,
    gd_out,
    middle_out,
    states_out,
    state_out,
    vec_out,
    cot_out,
    carry,
    back,
    back_sum,
    slope,
    att_scr,
    inv_scr,
):
    step = pl.program_id(0)
    per = TILE // STRETCH

    @pl.when(step == 0)
    def _():
        for pair in range(PAIRS):
            carry[pair] = unpack_state(inc_ref[...], pair)
        back[...] = jnp.zeros_like(back)
        back_sum[...] = jnp.zeros_like(back_sum)
        vec_out[...] = jnp.zeros_like(vec_out)

    block = same_head()
    ones_head = jnp.where(block, 1.0, 0.0).astype(bf16)
    low = first_head(CHUNK)
    one_low = jnp.where(low, 1.0, 0.0).astype(bf16)
    one_high = jnp.where(low, 0.0, 1.0).astype(bf16)
    ones_both = jnp.concatenate([one_low, one_high], axis=0)
    ones_all = jnp.ones((CHUNK, PAIR), bf16)
    wide_block = jnp.concatenate([block, block], axis=1)
    upper = sublanes(CHUNK, PAIR) < STRETCH
    inner = lanes(PAIR, PAIR) % HEAD_DIM
    zero_s = jnp.zeros((PAIR, PAIR), bf16)
    for i in range(per):
        cot_out[i * STRETCH : (i + 1) * STRETCH, :] = cot_ref[placing[step * per + i]]

    for chunk in range(TILE // CHUNK):
        rows = slice(chunk * CHUNK, (chunk + 1) * CHUNK)
        r0 = flag(restart[step * per + 2 * chunk])
        r1 = flag(restart[step * per + 2 * chunk + 1])
        mask = causal(r1, False)
        keep_low = jnp.where(upper, 1.0, 1.0 - r1)
        keep_key = jnp.where(upper, 1.0 - r1, 1.0)
        for pair in range(PAIRS):
            q = qkv_ref[rows, pair * PAIR : (pair + 1) * PAIR]
            k = qkv_ref[rows, MODEL + pair * PAIR : MODEL + (pair + 1) * PAIR]
            v = qkv_ref[rows, 2 * MODEL + pair * PAIR : 2 * MODEL + (pair + 1) * PAIR]
            state = carry[pair] * (1.0 - r0)
            state_b = state.astype(bf16)
            state_low = (state - state_b.astype(f32)).astype(bf16)
            states_out[chunk, pair * PAIR : (pair + 1) * PAIR, :] = jnp.concatenate(
                [
                    state_b[:, :PAIR],
                    jnp.where(
                        inner < 2, state_b[:, PAIR:], jnp.where(inner == 2, state_low[:, PAIR:], zero_s)
                    ),
                    state_low[:, :PAIR],
                ],
                axis=1,
            )
            mixing = nt(q, by_head(k, CHUNK)) * mask
            values = jnp.concatenate([by_head(v, CHUNK), ones_both], axis=1)
            out = nn(mixing.astype(bf16), values)
            out = out + nn((q.astype(f32) * keep_low).astype(bf16), state_b)
            inv = 1.0 / out[:, PAIR:]
            att = out[:, :PAIR] * inv
            att_scr[rows, col(pair)] = att
            inv_scr[rows, col(pair)] = inv
            att_out[rows, col(pair)] = att.astype(bf16)
            k_keep = (k.astype(f32) * keep_key).astype(bf16)
            added = tn(k_keep, jnp.concatenate([v, ones_all], axis=1))
            carry[pair] = state * (1.0 - r1) + jnp.where(wide_block, added, 0.0)

    middle = x_ref[...].astype(f32) + nn(att_out[...], w_out[...]) + b_out[...]
    n, scale = standardize(middle)
    normed = (n * gain[...] + shift[...]).astype(bf16)
    normed_out[...] = normed
    ff = w_up.shape[1]
    total = middle + b_down[...]
    for part in range(ff // MODEL):
        at = slice(part * MODEL, (part + 1) * MODEL)
        u = nn(normed, w_up[:, at]) + b_up[:, at]
        u2 = u * u
        t = jnp.tanh(u * (0.7978845608028654 + 0.035677408136300125 * u2))
        half = 0.5 + 0.5 * t
        act = (u * half).astype(bf16)
        active_out[:, at] = act
        rise = 0.7978845608028654 + 0.10703222440890037 * u2
        slope[:, at] = (half + 0.5 * u * (1.0 - t * t) * rise).astype(bf16)
        total = total + nn(act, w_down[at, :])
    total = total.astype(bf16)
    for i in range(per):
        result[placing[step * per + i]] = total[i * STRETCH : (i + 1) * STRETCH, :]

    cot = cot_out[...]
    up_grad = jnp.zeros((TILE, MODEL), f32)
    for part in range(ff // MODEL):
        at = slice(part * MODEL, (part + 1) * MODEL)
        g = (nt(cot, w_down[at, :]) * slope[:, at].astype(f32)).astype(bf16)
        hidden_out[:, at] = g
        vec_out[0:1, at] += jnp.sum(g.astype(f32), axis=0, keepdims=True)
        up_grad = up_grad + nt(g, w_up[:, at])
    cot_f = cot.astype(f32)
    vec_out[1:2, :MODEL] += jnp.sum(up_grad * n, axis=0, keepdims=True)
    vec_out[1:2, MODEL : 2 * MODEL] += jnp.sum(up_grad, axis=0, keepdims=True)
    vec_out[1:2, 3 * MODEL : 4 * MODEL] += jnp.sum(cot_f, axis=0, keepdims=True)
    grad_middle = cot_f + norm_back(up_grad, gain[...], n, scale)
    middle_out[...] = grad_middle
    branch = grad_middle.astype(bf16)
    branch_out[...] = branch
    vec_out[1:2, 2 * MODEL : 3 * MODEL] += jnp.sum(branch.astype(f32), axis=0, keepdims=True)
    grad_att = nt(branch, w_out[...])
    lane = lanes(CHUNK, PAIR) % HEAD_DIM
    for chunk in range(TILE // CHUNK):
        rows = slice(chunk * CHUNK, (chunk + 1) * CHUNK)
        o0 = flag(opened[step * per + 2 * chunk])
        o1 = flag(opened[step * per + 2 * chunk + 1])
        keep = jnp.where(upper, o0, o1)
        for pair in range(PAIRS):
            inv = inv_scr[rows, col(pair)]
            gn = (grad_att[rows, col(pair)].astype(bf16).astype(f32) * inv).astype(bf16)
            product = gn.astype(f32) * att_scr[rows, col(pair)]
            high = product.astype(bf16)
            low_part = (product - high.astype(f32)).astype(bf16)
            gd = -(nn(high, ones_head) + nn(low_part, ones_head))
            gd_high = gd.astype(bf16)
            gd_low = (gd - gd_high.astype(f32)).astype(bf16)
            zero = jnp.zeros_like(gd_high)
            gn_out[rows, col(pair)] = gn
            gd_out[rows, col(pair)] = jnp.where(
                (lane == 0) | (lane == 2), gd_high, jnp.where(lane == 1, gd_low, zero)
            )
            q = qkv_ref[rows, pair * PAIR : (pair + 1) * PAIR].astype(f32) * keep
            back[pair] += tn(q.astype(bf16), gn)
            back_sum[:, col(pair)] += jnp.sum(q * gd, axis=0, keepdims=True)

    @pl.when(step == pl.num_programs(0) - 1)
    def _():
        for pair in range(PAIRS):
            pack_state(state_out, pair, back[pair], back_sum[:, col(pair)])


def run_mid(placing, restart, opened, x, qkv, cot, inc, w_out, w_up, w_down, vectors):
    count, width = x.shape
    ff = w_up.shape[1]
    stretches = count // STRETCH
    chunks = count // CHUNK
    b_out, gain, shift, b_up, b_down = vectors
    return pl.pallas_call(
        mid_kernel,
        name="middle",
        grid_spec=pltpu.PrefetchScalarGridSpec(
            num_scalar_prefetch=3,
            grid=(count // TILE,),
            in_specs=[
                tiled(width),
                tiled(3 * MODEL),
                fixed(cot.shape),
                fixed(inc.shape),
                fixed(w_out.shape),
                fixed(w_up.shape),
                fixed(w_down.shape),
                fixed(b_out.shape),
                fixed(gain.shape),
                fixed(shift.shape),
                fixed(b_up.shape),
                fixed(b_down.shape),
            ],
            out_specs=[
                whole((stretches, STRETCH, width)),
                tiled(ff),
                tiled(ff),
                tiled(width),
                tiled(MODEL),
                tiled(width),
                tiled(MODEL),
                tiled(MODEL),
                tiled(width),
                pl.BlockSpec((TILE // CHUNK, MODEL, 3 * PAIR), lambda i, *_: (i, 0, 0)),
                whole((HEAD_DIM + 8, MODEL)),
                whole((8, ff)),
                tiled(width),
            ],
            scratch_shapes=[
                pltpu.VMEM((PAIRS, PAIR, 2 * PAIR), f32),
                pltpu.VMEM((PAIRS, PAIR, PAIR), f32),
                pltpu.VMEM((1, MODEL), f32),
                pltpu.VMEM((TILE, ff), bf16),
                pltpu.VMEM((TILE, MODEL), f32),
                pltpu.VMEM((TILE, MODEL), f32),
            ],
        ),
        out_shape=[
            jax.ShapeDtypeStruct((stretches, STRETCH, width), bf16),
            jax.ShapeDtypeStruct((count, ff), bf16),
            jax.ShapeDtypeStruct((count, ff), bf16),
            jax.ShapeDtypeStruct((count, width), bf16),
            jax.ShapeDtypeStruct((count, MODEL), bf16),
            jax.ShapeDtypeStruct((count, width), bf16),
            jax.ShapeDtypeStruct((count, MODEL), bf16),
            jax.ShapeDtypeStruct((count, MODEL), bf16),
            jax.ShapeDtypeStruct((count, width), f32),
            jax.ShapeDtypeStruct((chunks, MODEL, 3 * PAIR), bf16),
            jax.ShapeDtypeStruct((HEAD_DIM + 8, MODEL), f32),
            jax.ShapeDtypeStruct((8, ff), f32),
            jax.ShapeDtypeStruct((count, width), bf16),
        ],
        compiler_params=params(),
        cost_estimate=pl.CostEstimate(
            flops=2 * count * width * (2 * MODEL + 4 * ff) + (4 << 30),
            bytes_accessed=28 << 20,
            transcendentals=count * ff,
        ),
    )(placing, restart, opened, x, qkv, cot, inc, w_out, w_up, w_down, b_out, gain, shift, b_up, b_down)


def back_kernel(
    placing,
    restart,
    x_ref,
    qkv_ref,
    gn_ref,
    gd_ref,
    middle_ref,
    states_ref,
    inc_ref,
    weight,
    gain,
    grad_rows,
    mixed_out,
    vec_out,
    carry,
):
    step = pl.program_id(0)
    per = TILE // STRETCH
    tile = pl.num_programs(0) - 1 - step

    @pl.when(step == 0)
    def _():
        for pair in range(PAIRS):
            carry[pair] = unpack_state(inc_ref[...], pair)
        vec_out[...] = jnp.zeros_like(vec_out)

    block = same_head()
    wide_block = jnp.concatenate([block, block], axis=1)
    upper = sublanes(CHUNK, PAIR) < STRETCH
    lane = lanes(CHUNK, PAIR)
    inner = lane % HEAD_DIM
    marks = jnp.where(inner < 2, 1.0, 0.0).astype(bf16)
    mark_low = jnp.where(lane < 2, 1.0, 0.0).astype(bf16)
    mark_high = jnp.where((lane == HEAD_DIM) | (lane == HEAD_DIM + 1), 1.0, 0.0).astype(bf16)
    marks_both = jnp.concatenate([mark_low, mark_high], axis=0)
    ones_head = jnp.where(block, 1.0, 0.0).astype(bf16)

    for chunk in reversed(range(TILE // CHUNK)):
        rows = slice(chunk * CHUNK, (chunk + 1) * CHUNK)
        r0 = flag(restart[tile * per + 2 * chunk])
        r1 = flag(restart[tile * per + 2 * chunk + 1])
        r2 = flag(restart[tile * per + 2 * chunk + 2])
        mask = causal(r1, False)
        mask_t = causal(r1, True)
        keep_low = jnp.where(upper, 1.0, 1.0 - r1)
        keep_key = jnp.where(upper, 1.0 - r1, 1.0)
        for pair in range(PAIRS):
            q = qkv_ref[rows, pair * PAIR : (pair + 1) * PAIR]
            k = qkv_ref[rows, MODEL + pair * PAIR : MODEL + (pair + 1) * PAIR]
            v = qkv_ref[rows, 2 * MODEL + pair * PAIR : 2 * MODEL + (pair + 1) * PAIR]
            gn = gn_ref[rows, col(pair)]
            gdx = gd_ref[rows, col(pair)]
            state = states_ref[chunk, pair * PAIR : (pair + 1) * PAIR, :]
            grown = carry[pair] * (1.0 - r2)
            grown_s = grown[:, :PAIR].astype(bf16)
            grown_low = (grown[:, :PAIR] - grown_s.astype(f32)).astype(bf16)
            grown_z = grown[:, PAIR:]
            z_high = grown_z.astype(bf16)
            z_low = (grown_z - z_high.astype(f32)).astype(bf16)
            zero = jnp.zeros_like(z_high)
            grown_z = jnp.where(inner == 0, z_high, jnp.where(inner == 1, z_low, zero))
            k2 = by_head(k, CHUNK)
            q2 = by_head(q, CHUNK)
            v2 = by_head(v, CHUNK)
            gn2 = by_head(gn, CHUNK)
            gd2 = by_head(gdx, CHUNK)
            both = jnp.concatenate([gn, gdx], axis=1)
            mixing_t = (nt(k, q2) * mask_t).astype(bf16)
            g_mix = (nt(both, jnp.concatenate([v2, marks_both], axis=1)) * mask).astype(bf16)
            v_marks = jnp.concatenate([v, marks], axis=1)
            g_mix_t = (nt(v_marks, jnp.concatenate([gn2, gd2], axis=1)) * mask_t).astype(bf16)
            dq = nn(g_mix, k2) + (nt(both, state[:, : 2 * PAIR]) + nt(gn, state[:, 2 * PAIR :])) * keep_low
            grown_x = jnp.concatenate([grown_s, grown_z], axis=1)
            dk = nn(g_mix_t, q2) + (nt(v_marks, grown_x) + nt(v, grown_low)) * keep_key
            dv = nn(mixing_t, gn2) + nn(k, grown_s) * keep_key
            q_keep = (q.astype(f32) * keep_low).astype(bf16)
            added_s = tn(q_keep, gn)
            gd_all = nn(gdx * marks, ones_head)
            added_z = jnp.sum(q.astype(f32) * keep_low * gd_all, axis=0, keepdims=True)
            eye = sublanes(PAIR, PAIR) == lane
            diagonal = jnp.where(eye, added_z, 0.0)
            d_high = diagonal.astype(bf16)
            d_low = (diagonal - d_high.astype(f32)).astype(bf16)
            added_z = nn(d_high, ones_head) + nn(d_low, ones_head)
            added = jnp.concatenate([jnp.where(block, added_s, 0.0), added_z], axis=1)
            carry[pair] = (grown * (1.0 - r1) + added) * (1.0 - r0)
            mixed_out[rows, pair * PAIR : (pair + 1) * PAIR] = (
                dq * jnp.minimum(q.astype(f32), 1.0)
            ).astype(bf16)
            mixed_out[rows, MODEL + pair * PAIR : MODEL + (pair + 1) * PAIR] = (
                dk * jnp.minimum(k.astype(f32), 1.0)
            ).astype(bf16)
            mixed_out[rows, 2 * MODEL + pair * PAIR : 2 * MODEL + (pair + 1) * PAIR] = dv.astype(bf16)

    mixed = mixed_out[...]
    vec_out[0:1, :] += jnp.sum(mixed.astype(f32), axis=0, keepdims=True)
    upstream = nt(mixed, weight[...])
    n, scale = standardize(x_ref[...].astype(f32))
    vec_out[1:2, :MODEL] += jnp.sum(upstream * n, axis=0, keepdims=True)
    vec_out[1:2, MODEL : 2 * MODEL] += jnp.sum(upstream, axis=0, keepdims=True)
    total = (middle_ref[...] + norm_back(upstream, gain[...], n, scale)).astype(bf16)
    for i in range(per):
        grad_rows[placing[tile * per + i]] = total[i * STRETCH : (i + 1) * STRETCH, :]


def run_back(placing, restart, x, qkv, gn, gd, middle, states, inc, weight, gain):
    count, width = x.shape
    stretches = count // STRETCH
    steps = count // TILE
    return pl.pallas_call(
        back_kernel,
        name="back",
        grid_spec=pltpu.PrefetchScalarGridSpec(
            num_scalar_prefetch=2,
            grid=(steps,),
            in_specs=[
                tiled(width, steps),
                tiled(3 * MODEL, steps),
                tiled(MODEL, steps),
                tiled(MODEL, steps),
                tiled(width, steps),
                pl.BlockSpec(
                    (TILE // CHUNK, MODEL, 3 * PAIR), lambda i, *_: (steps - 1 - i, 0, 0)
                ),
                fixed(inc.shape),
                fixed(weight.shape),
                fixed(gain.shape),
            ],
            out_specs=[
                whole((stretches, STRETCH, width)),
                tiled(3 * MODEL, steps),
                whole((8, 3 * MODEL)),
            ],
            scratch_shapes=[pltpu.VMEM((PAIRS, PAIR, 2 * PAIR), f32)],
        ),
        out_shape=[
            jax.ShapeDtypeStruct((stretches, STRETCH, width), bf16),
            jax.ShapeDtypeStruct((count, 3 * MODEL), bf16),
            jax.ShapeDtypeStruct((8, 3 * MODEL), f32),
        ],
        compiler_params=params(),
        cost_estimate=pl.CostEstimate(
            flops=2 * count * width * 3 * MODEL + (6 << 30), bytes_accessed=14 << 20, transcendentals=0
        ),
    )(placing, restart, x, qkv, gn, gd, middle, states, inc, weight, gain)


def permute_kernel(slot, source, target, *, inverse):
    group = pl.program_id(0)
    for i in range(source.shape[1]):
        place = slot[group, i]
        if inverse:
            target[0, i] = source[0, place]
        else:
            target[0, place] = source[0, i]


def run_permute(slot, blocks, inverse):
    shape = (1,) + blocks.shape[1:]
    spec = pl.BlockSpec(shape, lambda i, *_: (i, 0, 0, 0))
    return pl.pallas_call(
        functools.partial(permute_kernel, inverse=inverse),
        name="permute",
        grid_spec=pltpu.PrefetchScalarGridSpec(
            num_scalar_prefetch=1,
            grid=(blocks.shape[0],),
            in_specs=[spec],
            out_specs=spec,
        ),
        out_shape=jax.ShapeDtypeStruct(blocks.shape, blocks.dtype),
        compiler_params=params(),
        cost_estimate=pl.CostEstimate(
            flops=0, bytes_accessed=2 * blocks.size * 2, transcendentals=0
        ),
    )(slot, blocks)


def index_tables(lengths, stretch_order, count):
    fsdp = lax.axis_size("fsdp")
    groups = lax.axis_size("dp")
    device = lax.axis_index(BOTH)
    base = device * count
    within = jnp.arange(count, dtype=jnp.int32)
    mine = base + within
    place = jnp.arange(stretch_order.shape[1], dtype=jnp.int32)
    here = place[None, None, :]
    landing = jnp.sum(
        jnp.where(stretch_order[:, None, :] == mine[None, :, None], here, 0), axis=-1
    )
    slot = jnp.sum((landing[:, None, :] < landing[:, :, None]).astype(jnp.int32), axis=-1)
    arrival = jnp.sum(
        jnp.where(here == mine[None, :, None], stretch_order[:, None, :], 0), axis=-1
    )
    source = arrival // count // fsdp
    ahead = (source[:, None, :] == source[:, :, None]) & (
        within[None, None, :] < within[None, :, None]
    )
    placing = source * (count // groups) + jnp.sum(ahead.astype(jnp.int32), axis=-1)
    index = jnp.arange(lengths.shape[1], dtype=jnp.int32)
    starts = jnp.sum(
        jnp.where(index[None, None, :] < index[None, :, None], lengths[:, None, :], 0), axis=-1
    )
    edge = base + jnp.arange(count + 1, dtype=jnp.int32)
    restart = jnp.any(starts[:, None, :] == edge[None, :, None], axis=-1).astype(jnp.int32)
    restart = jnp.where(edge[None, :] == stretch_order.shape[1], 1, restart)
    opened = 1 - jnp.any(
        (starts[:, None, :] >= base) & (starts[:, None, :] <= mine[None, :, None]), axis=-1
    ).astype(jnp.int32)
    last = base + count - 1
    closing = 1 - jnp.any(
        (starts[:, None, :] > mine[None, :, None]) & (starts[:, None, :] <= last), axis=-1
    ).astype(jnp.int32)
    hops = -(-(LONGEST - 1) // count)
    hop = jnp.arange(hops, dtype=jnp.int32)
    reach_back = base - 1 - hop * count
    from_before = 1.0 - jnp.any(
        (starts[:, None, :] > reach_back[None, :, None]) & (starts[:, None, :] <= base), axis=-1
    ).astype(f32)
    reach_on = base + (hop + 1) * count
    from_after = 1.0 - jnp.any(
        (starts[:, None, :] > last) & (starts[:, None, :] <= reach_on[None, :, None]), axis=-1
    ).astype(f32)
    return slot, placing, restart, opened, closing, from_before, from_after


def exchange(states, weights, forward):
    size = lax.axis_size("fsdp")
    total = None
    for hop in range(weights.shape[1]):
        step = hop + 1
        pairs = [
            (i, i + step) if forward else (i + step, i) for i in range(size - step)
        ]
        if not pairs:
            continue
        got = lax.ppermute(states, "fsdp", pairs).astype(f32) * weights[:, hop, None, None]
        total = got if total is None else total + got
    if total is None:
        total = jnp.zeros(states.shape, f32)
    return total


def halving_stages():
    stages = []
    dp, fsdp = lax.axis_size("dp"), lax.axis_size("fsdp")
    if dp > 1:
        stages.append(("dp", 1))
    bit = 1
    while bit < fsdp:
        stages.append(("fsdp", bit))
        bit *= 2
    bit = 2
    while bit < dp:
        stages.append(("dp", bit))
        bit *= 2
    return stages


def bit_dims():
    dims = []
    for axis in BOTH:
        bit = lax.axis_size(axis) // 2
        while bit:
            dims.append((axis, bit))
            bit //= 2
    return dims


def scatter_sum(x):
    dims = bit_dims()
    x = x.reshape((2,) * len(dims) + x.shape[1:])
    for axis, bit in halving_stages():
        dim = dims.index((axis, bit))
        size = lax.axis_size(axis)
        mine = (lax.axis_index(axis) // bit) % 2
        send = lax.dynamic_index_in_dim(x, 1 - mine, dim, True)
        keep = lax.dynamic_index_in_dim(x, mine, dim, True)
        got = lax.ppermute(send, axis, [(i, i ^ bit) for i in range(size)])
        x = (keep.astype(f32) + got.astype(f32)).astype(x.dtype)
    return x.reshape(x.shape[len(dims) :]).astype(f32)


def gather_all(x):
    dims = bit_dims()
    x = x.reshape((1,) * len(dims) + x.shape)
    for axis, bit in reversed(halving_stages()):
        dim = dims.index((axis, bit))
        size = lax.axis_size(axis)
        mine = (lax.axis_index(axis) // bit) % 2
        got = lax.ppermute(x, axis, [(i, i ^ bit) for i in range(size)])
        first = jnp.where(mine == 0, x, got)
        second = jnp.where(mine == 0, got, x)
        x = jnp.concatenate([first, second], axis=dim)
    return x.reshape((-1,) + x.shape[len(dims) + 1 :])


def scatter_all(x):
    return lax.psum_scatter(x, BOTH, scatter_dimension=0, tiled=True)


def to_dp(blocks):
    return lax.all_to_all(blocks, "dp", split_axis=0, concat_axis=0, tiled=True)


def body(
    tokens,
    cotangent,
    lengths,
    stretch_order,
    ln1_gain,
    ln1_bias,
    w_qkv,
    b_qkv,
    w_out,
    b_out,
    ln2_gain,
    ln2_bias,
    w_up,
    b_up,
    w_down,
    b_down,
):
    micro, rows, width = tokens.shape
    count = rows // STRETCH
    devices = lax.axis_size(BOTH)
    slot, placing, restart, opened, closing, from_before, from_after = index_tables(
        lengths, stretch_order, count
    )
    sent_rows = run_permute(slot, tokens.reshape(micro, count, STRETCH, width), False)
    sent_grads = run_permute(slot, cotangent.reshape(micro, count, STRETCH, width), False)
    moved = [to_dp(sent_rows[m]) for m in range(micro)]
    cots = [to_dp(sent_grads[m]) for m in range(micro)]
    small = (ln1_gain, ln1_bias, b_qkv, b_out, ln2_gain, ln2_bias, b_up, b_down)
    packed = gather_all(jnp.concatenate(small).reshape(1, -1))
    vectors, at = [], 0
    for item in small:
        size = item.shape[0]
        vectors.append(packed[:, at : at + size].reshape(1, -1).astype(f32))
        at += size
    gain_one, shift_one, bias_qkv, bias_out, gain_two, shift_two, bias_up, bias_down = vectors
    qkv_all = gather_all(w_qkv)
    out_all = gather_all(w_out)
    up_all = gather_all(w_up)
    down_all = gather_all(w_down)

    firsts = [
        run_qkv(placing[m], closing[m], moved[m], qkv_all, bias_qkv, gain_one, shift_one)
        for m in range(micro)
    ]
    incoming = exchange(jnp.stack([f[3] for f in firsts]), from_before, True)
    mids = [
        run_mid(
            placing[m],
            restart[m],
            opened[m],
            firsts[m][0],
            firsts[m][2],
            cots[m],
            incoming[m],
            out_all,
            up_all,
            down_all,
            (bias_out, gain_two, shift_two, bias_up, bias_down),
        )
        for m in range(micro)
    ]
    outgoing = exchange(jnp.stack([f[10] for f in mids]), from_after, False)
    backs = [
        run_back(
            placing[m],
            restart[m],
            firsts[m][0],
            firsts[m][2],
            mids[m][6],
            mids[m][7],
            mids[m][8],
            mids[m][9],
            outgoing[m],
            qkv_all,
            gain_one,
        )
        for m in range(micro)
    ]
    home = jnp.stack([to_dp(mids[m][0]) for m in range(micro)])
    home_grad = jnp.stack([to_dp(backs[m][0]) for m in range(micro)])
    result = run_permute(slot, home, True).reshape(micro, rows, width)
    input_grad = run_permute(slot, home_grad, True).reshape(micro, rows, width)

    def summed(pairs):
        total = None
        for left, right in pairs:
            part = tn(left, right)
            total = part if total is None else total + part
        return total

    def owned(total):
        return scatter_sum(total.astype(bf16).reshape(devices, -1, total.shape[1]))

    grad_up = owned(summed([(mids[m][3], mids[m][2]) for m in range(micro)]))
    grad_down = owned(summed([(mids[m][1], mids[m][12]) for m in range(micro)]))
    grad_out = owned(summed([(mids[m][4], mids[m][5]) for m in range(micro)]))
    grad_qkv = owned(summed([(firsts[m][1], backs[m][1]) for m in range(micro)]))
    vec_mid = sum(mids[m][11] for m in range(micro))
    vec_back = sum(backs[m][2] for m in range(micro))
    vec = (
        vec_back[1, :MODEL],
        vec_back[1, MODEL : 2 * MODEL],
        vec_back[0, : 2 * MODEL],
        vec_back[0, 2 * MODEL :],
        vec_mid[1, 2 * MODEL : 3 * MODEL],
        vec_mid[1, :MODEL],
        vec_mid[1, MODEL : 2 * MODEL],
        vec_mid[0],
        vec_mid[1, 3 * MODEL :],
    )
    bundle = scatter_all(
        jnp.concatenate([item.reshape(devices, -1) for item in vec], axis=1)
    ).reshape(-1)
    owned_vec, at = [], 0
    for item in vec:
        size = item.shape[0] // devices
        owned_vec.append(bundle[at : at + size])
        at += size
    g_gain1, g_bias1, g_qk, g_value, g_bout, g_gain2, g_bias2, g_bup, g_bdown = owned_vec
    return (
        result,
        input_grad,
        g_gain1,
        g_bias1,
        grad_qkv,
        g_qk,
        g_value,
        grad_out,
        g_bout,
        g_gain2,
        g_bias2,
        grad_up,
        g_bup,
        grad_down,
        g_bdown,
    )


def solution(mesh):
    rows = P(None, BOTH, None)
    vector = P(BOTH)
    matrix = P(BOTH, None)
    in_specs = (
        rows, rows, P(), P(), vector, vector, matrix, vector, matrix, vector, vector, vector,
        matrix, vector, matrix, vector,
    )
    out_specs = (
        rows, rows, vector, vector, matrix, vector, vector, matrix, vector, vector, vector,
        matrix, vector, matrix, vector,
    )
    return jax.shard_map(body, mesh=mesh, in_specs=in_specs, out_specs=out_specs, check_vma=False)
```

time: 1710 us -> 639 us (0.37)
  matrix products: 481 us -> 36.1 us
  blocking collectives: 429 us -> 47.2 us
  local copies, waits for them, and re-layouts: 341 us -> 39.7 us
  Pallas kernels: 0 us -> 201 us
  waiting for transfers between devices: 240 us -> 132 us
  other arithmetic: 123 us -> 41.2 us
  starting transfers between devices: 51.8 us -> 130 us
  between operations: 20.7 us -> 2.43 us
    dot_general x102 -> x12, matrix products: 481 us -> 36.1 us  [tn(): lax.dot_general(a, b, (((0,), (0,)), ((), ())), preferred_element_type=f32)]
    all_gather x7 -> x0, blocking collectives: 319 us -> none  [the longest x6 245 us: carried_in(): gathered = jax.tree.map(lambda a: lax.all_gather(a, axis), part)]
    pallas_call x0 -> x13, Pallas kernels: none -> 201 us  [the longest x3 87.2 us: run_mid(): pl.pallas_call(mid_kernel, name='middle', grid_spec=pltpu.PrefetchScalarG...]
    reduce_scatter x4 -> x0, waiting for transfers between devices: 183 us -> none  [the longest x1 144 us: body(): lax.psum_scatter(totals[9], ('dp', 'fsdp'), scatter_dimension=0, tiled=True)]
    ppermute x0 -> x51, waiting for transfers between devices: none -> 99 us  [the longest x20 55.5 us: scatter_sum(): got = lax.ppermute(send, axis, [(i, i ^ bit) for i in range(size)])]
    reshape x24 -> x1, local copies, waits for them, and re-layouts: 97.8 us -> 0.03 us  [gather_all(): return x.reshape((-1,) + x.shape[len(dims) + 1:])]
    ppermute x0 -> x51, starting transfers between devices: none -> 81.6 us  [the longest x20 41.8 us: scatter_sum(): got = lax.ppermute(send, axis, [(i, i ^ bit) for i in range(size)])]
    unnamed x3 -> x1, blocking collectives: 110 us -> 47.2 us
  transfers between devices with their start and end apart: 25 -> 63, of which waited for: 9 -> 27; matrix products, arithmetic and copies ran while one was open for 45% -> 17% of each run, Pallas kernels for 0% -> 32%
where the time goes in v1:
time: 639 us; the launch traced here: 629 us
  Pallas kernels  201 us (31%)
  waiting for transfers between devices  132 us (21%)
  starting transfers between devices  130 us (20%)
  blocking collectives  47.2 us (7%)
  other arithmetic  41.2 us (6%)
  local copies, waits for them, and re-layouts  39.7 us (6%)
  matrix products  36.1 us (6%)
    pallas_call x3, Pallas kernels, run_mid(): pl.pallas_call(mid_kernel, name='middle', grid_spec=pltpu.PrefetchScalarG...  87.2 us
    pallas_call x3, Pallas kernels, run_back(): pl.pallas_call(back_kernel, name='back', grid_spec=pltpu.PrefetchScalarGr...  69.3 us
    ppermute x20, waiting for transfers between devices, scatter_sum(): got = lax.ppermute(send, axis, [(i, i ^ bit) for i in range(size)])  55.5 us
    all_to_all x12, starting transfers between devices, to_dp(): return lax.all_to_all(blocks, 'dp', split_axis=0, concat_axis=0, tiled=True)  48.2 us
    unnamed x1, blocking collectives  47.2 us
    ppermute x20, starting transfers between devices, scatter_sum(): got = lax.ppermute(send, axis, [(i, i ^ bit) for i in range(size)])  41.8 us
    dot_general x12, matrix products, tn(): lax.dot_general(a, b, (((0,), (0,)), ((), ())), preferred_element_type=f32)  36.1 us
    all_to_all x12, waiting for transfers between devices, to_dp(): return lax.all_to_all(blocks, 'dp', split_axis=0, concat_axis=0, tiled=True)  32.7 us
  transfers between devices with their start and end apart: 63, of which 27 were waited for; matrix products, arithmetic and copies ran while one was open for 17% of the time, Pallas kernels for 32%

profile of v1, /device:TPU:0, one launch (start us, length us, event | category | flops | bytes accessed | tf_op | source)
XLA Modules:
  0.0 628.9 jit_solution(9031770159687630947)
XLA Ops:
  0.6 5.4 concatenate.86
  14.9 5.1 permute.4
  20.0 3.6 slice_bitcast_fusion.5
  23.7 4.3 all-to-all-start.3
  30.3 5.1 permute.5
  35.4 3.6 slice_bitcast_fusion.4
  67.9 7.8 %collective-permute-done.1 = bf16[2,1,1,1,1,16,1536]{6,5,4,3,2,1,0:T(8,128)(2,1)S(1)} collective-permute-done((bf16[2,1,1,1,1,16,1536]{6,5,4,3,2,1,0:T(8,128)(2,1)S(1)}, bf16[2,1,1,1,1,16,1536]{6,5,4,3,2,1,0:T(8,128)(2,1)S(1)}, u32[]{:S(2)}, u32[]{:S(2)}) %collective-permute-start.1) | collective-permute-done | bytes 98336 | tf_op jit(solution)/shard_map/ppermute | solution.py:749
  87.2 4.0 collective-permute-done.25
  92.9 3.8 collective-permute-done.20
  98.7 4.3 all-to-all-start.2
  109.7 8.1 %all-to-all-done.2.rows = bf16[16,64,512]{2,1,0:T(8,128)(2,1)} async-done(((bf16[16,64,512]{2,1,0:T(8,128)(2,1)}), bf16[16,64,512]{2,1,0:T(8,128)(2,1)}, u32[]{:S(2)}, u32[]{:S(2)}) %all-to-all-start.2) | async-done | bytes 1048608 | tf_op jit(solution)/shard_map/all_to_all | solution.py:761
  117.8 4.2 all-to-all-start
  124.6 7.9 %qkv.4 = (bf16[1024,512]{1,0:T(8,128)(2,1)}, bf16[1024,512]{1,0:T(8,128)(2,1)}, bf16[1024,1536]{1,0:T(8,128)(2,1)}, f32[72,512]{1,0:T(8,128)}) custom-call(s32[16]{0:T(128)} %get-tuple-element.244.placing, s32[16]{0:T(128)} %get-tuple-element.241.closing, bf16[16,64,512]{2,1,0:T(8,128)(2,1)} %all-to-all-done.2.rows, bf16[512,1536]{1,0:T(8,128)(2,1)} %bitcast.167, ...), custom_call_target="tpu_custom_call" | custom-call | flops 1610612736 | bytes 8388608 | tf_op jit(solution)/shard_map/qkv/pallas_call | solution.py:172
  132.5 7.8 %qkv.5 = (bf16[1024,512]{1,0:T(8,128)(2,1)}, bf16[1024,512]{1,0:T(8,128)(2,1)}, bf16[1024,1536]{1,0:T(8,128)(2,1)}, f32[72,512]{1,0:T(8,128)}) custom-call(s32[16]{0:T(128)} %get-tuple-element.243.placing, s32[16]{0:T(128)} %get-tuple-element.240.closing, bf16[16,64,512]{2,1,0:T(8,128)(2,1)} %all-to-all-done.3.rows, bf16[512,1536]{1,0:T(8,128)(2,1)} %bitcast.168, ...), custom_call_target="tpu_custom_call" | custom-call | flops 1610612736 | bytes 8388608 | tf_op jit(solution)/shard_map/qkv/pallas_call | solution.py:172
  140.3 4.3 all-to-all-start.1
  144.6 8.1 %qkv.3 = (bf16[1024,512]{1,0:T(8,128)(2,1)}, bf16[1024,512]{1,0:T(8,128)(2,1)}, bf16[1024,1536]{1,0:T(8,128)(2,1)}, f32[72,512]{1,0:T(8,128)}) custom-call(s32[16]{0:T(128)} %get-tuple-element.242.placing, s32[16]{0:T(128)} %get-tuple-element.239.closing, bf16[16,64,512]{2,1,0:T(8,128)(2,1)} %all-to-all-done.rows, bf16[512,1536]{1,0:T(8,128)(2,1)} %bitcast.169, ...), custom_call_target="tpu_custom_call" | custom-call | flops 1610612736 | bytes 8388608 | tf_op jit(solution)/shard_map/qkv/pallas_call | solution.py:172
  157.8 4.3 collective-permute-start.10
  166.6 9.0 %collective-permute-done.11 = f32[3,72,512]{2,1,0:T(8,128)S(1)} collective-permute-done((f32[3,72,512]{2,1,0:T(8,128)S(1)}, f32[3,72,512]{2,1,0:T(8,128)S(1)}, u32[]{:S(2)}, u32[]{:S(2)}) %collective-permute-start.11) | collective-permute-done | bytes 442400 | tf_op jit(solution)/shard_map/ppermute | solution.py:695
  179.9 4.0 all-to-all-start.7
  183.9 29.0 %middle.3 = (bf16[16,64,512]{2,1,0:T(8,128)(2,1)}, bf16[1024,2048]{1,0:T(8,128)(2,1)}, bf16[1024,2048]{1,0:T(8,128)(2,1)}, bf16[1024,512]{1,0:T(8,128)(2,1)}, bf...) custom-call(s32[16]{0:T(128)} %get-tuple-element.242.placing, ...), custom_call_target="tpu_custom_call" | custom-call | flops 13958643712 | bytes 29360128 | tf_op jit(solution)/shard_map/middle/pallas_call | solution.py:391
  216.5 29.0 %middle.5 = (bf16[16,64,512]{2,1,0:T(8,128)(2,1)}, bf16[1024,2048]{1,0:T(8,128)(2,1)}, bf16[1024,2048]{1,0:T(8,128)(2,1)}, bf16[1024,512]{1,0:T(8,128)(2,1)}, bf...) custom-call(s32[16]{0:T(128)} %get-tuple-element.243.placing, ...), custom_call_target="tpu_custom_call" | custom-call | flops 13958643712 | bytes 29360128 | tf_op jit(solution)/shard_map/middle/pallas_call | solution.py:391
  249.1 29.2 %middle.4 = (bf16[16,64,512]{2,1,0:T(8,128)(2,1)}, bf16[1024,2048]{1,0:T(8,128)(2,1)}, bf16[1024,2048]{1,0:T(8,128)(2,1)}, bf16[1024,512]{1,0:T(8,128)(2,1)}, bf...) custom-call(s32[16]{0:T(128)} %get-tuple-element.244.placing, ...), custom_call_target="tpu_custom_call" | custom-call | flops 13958643712 | bytes 29360128 | tf_op jit(solution)/shard_map/middle/pallas_call | solution.py:391
  296.7 4.1 add_convert_fusion.1
  310.4 10.9 %collective-permute-start.37 = (bf16[2,1,2,2,1,16,512]{6,5,4,3,2,1,0:T(8,128)(2,1)S(1)}, bf16[2,1,2,2,1,16,512]{6,5,4,3,2,1,0:T(8,128)(2,1)S(1)}, u32[]{:S(2)}, u32[]{:S(2)}) collective-permute-start(bf16[2,1,2,2,1,16,512]{6,5,4,3,2,1,0:T(8,128)(2,1)S(1)} %constant_dynamic-slice_fusion.12), channel_id=1, source_target_pairs={{0,1},{1,0},{2,3},{3,2},{4,5},{5,4},{6,7},{7,6},{8,9},{9,8},{10,11... | collective-permute-start | bytes 393224 | tf_op jit(solution)/shard_map/ppermute | solution.py:737
  322.3 17.8 %collective-permute-done.37 = bf16[2,1,2,2,1,16,512]{6,5,4,3,2,1,0:T(8,128)(2,1)S(1)} collective-permute-done((bf16[2,1,2,2,1,16,512]{6,5,4,3,2,1,0:T(8,128)(2,1)S(1)}, bf16[2,1,2,2,1,16,512]{6,5,4,3,2,1,0:T(8,128)(2,1)S(1)}, u32[]{:S(2)}, u32[]{:S(2)}) %collective-permute-start.37) | collective-permute-done | bytes 131104 | tf_op jit(solution)/shard_map/ppermute | solution.py:737
  340.2 11.0 %collective-permute-start.38 = (bf16[2,1,2,1,1,16,512]{6,5,4,3,2,1,0:T(8,128)(2,1)S(1)}, bf16[2,1,2,1,1,16,512]{6,5,4,3,2,1,0:T(8,128)(2,1)S(1)}, u32[]{:S(2)}, u32[]{:S(2)}) collective-permute-start(bf16[2,1,2,1,1,16,512]{6,5,4,3,2,1,0:T(8,128)(2,1)S(1)} %constant_dynamic-slice_fusion.11), channel_id=1, source_target_pairs={{0,2},{1,3},{2,0},{3,1},{4,6},{5,7},{6,4},{7,5},{8,10},{9,11},{10,... | collective-permute-start | bytes 196616 | tf_op jit(solution)/shard_map/ppermute | solution.py:737
  353.4 22.9 %back.4 = (bf16[16,64,512]{2,1,0:T(8,128)(2,1)}, bf16[1024,1536]{1,0:T(8,128)(2,1)}, f32[8,1536]{1,0:T(8,128)}) custom-call(s32[16]{0:T(128)} %get-tuple-element.244.placing, s32[17]{0:T(128)} %get-tuple-element.234.restart, bf16[1024,512]{1,0:T(8,128)(2,1)} %get-tuple-element.81.x_ref, bf16[1024,1536]{1,0:T(8,128)(2,1)} %get-tuple-element.82.qkv_ref, ...), custom_call_target="tpu_custom_call" | custom-call | flops 8053063680 | bytes 14680064 | tf_op jit(solution)/shard_map/back/pallas_call | solution.py:569
  376.3 23.0 %back.3 = (bf16[16,64,512]{2,1,0:T(8,128)(2,1)}, bf16[1024,1536]{1,0:T(8,128)(2,1)}, f32[8,1536]{1,0:T(8,128)}) custom-call(s32[16]{0:T(128)} %get-tuple-element.242.placing, s32[17]{0:T(128)} %get-tuple-element.232.restart, bf16[1024,512]{1,0:T(8,128)(2,1)} %get-tuple-element.75.x_ref, bf16[1024,1536]{1,0:T(8,128)(2,1)} %get-tuple-element.76.qkv_ref, ...), custom_call_target="tpu_custom_call" | custom-call | flops 8053063680 | bytes 14680064 | tf_op jit(solution)/shard_map/back/pallas_call | solution.py:569
  399.3 5.4 fusion.14
  404.7 23.4 %back.5 = (bf16[16,64,512]{2,1,0:T(8,128)(2,1)}, bf16[1024,1536]{1,0:T(8,128)(2,1)}, f32[8,1536]{1,0:T(8,128)}) custom-call(s32[16]{0:T(128)} %get-tuple-element.243.placing, s32[17]{0:T(128)} %get-tuple-element.233.restart, bf16[1024,512]{1,0:T(8,128)(2,1)} %get-tuple-element.84.x_ref, bf16[1024,1536]{1,0:T(8,128)(2,1)} %get-tuple-element.85.qkv_ref, ...), custom_call_target="tpu_custom_call" | custom-call | flops 8053063680 | bytes 14680064 | tf_op jit(solution)/shard_map/back/pallas_call | solution.py:569
  428.2 4.3 all-to-all-start.8
  433.3 5.0 convolution_add_fusion.1
  438.3 8.7 %all-to-all-done.8 = bf16[16,64,512]{2,1,0:T(8,128)(2,1)} async-done(((bf16[16,64,512]{2,1,0:T(8,128)(2,1)}), bf16[16,64,512]{2,1,0:T(8,128)(2,1)}, u32[]{:S(2)}, u32[]{:S(2)}) %all-to-all-start.8) | async-done | bytes 1048608 | tf_op jit(solution)/shard_map/all_to_all | solution.py:761
  447.0 4.2 all-to-all-start.6
  457.6 47.2 %all-reduce = f32[32,208]{1,0:T(8,128)S(1)} all-reduce(f32[32,208]{1,0:T(8,128)S(1)} %concatenate.107), channel_id=2, replica_groups=mesh['dp'=4,'fsdp'=8] {'dp','fsdp'}, use_global_device_ids=true, to_apply=%region_10.11.clone | all-reduce | flops 6656 | bytes 53248
  504.8 5.2 fusion
  510.0 3.7 all-to-all-start.11
  519.1 9.1 %all-to-all-done.11 = bf16[16,64,512]{2,1,0:T(8,128)(2,1)S(1)} async-done(((bf16[16,64,512]{2,1,0:T(8,128)(2,1)}), bf16[16,64,512]{2,1,0:T(8,128)(2,1)S(1)}, u32[]{:S(2)}, u32[]{:S(2)}) %all-to-all-start.11) | async-done | bytes 1048608 | tf_op jit(solution)/shard_map/all_to_all | solution.py:761
  534.3 12.1 %collective-permute-done.40 = bf16[1,1,1,1,1,16,512]{6,5,4,3,2,1,0:T(8,128)(2,1)S(1)} collective-permute-done((bf16[1,1,1,1,1,16,512]{6,5,4,3,2,1,0:T(8,128)(2,1)S(1)}, bf16[1,1,1,1,1,16,512]{6,5,4,3,2,1,0:T(8,128)(2,1)S(1)}, u32[]{:S(2)}, u32[]{:S(2)}) %collective-permute-start.40) | collective-permute-done | bytes 16416 | tf_op jit(solution)/shard_map/ppermute | solution.py:737
  550.6 5.1 permute.6
  555.7 4.4 all-to-all-start.10
  567.8 6.9 %all-to-all-done.10 = bf16[16,64,512]{2,1,0:T(8,128)(2,1)} async-done(((bf16[16,64,512]{2,1,0:T(8,128)(2,1)}), bf16[16,64,512]{2,1,0:T(8,128)(2,1)}, u32[]{:S(2)}, u32[]{:S(2)}) %all-to-all-start.10) | async-done | bytes 1048608 | tf_op jit(solution)/shard_map/all_to_all | solution.py:761
  574.6 3.8 pad_maximum_fusion.1.source
  578.5 5.2 permute.7
  589.9 7.9 %collective-permute-done.32 = bf16[2,1,2,2,1,16,1536]{6,5,4,3,2,1,0:T(8,128)(2,1)S(1)} collective-permute-done((bf16[2,1,2,2,1,16,1536]{6,5,4,3,2,1,0:T(8,128)(2,1)S(1)}, bf16[2,1,2,2,1,16,1536]{6,5,4,3,2,1,0:T(8,128)(2,1)S(1)}, u32[]{:S(2)}, u32[]{:S(2)}) %collective-permute-start.32) | collective-permute-done | bytes 393248 | tf_op jit(solution)/shard_map/ppermute | solution.py:737
  601.3 4.5 collective-permute-done.33
  609.0 4.9 collective-permute-done.48
  615.8 6.3 %collective-permute-done.44 = bf16[2,1,1,1,1,16,2048]{6,5,4,3,2,1,0:T(8,128)(2,1)S(1)} collective-permute-done((bf16[2,1,1,1,1,16,2048]{6,5,4,3,2,1,0:T(8,128)(2,1)S(1)}, bf16[2,1,1,1,1,16,2048]{6,5,4,3,2,1,0:T(8,128)(2,1)S(1)}, u32[]{:S(2)}, u32[]{:S(2)}) %collective-permute-start.44) | collective-permute-done | bytes 131104 | tf_op jit(solution)/shard_map/ppermute | solution.py:737
  (348 shorter events, 167.7 us)
Async XLA Ops:
  6.1 33.3 %collective-permute-start.5 = (bf16[1,1,1,1,1,1,208]{6,4,3,2,1,0,5:T(2,128)(2,1)S(1)}, bf16[1,1,1,1,1,1,208]{6,4,3,2,1,0,5:T(2,128)(2,1)S(1)}, u32[]{:S(2)}, u32[]{:S(2)}) collective-permute-start(bf16[1,1,1,1,1,1,208]{6,4,3,2,1,0,5:T(2,128)(2,1)S(1)} %reshape_reshape.15), channel_id=1, source_target_pairs={{0,16},{8,24},{16,0},{24,8},{1,17},{9,25},{17,1},{25,9},{2,18},{10... | collective-permute-start | bytes 1256 | tf_op jit(solution)/shard_map/ppermute | solution.py:749
  9.1 43.8 %collective-permute-start.13 = (bf16[1,1,1,1,1,16,512]{6,5,4,3,2,1,0:T(8,128)(2,1)}, bf16[1,1,1,1,1,16,512]{6,5,4,3,2,1,0:T(8,128)(2,1)S(1)}, u32[]{:S(2)}, u32[]{:S(2)}) collective-permute-start(bf16[1,1,1,1,1,16,512]{6,5,4,3,2,1,0:T(8,128)(2,1)} %bitcast.187), channel_id=1, source_target_pairs={{0,16},{8,24},{16,0},{24,8},{1,17},{9,25},{17,1},{25,9},{2,18},{10... | collective-permute-start | bytes 49160 | tf_op jit(solution)/shard_map/ppermute | solution.py:749
  9.2 53.6 %collective-permute-start = (bf16[1,1,1,1,1,16,1536]{6,5,4,3,2,1,0:T(8,128)(2,1)}, bf16[1,1,1,1,1,16,1536]{6,5,4,3,2,1,0:T(8,128)(2,1)S(1)}, u32[]{:S(2)}, u32[]{:S(2)}) collective-permute-start(bf16[1,1,1,1,1,16,1536]{6,5,4,3,2,1,0:T(8,128)(2,1)} %bitcast.186), channel_id=1, source_target_pairs={{0,16},{8,24},{16,0},{24,8},{1,17},{9,25},{17,1},{25,9},{2,18},{10... | collective-permute-start | bytes 147464 | tf_op jit(solution)/shard_map/ppermute | solution.py:749
  11.1 52.1 %collective-permute-start.23 = (bf16[1,1,1,1,1,64,512]{6,5,4,3,2,1,0:T(8,128)(2,1)}, bf16[1,1,1,1,1,64,512]{6,5,4,3,2,1,0:T(8,128)(2,1)S(1)}, u32[]{:S(2)}, u32[]{:S(2)}) collective-permute-start(bf16[1,1,1,1,1,64,512]{6,5,4,3,2,1,0:T(8,128)(2,1)} %bitcast.184), channel_id=1, source_target_pairs={{0,16},{8,24},{16,0},{24,8},{1,17},{9,25},{17,1},{25,9},{2,18},{10... | collective-permute-start | bytes 196616 | tf_op jit(solution)/shard_map/ppermute | solution.py:749
  11.2 54.7 %collective-permute-start.18 = (bf16[1,1,1,1,1,16,2048]{6,5,4,3,2,1,0:T(8,128)(2,1)}, bf16[1,1,1,1,1,16,2048]{6,5,4,3,2,1,0:T(8,128)(2,1)S(1)}, u32[]{:S(2)}, u32[]{:S(2)}) collective-permute-start(bf16[1,1,1,1,1,16,2048]{6,5,4,3,2,1,0:T(8,128)(2,1)} %bitcast.185), channel_id=1, source_target_pairs={{0,16},{8,24},{16,0},{24,8},{1,17},{9,25},{17,1},{25,9},{2,18},{10... | collective-permute-start | bytes 196616 | tf_op jit(solution)/shard_map/ppermute | solution.py:749
  23.7 75.0 %all-to-all-start.3 = ((bf16[16,64,512]{2,1,0:T(8,128)(2,1)}), bf16[16,64,512]{2,1,0:T(8,128)(2,1)}, u32[]{:S(2)}, u32[]{:S(2)}) async-start(bf16[16,64,512]{2,1,0:T(8,128)(2,1)} %get-tuple-element.160), calls=%async_computation.3 | async-start | bytes 2097152 | tf_op jit(solution)/shard_map/all_to_all | solution.py:761
  62.8 13.0 %collective-permute-start.1 = (bf16[2,1,1,1,1,16,1536]{6,5,4,3,2,1,0:T(8,128)(2,1)S(1)}, bf16[2,1,1,1,1,16,1536]{6,5,4,3,2,1,0:T(8,128)(2,1)S(1)}, u32[]{:S(2)}, u32[]{:S(2)}) collective-permute-start(bf16[2,1,1,1,1,16,1536]{6,5,4,3,2,1,0:T(8,128)(2,1)S(1)} %pad_maximum_fusion.21), channel_id=1, source_target_pairs={{0,4},{1,5},{2,6},{3,7},{4,0},{5,1},{6,2},{7,3},{8,12},{9,13},{10,... | collective-permute-start | bytes 294920 | tf_op jit(solution)/shard_map/ppermute | solution.py:749
  63.2 15.3 %collective-permute-start.24 = (bf16[2,1,1,1,1,64,512]{6,5,4,3,2,1,0:T(8,128)(2,1)S(1)}, bf16[2,1,1,1,1,64,512]{6,5,4,3,2,1,0:T(8,128)(2,1)S(1)}, u32[]{:S(2)}, u32[]{:S(2)}) collective-permute-start(bf16[2,1,1,1,1,64,512]{6,5,4,3,2,1,0:T(8,128)(2,1)S(1)} %pad_maximum_fusion.20), channel_id=1, source_target_pairs={{0,4},{1,5},{2,6},{3,7},{4,0},{5,1},{6,2},{7,3},{8,12},{9,13},{10,... | collective-permute-start | bytes 393224 | tf_op jit(solution)/shard_map/ppermute | solution.py:749
  65.9 15.5 %collective-permute-start.19 = (bf16[2,1,1,1,1,16,2048]{6,5,4,3,2,1,0:T(8,128)(2,1)S(1)}, bf16[2,1,1,1,1,16,2048]{6,5,4,3,2,1,0:T(8,128)(2,1)S(1)}, u32[]{:S(2)}, u32[]{:S(2)}) collective-permute-start(bf16[2,1,1,1,1,16,2048]{6,5,4,3,2,1,0:T(8,128)(2,1)S(1)} %pad_maximum_fusion.19), channel_id=1, source_target_pairs={{0,4},{1,5},{2,6},{3,7},{4,0},{5,1},{6,2},{7,3},{8,12},{9,13},{10,... | collective-permute-start | bytes 393224 | tf_op jit(solution)/shard_map/ppermute | solution.py:749
  66.4 15.1 %collective-permute-start.16 = (bf16[2,1,2,2,1,16,512]{6,5,4,3,2,1,0:T(8,128)(2,1)S(1)}, bf16[2,1,2,2,1,16,512]{6,5,4,3,2,1,0:T(8,128)(2,1)S(1)}, u32[]{:S(2)}, u32[]{:S(2)}) collective-permute-start(bf16[2,1,2,2,1,16,512]{6,5,4,3,2,1,0:T(8,128)(2,1)S(1)} %pad_maximum_fusion.18), channel_id=1, source_target_pairs={{0,1},{1,0},{2,3},{3,2},{4,5},{5,4},{6,7},{7,6},{8,9},{9,8},{10,11... | collective-permute-start | bytes 393224 | tf_op jit(solution)/shard_map/ppermute | solution.py:749
  81.4 15.3 %collective-permute-start.20 = (bf16[2,1,2,1,1,16,2048]{6,5,4,3,2,1,0:T(8,128)(2,1)S(1)}, bf16[2,1,2,1,1,16,2048]{6,5,4,3,2,1,0:T(8,128)(2,1)S(1)}, u32[]{:S(2)}, u32[]{:S(2)}) collective-permute-start(bf16[2,1,2,1,1,16,2048]{6,5,4,3,2,1,0:T(8,128)(2,1)S(1)} %pad_maximum_fusion.15), channel_id=1, source_target_pairs={{0,2},{1,3},{2,0},{3,1},{4,6},{5,7},{6,4},{7,5},{8,10},{9,11},{10,... | collective-permute-start | bytes 786440 | tf_op jit(solution)/shard_map/ppermute | solution.py:749
  82.3 23.1 %collective-permute-start.17 = (bf16[2,1,2,2,2,16,512]{6,5,4,3,2,1,0:T(8,128)(2,1)}, bf16[2,1,2,2,2,16,512]{6,5,4,3,2,1,0:T(8,128)(2,1)}, u32[]{:S(2)}, u32[]{:S(2)}) collective-permute-start(bf16[2,1,2,2,2,16,512]{6,5,4,3,2,1,0:T(8,128)(2,1)} %pad_maximum_fusion.14), channel_id=1, source_target_pairs={{0,8},{8,0},{16,24},{24,16},{1,9},{9,1},{17,25},{25,17},{2,10},{10... | collective-permute-start | bytes 786440 | tf_op jit(solution)/shard_map/ppermute | solution.py:749
  91.3 17.3 %collective-permute-start.26 = (bf16[2,1,2,2,1,64,512]{6,5,4,3,2,1,0:T(8,128)(2,1)S(1)}, bf16[2,1,2,2,1,64,512]{6,5,4,3,2,1,0:T(8,128)(2,1)S(1)}, u32[]{:S(2)}, u32[]{:S(2)}) collective-permute-start(bf16[2,1,2,2,1,64,512]{6,5,4,3,2,1,0:T(8,128)(2,1)S(1)} %pad_maximum_fusion.10), channel_id=1, source_target_pairs={{0,1},{1,0},{2,3},{3,2},{4,5},{5,4},{6,7},{7,6},{8,9},{9,8},{10,11... | collective-permute-start | bytes 1572872 | tf_op jit(solution)/shard_map/ppermute | solution.py:749
  98.7 23.3 %collective-permute-start.4 = (bf16[2,1,2,2,2,16,1536]{6,5,4,3,2,1,0:T(8,128)(2,1)}, bf16[2,1,2,2,2,16,1536]{6,5,4,3,2,1,0:T(8,128)(2,1)}, u32[]{:S(2)}, u32[]{:S(2)}) collective-permute-start(bf16[2,1,2,2,2,16,1536]{6,5,4,3,2,1,0:T(8,128)(2,1)} %pad_maximum_fusion.7), channel_id=1, source_target_pairs={{0,8},{8,0},{16,24},{24,16},{1,9},{9,1},{17,25},{25,17},{2,10},{10... | collective-permute-start | bytes 2359304 | tf_op jit(solution)/shard_map/ppermute | solution.py:749
  98.7 19.0 %all-to-all-start.2 = ((bf16[16,64,512]{2,1,0:T(8,128)(2,1)}), bf16[16,64,512]{2,1,0:T(8,128)(2,1)}, u32[]{:S(2)}, u32[]{:S(2)}) async-start(bf16[16,64,512]{2,1,0:T(8,128)(2,1)} %get-tuple-element.161), calls=%async_computation.2 | async-start | bytes 2097152 | tf_op jit(solution)/shard_map/all_to_all | solution.py:761
  103.8 58.3 %collective-permute-start.21 = (bf16[2,1,2,2,1,16,2048]{6,5,4,3,2,1,0:T(8,128)(2,1)}, bf16[2,1,2,2,1,16,2048]{6,5,4,3,2,1,0:T(8,128)(2,1)}, u32[]{:S(2)}, u32[]{:S(2)}) collective-permute-start(bf16[2,1,2,2,1,16,2048]{6,5,4,3,2,1,0:T(8,128)(2,1)} %pad_maximum_fusion.9), channel_id=1, source_target_pairs={{0,1},{1,0},{2,3},{3,2},{4,5},{5,4},{6,7},{7,6},{8,9},{9,8},{10,11... | collective-permute-start | bytes 1572872 | tf_op jit(solution)/shard_map/ppermute | solution.py:749
  109.7 66.9 %collective-permute-start.27 = (bf16[2,1,2,2,2,64,512]{6,5,4,3,2,1,0:T(8,128)(2,1)}, bf16[2,1,2,2,2,64,512]{6,5,4,3,2,1,0:T(8,128)(2,1)S(1)}, u32[]{:S(2)}, u32[]{:S(2)}) collective-permute-start(bf16[2,1,2,2,2,64,512]{6,5,4,3,2,1,0:T(8,128)(2,1)} %pad_maximum_fusion.6), channel_id=1, source_target_pairs={{0,8},{8,0},{16,24},{24,16},{1,9},{9,1},{17,25},{25,17},{2,10},{10... | collective-permute-start | bytes 3145736 | tf_op jit(solution)/shard_map/ppermute | solution.py:749
  117.8 22.5 %all-to-all-start = ((bf16[16,64,512]{2,1,0:T(8,128)(2,1)}), bf16[16,64,512]{2,1,0:T(8,128)(2,1)}, u32[]{:S(2)}, u32[]{:S(2)}) async-start(bf16[16,64,512]{2,1,0:T(8,128)(2,1)} %get-tuple-element.159), calls=%async_computation | async-start | bytes 2097152 | tf_op jit(solution)/shard_map/all_to_all | solution.py:761
  140.3 39.6 %all-to-all-start.1 = ((bf16[16,64,512]{2,1,0:T(8,128)(2,1)}), bf16[16,64,512]{2,1,0:T(8,128)(2,1)}, u32[]{:S(2)}, u32[]{:S(2)}) async-start(bf16[16,64,512]{2,1,0:T(8,128)(2,1)} %get-tuple-element.156), calls=%async_computation.1 | async-start | bytes 2097152 | tf_op jit(solution)/shard_map/all_to_all | solution.py:761
  153.7 12.9 %collective-permute-start.12 = (f32[3,72,512]{2,1,0:T(8,128)S(1)}, f32[3,72,512]{2,1,0:T(8,128)S(1)}, u32[]{:S(2)}, u32[]{:S(2)}) collective-permute-start(f32[3,72,512]{2,1,0:T(8,128)S(1)} %pad_maximum_fusion.11), channel_id=1, source_target_pairs={{0,3},{1,4},{2,5},{3,6},{4,7},{8,11},{9,12},{10,13},{11,14},{12,15... | collective-permute-start | bytes 1327112 | tf_op jit(solution)/shard_map/ppermute | solution.py:695
  156.1 19.5 %collective-permute-start.11 = (f32[3,72,512]{2,1,0:T(8,128)S(1)}, f32[3,72,512]{2,1,0:T(8,128)S(1)}, u32[]{:S(2)}, u32[]{:S(2)}) collective-permute-start(f32[3,72,512]{2,1,0:T(8,128)S(1)} %pad_maximum_fusion.11), channel_id=1, source_target_pairs={{0,2},{1,3},{2,4},{3,5},{4,6},{5,7},{8,10},{9,11},{10,12},{11,13},... | collective-permute-start | bytes 1327112 | tf_op jit(solution)/shard_map/ppermute | solution.py:695
  157.8 17.8 %collective-permute-start.10 = (f32[3,72,512]{2,1,0:T(8,128)S(1)}, f32[3,72,512]{2,1,0:T(8,128)S(1)}, u32[]{:S(2)}, u32[]{:S(2)}) collective-permute-start(f32[3,72,512]{2,1,0:T(8,128)S(1)} %pad_maximum_fusion.11), channel_id=1, source_target_pairs={{0,1},{1,2},{2,3},{3,4},{4,5},{5,6},{6,7},{8,9},{9,10},{10,11},{11... | collective-permute-start | bytes 1327112 | tf_op jit(solution)/shard_map/ppermute | solution.py:695
  163.4 14.8 %collective-permute-start.22 = (bf16[2,1,2,2,2,16,2048]{6,5,4,3,2,1,0:T(8,128)(2,1)S(1)}, bf16[2,1,2,2,2,16,2048]{6,5,4,3,2,1,0:T(8,128)(2,1)S(1)}, u32[]{:S(2)}, u32[]{:S(2)}) collective-permute-start(bf16[2,1,2,2,2,16,2048]{6,5,4,3,2,1,0:T(8,128)(2,1)S(1)} %pad_maximum_fusion.5), channel_id=1, source_target_pairs={{0,8},{8,0},{16,24},{24,16},{1,9},{9,1},{17,25},{25,17},{2,10},{10... | collective-permute-start | bytes 3145736 | tf_op jit(solution)/shard_map/ppermute | solution.py:749
  179.9 33.0 %all-to-all-start.7 = ((bf16[16,64,512]{2,1,0:T(8,128)(2,1)}), bf16[16,64,512]{2,1,0:T(8,128)(2,1)S(1)}, u32[]{:S(2)}, u32[]{:S(2)}) async-start(bf16[16,64,512]{2,1,0:T(8,128)(2,1)} %get-tuple-element.157), calls=%async_computation.7 | async-start | bytes 2097152 | tf_op jit(solution)/shard_map/all_to_all | solution.py:761
  213.0 32.5 %all-to-all-start.5 = ((bf16[16,64,512]{2,1,0:T(8,128)(2,1)}), bf16[16,64,512]{2,1,0:T(8,128)(2,1)S(1)}, u32[]{:S(2)}, u32[]{:S(2)}) async-start(bf16[16,64,512]{2,1,0:T(8,128)(2,1)} %get-tuple-element.158), calls=%async_computation.5 | async-start | bytes 2097152 | tf_op jit(solution)/shard_map/all_to_all | solution.py:761
  245.5 182.6 %all-to-all-start.4 = ((bf16[16,64,512]{2,1,0:T(8,128)(2,1)}), bf16[16,64,512]{2,1,0:T(8,128)(2,1)S(1)}, u32[]{:S(2)}, u32[]{:S(2)}) async-start(bf16[16,64,512]{2,1,0:T(8,128)(2,1)} %get-tuple-element.80), calls=%async_computation.4 | async-start | bytes 2097152 | tf_op jit(solution)/shard_map/all_to_all | solution.py:761
  283.9 25.3 %collective-permute-start.36 = (bf16[2,1,2,2,2,16,512]{6,5,4,3,2,1,0:T(8,128)(2,1)S(1)}, bf16[2,1,2,2,2,16,512]{6,5,4,3,2,1,0:T(8,128)(2,1)}, u32[]{:S(2)}, u32[]{:S(2)}) collective-permute-start(bf16[2,1,2,2,2,16,512]{6,5,4,3,2,1,0:T(8,128)(2,1)S(1)} %constant_dynamic-slice_fusion.13), channel_id=1, source_target_pairs={{0,8},{8,0},{16,24},{24,16},{1,9},{9,1},{17,25},{25,17},{2,10},{10... | collective-permute-start | bytes 786440 | tf_op jit(solution)/shard_map/ppermute | solution.py:737
  285.2 65.9 %collective-permute-start.29 = (f32[3,72,512]{2,1,0:T(8,128)}, f32[3,72,512]{2,1,0:T(8,128)}, u32[]{:S(2)}, u32[]{:S(2)}) collective-permute-start(f32[3,72,512]{2,1,0:T(8,128)} %pad_maximum_fusion.12), channel_id=1, source_target_pairs={{2,0},{3,1},{4,2},{5,3},{6,4},{7,5},{10,8},{11,9},{12,10},{13,11},... | collective-permute-start | bytes 1327112 | tf_op jit(solution)/shard_map/ppermute | solution.py:695
  303.8 36.3 %collective-permute-start.30 = (f32[3,72,512]{2,1,0:T(8,128)}, f32[3,72,512]{2,1,0:T(8,128)}, u32[]{:S(2)}, u32[]{:S(2)}) collective-permute-start(f32[3,72,512]{2,1,0:T(8,128)} %pad_maximum_fusion.12), channel_id=1, source_target_pairs={{3,0},{4,1},{5,2},{6,3},{7,4},{11,8},{12,9},{13,10},{14,11},{15,12... | collective-permute-start | bytes 1327112 | tf_op jit(solution)/shard_map/ppermute | solution.py:695
  305.1 46.0 %collective-permute-start.28 = (f32[3,72,512]{2,1,0:T(8,128)}, f32[3,72,512]{2,1,0:T(8,128)}, u32[]{:S(2)}, u32[]{:S(2)}) collective-permute-start(f32[3,72,512]{2,1,0:T(8,128)} %pad_maximum_fusion.12), channel_id=1, source_target_pairs={{1,0},{2,1},{3,2},{4,3},{5,4},{6,5},{7,6},{9,8},{10,9},{11,10},{12... | collective-permute-start | bytes 1327112 | tf_op jit(solution)/shard_map/ppermute | solution.py:695
  309.1 251.0 %collective-permute-start.41 = (bf16[2,1,2,2,2,16,2048]{6,5,4,3,2,1,0:T(8,128)(2,1)}, bf16[2,1,2,2,2,16,2048]{6,5,4,3,2,1,0:T(8,128)(2,1)}, u32[]{:S(2)}, u32[]{:S(2)}) collective-permute-start(bf16[2,1,2,2,2,16,2048]{6,5,4,3,2,1,0:T(8,128)(2,1)} %constant_dynamic-slice_fusion.8), channel_id=1, source_target_pairs={{0,8},{8,0},{16,24},{24,16},{1,9},{9,1},{17,25},{25,17},{2,10},{10... | collective-permute-start | bytes 3145736 | tf_op jit(solution)/shard_map/ppermute | solution.py:737
  310.4 29.8 %collective-permute-start.37 = (bf16[2,1,2,2,1,16,512]{6,5,4,3,2,1,0:T(8,128)(2,1)S(1)}, bf16[2,1,2,2,1,16,512]{6,5,4,3,2,1,0:T(8,128)(2,1)S(1)}, u32[]{:S(2)}, u32[]{:S(2)}) collective-permute-start(bf16[2,1,2,2,1,16,512]{6,5,4,3,2,1,0:T(8,128)(2,1)S(1)} %constant_dynamic-slice_fusion.12), channel_id=1, source_target_pairs={{0,1},{1,0},{2,3},{3,2},{4,5},{5,4},{6,7},{7,6},{8,9},{9,8},{10,11... | collective-permute-start | bytes 393224 | tf_op jit(solution)/shard_map/ppermute | solution.py:737
  340.1 225.2 %collective-permute-start.46 = (bf16[2,1,2,2,2,64,512]{6,5,4,3,2,1,0:T(8,128)(2,1)}, bf16[2,1,2,2,2,64,512]{6,5,4,3,2,1,0:T(8,128)(2,1)}, u32[]{:S(2)}, u32[]{:S(2)}) collective-permute-start(bf16[2,1,2,2,2,64,512]{6,5,4,3,2,1,0:T(8,128)(2,1)} %constant_dynamic-slice_fusion.3), channel_id=1, source_target_pairs={{0,8},{8,0},{16,24},{24,16},{1,9},{9,1},{17,25},{25,17},{2,10},{10... | collective-permute-start | bytes 3145736 | tf_op jit(solution)/shard_map/ppermute | solution.py:737
  340.2 176.2 %collective-permute-start.38 = (bf16[2,1,2,1,1,16,512]{6,5,4,3,2,1,0:T(8,128)(2,1)S(1)}, bf16[2,1,2,1,1,16,512]{6,5,4,3,2,1,0:T(8,128)(2,1)S(1)}, u32[]{:S(2)}, u32[]{:S(2)}) collective-permute-start(bf16[2,1,2,1,1,16,512]{6,5,4,3,2,1,0:T(8,128)(2,1)S(1)} %constant_dynamic-slice_fusion.11), channel_id=1, source_target_pairs={{0,2},{1,3},{2,0},{3,1},{4,6},{5,7},{6,4},{7,5},{8,10},{9,11},{10,... | collective-permute-start | bytes 196616 | tf_op jit(solution)/shard_map/ppermute | solution.py:737
  428.2 18.8 %all-to-all-start.8 = ((bf16[16,64,512]{2,1,0:T(8,128)(2,1)}), bf16[16,64,512]{2,1,0:T(8,128)(2,1)}, u32[]{:S(2)}, u32[]{:S(2)}) async-start(bf16[16,64,512]{2,1,0:T(8,128)(2,1)} %get-tuple-element.86), calls=%async_computation.8 | async-start | bytes 2097152 | tf_op jit(solution)/shard_map/all_to_all | solution.py:761
  447.0 63.0 %all-to-all-start.6 = ((bf16[16,64,512]{2,1,0:T(8,128)(2,1)}), bf16[16,64,512]{2,1,0:T(8,128)(2,1)}, u32[]{:S(2)}, u32[]{:S(2)}) async-start(bf16[16,64,512]{2,1,0:T(8,128)(2,1)} %get-tuple-element.83), calls=%async_computation.6 | async-start | bytes 2097152 | tf_op jit(solution)/shard_map/all_to_all | solution.py:761
  510.0 18.1 %all-to-all-start.11 = ((bf16[16,64,512]{2,1,0:T(8,128)(2,1)}), bf16[16,64,512]{2,1,0:T(8,128)(2,1)S(1)}, u32[]{:S(2)}, u32[]{:S(2)}) async-start(bf16[16,64,512]{2,1,0:T(8,128)(2,1)} %get-tuple-element.104), calls=%async_computation.11 | async-start | bytes 2097152 | tf_op jit(solution)/shard_map/all_to_all | solution.py:761
  516.4 15.2 %collective-permute-start.39 = (bf16[2,1,1,1,1,16,512]{6,5,4,3,2,1,0:T(8,128)(2,1)S(1)}, bf16[2,1,1,1,1,16,512]{6,5,4,3,2,1,0:T(8,128)(2,1)S(1)}, u32[]{:S(2)}, u32[]{:S(2)}) collective-permute-start(bf16[2,1,1,1,1,16,512]{6,5,4,3,2,1,0:T(8,128)(2,1)S(1)} %constant_dynamic-slice_fusion.10), channel_id=1, source_target_pairs={{0,4},{1,5},{2,6},{3,7},{4,0},{5,1},{6,2},{7,3},{8,12},{9,13},{10,... | collective-permute-start | bytes 98312 | tf_op jit(solution)/shard_map/ppermute | solution.py:737
  528.1 27.6 %all-to-all-start.9 = ((bf16[16,64,512]{2,1,0:T(8,128)(2,1)}), bf16[16,64,512]{2,1,0:T(8,128)(2,1)S(1)}, u32[]{:S(2)}, u32[]{:S(2)}) async-start(bf16[16,64,512]{2,1,0:T(8,128)(2,1)} %get-tuple-element.94), calls=%async_computation.9 | async-start | bytes 2097152 | tf_op jit(solution)/shard_map/all_to_all | solution.py:761
  531.7 14.7 %collective-permute-start.40 = (bf16[1,1,1,1,1,16,512]{6,5,4,3,2,1,0:T(8,128)(2,1)S(1)}, bf16[1,1,1,1,1,16,512]{6,5,4,3,2,1,0:T(8,128)(2,1)S(1)}, u32[]{:S(2)}, u32[]{:S(2)}) collective-permute-start(bf16[1,1,1,1,1,16,512]{6,5,4,3,2,1,0:T(8,128)(2,1)S(1)} %constant_dynamic-slice_fusion.9), channel_id=1, source_target_pairs={{0,16},{8,24},{16,0},{24,8},{1,17},{9,25},{17,1},{25,9},{2,18},{10... | collective-permute-start | bytes 49160 | tf_op jit(solution)/shard_map/ppermute | solution.py:737
  534.3 49.3 %collective-permute-start.31 = (bf16[2,1,2,2,2,16,1536]{6,5,4,3,2,1,0:T(8,128)(2,1)}, bf16[2,1,2,2,2,16,1536]{6,5,4,3,2,1,0:T(8,128)(2,1)}, u32[]{:S(2)}, u32[]{:S(2)}) collective-permute-start(bf16[2,1,2,2,2,16,1536]{6,5,4,3,2,1,0:T(8,128)(2,1)} %constant_dynamic-slice_fusion.18), channel_id=1, source_target_pairs={{0,8},{8,0},{16,24},{24,16},{1,9},{9,1},{17,25},{25,17},{2,10},{10... | collective-permute-start | bytes 2359304 | tf_op jit(solution)/shard_map/ppermute | solution.py:737
  555.7 19.0 %all-to-all-start.10 = ((bf16[16,64,512]{2,1,0:T(8,128)(2,1)}), bf16[16,64,512]{2,1,0:T(8,128)(2,1)}, u32[]{:S(2)}, u32[]{:S(2)}) async-start(bf16[16,64,512]{2,1,0:T(8,128)(2,1)} %get-tuple-element.99), calls=%async_computation.10 | async-start | bytes 2097152 | tf_op jit(solution)/shard_map/all_to_all | solution.py:761
  563.1 24.3 %collective-permute-start.42 = (bf16[2,1,2,2,1,16,2048]{6,5,4,3,2,1,0:T(8,128)(2,1)}, bf16[2,1,2,2,1,16,2048]{6,5,4,3,2,1,0:T(8,128)(2,1)}, u32[]{:S(2)}, u32[]{:S(2)}) collective-permute-start(bf16[2,1,2,2,1,16,2048]{6,5,4,3,2,1,0:T(8,128)(2,1)} %constant_dynamic-slice_fusion.7), channel_id=1, source_target_pairs={{0,1},{1,0},{2,3},{3,2},{4,5},{5,4},{6,7},{7,6},{8,9},{9,8},{10,11... | collective-permute-start | bytes 1572872 | tf_op jit(solution)/shard_map/ppermute | solution.py:737
  567.7 31.4 %collective-permute-start.47 = (bf16[2,1,2,2,1,64,512]{6,5,4,3,2,1,0:T(8,128)(2,1)}, bf16[2,1,2,2,1,64,512]{6,5,4,3,2,1,0:T(8,128)(2,1)}, u32[]{:S(2)}, u32[]{:S(2)}) collective-permute-start(bf16[2,1,2,2,1,64,512]{6,5,4,3,2,1,0:T(8,128)(2,1)} %constant_dynamic-slice_fusion.2), channel_id=1, source_target_pairs={{0,1},{1,0},{2,3},{3,2},{4,5},{5,4},{6,7},{7,6},{8,9},{9,8},{10,11... | collective-permute-start | bytes 1572872 | tf_op jit(solution)/shard_map/ppermute | solution.py:737
  585.1 12.7 %collective-permute-start.32 = (bf16[2,1,2,2,1,16,1536]{6,5,4,3,2,1,0:T(8,128)(2,1)S(1)}, bf16[2,1,2,2,1,16,1536]{6,5,4,3,2,1,0:T(8,128)(2,1)S(1)}, u32[]{:S(2)}, u32[]{:S(2)}) collective-permute-start(bf16[2,1,2,2,1,16,1536]{6,5,4,3,2,1,0:T(8,128)(2,1)S(1)} %constant_dynamic-slice_fusion.17), channel_id=1, source_target_pairs={{0,1},{1,0},{2,3},{3,2},{4,5},{5,4},{6,7},{7,6},{8,9},{9,8},{10,11... | collective-permute-start | bytes 1179656 | tf_op jit(solution)/shard_map/ppermute | solution.py:737
  588.6 19.3 %collective-permute-start.43 = (bf16[2,1,2,1,1,16,2048]{6,5,4,3,2,1,0:T(8,128)(2,1)S(1)}, bf16[2,1,2,1,1,16,2048]{6,5,4,3,2,1,0:T(8,128)(2,1)S(1)}, u32[]{:S(2)}, u32[]{:S(2)}) collective-permute-start(bf16[2,1,2,1,1,16,2048]{6,5,4,3,2,1,0:T(8,128)(2,1)S(1)} %constant_dynamic-slice_fusion.6), channel_id=1, source_target_pairs={{0,2},{1,3},{2,0},{3,1},{4,6},{5,7},{6,4},{7,5},{8,10},{9,11},{10,... | collective-permute-start | bytes 786440 | tf_op jit(solution)/shard_map/ppermute | solution.py:737
  600.4 13.5 %collective-permute-start.48 = (bf16[2,1,2,1,1,64,512]{6,5,4,3,2,1,0:T(8,128)(2,1)S(1)}, bf16[2,1,2,1,1,64,512]{6,5,4,3,2,1,0:T(8,128)(2,1)S(1)}, u32[]{:S(2)}, u32[]{:S(2)}) collective-permute-start(bf16[2,1,2,1,1,64,512]{6,5,4,3,2,1,0:T(8,128)(2,1)S(1)} %constant_dynamic-slice_fusion.1), channel_id=1, source_target_pairs={{0,2},{1,3},{2,0},{3,1},{4,6},{5,7},{6,4},{7,5},{8,10},{9,11},{10,... | collective-permute-start | bytes 786440 | tf_op jit(solution)/shard_map/ppermute | solution.py:737
  608.0 14.1 %collective-permute-start.44 = (bf16[2,1,1,1,1,16,2048]{6,5,4,3,2,1,0:T(8,128)(2,1)S(1)}, bf16[2,1,1,1,1,16,2048]{6,5,4,3,2,1,0:T(8,128)(2,1)S(1)}, u32[]{:S(2)}, u32[]{:S(2)}) collective-permute-start(bf16[2,1,1,1,1,16,2048]{6,5,4,3,2,1,0:T(8,128)(2,1)S(1)} %constant_dynamic-slice_fusion.5), channel_id=1, source_target_pairs={{0,4},{1,5},{2,6},{3,7},{4,0},{5,1},{6,2},{7,3},{8,12},{9,13},{10,... | collective-permute-start | bytes 393224 | tf_op jit(solution)/shard_map/ppermute | solution.py:737
  (58 other events, 594.4 us)

commit v2 on v1

v2 whole, which is shorter than its diff:
```python
import functools

import jax
import jax.numpy as jnp
from jax import lax
from jax.experimental import pallas as pl
from jax.experimental.pallas import tpu as pltpu
from jax.sharding import PartitionSpec as P

HEADS = 8
HEAD_DIM = 64
STRETCH = 64
LONGEST = 48
CHUNK = 2 * STRETCH
TILE = 4 * CHUNK
PAIRS = HEADS // 2
PAIR = 2 * HEAD_DIM
MODEL = HEADS * HEAD_DIM
BOTH = ("dp", "fsdp")
EPS = 1e-05
VMEM_LIMIT = 60 * 1024 * 1024

f32 = jnp.float32
bf16 = jnp.bfloat16


def nn(a, b):
    return lax.dot_general(a, b, (((1,), (0,)), ((), ())), preferred_element_type=f32)


def nt(a, b):
    return lax.dot_general(a, b, (((1,), (1,)), ((), ())), preferred_element_type=f32)


def tn(a, b):
    return lax.dot_general(a, b, (((0,), (0,)), ((), ())), preferred_element_type=f32)


def lanes(rows, width):
    return lax.broadcasted_iota(jnp.int32, (rows, width), 1)


def sublanes(rows, width):
    return lax.broadcasted_iota(jnp.int32, (rows, width), 0)


def first_head(rows):
    return lanes(rows, PAIR) < HEAD_DIM


def same_head():
    return (sublanes(PAIR, PAIR) // HEAD_DIM) == (lanes(PAIR, PAIR) // HEAD_DIM)


def by_head(x, rows):
    low = first_head(rows)
    zero = jnp.zeros_like(x)
    return jnp.concatenate([jnp.where(low, x, zero), jnp.where(low, zero, x)], axis=0)


def flag(value):
    return value.astype(f32)


def col(pair):
    return slice(pair * PAIR, (pair + 1) * PAIR)


def standardize(x):
    centre = jnp.mean(x, axis=-1, keepdims=True)
    centred = x - centre
    spread = jnp.mean(centred * centred, axis=-1, keepdims=True)
    scale = lax.rsqrt(spread + EPS)
    return centred * scale, scale


def norm_back(upstream, gain, n, scale):
    ug = upstream * gain
    return scale * (
        ug
        - jnp.mean(ug, axis=-1, keepdims=True)
        - n * jnp.mean(ug * n, axis=-1, keepdims=True)
    )


def unpack_state(block, pair):
    part = block[:HEAD_DIM, col(pair)]
    low = first_head(HEAD_DIM)
    zero = jnp.zeros_like(part)
    state = jnp.concatenate([jnp.where(low, part, zero), jnp.where(low, zero, part)], axis=0)
    row = block[HEAD_DIM : HEAD_DIM + 1, col(pair)]
    eye = sublanes(PAIR, PAIR) == lanes(PAIR, PAIR)
    diagonal = jnp.where(eye, row, 0.0)
    ones = jnp.where(same_head(), 1.0, 0.0).astype(bf16)
    high = diagonal.astype(bf16)
    low_part = (diagonal - high.astype(f32)).astype(bf16)
    sums = nn(high, ones) + nn(low_part, ones)
    return jnp.concatenate([state, sums], axis=1)


def pack_state(ref, pair, state, row):
    low = first_head(HEAD_DIM)
    ref[0, :HEAD_DIM, col(pair)] = jnp.where(low, state[:HEAD_DIM], state[HEAD_DIM:])
    ref[0, HEAD_DIM : HEAD_DIM + 1, col(pair)] = row
    ref[0, HEAD_DIM + 1 :, col(pair)] = jnp.zeros((7, PAIR), f32)


def pick(ref, place):
    per = ref.shape[2]
    return ref[lax.div(place, per), 0, lax.rem(place, per)]


def put(ref, place, value):
    per = ref.shape[2]
    ref[lax.div(place, per), 0, lax.rem(place, per)] = value


def group_spec(shape, first):
    block = (shape[0], 1) + tuple(shape[2:])
    return pl.BlockSpec(block, lambda i, *_: (0, first + i, 0, 0, 0))


def fixed(shape):
    zeros = (0,) * len(shape)
    return pl.BlockSpec(tuple(shape), lambda *_: zeros, pipeline_mode=pl.Buffered(1))


def member_spec(first=0):
    return pl.BlockSpec((1, HEAD_DIM + 8, MODEL), lambda i, *_: (first + i, 0, 0))


def tile_spec(width, tiles, reverse=False):
    if reverse:
        return pl.BlockSpec((TILE, width), lambda i, t, *_: (i * tiles + tiles - 1 - t, 0))
    return pl.BlockSpec((TILE, width), lambda i, t, *_: (i * tiles + t, 0))


def states_spec(tiles, reverse=False):
    block = (TILE // CHUNK, MODEL, 3 * PAIR)
    if reverse:
        return pl.BlockSpec(block, lambda i, t, *_: (i * tiles + tiles - 1 - t, 0, 0))
    return pl.BlockSpec(block, lambda i, t, *_: (i * tiles + t, 0, 0))


def params():
    return pltpu.CompilerParams(
        dimension_semantics=("arbitrary", "arbitrary"), vmem_limit_bytes=VMEM_LIMIT
    )


ANYWHERE = pl.BlockSpec(memory_space=pl.ANY)


def featured(mixed):
    return jnp.where(mixed > 0, mixed + 1.0, jnp.exp(jnp.minimum(mixed, 0.0))).astype(bf16)


def state_kernel(placing, closing, rows, weight, bias, gain, shift, state_out, x_scr, acc, sums):
    micro, step = pl.program_id(0), pl.program_id(1)
    per = TILE // STRETCH

    @pl.when(step == 0)
    def _():
        acc[...] = jnp.zeros_like(acc)
        sums[...] = jnp.zeros_like(sums)

    for i in range(per):
        x_scr[i * STRETCH : (i + 1) * STRETCH, :] = pick(rows, placing[micro, step * per + i])
    n, _ = standardize(x_scr[...].astype(f32))
    normed = (n * gain[...] + shift[...]).astype(bf16)
    keep = jnp.concatenate(
        [jnp.full((STRETCH, 1), flag(closing[micro, step * per + i]), f32) for i in range(per)],
        axis=0,
    )
    at = slice(MODEL, 2 * MODEL)
    keys = featured(nn(normed, weight[:, at]) + bias[:, at]).astype(f32) * keep
    sums[...] += jnp.sum(keys, axis=0, keepdims=True)
    keys = keys.astype(bf16)
    at = slice(2 * MODEL, 3 * MODEL)
    values = (nn(normed, weight[:, at]) + bias[:, at]).astype(bf16)
    for pair in range(PAIRS):
        acc[pair] += tn(keys[:, col(pair)], values[:, col(pair)])

    @pl.when(step == pl.num_programs(1) - 1)
    def _():
        for pair in range(PAIRS):
            pack_state(state_out, pair, acc[pair], sums[:, col(pair)])


def run_state(placing, closing, rows, weight, bias, gain, shift):
    micro, count = placing.shape
    width = rows.shape[-1]
    tiles = count * STRETCH // TILE
    return pl.pallas_call(
        state_kernel,
        name="end_state",
        grid_spec=pltpu.PrefetchScalarGridSpec(
            num_scalar_prefetch=2,
            grid=(micro, tiles),
            in_specs=[
                group_spec(rows.shape, 0),
                fixed(weight.shape),
                fixed(bias.shape),
                fixed(gain.shape),
                fixed(shift.shape),
            ],
            out_specs=member_spec(),
            scratch_shapes=[
                pltpu.VMEM((TILE, width), bf16),
                pltpu.VMEM((PAIRS, PAIR, PAIR), f32),
                pltpu.VMEM((1, MODEL), f32),
            ],
        ),
        out_shape=jax.ShapeDtypeStruct((micro, HEAD_DIM + 8, MODEL), f32),
        compiler_params=params(),
        cost_estimate=pl.CostEstimate(
            flops=4 * micro * count * STRETCH * width * MODEL,
            bytes_accessed=5 << 20,
            transcendentals=micro * count * STRETCH * MODEL,
        ),
    )(placing, closing, rows, weight, bias, gain, shift)


def causal(second, transposed):
    i = sublanes(CHUNK, 2 * CHUNK)
    j = lanes(CHUNK, 2 * CHUNK) % CHUNK
    if transposed:
        i, j = j, i
    crosses = (i >= STRETCH) & (j < STRETCH)
    return jnp.where(crosses, 1.0 - second, jnp.where(j <= i, 1.0, 0.0))


def mid_kernel(
    placing,
    restart,
    opened,
    owner,
    _,
    rows_ref,
    cot_ref,
    inc_ref,
    w_qkv,
    w_out,
    w_up,
    w_down,
    b_qkv,
    gain_one,
    shift_one,
    b_out,
    gain,
    shift,
    b_up,
    b_down,
    *refs,
    first,
    resumes,
    final,
):
    before, refs = (refs[:3], refs[3:]) if resumes else ((), refs)
    result, qkv_ref, branch_out, gn_out, gd_out, states_out, state_out, vec_out = refs[:8]
    refs = refs[8:]
    if final:
        keep_out, send_out, acc_up, acc_down, acc_out, turned = refs[:6]
        refs = refs[6:]
    else:
        acc_up, acc_down, acc_out = refs[:3]
        refs = refs[3:]
    carry, back, back_sum, att_scr, inv_scr, att_b, x_scr, cot_scr = refs[:8]
    sems = refs[8] if resumes else None
    member, step = pl.program_id(0), pl.program_id(1)
    micro = first + member
    per = TILE // STRETCH
    opening = (member == 0) & (step == 0)

    @pl.when(opening)
    def _():
        vec_out[...] = jnp.zeros_like(vec_out)
        if resumes:
            for n, (source, target) in enumerate(zip(before, (acc_up, acc_down, acc_out))):
                pltpu.make_async_copy(source, target, sems.at[n]).start()
        else:
            acc_up[...] = jnp.zeros_like(acc_up)
            acc_down[...] = jnp.zeros_like(acc_down)
            acc_out[...] = jnp.zeros_like(acc_out)

    @pl.when(step == 0)
    def _():
        for pair in range(PAIRS):
            carry[pair] = unpack_state(inc_ref[0], pair)
        back[...] = jnp.zeros_like(back)
        back_sum[...] = jnp.zeros_like(back_sum)

    block = same_head()
    ones_head = jnp.where(block, 1.0, 0.0).astype(bf16)
    ones_twice = jnp.concatenate([ones_head, ones_head], axis=0)
    low = first_head(CHUNK)
    one_low = jnp.where(low, 1.0, 0.0).astype(bf16)
    one_high = jnp.where(low, 0.0, 1.0).astype(bf16)
    ones_both = jnp.concatenate([one_low, one_high], axis=0)
    ones_all = jnp.ones((CHUNK, PAIR), bf16)
    wide_block = jnp.concatenate([block, block], axis=1)
    upper = sublanes(CHUNK, PAIR) < STRETCH
    inner = lanes(PAIR, PAIR) % HEAD_DIM
    zero_s = jnp.zeros((PAIR, PAIR), bf16)
    for i in range(per):
        x_scr[i * STRETCH : (i + 1) * STRETCH, :] = pick(rows_ref, placing[micro, step * per + i])
        cot_scr[i * STRETCH : (i + 1) * STRETCH, :] = pick(cot_ref, placing[micro, step * per + i])

    x = x_scr[...].astype(f32)
    n, _ = standardize(x)
    normed = (n * gain_one[...] + shift_one[...]).astype(bf16)
    for part in range(2):
        at = slice(part * MODEL, (part + 1) * MODEL)
        qkv_ref[:, at] = featured(nn(normed, w_qkv[:, at]) + b_qkv[:, at])
    at = slice(2 * MODEL, 3 * MODEL)
    qkv_ref[:, at] = (nn(normed, w_qkv[:, at]) + b_qkv[:, at]).astype(bf16)

    for chunk in range(TILE // CHUNK):
        rows = slice(chunk * CHUNK, (chunk + 1) * CHUNK)
        r0 = flag(restart[micro, step * per + 2 * chunk])
        r1 = flag(restart[micro, step * per + 2 * chunk + 1])
        mask = causal(r1, False)
        keep_low = jnp.where(upper, 1.0, 1.0 - r1)
        keep_key = jnp.where(upper, 1.0 - r1, 1.0)
        for pair in range(PAIRS):
            q = qkv_ref[rows, pair * PAIR : (pair + 1) * PAIR]
            k = qkv_ref[rows, MODEL + pair * PAIR : MODEL + (pair + 1) * PAIR]
            v = qkv_ref[rows, 2 * MODEL + pair * PAIR : 2 * MODEL + (pair + 1) * PAIR]
            state = carry[pair] * (1.0 - r0)
            state_b = state.astype(bf16)
            state_low = (state - state_b.astype(f32)).astype(bf16)
            states_out[chunk, pair * PAIR : (pair + 1) * PAIR, :] = jnp.concatenate(
                [
                    state_b[:, :PAIR],
                    jnp.where(
                        inner < 2, state_b[:, PAIR:], jnp.where(inner == 2, state_low[:, PAIR:], zero_s)
                    ),
                    state_low[:, :PAIR],
                ],
                axis=1,
            )
            mixing = nt(q, by_head(k, CHUNK)) * mask
            values = jnp.concatenate([by_head(v, CHUNK), ones_both], axis=1)
            out = nn(mixing.astype(bf16), values)
            out = out + nn((q.astype(f32) * keep_low).astype(bf16), state_b)
            inv = 1.0 / out[:, PAIR:]
            att = out[:, :PAIR] * inv
            att_scr[rows, col(pair)] = att
            inv_scr[rows, col(pair)] = inv
            att_b[rows, col(pair)] = att.astype(bf16)
            k_keep = (k.astype(f32) * keep_key).astype(bf16)
            added = tn(k_keep, jnp.concatenate([v, ones_all], axis=1))
            carry[pair] = state * (1.0 - r1) + jnp.where(wide_block, added, 0.0)

    middle = x_scr[...].astype(f32) + nn(att_b[...], w_out[...]) + b_out[...]
    n, scale = standardize(middle)
    normed = (n * gain[...] + shift[...]).astype(bf16)
    normed_t = normed.T
    cot = cot_scr[...]
    cot_t = cot.T
    ff = w_up.shape[1]
    total = middle + b_down[...]
    up_grad = jnp.zeros((TILE, MODEL), f32)
    if resumes:

        @pl.when(opening)
        def _():
            for n_, (source, target) in enumerate(zip(before, (acc_up, acc_down, acc_out))):
                pltpu.make_async_copy(source, target, sems.at[n_]).wait()

    for part in range(ff // MODEL):
        at = slice(part * MODEL, (part + 1) * MODEL)
        u = nn(normed, w_up[:, at]) + b_up[:, at]
        u2 = u * u
        t = jnp.tanh(u * (0.7978845608028654 + 0.035677408136300125 * u2))
        half = 0.5 + 0.5 * t
        act = (u * half).astype(bf16)
        rise = 0.7978845608028654 + 0.10703222440890037 * u2
        slope = half + 0.5 * u * (1.0 - t * t) * rise
        g = (nt(cot, w_down[at, :]) * slope).astype(bf16)
        total = total + nn(act, w_down[at, :])
        acc_down[:, at] += nn(cot_t, act)
        vec_out[0:1, at] += jnp.sum(g.astype(f32), axis=0, keepdims=True)
        up_grad = up_grad + nt(g, w_up[:, at])
        acc_up[:, at] += nn(normed_t, g)
    total = total.astype(bf16)
    for i in range(per):
        put(result, placing[micro, step * per + i], total[i * STRETCH : (i + 1) * STRETCH, :])

    cot_f = cot.astype(f32)
    vec_out[1:2, :MODEL] += jnp.sum(up_grad * n, axis=0, keepdims=True)
    vec_out[1:2, MODEL : 2 * MODEL] += jnp.sum(up_grad, axis=0, keepdims=True)
    vec_out[1:2, 3 * MODEL : 4 * MODEL] += jnp.sum(cot_f, axis=0, keepdims=True)
    branch = (cot_f + norm_back(up_grad, gain[...], n, scale)).astype(bf16)
    branch_out[...] = branch
    vec_out[1:2, 2 * MODEL : 3 * MODEL] += jnp.sum(branch.astype(f32), axis=0, keepdims=True)
    grad_att = nt(branch, w_out[...])
    acc_out[...] += tn(att_b[...], branch)
    lane = lanes(CHUNK, PAIR) % HEAD_DIM
    for chunk in range(TILE // CHUNK):
        rows = slice(chunk * CHUNK, (chunk + 1) * CHUNK)
        o0 = flag(opened[micro, step * per + 2 * chunk])
        o1 = flag(opened[micro, step * per + 2 * chunk + 1])
        keep = jnp.where(upper, o0, o1)
        for pair in range(PAIRS):
            inv = inv_scr[rows, col(pair)]
            gn = (grad_att[rows, col(pair)].astype(bf16).astype(f32) * inv).astype(bf16)
            product = gn.astype(f32) * att_scr[rows, col(pair)]
            high = product.astype(bf16)
            low_part = (product - high.astype(f32)).astype(bf16)
            gd = -nn(jnp.concatenate([high, low_part], axis=1), ones_twice)
            gd_high = gd.astype(bf16)
            gd_low = (gd - gd_high.astype(f32)).astype(bf16)
            zero = jnp.zeros_like(gd_high)
            gn_out[rows, col(pair)] = gn
            gd_out[rows, col(pair)] = jnp.where(
                (lane == 0) | (lane == 2), gd_high, jnp.where(lane == 1, gd_low, zero)
            )
            q = qkv_ref[rows, pair * PAIR : (pair + 1) * PAIR].astype(f32) * keep
            back[pair] += tn(q.astype(bf16), gn)
            back_sum[:, col(pair)] += jnp.sum(q * gd, axis=0, keepdims=True)

    @pl.when(step == pl.num_programs(1) - 1)
    def _():
        for pair in range(PAIRS):
            pack_state(state_out, pair, back[pair], back_sum[:, col(pair)])

    if final:

        @pl.when((member == pl.num_programs(0) - 1) & (step == pl.num_programs(1) - 1))
        def _():
            parts = ff // MODEL
            devices = 2 * keep_out.shape[0]
            less = MODEL // devices
            more = parts * less
            for part in range(parts):
                at = slice(part * MODEL, (part + 1) * MODEL)
                turned[at, :] = acc_down[:, at].T
            for j in range(devices):
                d = owner[j]
                target = keep_out if j < devices // 2 else send_out
                seat = j % (devices // 2)
                here = pl.ds(pl.multiple_of(d * less, less), less)
                for part in range(parts):
                    target[seat, part * less : (part + 1) * less, :] = acc_up[
                        here, part * MODEL : (part + 1) * MODEL
                    ].astype(target.dtype)
                there = pl.ds(pl.multiple_of(d * more, more), more)
                target[seat, more : 2 * more, :] = turned[there, :].astype(target.dtype)
                target[seat, 2 * more :, :] = acc_out[here, :].astype(target.dtype)


def run_mid(tables, first, members, target, rows, cot, inc, weights, vectors, before, owner):
    micro, count = tables[0].shape
    width = rows.shape[-1]
    ff = weights[2].shape[1]
    count = count * STRETCH
    tiles = count // TILE
    total = members * count
    resumes, final = before is not None, owner is not None
    f32_sums = [(width, ff), (width, ff), (MODEL, width)]
    devices = lax.axis_size(BOTH) if final else 0
    if not final:
        owner = jnp.zeros((8,), jnp.int32)
    half = (devices // 2, (2 * ff + MODEL) // max(devices, 1), MODEL)
    out_specs = [
        group_spec(target.shape, 0),
        tile_spec(3 * MODEL, tiles),
        tile_spec(width, tiles),
        tile_spec(MODEL, tiles),
        tile_spec(MODEL, tiles),
        states_spec(tiles),
        member_spec(),
        fixed((8, ff)),
    ]
    out_shape = [
        jax.ShapeDtypeStruct(target.shape, bf16),
        jax.ShapeDtypeStruct((total, 3 * MODEL), bf16),
        jax.ShapeDtypeStruct((total, width), bf16),
        jax.ShapeDtypeStruct((total, MODEL), bf16),
        jax.ShapeDtypeStruct((total, MODEL), bf16),
        jax.ShapeDtypeStruct((total // CHUNK, MODEL, 3 * PAIR), bf16),
        jax.ShapeDtypeStruct((members, HEAD_DIM + 8, MODEL), f32),
        jax.ShapeDtypeStruct((8, ff), f32),
    ]
    if final:
        out_specs += [fixed(half), fixed(half)]
        out_shape += [jax.ShapeDtypeStruct(half, f32), jax.ShapeDtypeStruct(half, bf16)]
        scratch = [pltpu.VMEM(shape, f32) for shape in f32_sums] + [pltpu.VMEM((ff, width), f32)]
    else:
        out_specs += [fixed(shape) for shape in f32_sums]
        out_shape += [jax.ShapeDtypeStruct(shape, f32) for shape in f32_sums]
        scratch = []
    scratch += [
        pltpu.VMEM((PAIRS, PAIR, 2 * PAIR), f32),
        pltpu.VMEM((PAIRS, PAIR, PAIR), f32),
        pltpu.VMEM((1, MODEL), f32),
        pltpu.VMEM((TILE, MODEL), f32),
        pltpu.VMEM((TILE, MODEL), f32),
        pltpu.VMEM((TILE, MODEL), bf16),
        pltpu.VMEM((TILE, width), bf16),
        pltpu.VMEM((TILE, width), bf16),
    ]
    if resumes:
        scratch.append(pltpu.SemaphoreType.DMA((3,)))
    return pl.pallas_call(
        functools.partial(mid_kernel, first=first, resumes=resumes, final=final),
        name="middle",
        grid_spec=pltpu.PrefetchScalarGridSpec(
            num_scalar_prefetch=4,
            grid=(members, tiles),
            in_specs=[
                ANYWHERE,
                group_spec(rows.shape, first),
                group_spec(cot[0].shape, cot[1]),
                member_spec(first),
            ]
            + [fixed(item.shape) for item in weights + vectors]
            + [ANYWHERE] * (3 if resumes else 0),
            out_specs=out_specs,
            scratch_shapes=scratch,
        ),
        out_shape=out_shape,
        compiler_params=params(),
        input_output_aliases={4: 0},
        cost_estimate=pl.CostEstimate(
            flops=2 * total * width * (6 * MODEL + 6 * ff) + (members << 32),
            bytes_accessed=members * (20 << 20),
            transcendentals=total * ff,
        ),
    )(*tables, owner, target, rows, cot[0], inc, *weights, *vectors, *(before or ()))


def back_kernel(
    placing,
    restart,
    owner,
    _,
    rows_ref,
    qkv_ref,
    gn_ref,
    gd_ref,
    branch_ref,
    states_ref,
    inc_ref,
    weight,
    gain,
    shift,
    owner_col,
    *refs,
    first,
    resumes,
    final,
    widths,
    sums,
):
    before, refs = (refs[:1], refs[1:]) if resumes else ((), refs)
    vec_others, refs = refs[:sums], refs[sums:]
    grad_rows, vec_out = refs[:2]
    refs = refs[2:]
    if final:
        keep_out, send_out, acc = refs[:3]
        refs = refs[3:]
    else:
        acc = refs[0]
        refs = refs[1:]
    carry, x_scr, mixed_scr = refs[:3]
    sems = refs[3] if resumes else None
    member, step = pl.program_id(0), pl.program_id(1)
    micro = first + member
    per = TILE // STRETCH
    tile = pl.num_programs(1) - 1 - step
    opening = (member == 0) & (step == 0)
    lane = lanes(CHUNK, PAIR)
    inner = lane % HEAD_DIM

    @pl.when(opening)
    def _():
        vec_out[...] = jnp.zeros_like(vec_out)
        if resumes:
            pltpu.make_async_copy(before[0], acc, sems.at[0]).start()
        else:
            acc[...] = jnp.zeros_like(acc)

    @pl.when(step == 0)
    def _():
        only = jnp.concatenate([jnp.ones((PAIR, PAIR), f32), jnp.where(inner == 0, 1.0, 0.0)], axis=1)
        for pair in range(PAIRS):
            carry[pair] = unpack_state(inc_ref[0], pair) * only

    block = same_head()
    wide_block = jnp.concatenate([block, block], axis=1)
    upper = sublanes(CHUNK, PAIR) < STRETCH
    marks = jnp.where((inner < 2) | (inner == 3), 1.0, 0.0).astype(bf16)
    mark_low = jnp.where(lane < 2, 1.0, 0.0).astype(bf16)
    mark_high = jnp.where((lane == HEAD_DIM) | (lane == HEAD_DIM + 1), 1.0, 0.0).astype(bf16)
    marks_both = jnp.concatenate([mark_low, mark_high], axis=0)
    for i in range(per):
        x_scr[i * STRETCH : (i + 1) * STRETCH, :] = pick(rows_ref, placing[micro, tile * per + i])

    for chunk in reversed(range(TILE // CHUNK)):
        rows = slice(chunk * CHUNK, (chunk + 1) * CHUNK)
        r0 = flag(restart[micro, tile * per + 2 * chunk])
        r1 = flag(restart[micro, tile * per + 2 * chunk + 1])
        r2 = flag(restart[micro, tile * per + 2 * chunk + 2])
        mask = causal(r1, False)
        mask_t = causal(r1, True)
        keep_low = jnp.where(upper, 1.0, 1.0 - r1)
        keep_key = jnp.where(upper, 1.0 - r1, 1.0)
        for pair in range(PAIRS):
            q = qkv_ref[rows, pair * PAIR : (pair + 1) * PAIR]
            k = qkv_ref[rows, MODEL + pair * PAIR : MODEL + (pair + 1) * PAIR]
            v = qkv_ref[rows, 2 * MODEL + pair * PAIR : 2 * MODEL + (pair + 1) * PAIR]
            gn = gn_ref[rows, col(pair)]
            gdx = gd_ref[rows, col(pair)]
            state = states_ref[chunk, pair * PAIR : (pair + 1) * PAIR, :]
            grown = carry[pair] * (1.0 - r2)
            grown_b = grown.astype(bf16)
            rest = grown - grown_b.astype(f32)
            grown_low = rest[:, :PAIR].astype(bf16)
            z_low = pltpu.roll(rest[:, PAIR:], 3, 1).astype(bf16)
            z_both = jnp.where(inner < 2, grown_b[:, PAIR:], jnp.where(inner == 3, z_low, jnp.zeros_like(z_low)))
            grown_x = jnp.concatenate([grown_b[:, :PAIR], z_both], axis=1)
            k2 = by_head(k, CHUNK)
            q2 = by_head(q, CHUNK)
            v2 = by_head(v, CHUNK)
            gn2 = by_head(gn, CHUNK)
            gd2 = by_head(gdx, CHUNK)
            both = jnp.concatenate([gn, gdx], axis=1)
            mixing_t = (nt(k, q2) * mask_t).astype(bf16)
            g_mix = (nt(both, jnp.concatenate([v2, marks_both], axis=1)) * mask).astype(bf16)
            v_marks = jnp.concatenate([v, marks], axis=1)
            g_mix_t = (nt(v_marks, jnp.concatenate([gn2, gd2], axis=1)) * mask_t).astype(bf16)
            dq = nn(g_mix, k2) + (nt(both, state[:, : 2 * PAIR]) + nt(gn, state[:, 2 * PAIR :])) * keep_low
            dk = nn(g_mix_t, q2) + (nt(v_marks, grown_x) + nt(v, grown_low)) * keep_key
            dv = nn(mixing_t, gn2) + nn(k, grown_b[:, :PAIR]) * keep_key
            q_keep = (q.astype(f32) * keep_low).astype(bf16)
            added = tn(q_keep, both)
            carry[pair] = (grown * (1.0 - r1) + jnp.where(wide_block, added, 0.0)) * (1.0 - r0)
            mixed_scr[rows, pair * PAIR : (pair + 1) * PAIR] = (
                dq * jnp.minimum(q.astype(f32), 1.0)
            ).astype(bf16)
            mixed_scr[rows, MODEL + pair * PAIR : MODEL + (pair + 1) * PAIR] = (
                dk * jnp.minimum(k.astype(f32), 1.0)
            ).astype(bf16)
            mixed_scr[rows, 2 * MODEL + pair * PAIR : 2 * MODEL + (pair + 1) * PAIR] = dv.astype(bf16)

    mixed = mixed_scr[...]
    vec_out[0:1, :] += jnp.sum(mixed.astype(f32), axis=0, keepdims=True)
    upstream = nt(mixed, weight[...])
    n, scale = standardize(x_scr[...].astype(f32))
    normed_t = (n * gain[...] + shift[...]).astype(bf16).T
    if resumes:

        @pl.when(opening)
        def _():
            pltpu.make_async_copy(before[0], acc, sems.at[0]).wait()

    for part in range(3):
        at = slice(part * MODEL, (part + 1) * MODEL)
        acc[:, at] += nn(normed_t, mixed[:, at])
    vec_out[1:2, :MODEL] += jnp.sum(upstream * n, axis=0, keepdims=True)
    vec_out[1:2, MODEL : 2 * MODEL] += jnp.sum(upstream, axis=0, keepdims=True)
    total = (branch_ref[...].astype(f32) + norm_back(upstream, gain[...], n, scale)).astype(bf16)
    for i in range(per):
        put(grad_rows, placing[micro, tile * per + i], total[i * STRETCH : (i + 1) * STRETCH, :])

    if final:

        @pl.when((member == pl.num_programs(0) - 1) & (step == pl.num_programs(1) - 1))
        def _():
            half = keep_out.shape[0]
            devices = 2 * half
            less = MODEL // devices
            for j in range(devices):
                here = pl.ds(pl.multiple_of(owner[j] * less, less), less)
                target = keep_out if j < half else send_out
                for part in range(3):
                    target[j % half, part * less : (part + 1) * less, :] = acc[
                        here, part * MODEL : (part + 1) * MODEL
                    ].astype(target.dtype)
            mid = sum(ref[...] for ref in vec_others if ref.shape[1] == vec_others[0].shape[1])
            rear = vec_out[...] + sum(
                ref[...] for ref in vec_others if ref.shape[1] != vec_others[0].shape[1]
            )
            sources = (
                rear[1:2, :MODEL],
                rear[1:2, MODEL : 2 * MODEL],
                rear[0:1, : 2 * MODEL],
                rear[0:1, 2 * MODEL :],
                mid[1:2, 2 * MODEL : 3 * MODEL],
                mid[1:2, :MODEL],
                mid[1:2, MODEL : 2 * MODEL],
                mid[0:1, :],
                mid[1:2, 3 * MODEL : 4 * MODEL],
            )
            rows16 = sublanes(16, MODEL)
            pieces = []
            for source, width in zip(sources, widths, strict=True):
                size = devices * width
                mine = (lanes(devices, size) // width) == owner_col[...]
                picked = jnp.where(mine, source, 0.0)
                gather = jnp.where(
                    (sublanes(size, PAIR) % width) == lanes(size, PAIR), 1.0, 0.0
                ).astype(bf16)
                high = picked.astype(bf16)
                low = (picked - high.astype(f32)).astype(bf16)
                pieces.append(nn(high, gather) + nn(low, gather))
            rest = jnp.zeros((1, MODEL - PAIR), f32)
            for j in range(devices):
                block16 = jnp.zeros((16, MODEL), f32)
                for v, piece in enumerate(pieces):
                    row = jnp.concatenate([piece[j : j + 1, :], rest], axis=1)
                    block16 = block16 + jnp.where(rows16 == v, row, 0.0)
                target = keep_out if j < half else send_out
                target[j % half, 3 * less :, :] = block16.astype(target.dtype)


def run_back(tables, first, members, target, rows, mid, inc, weight, gain, shift, before, owner, others, widths):
    (group, seat), (saved, at) = target, mid
    micro, count = tables[0].shape
    width = rows.shape[-1]
    count = count * STRETCH
    tiles = count // TILE
    resumes, final = before is not None, owner is not None
    devices = lax.axis_size(BOTH) if final else 0
    if not final:
        owner = jnp.zeros((8,), jnp.int32)
        others = []
    half = (devices // 2, 3 * MODEL // max(devices, 1) + 16, MODEL)
    out_specs = [group_spec(group.shape, seat), fixed((8, 3 * MODEL))]
    out_shape = [
        jax.ShapeDtypeStruct(group.shape, bf16),
        jax.ShapeDtypeStruct((8, 3 * MODEL), f32),
    ]
    scratch = []
    if final:
        out_specs += [fixed(half), fixed(half)]
        out_shape += [jax.ShapeDtypeStruct(half, f32), jax.ShapeDtypeStruct(half, bf16)]
        scratch.append(pltpu.VMEM((width, 3 * MODEL), f32))
    else:
        out_specs.append(fixed((width, 3 * MODEL)))
        out_shape.append(jax.ShapeDtypeStruct((width, 3 * MODEL), f32))
    scratch += [
        pltpu.VMEM((PAIRS, PAIR, 2 * PAIR), f32),
        pltpu.VMEM((TILE, width), bf16),
        pltpu.VMEM((TILE, 3 * MODEL), bf16),
    ]
    if resumes:
        scratch.append(pltpu.SemaphoreType.DMA((1,)))

    def tile(width_):
        return pl.BlockSpec((TILE, width_), lambda i, t, *_: ((at + i) * tiles + tiles - 1 - t, 0))

    return pl.pallas_call(
        functools.partial(
            back_kernel, first=first, resumes=resumes, final=final, widths=widths, sums=len(others)
        ),
        name="back",
        grid_spec=pltpu.PrefetchScalarGridSpec(
            num_scalar_prefetch=3,
            grid=(members, tiles),
            in_specs=[
                ANYWHERE,
                group_spec(rows.shape, first),
                tile(3 * MODEL),
                tile(MODEL),
                tile(MODEL),
                tile(width),
                pl.BlockSpec(
                    (TILE // CHUNK, MODEL, 3 * PAIR),
                    lambda i, t, *_: ((at + i) * tiles + tiles - 1 - t, 0, 0),
                ),
                member_spec(at),
                fixed(weight.shape),
                fixed(gain.shape),
                fixed(shift.shape),
                fixed((owner.shape[0], 1)),
            ]
            + ([ANYWHERE] if resumes else [])
            + [fixed(item.shape) for item in others],
            out_specs=out_specs,
            scratch_shapes=scratch,
        ),
        out_shape=out_shape,
        input_output_aliases={3: 0},
        compiler_params=params(),
        cost_estimate=pl.CostEstimate(
            flops=members * (2 * count * width * 6 * MODEL + (8 << 30)),
            bytes_accessed=members * (14 << 20),
            transcendentals=0,
        ),
    )(
        tables[0],
        tables[1],
        owner,
        group,
        rows,
        saved[1],
        saved[3],
        saved[4],
        saved[2],
        saved[5],
        inc,
        weight,
        gain,
        shift,
        owner[:, None],
        *(() if before is None else (before,)),
        *others,
    )


def send_kernel(slot, source, target):
    micro = pl.program_id(0)
    for i in range(source.shape[1]):
        put(target, slot[micro, i], source[0, i])


def run_send(slot, rows, first, members):
    micro, count, width = rows.shape
    stretches = count // STRETCH
    groups = lax.axis_size("dp")
    shape = (groups, members, stretches // groups, STRETCH, width)
    return pl.pallas_call(
        send_kernel,
        name="send",
        grid_spec=pltpu.PrefetchScalarGridSpec(
            num_scalar_prefetch=1,
            grid=(members,),
            in_specs=[
                pl.BlockSpec((1, stretches, STRETCH, width), lambda i, *_: (first + i, 0, 0, 0))
            ],
            out_specs=pl.BlockSpec((groups, 1) + shape[2:], lambda i, *_: (0, i, 0, 0, 0)),
        ),
        out_shape=jax.ShapeDtypeStruct(shape, rows.dtype),
        compiler_params=pltpu.CompilerParams(vmem_limit_bytes=VMEM_LIMIT),
        cost_estimate=pl.CostEstimate(
            flops=0, bytes_accessed=4 * members * count * width, transcendentals=0
        ),
    )(slot[first : first + members], rows.reshape(micro, stretches, STRETCH, width))


def land_kernel(slot, _, source, target):
    micro = pl.program_id(0)
    for i in range(target.shape[1]):
        target[0, i] = pick(source, slot[micro, i])


def run_land(slot, landed, output, first):
    members = landed.shape[1]
    shape = output.shape
    block = (landed.shape[0], 1) + landed.shape[2:]
    return pl.pallas_call(
        land_kernel,
        name="land",
        grid_spec=pltpu.PrefetchScalarGridSpec(
            num_scalar_prefetch=1,
            grid=(members,),
            in_specs=[
                pl.BlockSpec(memory_space=pl.ANY),
                pl.BlockSpec(block, lambda i, *_: (0, i, 0, 0, 0)),
            ],
            out_specs=pl.BlockSpec((1,) + shape[1:], lambda i, *_: (first + i, 0, 0, 0)),
        ),
        out_shape=jax.ShapeDtypeStruct(shape, output.dtype),
        input_output_aliases={1: 0},
        compiler_params=pltpu.CompilerParams(vmem_limit_bytes=VMEM_LIMIT),
        cost_estimate=pl.CostEstimate(flops=0, bytes_accessed=4 * landed.size, transcendentals=0),
    )(slot[first : first + members], output, landed)


def blank(shape):
    return pl.pallas_call(
        lambda ref: None,
        name="blank",
        out_specs=pl.BlockSpec(memory_space=pl.ANY),
        out_shape=jax.ShapeDtypeStruct(shape, bf16),
    )()


def index_tables(lengths, stretch_order, count):
    fsdp = lax.axis_size("fsdp")
    groups = lax.axis_size("dp")
    device = lax.axis_index(BOTH)
    base = device * count
    within = jnp.arange(count, dtype=jnp.int32)
    mine = base + within
    place = jnp.arange(stretch_order.shape[1], dtype=jnp.int32)
    here = place[None, None, :]
    landing = jnp.sum(
        jnp.where(stretch_order[:, None, :] == mine[None, :, None], here, 0), axis=-1
    )
    slot = jnp.sum((landing[:, None, :] < landing[:, :, None]).astype(jnp.int32), axis=-1)
    arrival = jnp.sum(
        jnp.where(here == mine[None, :, None], stretch_order[:, None, :], 0), axis=-1
    )
    source = arrival // count // fsdp
    ahead = (source[:, None, :] == source[:, :, None]) & (
        within[None, None, :] < within[None, :, None]
    )
    placing = source * (count // groups) + jnp.sum(ahead.astype(jnp.int32), axis=-1)
    index = jnp.arange(lengths.shape[1], dtype=jnp.int32)
    starts = jnp.sum(
        jnp.where(index[None, None, :] < index[None, :, None], lengths[:, None, :], 0), axis=-1
    )
    edge = base + jnp.arange(count + 1, dtype=jnp.int32)
    restart = jnp.any(starts[:, None, :] == edge[None, :, None], axis=-1).astype(jnp.int32)
    restart = jnp.where(edge[None, :] == stretch_order.shape[1], 1, restart)
    opened = 1 - jnp.any(
        (starts[:, None, :] >= base) & (starts[:, None, :] <= mine[None, :, None]), axis=-1
    ).astype(jnp.int32)
    last = base + count - 1
    closing = 1 - jnp.any(
        (starts[:, None, :] > mine[None, :, None]) & (starts[:, None, :] <= last), axis=-1
    ).astype(jnp.int32)
    hops = -(-(LONGEST - 1) // count)
    hop = jnp.arange(hops, dtype=jnp.int32)
    reach_back = base - 1 - hop * count
    from_before = 1.0 - jnp.any(
        (starts[:, None, :] > reach_back[None, :, None]) & (starts[:, None, :] <= base), axis=-1
    ).astype(f32)
    reach_on = base + (hop + 1) * count
    from_after = 1.0 - jnp.any(
        (starts[:, None, :] > last) & (starts[:, None, :] <= reach_on[None, :, None]), axis=-1
    ).astype(f32)
    return slot, placing, restart, opened, closing, from_before, from_after


def exchange(states, hops, forward):
    size = lax.axis_size("fsdp")
    got = []
    for hop in range(min(hops, size - 1)):
        step = hop + 1
        pairs = [(i, i + step) if forward else (i + step, i) for i in range(size - step)]
        got.append(lax.ppermute(states, "fsdp", pairs))
    return got


def joined(got, weights, *others):
    got = after(got, *others)
    return sum(item * weights[:, hop, None, None] for hop, item in enumerate(got))


def halving_stages():
    stages = []
    dp, fsdp = lax.axis_size("dp"), lax.axis_size("fsdp")
    if dp > 1:
        stages.append(("dp", 1))
    bit = 1
    while bit < fsdp:
        stages.append(("fsdp", bit))
        bit *= 2
    bit = 2
    while bit < dp:
        stages.append(("dp", bit))
        bit *= 2
    return stages


def order_tables():
    stages = halving_stages()
    fsdp = lax.axis_size("fsdp")
    devices = lax.axis_size(BOTH)
    me = lax.axis_index(BOTH)
    index = jnp.arange(devices, dtype=jnp.int32)
    bits = [bit * (fsdp if axis == "dp" else 1) for axis, bit in stages]
    place = jnp.zeros((devices,), jnp.int32)
    owner = jnp.zeros((devices,), jnp.int32)
    for s, bit in enumerate(bits):
        rank = len(bits) - 1 - s
        place = place + jnp.where(((index ^ me) & bit) != 0, 1 << rank, 0)
        owner = owner + jnp.where(((index >> rank) & 1) != 0, bit, 0)
    return place, owner ^ me


def after(x, *others):
    return lax.optimization_barrier((x, others))[0]


def swap(x, axis, bit):
    return lax.ppermute(x, axis, [(i, i ^ bit) for i in range(lax.axis_size(axis))])


def gather_halves(parts):
    stages = list(reversed(halving_stages()))
    done, steps = [], []
    for n, x in enumerate(parts):
        own = []
        for s, (axis, bit) in enumerate(stages):
            if n:
                x = after(x, done[s])
            got = swap(x, axis, bit)
            if s == len(stages) - 1:
                own.append(got)
                steps.append((x, got))
            else:
                x = jnp.concatenate([x, got], axis=0)
                own.append(x)
        done = own
        if n == 0:
            first = own
    return steps, first


def scatter_stages():
    return len(halving_stages())


def scatter_step(keep, send, s, between=None):
    stages = halving_stages()
    got = swap(send, *stages[s])
    if between is not None:
        beside = between()
        got = after(got, beside[1])
        return (*scatter_join(keep, got, s == len(stages) - 1), beside)
    return scatter_join(keep, got, s == len(stages) - 1)


def scatter_join(keep, got, last):
    if last:
        return keep[0] + got[0].astype(f32), None
    half = keep.shape[0] // 2
    send = (keep[half:] + got[half:].astype(f32)).astype(bf16)
    return keep[:half] + got[:half].astype(f32), send


def pack_kernel(qkv, out, up, down, *refs):
    *small, first, second = refs
    rows = qkv.shape[0]
    for c in range(3):
        first[0, c * rows : (c + 1) * rows, :] = qkv[:, c * MODEL : (c + 1) * MODEL]
    row = sublanes(16, PAIR)
    side = jnp.zeros((16, PAIR), f32)
    for v, item in enumerate(small):
        width = item.shape[1]
        spread = jnp.where(sublanes(width, PAIR) == lanes(width, PAIR), 1.0, 0.0).astype(bf16)
        tall = jnp.broadcast_to(item[...].astype(f32), (16, width)).astype(bf16)
        side = side + jnp.where(row == v, nn(tall, spread), 0.0)
    side = jnp.concatenate([side, jnp.zeros((16, MODEL - PAIR), f32)], axis=1)
    first[0, 3 * rows : 3 * rows + 16, :] = side.astype(bf16)
    parts = up.shape[1] // MODEL
    for c in range(parts):
        second[0, c * rows : (c + 1) * rows, :] = up[:, c * MODEL : (c + 1) * MODEL]
    second[0, parts * rows : 2 * parts * rows, :] = down[...]
    second[0, 2 * parts * rows :, :] = out[...]


def run_pack(qkv, out, up, down, small):
    rows = qkv.shape[0]
    parts = up.shape[1] // MODEL
    return pl.pallas_call(
        pack_kernel,
        name="pack",
        out_shape=[
            jax.ShapeDtypeStruct((1, 3 * rows + 16, MODEL), bf16),
            jax.ShapeDtypeStruct((1, (2 * parts + 1) * rows, MODEL), bf16),
        ],
    )(qkv, out, up, down, *(item[None] for item in small))


def sort_first_kernel(place, own, got, owner, qkv, vectors, *, widths):
    half, total, _ = own.shape
    rows = total // 4

    def part(d):
        p = place[d]
        q = lax.rem(p, half)
        return jnp.where(p < half, own[q, : 3 * rows, :], got[q, : 3 * rows, :])

    for d in range(2 * half):
        block = part(d)
        for c in range(3):
            qkv[d * rows : (d + 1) * rows, c * MODEL : (c + 1) * MODEL] = block[
                c * rows : (c + 1) * rows, :
            ]
    small = jnp.concatenate(
        [own[:, 3 * rows :, :PAIR].astype(f32), got[:, 3 * rows :, :PAIR].astype(f32)], axis=0
    )
    row = lax.broadcasted_iota(jnp.int32, small.shape, 1)
    vectors[...] = jnp.zeros_like(vectors)
    for v, width in enumerate(widths):
        values = jnp.sum(jnp.where(row == v, small, 0.0), axis=1)
        size = 2 * half * width
        lane = lanes(PAIR, size) % width
        spread = jnp.where(lane == sublanes(PAIR, size), 1.0, 0.0).astype(bf16)
        wide = nn(values.astype(bf16), spread)
        mine = (lanes(2 * half, size) // width) == owner[...]
        vectors[v : v + 1, :size] = jnp.sum(jnp.where(mine, wide, 0.0), axis=0, keepdims=True)


def run_sort_first(place, owner, own, got, widths):
    devices = place.shape[0]
    rows = own.shape[1] // 4
    vmem = pl.BlockSpec(memory_space=pltpu.VMEM)
    return pl.pallas_call(
        functools.partial(sort_first_kernel, widths=widths),
        name="sort_first",
        in_specs=[pl.BlockSpec(memory_space=pltpu.SMEM), vmem, vmem, vmem],
        out_specs=[vmem, vmem],
        out_shape=[
            jax.ShapeDtypeStruct((devices * rows, 3 * MODEL), bf16),
            jax.ShapeDtypeStruct((8, devices * max(widths)), f32),
        ],
        compiler_params=pltpu.CompilerParams(vmem_limit_bytes=VMEM_LIMIT),
    )(place, own, got, owner[:, None])


def sort_second_kernel(gathered, up, down, out):
    devices, total, _ = gathered.shape
    parts = up.shape[1] // MODEL
    rows = total // (2 * parts + 1)
    tall = parts * rows
    for d in range(devices):
        for c in range(parts):
            up[d * rows : (d + 1) * rows, c * MODEL : (c + 1) * MODEL] = gathered[
                d, c * rows : (c + 1) * rows, :
            ]
        down[d * tall : (d + 1) * tall, :] = gathered[d, tall : 2 * tall, :]
        out[d * rows : (d + 1) * rows, :] = gathered[d, 2 * tall :, :]


def run_sort_second(gathered, ff):
    devices = gathered.shape[0]
    rows = gathered.shape[1] // (2 * (ff // MODEL) + 1)
    vmem = pl.BlockSpec(memory_space=pltpu.VMEM)
    return pl.pallas_call(
        sort_second_kernel,
        name="sort_second",
        in_specs=[vmem],
        out_specs=[vmem, vmem, vmem],
        out_shape=[
            jax.ShapeDtypeStruct((devices * rows, ff), bf16),
            jax.ShapeDtypeStruct((ff, MODEL), bf16),
            jax.ShapeDtypeStruct((devices * rows, MODEL), bf16),
        ],
        compiler_params=pltpu.CompilerParams(vmem_limit_bytes=VMEM_LIMIT),
    )(gathered)


def gather_all(x):
    return lax.all_gather(x, BOTH, axis=0, tiled=True)


def scatter_all(x):
    return lax.psum_scatter(x, BOTH, scatter_dimension=0, tiled=True)


def to_dp(group):
    return lax.all_to_all(group, "dp", split_axis=0, concat_axis=0, tiled=True)


def groups_of(micro):
    return [(0, micro - 1), (micro - 1, 1)] if micro > 1 else [(0, 1)]


def find(groups, m):
    for g, (first, members) in enumerate(groups):
        if first <= m < first + members:
            return g, m - first


def body(
    tokens,
    cotangent,
    lengths,
    stretch_order,
    ln1_gain,
    ln1_bias,
    w_qkv,
    b_qkv,
    w_out,
    b_out,
    ln2_gain,
    ln2_bias,
    w_up,
    b_up,
    w_down,
    b_down,
):
    micro, rows, width = tokens.shape
    count = rows // STRETCH
    devices = lax.axis_size(BOTH)
    ff = w_up.shape[1]
    dp = lax.axis_size("dp")
    slot, placing, restart, opened, closing, from_before, from_after = index_tables(
        lengths, stretch_order, count
    )
    small = (ln1_gain, ln1_bias, b_qkv, b_out, ln2_gain, ln2_bias, b_up, b_down)
    in_parts = (width // devices) % 16 == 0
    groups = groups_of(micro)
    sent = run_send(slot, tokens, 0, micro)
    moved = to_dp(sent)
    if in_parts:
        place, owner = order_tables()
        first_part, second_part = run_pack(w_qkv, w_out, w_up, w_down, small)
        halves, _ = gather_halves([after(first_part, sent)])
        qkv_all, vectors = run_sort_first(
            place, owner, *halves[0], [item.shape[0] for item in small]
        )
        second_part = gather_all(second_part)
        vectors = [
            vectors[v : v + 1, : devices * item.shape[0]] for v, item in enumerate(small)
        ]
    else:
        owner = None
        qkv_all, out_all = gather_all(w_qkv), gather_all(w_out)
        up_all, down_all = gather_all(w_up), gather_all(w_down)
        vectors = [gather_all(item).astype(f32)[None] for item in small]
    gain_one, shift_one, bias_qkv, bias_out, gain_two, shift_two, bias_up, bias_down = vectors
    tables = (placing, restart, opened)
    vectors = [bias_qkv, gain_one, shift_one, bias_out, gain_two, shift_two, bias_up, bias_down]

    hops = from_before.shape[1]
    states = run_state(placing, closing, moved, qkv_all, bias_qkv, gain_one, shift_one)
    incoming = exchange(states, hops, True)
    cots = [
        to_dp(run_send(slot, after(cotangent, states), first, members))
        for first, members in groups
    ]
    if in_parts:
        up_all, down_all, out_all = run_sort_second(after(second_part, states), ff)
    incoming = joined(incoming, from_before, out_all)
    weights = [qkv_all, out_all, up_all, down_all]
    mids, sums = [], None
    for g, (first, members) in enumerate(groups):
        target = blank((dp, members, count // dp, STRETCH, width))
        out = run_mid(
            tables,
            first,
            members,
            target,
            moved,
            (cots[g], 0),
            incoming,
            weights,
            vectors,
            sums,
            owner if g == len(groups) - 1 else None,
        )
        sums = out[8:]
        mids.append(out)
    outgoing = [exchange(out[6], hops, False) for out in mids]
    reach = [from_after[first : first + members] for first, members in groups]
    homes = [to_dp(out[0]) for out in mids]
    sizes = [MODEL, MODEL, 2 * MODEL, MODEL, MODEL, MODEL, MODEL, ff, MODEL]
    widths = [size // devices for size in sizes]
    last = scatter_stages() - 1
    late = len(groups) - 1
    outgoing[0] = joined(outgoing[0], reach[0], *([mids[-1][7]] if late else []))
    if in_parts:
        done = 0
        keep, send = sums
        if late:
            send = after(send, outgoing[0], homes[0])
        keep, send = scatter_step(keep, send, done)
    vec_mid = [f[7] for f in mids]
    vec_back, total = [], None
    grad_rows = [blank((dp, members, count // dp, STRETCH, width)) for _, members in groups]
    for m in range(micro):
        g, seat = find(groups, m)
        saved = list(mids[g])
        if late and g == late:
            outgoing[g] = joined(outgoing[g], reach[g], vec_back[0])

        def run(m=m, g=g, seat=seat, saved=saved, total=total, vec_back=tuple(vec_back)):
            return run_back(
                tables,
                m,
                1,
                (grad_rows[g], seat),
                moved,
                (saved, seat),
                outgoing[g],
                qkv_all,
                gain_one,
                shift_one,
                total,
                owner if m == micro - 1 else None,
                vec_mid + list(vec_back),
                widths,
            )

        if in_parts and done < last - 1:
            done += 1
            saved[2], keep, send = lax.optimization_barrier((saved[2], keep, send))
            keep, send, out = scatter_step(keep, send, done, run)
        else:
            out = run()
        grad_rows[g] = out[0]
        vec_back.append(out[1])
        total = out[2]
        if m == 0 and late:
            homes[late] = after(homes[late], out[1])
    narrow = out[2:]
    result = blank((micro, count, STRETCH, width))
    input_grad = blank((micro, count, STRETCH, width))
    for (first, _), home in zip(groups, homes, strict=True):
        result = run_land(slot, home, result, first)
    grad_homes = [to_dp(group) for group in grad_rows]
    for (first, _), home in zip(groups, grad_homes, strict=True):
        input_grad = run_land(slot, home, input_grad, first)
    result = result.reshape(micro, rows, width)
    input_grad = input_grad.reshape(micro, rows, width)
    if in_parts:
        part = width // devices
        narrow_keep, narrow_send = narrow
        if len(groups) > 1:
            narrow_send = after(narrow_send, grad_homes[0])
        while done < last:
            done += 1
            narrow_send = after(narrow_send, keep, send)
            keep, send = scatter_step(keep, send, done)
        parts = ff // MODEL
        grad_up = jnp.concatenate([keep[c * part : (c + 1) * part] for c in range(parts)], axis=1)
        grad_down = keep[parts * part : 2 * parts * part]
        grad_out = keep[2 * parts * part :]
        keep, send = narrow_keep, narrow_send
        for step in range(last + 1):
            keep, send = scatter_step(keep, send, step)
        grad_qkv = jnp.concatenate([keep[c * part : (c + 1) * part] for c in range(3)], axis=1)
        owned_vec = [keep[3 * part + v, :size] for v, size in enumerate(widths)]
    else:
        grad_up, grad_down, grad_out = (scatter_all(x) for x in (sums[0], sums[1].T, sums[2]))
        grad_qkv = scatter_all(total)
        mid, back = sum(vec_mid), sum(vec_back)
        vec = (
            back[1, :MODEL],
            back[1, MODEL : 2 * MODEL],
            back[0, : 2 * MODEL],
            back[0, 2 * MODEL :],
            mid[1, 2 * MODEL : 3 * MODEL],
            mid[1, :MODEL],
            mid[1, MODEL : 2 * MODEL],
            mid[0],
            mid[1, 3 * MODEL :],
        )
        owned_vec = [scatter_all(item) for item in vec]
    g_gain1, g_bias1, g_qk, g_value, g_bout, g_gain2, g_bias2, g_bup, g_bdown = owned_vec
    return (
        result,
        input_grad,
        g_gain1,
        g_bias1,
        grad_qkv,
        g_qk,
        g_value,
        grad_out,
        g_bout,
        g_gain2,
        g_bias2,
        grad_up,
        g_bup,
        grad_down,
        g_bdown,
    )


def solution(mesh):
    rows = P(None, BOTH, None)
    vector = P(BOTH)
    matrix = P(BOTH, None)
    in_specs = (
        rows, rows, P(), P(), vector, vector, matrix, vector, matrix, vector, vector, vector,
        matrix, vector, matrix, vector,
    )
    out_specs = (
        rows, rows, vector, vector, matrix, vector, vector, matrix, vector, vector, vector,
        matrix, vector, matrix, vector,
    )
    return jax.shard_map(body, mesh=mesh, in_specs=in_specs, out_specs=out_specs, check_vma=False)
```

time: 639 us -> 427 us (0.67)
  waiting for transfers between devices: 132 us -> 77.2 us
  starting transfers between devices: 130 us -> 80.2 us
  blocking collectives: 47.2 us -> 0 us
  matrix products: 36.1 us -> 0 us
  local copies, waits for them, and re-layouts: 39.7 us -> 17.6 us
  other arithmetic: 41.2 us -> 24.9 us
  between operations: 2.43 us -> 14.7 us
    unnamed x1 -> x0, blocking collectives: 47.2 us -> none
    dot_general x12 -> x0, matrix products: 36.1 us -> none  [tn(): lax.dot_general(a, b, (((0,), (0,)), ((), ())), preferred_element_type=f32)]
    ppermute x51 -> x24, waiting for transfers between devices: 99 us -> 67.7 us  [the longest x15 59.7 us: swap(): lax.ppermute(x, axis, [(i, i ^ bit) for i in range(lax.axis_size(axis))])]
    ppermute x51 -> x24, starting transfers between devices: 81.6 us -> 54.9 us  [the longest x15 38.7 us: swap(): lax.ppermute(x, axis, [(i, i ^ bit) for i in range(lax.axis_size(axis))])]
    all_to_all x12 -> x7, waiting for transfers between devices: 32.7 us -> 9.49 us  [to_dp(): return lax.all_to_all(group, 'dp', split_axis=0, concat_axis=0, tiled=True)]
    all_to_all x12 -> x7, starting transfers between devices: 48.2 us -> 25.3 us  [to_dp(): return lax.all_to_all(group, 'dp', split_axis=0, concat_axis=0, tiled=True)]
    squeeze x8 -> x3, local copies, waits for them, and re-layouts: 11 us -> 1.57 us  [body(): owned_vec = [keep[3 * part + v, :size] for v, size in enumerate(widths)]]
    another operation x4 -> x0, other arithmetic: 9.16 us -> none  [the longest x1 3.82 us: body(): home_grad = jnp.stack([to_dp(backs[m][0]) for m in range(micro)])]
  transfers between devices with their start and end apart: 63 -> 32, of which waited for: 27 -> 15; matrix products, arithmetic and copies ran while one was open for 17% -> 7% of each run, Pallas kernels for 32% -> 46%
where the time goes in v2:
time: 427 us; the launch traced here: 421 us
  Pallas kernels  206 us (48%)
  starting transfers between devices  80.2 us (19%)
  waiting for transfers between devices  77.2 us (18%)
  other arithmetic  24.9 us (6%)
  local copies, waits for them, and re-layouts  17.6 us (4%)
  between operations  14.7 us (3%)
    pallas_call x2, Pallas kernels, run_mid(): pl.pallas_call(functools.partial(mid_kernel, first=first, resumes=resumes...  100 us
    pallas_call x3, Pallas kernels, run_back(): pl.pallas_call(functools.partial(back_kernel, first=first, resumes=resume...  60 us
    ppermute x15, waiting for transfers between devices, swap(): lax.ppermute(x, axis, [(i, i ^ bit) for i in range(lax.axis_size(axis))])  59.7 us
    ppermute x15, starting transfers between devices, swap(): lax.ppermute(x, axis, [(i, i ^ bit) for i in range(lax.axis_size(axis))])  38.7 us
    all_to_all x7, starting transfers between devices, to_dp(): return lax.all_to_all(group, 'dp', split_axis=0, concat_axis=0, tiled=True)  25.3 us
    ppermute x9, starting transfers between devices, exchange(): got.append(lax.ppermute(states, 'fsdp', pairs))  16.2 us
    pallas_call x4, Pallas kernels, run_land(): pl.pallas_call(land_kernel, name='land', grid_spec=pltpu.PrefetchScalarGr...  12.5 us
    pallas_call x3, Pallas kernels, run_send(): pl.pallas_call(send_kernel, name='send', grid_spec=pltpu.PrefetchScalarGr...  11.7 us
  transfers between devices with their start and end apart: 32, of which 15 were waited for; matrix products, arithmetic and copies ran while one was open for 7% of the time, Pallas kernels for 46%

profile of v2, /device:TPU:0, one launch (start us, length us, event | category | flops | bytes accessed | tf_op | source)
XLA Modules:
  0.0 420.6 jit_solution(12599019154070233531)
XLA Ops:
  7.2 1.8 pack.1
  10.8 5.3 %send.3 = bf16[4,3,4,64,512]{4,3,2,1,0:T(8,128)(2,1)} custom-call(s32[3,16]{1,0:T(4,128)} %convert_reduce_fusion.1.slot, bf16[3,16,64,512]{3,2,1,0:T(8,128)(2,1)} %bitcast.56), custom_call_target="tpu_custom_call" | custom-call | bytes 6291456 | tf_op jit(solution)/shard_map/send/pallas_call | solution.py:825
  16.2 2.9 collective-permute-start
  19.1 2.2 collective-permute-done
  21.4 3.2 collective-permute-start.1
  24.6 3.7 all-to-all-start
  28.3 3.4 collective-permute-done.1
  33.2 6.2 %collective-permute-done.2 = bf16[4,64,512]{2,1,0:T(8,128)(2,1)S(1)} collective-permute-done((bf16[4,64,512]{2,1,0:T(8,128)(2,1)S(1)}, bf16[4,64,512]{2,1,0:T(8,128)(2,1)S(1)}, u32[]{:S(2)}, u32[]{:S(2)}) %collective-permute-start.2) | collective-permute-done | bytes 262176 | tf_op jit(solution)/shard_map/ppermute | solution.py:982
  43.7 10.1 %collective-permute-done.3 = bf16[8,64,512]{2,1,0:T(8,128)(2,1)S(1)} collective-permute-done((bf16[8,64,512]{2,1,0:T(8,128)(2,1)S(1)}, bf16[8,64,512]{2,1,0:T(8,128)(2,1)S(1)}, u32[]{:S(2)}, u32[]{:S(2)}) %collective-permute-start.3) | collective-permute-done | bytes 524320 | tf_op jit(solution)/shard_map/ppermute | solution.py:982
  57.6 3.5 sort_first.1
  64.0 9.3 %all-to-all-done.rows.rows_ref = bf16[4,3,4,64,512]{4,3,2,1,0:T(8,128)(2,1)S(1)} async-done(((bf16[4,3,4,64,512]{4,3,2,1,0:T(8,128)(2,1)}), bf16[4,3,4,64,512]{4,3,2,1,0:T(8,128)(2,1)S(1)}, u32[]{:S(2)}, u32[]{:S(2)}) %all-to-all-start) | async-done | bytes 3145760 | tf_op jit(solution)/shard_map/all_to_all | solution.py:1150
  75.0 11.6 %end_state.1 = f32[3,72,512]{2,1,0:T(8,128)} custom-call(s32[3,16]{1,0:T(4,128)} %get-tuple-element.200.placing, s32[3,16]{1,0:T(4,128)} %get-tuple-element.199.closing, bf16[4,3,4,64,512]{4,3,2,1,0:T(8,128)(2,1)} %copy-done.4, bf16[512,1536]{1,0:T(8,128)(2,1)} %get-tuple-element.81.weight.w_qkv, f32[1,1536]{1,0:T(1,128)} %slice.248.bias.b_qkv, ...), custom_call_target="tpu_custom_call" | custom-call | flops 3221225472 | bytes 5242880 | tf_op jit(solution)/shard_map/end_state/pallas_call | solution.py:194
  86.6 3.4 send.4
  90.0 3.6 all-to-all-start.1
  94.8 3.5 collective-permute-start.5
  98.3 3.6 collective-permute-start.6
  105.9 3.0 send.5
  108.9 4.5 %sort_second.1 = (bf16[512,2048]{1,0:T(8,128)(2,1)}, bf16[2048,512]{1,0:T(8,128)(2,1)}, bf16[512,512]{1,0:T(8,128)(2,1)}) custom-call(bf16[32,144,512]{2,1,0:T(8,128)(2,1)} %all-gather.2.cloned.1.call-done.gathered), custom_call_target="tpu_custom_call" | custom-call | tf_op jit(solution)/shard_map/sort_second/pallas_call | solution.py:1127
  113.5 8.0 %collective-permute-done.7 = f32[3,72,512]{2,1,0:T(8,128)S(1)} collective-permute-done((f32[3,72,512]{2,1,0:T(8,128)}, f32[3,72,512]{2,1,0:T(8,128)S(1)}, u32[]{:S(2)}, u32[]{:S(2)}) %collective-permute-start.7) | collective-permute-done | bytes 442400 | tf_op jit(solution)/shard_map/ppermute | solution.py:936
  122.5 3.5 all-to-all-start.3
  126.5 62.8 %middle.2 = (bf16[4,2,4,64,512]{4,3,2,1,0:T(8,128)(2,1)}, bf16[2048,1536]{1,0:T(8,128)(2,1)}, bf16[2048,512]{1,0:T(8,128)(2,1)}, bf16[2048,512]{1,0:T(8,128)(2,1...) custom-call(s32[3,16]{1,0:T(4,128)} %get-tuple-element.200.placing, ...), custom_call_target="tpu_custom_call", output_to_operand_aliasing={{0}: (4, {})} | custom-call | flops 40802189312 | bytes 41943040 | tf_op jit(solution)/shard_map/middle/pallas_call | solution.py:506
  193.3 3.6 all-to-all-start.2
  196.9 37.7 %middle.3 = (bf16[4,1,4,64,512]{4,3,2,1,0:T(8,128)(2,1)}, bf16[1024,1536]{1,0:T(8,128)(2,1)}, bf16[1024,512]{1,0:T(8,128)(2,1)}, bf16[1024,512]{1,0:T(8,128)(2,1...) custom-call(s32[3,16]{1,0:T(4,128)} %get-tuple-element.200.placing, ...), custom_call_target="tpu_custom_call", output_to_operand_aliasing={{0}: (4, {})} | custom-call | flops 20401094656 | bytes 20971520 | tf_op jit(solution)/shard_map/middle/pallas_call | solution.py:506
  234.6 1.9 multiply_add_fusion.1.inc_ref
  237.0 4.4 %collective-permute-done.11 = bf16[16,144,512]{2,1,0:T(8,128)(2,1)S(1)} collective-permute-done((bf16[16,144,512]{2,1,0:T(8,128)(2,1)}, bf16[16,144,512]{2,1,0:T(8,128)(2,1)S(1)}, u32[]{:S(2)}, u32[]{:S(2)}) %collective-permute-start.11) | collective-permute-done | bytes 2359328 | tf_op jit(solution)/shard_map/ppermute | solution.py:982
  241.3 3.4 add_convert_fusion
  244.7 8.5 %collective-permute-start.12 = (bf16[8,144,512]{2,1,0:T(8,128)(2,1)S(1)}, bf16[8,144,512]{2,1,0:T(8,128)(2,1)}, u32[]{:S(2)}, u32[]{:S(2)}) collective-permute-start(bf16[8,144,512]{2,1,0:T(8,128)(2,1)S(1)} %get-tuple-element.115), channel_id=1, source_target_pairs={{0,1},{1,0},{2,3},{3,2},{4,5},{5,4},{6,7},{7,6},{8,9},{9,8},{10,11... | collective-permute-start | bytes 3538952 | tf_op jit(solution)/shard_map/ppermute | solution.py:982
  257.7 19.4 %back.3 = (bf16[4,2,4,64,512]{4,3,2,1,0:T(8,128)(2,1)}, f32[8,1536]{1,0:T(8,128)}, f32[512,1536]{1,0:T(8,128)}) custom-call(s32[3,16]{1,0:T(4,128)} %get-tuple-element.200.placing, s32[3,17]{1,0:T(4,128)} %convert_select_fusion.restart, s32[8]{0:T(128)} %broadcast_12_owner.2.owner, ...), custom_call_target="tpu_custom_call", output_to_operand_aliasing={{0}: (3, {})} | custom-call | flops 11811160064 | bytes 14680064 | tf_op jit(solution)/shard_map/back/pallas_call | solution.py:755
  277.1 8.2 %collective-permute-done.12 = bf16[8,144,512]{2,1,0:T(8,128)(2,1)} collective-permute-done((bf16[8,144,512]{2,1,0:T(8,128)(2,1)S(1)}, bf16[8,144,512]{2,1,0:T(8,128)(2,1)}, u32[]{:S(2)}, u32[]{:S(2)}) %collective-permute-start.12) | collective-permute-done | bytes 1179680 | tf_op jit(solution)/shard_map/ppermute | solution.py:982
  285.3 2.5 add_convert_fusion.1
  287.7 11.1 %collective-permute-start.13 = (bf16[4,144,512]{2,1,0:T(8,128)(2,1)}, bf16[4,144,512]{2,1,0:T(8,128)(2,1)S(1)}, u32[]{:S(2)}, u32[]{:S(2)}) collective-permute-start(bf16[4,144,512]{2,1,0:T(8,128)(2,1)} %get-tuple-element.125), channel_id=1, source_target_pairs={{0,2},{1,3},{2,0},{3,1},{4,6},{5,7},{6,4},{7,5},{8,10},{9,11},{10,... | collective-permute-start | bytes 1769480 | tf_op jit(solution)/shard_map/ppermute | solution.py:982
  298.8 19.8 %back.4 = (bf16[4,2,4,64,512]{4,3,2,1,0:T(8,128)(2,1)}, f32[8,1536]{1,0:T(8,128)}, f32[512,1536]{1,0:T(8,128)}) custom-call(s32[3,16]{1,0:T(4,128)} %get-tuple-element.200.placing, s32[3,17]{1,0:T(4,128)} %convert_select_fusion.restart, s32[8]{0:T(128)} %broadcast_12_owner.2.owner, ...), custom_call_target="tpu_custom_call", output_to_operand_aliasing={{0}: (3, {})} | custom-call | flops 11811160064 | bytes 14680064 | tf_op jit(solution)/shard_map/back/pallas_call | solution.py:755
  321.2 3.7 multiply_add_fusion.2.inc_ref
  324.9 3.8 all-to-all-start.5
  328.8 6.3 %collective-permute-done.17 = bf16[2,144,512]{2,1,0:T(8,128)(2,1)S(1)} collective-permute-done((bf16[2,144,512]{2,1,0:T(8,128)(2,1)}, bf16[2,144,512]{2,1,0:T(8,128)(2,1)S(1)}, u32[]{:S(2)}, u32[]{:S(2)}) %collective-permute-start.17) | collective-permute-done | bytes 294944 | tf_op jit(solution)/shard_map/ppermute | solution.py:982
  336.6 20.8 %back.5 = (bf16[4,1,4,64,512]{4,3,2,1,0:T(8,128)(2,1)}, f32[8,1536]{1,0:T(8,128)}, f32[16,64,512]{2,1,0:T(8,128)}, bf16[16,64,512]{2,1,0:T(8,128)(2,1)}) custom-call(s32[3,16]{1,0:T(4,128)} %get-tuple-element.200.placing, s32[3,17]{1,0:T(4,128)} %convert_select_fusion.restart, s32[32]{0:T(128)} %fusion.26.owner, ...), custom_call_target="tpu_custom_call", output_to_operand_aliasing={{0}: (3, {})} | custom-call | flops 11811160064 | bytes 14680064 | tf_op jit(solution)/shard_map/back/pallas_call | solution.py:755
  357.7 2.9 collective-permute-done.18
  360.6 2.8 add_convert_fusion.2
  363.4 2.5 collective-permute-start.19
  365.9 3.5 all-to-all-start.4
  369.4 8.9 %collective-permute-done.19 = bf16[8,64,512]{2,1,0:T(8,128)(2,1)S(1)} collective-permute-done((bf16[8,64,512]{2,1,0:T(8,128)(2,1)}, bf16[8,64,512]{2,1,0:T(8,128)(2,1)S(1)}, u32[]{:S(2)}, u32[]{:S(2)}) %collective-permute-start.19) | collective-permute-done | bytes 524320 | tf_op jit(solution)/shard_map/ppermute | solution.py:982
  380.4 3.3 land.4._
  384.8 2.9 land.5
  387.7 3.5 all-to-all-start.6
  392.0 2.2 collective-permute-start.21
  394.8 6.8 %collective-permute-done.21 = bf16[2,64,512]{2,1,0:T(8,128)(2,1)S(1)} collective-permute-done((bf16[2,64,512]{2,1,0:T(8,128)(2,1)S(1)}, bf16[2,64,512]{2,1,0:T(8,128)(2,1)S(1)}, u32[]{:S(2)}, u32[]{:S(2)}) %collective-permute-start.21) | collective-permute-done | bytes 131104 | tf_op jit(solution)/shard_map/ppermute | solution.py:982
  404.1 3.3 land.6._
  408.3 2.9 land.7
  (122 shorter events, 46.0 us)
Async XLA Ops:
  7.2 101.7 %all-gather.2.cloned.1.call-start = ((), (), s32[]{:S(2)}) async-start(), calls=%async_computation.7 | async-start | bytes 4866048 | tf_op jit(solution)/shard_map/all_gather | solution.py:1142
  10.8 5.3 %copy-start.8 = (bf16[1,64,512]{2,1,0:T(8,128)(2,1)S(1)}, bf16[1,64,512]{2,1,0:T(8,128)(2,1)}, u32[]{:S(2)}) copy-start(bf16[1,64,512]{2,1,0:T(8,128)(2,1)} %get-tuple-element.80) | copy-start | bytes 196612
  16.2 5.2 %collective-permute-start = (bf16[1,64,512]{2,1,0:T(8,128)(2,1)S(1)}, bf16[1,64,512]{2,1,0:T(8,128)(2,1)S(1)}, u32[]{:S(2)}, u32[]{:S(2)}) collective-permute-start(bf16[1,64,512]{2,1,0:T(8,128)(2,1)S(1)} %copy-done.8), channel_id=1, source_target_pairs={{0,16},{8,24},{16,0},{24,8},{1,17},{9,25},{17,1},{25,9},{2,18},{10... | collective-permute-start | bytes 196616 | tf_op jit(solution)/shard_map/ppermute | solution.py:982
  21.4 10.4 %collective-permute-start.1 = (bf16[2,64,512]{2,1,0:T(8,128)(2,1)S(1)}, bf16[2,64,512]{2,1,0:T(8,128)(2,1)S(1)}, u32[]{:S(2)}, u32[]{:S(2)}) collective-permute-start(bf16[2,64,512]{2,1,0:T(8,128)(2,1)S(1)} %pad_maximum_fusion.2), channel_id=1, source_target_pairs={{0,4},{1,5},{2,6},{3,7},{4,0},{5,1},{6,2},{7,3},{8,12},{9,13},{10,... | collective-permute-start | bytes 393224 | tf_op jit(solution)/shard_map/ppermute | solution.py:982
  24.6 48.8 %all-to-all-start = ((bf16[4,3,4,64,512]{4,3,2,1,0:T(8,128)(2,1)}), bf16[4,3,4,64,512]{4,3,2,1,0:T(8,128)(2,1)S(1)}, u32[]{:S(2)}, u32[]{:S(2)}) async-start(bf16[4,3,4,64,512]{4,3,2,1,0:T(8,128)(2,1)} %send.3), calls=%async_computation | async-start | bytes 6291456 | tf_op jit(solution)/shard_map/all_to_all | solution.py:1150
  28.3 26.3 %copy-start.9 = (s32[3,16]{1,0:T(4,128)S(1)}, s32[3,16]{1,0:T(4,128)}, u32[]{:S(2)}) copy-start(s32[3,16]{1,0:T(4,128)} %convert_reduce_fusion.1.slot) | copy-start | bytes 580
  31.8 7.7 %collective-permute-start.2 = (bf16[4,64,512]{2,1,0:T(8,128)(2,1)S(1)}, bf16[4,64,512]{2,1,0:T(8,128)(2,1)S(1)}, u32[]{:S(2)}, u32[]{:S(2)}) collective-permute-start(bf16[4,64,512]{2,1,0:T(8,128)(2,1)S(1)} %pad_maximum_fusion.1), channel_id=1, source_target_pairs={{0,2},{1,3},{2,0},{3,1},{4,6},{5,7},{6,4},{7,5},{8,10},{9,11},{10,... | collective-permute-start | bytes 786440 | tf_op jit(solution)/shard_map/ppermute | solution.py:982
  39.5 14.3 %collective-permute-start.3 = (bf16[8,64,512]{2,1,0:T(8,128)(2,1)S(1)}, bf16[8,64,512]{2,1,0:T(8,128)(2,1)S(1)}, u32[]{:S(2)}, u32[]{:S(2)}) collective-permute-start(bf16[8,64,512]{2,1,0:T(8,128)(2,1)S(1)} %pad_maximum_fusion), channel_id=1, source_target_pairs={{0,1},{1,0},{2,3},{3,2},{4,5},{5,4},{6,7},{7,6},{8,9},{9,8},{10,11... | collective-permute-start | bytes 1572872 | tf_op jit(solution)/shard_map/ppermute | solution.py:982
  43.0 13.4 %copy-start.10 = (s32[3,16]{1,0:T(4,128)S(1)}, s32[3,16]{1,0:T(4,128)}, u32[]{:S(2)}) copy-start(s32[3,16]{1,0:T(4,128)} %param.18) | copy-start | bytes 580
  54.6 3.0 collective-permute-start.4
  73.4 1.7 copy-start.4
  90.0 32.5 %all-to-all-start.1 = ((bf16[4,2,4,64,512]{4,3,2,1,0:T(8,128)(2,1)}), bf16[4,2,4,64,512]{4,3,2,1,0:T(8,128)(2,1)S(1)}, u32[]{:S(2)}, u32[]{:S(2)}) async-start(bf16[4,2,4,64,512]{4,3,2,1,0:T(8,128)(2,1)} %send.4), calls=%async_computation.1 | async-start | bytes 4194304 | tf_op jit(solution)/shard_map/all_to_all | solution.py:1150
  94.8 18.6 %collective-permute-start.5 = (f32[3,72,512]{2,1,0:T(8,128)}, f32[3,72,512]{2,1,0:T(8,128)S(1)}, u32[]{:S(2)}, u32[]{:S(2)}) collective-permute-start(f32[3,72,512]{2,1,0:T(8,128)} %end_state.1), channel_id=1, source_target_pairs={{0,1},{1,2},{2,3},{3,4},{4,5},{5,6},{6,7},{8,9},{9,10},{10,11},{11... | collective-permute-start | bytes 1327112 | tf_op jit(solution)/shard_map/ppermute | solution.py:936
  98.3 15.1 %collective-permute-start.6 = (f32[3,72,512]{2,1,0:T(8,128)}, f32[3,72,512]{2,1,0:T(8,128)S(1)}, u32[]{:S(2)}, u32[]{:S(2)}) collective-permute-start(f32[3,72,512]{2,1,0:T(8,128)} %end_state.1), channel_id=1, source_target_pairs={{0,2},{1,3},{2,4},{3,5},{4,6},{5,7},{8,10},{9,11},{10,12},{11,13},... | collective-permute-start | bytes 1327112 | tf_op jit(solution)/shard_map/ppermute | solution.py:936
  101.9 19.5 %collective-permute-start.7 = (f32[3,72,512]{2,1,0:T(8,128)}, f32[3,72,512]{2,1,0:T(8,128)S(1)}, u32[]{:S(2)}, u32[]{:S(2)}) collective-permute-start(f32[3,72,512]{2,1,0:T(8,128)} %end_state.1), channel_id=1, source_target_pairs={{0,3},{1,4},{2,5},{3,6},{4,7},{8,11},{9,12},{10,13},{11,14},{12,15... | collective-permute-start | bytes 1327112 | tf_op jit(solution)/shard_map/ppermute | solution.py:936
  122.5 4.0 copy-start.6
  122.5 70.8 %all-to-all-start.3 = ((bf16[4,1,4,64,512]{4,3,2,1,0:T(8,128)(2,1)}), bf16[4,1,4,64,512]{4,3,2,1,0:T(8,128)(2,1)S(1)}, u32[]{:S(2)}, u32[]{:S(2)}) async-start(bf16[4,1,4,64,512]{4,3,2,1,0:T(8,128)(2,1)} %send.5), calls=%async_computation.3 | async-start | bytes 2097152 | tf_op jit(solution)/shard_map/all_to_all | solution.py:1150
  189.3 45.2 %collective-permute-start.10 = (f32[2,72,512]{2,1,0:T(8,128)}, f32[2,72,512]{2,1,0:T(8,128)S(1)}, u32[]{:S(2)}, u32[]{:S(2)}) collective-permute-start(f32[2,72,512]{2,1,0:T(8,128)} %get-tuple-element.103), channel_id=1, source_target_pairs={{3,0},{4,1},{5,2},{6,3},{7,4},{11,8},{12,9},{13,10},{14,11},{15,12... | collective-permute-start | bytes 884744 | tf_op jit(solution)/shard_map/ppermute | solution.py:936
  190.6 43.9 %collective-permute-start.8 = (f32[2,72,512]{2,1,0:T(8,128)}, f32[2,72,512]{2,1,0:T(8,128)}, u32[]{:S(2)}, u32[]{:S(2)}) collective-permute-start(f32[2,72,512]{2,1,0:T(8,128)} %get-tuple-element.103), channel_id=1, source_target_pairs={{1,0},{2,1},{3,2},{4,3},{5,4},{6,5},{7,6},{9,8},{10,9},{11,10},{12... | collective-permute-start | bytes 884744 | tf_op jit(solution)/shard_map/ppermute | solution.py:936
  191.9 42.6 %collective-permute-start.9 = (f32[2,72,512]{2,1,0:T(8,128)}, f32[2,72,512]{2,1,0:T(8,128)}, u32[]{:S(2)}, u32[]{:S(2)}) collective-permute-start(f32[2,72,512]{2,1,0:T(8,128)} %get-tuple-element.103), channel_id=1, source_target_pairs={{2,0},{3,1},{4,2},{5,3},{6,4},{7,5},{10,8},{11,9},{12,10},{13,11},... | collective-permute-start | bytes 884744 | tf_op jit(solution)/shard_map/ppermute | solution.py:936
  193.2 3.6 copy-start.7
  193.3 43.2 %all-to-all-start.2 = ((bf16[4,2,4,64,512]{4,3,2,1,0:T(8,128)(2,1)}), bf16[4,2,4,64,512]{4,3,2,1,0:T(8,128)(2,1)S(1)}, u32[]{:S(2)}, u32[]{:S(2)}) async-start(bf16[4,2,4,64,512]{4,3,2,1,0:T(8,128)(2,1)} %get-tuple-element.92), calls=%async_computation.2 | async-start | bytes 4194304 | tf_op jit(solution)/shard_map/all_to_all | solution.py:1150
  236.5 4.8 %copy-start = (bf16[4,2,4,64,512]{4,3,2,1,0:T(8,128)(2,1)}, bf16[4,2,4,64,512]{4,3,2,1,0:T(8,128)(2,1)S(1)}, u32[]{:S(2)}) copy-start(bf16[4,2,4,64,512]{4,3,2,1,0:T(8,128)(2,1)S(1)} %all-to-all-done.2.source) | copy-start | bytes 6291460
  236.5 4.8 %collective-permute-start.11 = (bf16[16,144,512]{2,1,0:T(8,128)(2,1)}, bf16[16,144,512]{2,1,0:T(8,128)(2,1)S(1)}, u32[]{:S(2)}, u32[]{:S(2)}) collective-permute-start(bf16[16,144,512]{2,1,0:T(8,128)(2,1)} %get-tuple-element.108), channel_id=1, source_target_pairs={{0,8},{8,0},{16,24},{24,16},{1,9},{9,1},{17,25},{25,17},{2,10},{10... | collective-permute-start | bytes 7077896 | tf_op jit(solution)/shard_map/ppermute | solution.py:982
  244.7 40.5 %collective-permute-start.12 = (bf16[8,144,512]{2,1,0:T(8,128)(2,1)S(1)}, bf16[8,144,512]{2,1,0:T(8,128)(2,1)}, u32[]{:S(2)}, u32[]{:S(2)}) collective-permute-start(bf16[8,144,512]{2,1,0:T(8,128)(2,1)S(1)} %get-tuple-element.115), channel_id=1, source_target_pairs={{0,1},{1,0},{2,3},{3,2},{4,5},{5,4},{6,7},{7,6},{8,9},{9,8},{10,11... | collective-permute-start | bytes 3538952 | tf_op jit(solution)/shard_map/ppermute | solution.py:982
  253.2 68.0 %collective-permute-start.14 = (f32[1,72,512]{2,1,0:T(8,128)}, f32[1,72,512]{2,1,0:T(8,128)}, u32[]{:S(2)}, u32[]{:S(2)}) collective-permute-start(f32[1,72,512]{2,1,0:T(8,128)} %get-tuple-element.130), channel_id=1, source_target_pairs={{1,0},{2,1},{3,2},{4,3},{5,4},{6,5},{7,6},{9,8},{10,9},{11,10},{12... | collective-permute-start | bytes 442376 | tf_op jit(solution)/shard_map/ppermute | solution.py:936
  254.5 66.7 %collective-permute-start.15 = (f32[1,72,512]{2,1,0:T(8,128)}, f32[1,72,512]{2,1,0:T(8,128)}, u32[]{:S(2)}, u32[]{:S(2)}) collective-permute-start(f32[1,72,512]{2,1,0:T(8,128)} %get-tuple-element.130), channel_id=1, source_target_pairs={{2,0},{3,1},{4,2},{5,3},{6,4},{7,5},{10,8},{11,9},{12,10},{13,11},... | collective-permute-start | bytes 442376 | tf_op jit(solution)/shard_map/ppermute | solution.py:936
  255.8 65.4 %collective-permute-start.16 = (f32[1,72,512]{2,1,0:T(8,128)}, f32[1,72,512]{2,1,0:T(8,128)}, u32[]{:S(2)}, u32[]{:S(2)}) collective-permute-start(f32[1,72,512]{2,1,0:T(8,128)} %get-tuple-element.130), channel_id=1, source_target_pairs={{3,0},{4,1},{5,2},{6,3},{7,4},{11,8},{12,9},{13,10},{14,11},{15,12... | collective-permute-start | bytes 442376 | tf_op jit(solution)/shard_map/ppermute | solution.py:936
  287.7 30.9 %collective-permute-start.13 = (bf16[4,144,512]{2,1,0:T(8,128)(2,1)}, bf16[4,144,512]{2,1,0:T(8,128)(2,1)S(1)}, u32[]{:S(2)}, u32[]{:S(2)}) collective-permute-start(bf16[4,144,512]{2,1,0:T(8,128)(2,1)} %get-tuple-element.125), channel_id=1, source_target_pairs={{0,2},{1,3},{2,0},{3,1},{4,6},{5,7},{6,4},{7,5},{8,10},{9,11},{10,... | collective-permute-start | bytes 1769480 | tf_op jit(solution)/shard_map/ppermute | solution.py:982
  319.8 15.3 %collective-permute-start.17 = (bf16[2,144,512]{2,1,0:T(8,128)(2,1)}, bf16[2,144,512]{2,1,0:T(8,128)(2,1)S(1)}, u32[]{:S(2)}, u32[]{:S(2)}) collective-permute-start(bf16[2,144,512]{2,1,0:T(8,128)(2,1)} %get-tuple-element.141), channel_id=1, source_target_pairs={{0,4},{1,5},{2,6},{3,7},{4,0},{5,1},{6,2},{7,3},{8,12},{9,13},{10,... | collective-permute-start | bytes 884744 | tf_op jit(solution)/shard_map/ppermute | solution.py:982
  321.2 13.9 %copy-start.5 = (f32[2,144,512]{2,1,0:T(8,128)S(1)}, f32[2,144,512]{2,1,0:T(8,128)}, u32[]{:S(2)}) copy-start(f32[2,144,512]{2,1,0:T(8,128)} %get-tuple-element.140) | copy-start | bytes 1769476
  324.9 32.7 %all-to-all-start.5 = ((bf16[4,2,4,64,512]{4,3,2,1,0:T(8,128)(2,1)}), bf16[4,2,4,64,512]{4,3,2,1,0:T(8,128)(2,1)S(1)}, u32[]{:S(2)}, u32[]{:S(2)}) async-start(bf16[4,2,4,64,512]{4,3,2,1,0:T(8,128)(2,1)} %get-tuple-element.119), calls=%async_computation.5 | async-start | bytes 4194304 | tf_op jit(solution)/shard_map/all_to_all | solution.py:1150
  335.1 22.4 %collective-permute-start.23 = (bf16[1,144,512]{2,1,0:T(8,128)(2,1)S(1)}, bf16[1,144,512]{2,1,0:T(8,128)(2,1)S(1)}, u32[]{:S(2)}, u32[]{:S(2)}) collective-permute-start(bf16[1,144,512]{2,1,0:T(8,128)(2,1)S(1)} %add_convert_fusion.4), channel_id=1, source_target_pairs={{0,16},{8,24},{16,0},{24,8},{1,17},{9,25},{17,1},{25,9},{2,18},{10... | collective-permute-start | bytes 442376 | tf_op jit(solution)/shard_map/ppermute | solution.py:982
  357.6 5.7 %copy-start.1 = (bf16[4,2,4,64,512]{4,3,2,1,0:T(8,128)(2,1)}, bf16[4,2,4,64,512]{4,3,2,1,0:T(8,128)(2,1)S(1)}, u32[]{:S(2)}) copy-start(bf16[4,2,4,64,512]{4,3,2,1,0:T(8,128)(2,1)S(1)} %all-to-all-done.5.source) | copy-start | bytes 6291460
  357.7 2.9 collective-permute-start.18
  363.4 14.9 %collective-permute-start.19 = (bf16[8,64,512]{2,1,0:T(8,128)(2,1)}, bf16[8,64,512]{2,1,0:T(8,128)(2,1)S(1)}, u32[]{:S(2)}, u32[]{:S(2)}) collective-permute-start(bf16[8,64,512]{2,1,0:T(8,128)(2,1)} %get-tuple-element.163), channel_id=1, source_target_pairs={{0,1},{1,0},{2,3},{3,2},{4,5},{5,4},{6,7},{7,6},{8,9},{9,8},{10,11... | collective-permute-start | bytes 1572872 | tf_op jit(solution)/shard_map/ppermute | solution.py:982
  365.9 18.0 %all-to-all-start.4 = ((bf16[4,1,4,64,512]{4,3,2,1,0:T(8,128)(2,1)}), bf16[4,1,4,64,512]{4,3,2,1,0:T(8,128)(2,1)S(1)}, u32[]{:S(2)}, u32[]{:S(2)}) async-start(bf16[4,1,4,64,512]{4,3,2,1,0:T(8,128)(2,1)} %get-tuple-element.96), calls=%async_computation.4 | async-start | bytes 2097152 | tf_op jit(solution)/shard_map/all_to_all | solution.py:1150
  379.2 12.8 %collective-permute-start.20 = (bf16[4,64,512]{2,1,0:T(8,128)(2,1)}, bf16[4,64,512]{2,1,0:T(8,128)(2,1)S(1)}, u32[]{:S(2)}, u32[]{:S(2)}) collective-permute-start(bf16[4,64,512]{2,1,0:T(8,128)(2,1)} %get-tuple-element.167), channel_id=1, source_target_pairs={{0,2},{1,3},{2,0},{3,1},{4,6},{5,7},{6,4},{7,5},{8,10},{9,11},{10,... | collective-permute-start | bytes 786440 | tf_op jit(solution)/shard_map/ppermute | solution.py:982
  383.8 1.0 copy-start.3
  387.7 19.6 %all-to-all-start.6 = ((bf16[4,1,4,64,512]{4,3,2,1,0:T(8,128)(2,1)}), bf16[4,1,4,64,512]{4,3,2,1,0:T(8,128)(2,1)S(1)}, u32[]{:S(2)}, u32[]{:S(2)}) async-start(bf16[4,1,4,64,512]{4,3,2,1,0:T(8,128)(2,1)} %get-tuple-element.136), calls=%async_computation.6 | async-start | bytes 2097152 | tf_op jit(solution)/shard_map/all_to_all | solution.py:1150
  392.0 9.6 %collective-permute-start.21 = (bf16[2,64,512]{2,1,0:T(8,128)(2,1)S(1)}, bf16[2,64,512]{2,1,0:T(8,128)(2,1)S(1)}, u32[]{:S(2)}, u32[]{:S(2)}) collective-permute-start(bf16[2,64,512]{2,1,0:T(8,128)(2,1)S(1)} %get-tuple-element.169), channel_id=1, source_target_pairs={{0,4},{1,5},{2,6},{3,7},{4,0},{5,1},{6,2},{7,3},{8,12},{9,13},{10,... | collective-permute-start | bytes 393224 | tf_op jit(solution)/shard_map/ppermute | solution.py:982
  401.7 9.6 %collective-permute-start.22 = (bf16[1,64,512]{2,1,0:T(8,128)(2,1)S(1)}, bf16[1,64,512]{2,1,0:T(8,128)(2,1)S(1)}, u32[]{:S(2)}, u32[]{:S(2)}) collective-permute-start(bf16[1,64,512]{2,1,0:T(8,128)(2,1)S(1)} %fusion.2), channel_id=1, source_target_pairs={{0,16},{8,24},{16,0},{24,8},{1,17},{9,25},{17,1},{25,9},{2,18},{10... | collective-permute-start | bytes 196616 | tf_op jit(solution)/shard_map/ppermute | solution.py:982
  407.4 1.0 copy-start.2
Sparse Core Ops, SparseCore 0:
  10.9 74.6 all-gather.1

commit v3 on v2

--- a/solution.py
+++ b/solution.py
@@ -151,11 +151,20 @@
 ANYWHERE = pl.BlockSpec(memory_space=pl.ANY)
 
 
+GAIN_ONE, SHIFT_ONE, BIAS_QKV, BIAS_OUT, GAIN_TWO, SHIFT_TWO, BIAS_UP, BIAS_DOWN = range(8)
+
+
+def vector(ref, row):
+    width = 3 * MODEL if row == BIAS_QKV else ref.shape[1] if row == BIAS_UP else MODEL
+    return ref[row : row + 1, :width]
+
+
 def featured(mixed):
     return jnp.where(mixed > 0, mixed + 1.0, jnp.exp(jnp.minimum(mixed, 0.0))).astype(bf16)
 
 
-def state_kernel(placing, closing, rows, weight, bias, gain, shift, state_out, x_scr, acc, sums):
+def state_kernel(placing, closing, rows, weight, vec, state_out, x_scr, acc, sums):
+    gain, shift, bias = vector(vec, GAIN_ONE), vector(vec, SHIFT_ONE), vector(vec, BIAS_QKV)
     micro, step = pl.program_id(0), pl.program_id(1)
     per = TILE // STRETCH
 
@@ -167,7 +176,7 @@
     for i in range(per):
         x_scr[i * STRETCH : (i + 1) * STRETCH, :] = pick(rows, placing[micro, step * per + i])
     n, _ = standardize(x_scr[...].astype(f32))
-    normed = (n * gain[...] + shift[...]).astype(bf16)
+    normed = (n * gain + shift).astype(bf16)
     keep = jnp.concatenate(
         [jnp.full((STRETCH, 1), flag(closing[micro, step * per + i]), f32) for i in range(per)],
         axis=0,
@@ -187,7 +196,7 @@
             pack_state(state_out, pair, acc[pair], sums[:, col(pair)])
 
 
-def run_state(placing, closing, rows, weight, bias, gain, shift):
+def run_state(placing, closing, rows, weight, vec):
     micro, count = placing.shape
     width = rows.shape[-1]
     tiles = count * STRETCH // TILE
@@ -200,9 +209,7 @@
             in_specs=[
                 group_spec(rows.shape, 0),
                 fixed(weight.shape),
-                fixed(bias.shape),
-                fixed(gain.shape),
-                fixed(shift.shape),
+                fixed(vec.shape),
             ],
             out_specs=member_spec(),
             scratch_shapes=[
@@ -214,11 +221,9 @@
         out_shape=jax.ShapeDtypeStruct((micro, HEAD_DIM + 8, MODEL), f32),
         compiler_params=params(),
         cost_estimate=pl.CostEstimate(
-            flops=4 * micro * count * STRETCH * width * MODEL,
-            bytes_accessed=5 << 20,
-            transcendentals=micro * count * STRETCH * MODEL,
+            flops=11 << 30, bytes_accessed=5 << 20, transcendentals=0
         ),
-    )(placing, closing, rows, weight, bias, gain, shift)
+    )(placing, closing, rows, weight, vec)
 
 
 def causal(second, transposed):
@@ -228,6 +233,13 @@
         i, j = j, i
     crosses = (i >= STRETCH) & (j < STRETCH)
     return jnp.where(crosses, 1.0 - second, jnp.where(j <= i, 1.0, 0.0))
+
+
+def start_all(when, copies):
+    @pl.when(when)
+    def _():
+        for copy in copies:
+            copy.start()
 
 
 def mid_kernel(
@@ -240,45 +252,48 @@
     cot_ref,
     inc_ref,
     w_qkv,
-    w_out,
-    w_up,
-    w_down,
-    b_qkv,
-    gain_one,
-    shift_one,
-    b_out,
-    gain,
-    shift,
-    b_up,
-    b_down,
+    vec,
+    w_out_far,
+    w_up_far,
+    w_down_far,
     *refs,
     first,
     resumes,
     final,
 ):
+    gain_one, shift_one, b_qkv = vector(vec, GAIN_ONE), vector(vec, SHIFT_ONE), vector(vec, BIAS_QKV)
+    gain, shift = vector(vec, GAIN_TWO), vector(vec, SHIFT_TWO)
+    b_out, b_up, b_down = vector(vec, BIAS_OUT), vector(vec, BIAS_UP), vector(vec, BIAS_DOWN)
     before, refs = (refs[:3], refs[3:]) if resumes else ((), refs)
     result, qkv_ref, branch_out, gn_out, gd_out, states_out, state_out, vec_out = refs[:8]
     refs = refs[8:]
     if final:
-        keep_out, send_out, acc_up, acc_down, acc_out, turned = refs[:6]
+        keep_out, send_out, turned, acc_up, acc_down, acc_out = refs[:6]
         refs = refs[6:]
     else:
-        acc_up, acc_down, acc_out = refs[:3]
-        refs = refs[3:]
-    carry, back, back_sum, att_scr, inv_scr, att_b, x_scr, cot_scr = refs[:8]
-    sems = refs[8] if resumes else None
+        far_up, far_down, far_out, acc_up, acc_down, acc_out = refs[:6]
+        refs = refs[6:]
+    carry, back, back_sum, att_scr, inv_scr, att_b, x_scr, cot_scr, w_out, w_up, w_down, sems = refs
     member, step = pl.program_id(0), pl.program_id(1)
     micro = first + member
     per = TILE // STRETCH
     opening = (member == 0) & (step == 0)
+    closing = (member == pl.num_programs(0) - 1) & (step == pl.num_programs(1) - 1)
+    arriving = [
+        pltpu.make_async_copy(source, target, sems.at[n])
+        for n, (source, target) in enumerate(
+            [(w_out_far, w_out), (w_up_far, w_up), (w_down_far, w_down)]
+            + list(zip(before, (acc_up, acc_down, acc_out)))
+        )
+    ]
+    leaving = []
 
     @pl.when(opening)
     def _():
         vec_out[...] = jnp.zeros_like(vec_out)
-        if resumes:
-            for n, (source, target) in enumerate(zip(before, (acc_up, acc_down, acc_out))):
-                pltpu.make_async_copy(source, target, sems.at[n]).start()
-        else:
+        for copy in arriving:
+            copy.start()
+        if not resumes:
             acc_up[...] = jnp.zeros_like(acc_up)
             acc_down[...] = jnp.zeros_like(acc_down)
             acc_out[...] = jnp.zeros_like(acc_out)
@@ -308,7 +323,7 @@
 
     x = x_scr[...].astype(f32)
     n, _ = standardize(x)
-    normed = (n * gain_one[...] + shift_one[...]).astype(bf16)
+    normed = (n * gain_one + shift_one).astype(bf16)
     for part in range(2):
         at = slice(part * MODEL, (part + 1) * MODEL)
         qkv_ref[:, at] = featured(nn(normed, w_qkv[:, at]) + b_qkv[:, at])
@@ -352,22 +367,20 @@
             added = tn(k_keep, jnp.concatenate([v, ones_all], axis=1))
             carry[pair] = state * (1.0 - r1) + jnp.where(wide_block, added, 0.0)
 
-    middle = x_scr[...].astype(f32) + nn(att_b[...], w_out[...]) + b_out[...]
+    @pl.when(opening)
+    def _():
+        for copy in arriving:
+            copy.wait()
+
+    middle = x_scr[...].astype(f32) + nn(att_b[...], w_out[...]) + b_out
     n, scale = standardize(middle)
-    normed = (n * gain[...] + shift[...]).astype(bf16)
+    normed = (n * gain + shift).astype(bf16)
     normed_t = normed.T
     cot = cot_scr[...]
     cot_t = cot.T
     ff = w_up.shape[1]
-    total = middle + b_down[...]
+    total = middle + b_down
     up_grad = jnp.zeros((TILE, MODEL), f32)
-    if resumes:
-
-        @pl.when(opening)
-        def _():
-            for n_, (source, target) in enumerate(zip(before, (acc_up, acc_down, acc_out))):
-                pltpu.make_async_copy(source, target, sems.at[n_]).wait()
-
     for part in range(ff // MODEL):
         at = slice(part * MODEL, (part + 1) * MODEL)
         u = nn(normed, w_up[:, at]) + b_up[:, at]
@@ -375,14 +388,18 @@
         t = jnp.tanh(u * (0.7978845608028654 + 0.035677408136300125 * u2))
         half = 0.5 + 0.5 * t
         act = (u * half).astype(bf16)
-        rise = 0.7978845608028654 + 0.10703222440890037 * u2
-        slope = half + 0.5 * u * (1.0 - t * t) * rise
+        rise = 1.5957691216057308 + 0.21406444881780074 * u2
+        slope = half + u * half * (1.0 - half) * rise
         g = (nt(cot, w_down[at, :]) * slope).astype(bf16)
         total = total + nn(act, w_down[at, :])
         acc_down[:, at] += nn(cot_t, act)
         vec_out[0:1, at] += jnp.sum(g.astype(f32), axis=0, keepdims=True)
         up_grad = up_grad + nt(g, w_up[:, at])
         acc_up[:, at] += nn(normed_t, g)
+        if not final:
+            leaving.append(pltpu.make_async_copy(acc_down.at[:, at], far_down.at[:, at], sems.at[6 + 2 * part]))
+            leaving.append(pltpu.make_async_copy(acc_up.at[:, at], far_up.at[:, at], sems.at[7 + 2 * part]))
+            start_all(closing, leaving[-2:])
     total = total.astype(bf16)
     for i in range(per):
         put(result, placing[micro, step * per + i], total[i * STRETCH : (i + 1) * STRETCH, :])
@@ -391,11 +408,14 @@
     vec_out[1:2, :MODEL] += jnp.sum(up_grad * n, axis=0, keepdims=True)
     vec_out[1:2, MODEL : 2 * MODEL] += jnp.sum(up_grad, axis=0, keepdims=True)
     vec_out[1:2, 3 * MODEL : 4 * MODEL] += jnp.sum(cot_f, axis=0, keepdims=True)
-    branch = (cot_f + norm_back(up_grad, gain[...], n, scale)).astype(bf16)
+    branch = (cot_f + norm_back(up_grad, gain, n, scale)).astype(bf16)
     branch_out[...] = branch
     vec_out[1:2, 2 * MODEL : 3 * MODEL] += jnp.sum(branch.astype(f32), axis=0, keepdims=True)
     grad_att = nt(branch, w_out[...])
     acc_out[...] += tn(att_b[...], branch)
+    if not final:
+        leaving.append(pltpu.make_async_copy(acc_out, far_out, sems.at[6 + 2 * (ff // MODEL)]))
+        start_all(closing, leaving[-1:])
     lane = lanes(CHUNK, PAIR) % HEAD_DIM
     for chunk in range(TILE // CHUNK):
         rows = slice(chunk * CHUNK, (chunk + 1) * CHUNK)
@@ -425,9 +445,16 @@
         for pair in range(PAIRS):
             pack_state(state_out, pair, back[pair], back_sum[:, col(pair)])
 
-    if final:
-
-        @pl.when((member == pl.num_programs(0) - 1) & (step == pl.num_programs(1) - 1))
+    if not final:
+
+        @pl.when(closing)
+        def _():
+            for copy in leaving:
+                copy.wait()
+
+    else:
+
+        @pl.when(closing)
         def _():
             parts = ff // MODEL
             devices = 2 * keep_out.shape[0]
@@ -450,7 +477,7 @@
                 target[seat, 2 * more :, :] = acc_out[here, :].astype(target.dtype)
 
 
-def run_mid(tables, first, members, target, rows, cot, inc, weights, vectors, before, owner):
+def run_mid(tables, first, members, target, rows, cot, inc, weights, vec, before, owner):
     micro, count = tables[0].shape
     width = rows.shape[-1]
     ff = weights[2].shape[1]
@@ -459,10 +486,6 @@
     total = members * count
     resumes, final = before is not None, owner is not None
     f32_sums = [(width, ff), (width, ff), (MODEL, width)]
-    devices = lax.axis_size(BOTH) if final else 0
-    if not final:
-        owner = jnp.zeros((8,), jnp.int32)
-    half = (devices // 2, (2 * ff + MODEL) // max(devices, 1), MODEL)
     out_specs = [
         group_spec(target.shape, 0),
         tile_spec(3 * MODEL, tiles),
@@ -484,13 +507,17 @@
         jax.ShapeDtypeStruct((8, ff), f32),
     ]
     if final:
+        devices = owner.shape[0]
+        half = (devices // 2, (2 * ff + MODEL) // devices, MODEL)
         out_specs += [fixed(half), fixed(half)]
         out_shape += [jax.ShapeDtypeStruct(half, f32), jax.ShapeDtypeStruct(half, bf16)]
-        scratch = [pltpu.VMEM(shape, f32) for shape in f32_sums] + [pltpu.VMEM((ff, width), f32)]
     else:
-        out_specs += [fixed(shape) for shape in f32_sums]
+        out_specs += [ANYWHERE] * 3
         out_shape += [jax.ShapeDtypeStruct(shape, f32) for shape in f32_sums]
-        scratch = []
+    if not final:
+        owner = jnp.zeros((8,), jnp.int32)
+    scratch = [pltpu.VMEM((ff, width), f32)] if final else []
+    scratch += [pltpu.VMEM(shape, f32) for shape in f32_sums]
     scratch += [
         pltpu.VMEM((PAIRS, PAIR, 2 * PAIR), f32),
         pltpu.VMEM((PAIRS, PAIR, PAIR), f32),
@@ -501,8 +528,8 @@
         pltpu.VMEM((TILE, width), bf16),
         pltpu.VMEM((TILE, width), bf16),
     ]
-    if resumes:
-        scratch.append(pltpu.SemaphoreType.DMA((3,)))
+    scratch += [pltpu.VMEM(item.shape, bf16) for item in weights[1:]]
+    scratch.append(pltpu.SemaphoreType.DMA((7 + 2 * (ff // MODEL),)))
     return pl.pallas_call(
         functools.partial(mid_kernel, first=first, resumes=resumes, final=final),
         name="middle",
@@ -515,8 +542,8 @@
                 group_spec(cot[0].shape, cot[1]),
                 member_spec(first),
             ]
-            + [fixed(item.shape) for item in weights + vectors]
-            + [ANYWHERE] * (3 if resumes else 0),
+            + [fixed(weights[0].shape), fixed(vec.shape)]
+            + [ANYWHERE] * (6 if resumes else 3),
             out_specs=out_specs,
             scratch_shapes=scratch,
         ),
@@ -524,11 +551,9 @@
         compiler_params=params(),
         input_output_aliases={4: 0},
         cost_estimate=pl.CostEstimate(
-            flops=2 * total * width * (6 * MODEL + 6 * ff) + (members << 32),
-            bytes_accessed=members * (20 << 20),
-            transcendentals=total * ff,
+            flops=members * (24 << 30), bytes_accessed=members << 24, transcendentals=0
         ),
-    )(*tables, owner, target, rows, cot[0], inc, *weights, *vectors, *(before or ()))
+    )(*tables, owner, target, rows, cot[0], inc, weights[0], vec, *weights[1:], *(before or ()))
 
 
 def back_kernel(
@@ -544,8 +569,7 @@
     states_ref,
     inc_ref,
     weight,
-    gain,
-    shift,
+    vec,
     owner_col,
     *refs,
     first,
@@ -554,6 +578,7 @@
     widths,
     sums,
 ):
+    gain, shift = vector(vec, GAIN_ONE), vector(vec, SHIFT_ONE)
     before, refs = (refs[:1], refs[1:]) if resumes else ((), refs)
     vec_others, refs = refs[:sums], refs[sums:]
     grad_rows, vec_out = refs[:2]
@@ -649,7 +674,7 @@
     vec_out[0:1, :] += jnp.sum(mixed.astype(f32), axis=0, keepdims=True)
     upstream = nt(mixed, weight[...])
     n, scale = standardize(x_scr[...].astype(f32))
-    normed_t = (n * gain[...] + shift[...]).astype(bf16).T
+    normed_t = (n * gain + shift).astype(bf16).T
     if resumes:
 
         @pl.when(opening)
@@ -661,7 +686,7 @@
         acc[:, at] += nn(normed_t, mixed[:, at])
     vec_out[1:2, :MODEL] += jnp.sum(upstream * n, axis=0, keepdims=True)
     vec_out[1:2, MODEL : 2 * MODEL] += jnp.sum(upstream, axis=0, keepdims=True)
-    total = (branch_ref[...].astype(f32) + norm_back(upstream, gain[...], n, scale)).astype(bf16)
+    total = (branch_ref[...].astype(f32) + norm_back(upstream, gain, n, scale)).astype(bf16)
     for i in range(per):
         put(grad_rows, placing[micro, tile * per + i], total[i * STRETCH : (i + 1) * STRETCH, :])
 
@@ -716,7 +741,7 @@
                 target[j % half, 3 * less :, :] = block16.astype(target.dtype)
 
 
-def run_back(tables, first, members, target, rows, mid, inc, weight, gain, shift, before, owner, others, widths):
+def run_back(tables, first, members, target, rows, mid, inc, weight, vec, before, owner, others, widths):
     (group, seat), (saved, at) = target, mid
     micro, count = tables[0].shape
     width = rows.shape[-1]
@@ -773,8 +798,7 @@
                 ),
                 member_spec(at),
                 fixed(weight.shape),
-                fixed(gain.shape),
-                fixed(shift.shape),
+                fixed(vec.shape),
                 fixed((owner.shape[0], 1)),
             ]
             + ([ANYWHERE] if resumes else [])
@@ -786,9 +810,7 @@
         input_output_aliases={3: 0},
         compiler_params=params(),
         cost_estimate=pl.CostEstimate(
-            flops=members * (2 * count * width * 6 * MODEL + (8 << 30)),
-            bytes_accessed=members * (14 << 20),
-            transcendentals=0,
+            flops=members * (15 << 30), bytes_accessed=members << 24, transcendentals=0
         ),
     )(
         tables[0],
@@ -803,8 +825,7 @@
         saved[5],
         inc,
         weight,
-        gain,
-        shift,
+        vec,
         owner[:, None],
         *(() if before is None else (before,)),
         *others,
@@ -924,7 +945,11 @@
     from_after = 1.0 - jnp.any(
         (starts[:, None, :] > last) & (starts[:, None, :] <= reach_on[None, :, None]), axis=-1
     ).astype(f32)
-    return slot, placing, restart, opened, closing, from_before, from_after
+    first = base - hop * count
+    unbroken = 1.0 - jnp.any(
+        (starts[:, None, :] >= first[None, :, None]) & (starts[:, None, :] <= last), axis=-1
+    ).astype(f32)
+    return slot, placing, restart, opened, closing, from_before, from_after, unbroken
 
 
 def exchange(states, hops, forward):
@@ -935,6 +960,17 @@
         pairs = [(i, i + step) if forward else (i + step, i) for i in range(size - step)]
         got.append(lax.ppermute(states, "fsdp", pairs))
     return got
+
+
+def passed_on(states, weights, unbroken, beside):
+    size = lax.axis_size("fsdp")
+    total, own, step = jnp.zeros_like(states), states, 1
+    while step <= weights.shape[1] and step < size:
+        got = lax.ppermute(own, "fsdp", [(i, i + step) for i in range(size - step)])
+        total = total + got * weights[:, step - 1, None, None]
+        own = after(own + got * unbroken[:, step - 1, None, None], beside)
+        step *= 2
+    return total
 
 
 def joined(got, weights, *others):
@@ -982,39 +1018,20 @@
     return lax.ppermute(x, axis, [(i, i ^ bit) for i in range(lax.axis_size(axis))])
 
 
-def gather_halves(parts):
+def gather_halves(x, ties):
     stages = list(reversed(halving_stages()))
-    done, steps = [], []
-    for n, x in enumerate(parts):
-        own = []
-        for s, (axis, bit) in enumerate(stages):
-            if n:
-                x = after(x, done[s])
-            got = swap(x, axis, bit)
-            if s == len(stages) - 1:
-                own.append(got)
-                steps.append((x, got))
-            else:
-                x = jnp.concatenate([x, got], axis=0)
-                own.append(x)
-        done = own
-        if n == 0:
-            first = own
-    return steps, first
-
-
-def scatter_stages():
-    return len(halving_stages())
-
-
-def scatter_step(keep, send, s, between=None):
+    steps = []
+    for s, (axis, bit) in enumerate(stages[:-1]):
+        if s in ties:
+            x = after(x, ties[s])
+        x = jnp.concatenate([x, swap(x, axis, bit)], axis=0)
+        steps.append(x)
+    return (x, swap(x, *stages[-1])), steps
+
+
+def scatter_step(keep, send, s):
     stages = halving_stages()
-    got = swap(send, *stages[s])
-    if between is not None:
-        beside = between()
-        got = after(got, beside[1])
-        return (*scatter_join(keep, got, s == len(stages) - 1), beside)
-    return scatter_join(keep, got, s == len(stages) - 1)
+    return scatter_join(keep, swap(send, *stages[s]), s == len(stages) - 1)
 
 
 def scatter_join(keep, got, last):
@@ -1023,6 +1040,25 @@
     half = keep.shape[0] // 2
     send = (keep[half:] + got[half:].astype(f32)).astype(bf16)
     return keep[:half] + got[:half].astype(f32), send
+
+
+def finish_kernel(keep, got, qkv, *vectors):
+    total = keep[0] + got[0].astype(f32)
+    rows = qkv.shape[0]
+    for part in range(3):
+        qkv[:, part * MODEL : (part + 1) * MODEL] = total[part * rows : (part + 1) * rows, :]
+    for v, ref in enumerate(vectors):
+        ref[...] = total[3 * rows + v : 3 * rows + v + 1, : ref.shape[1]]
+
+
+def run_finish(keep, got, widths):
+    rows = (keep.shape[1] - 16) // 3
+    return pl.pallas_call(
+        finish_kernel,
+        name="finish",
+        out_shape=[jax.ShapeDtypeStruct((rows, 3 * MODEL), f32)]
+        + [jax.ShapeDtypeStruct((1, width), f32) for width in widths],
+    )(keep, got)
 
 
 def pack_kernel(qkv, out, up, down, *refs):
@@ -1183,44 +1219,39 @@
     devices = lax.axis_size(BOTH)
     ff = w_up.shape[1]
     dp = lax.axis_size("dp")
-    slot, placing, restart, opened, closing, from_before, from_after = index_tables(
+    slot, placing, restart, opened, closing, from_before, from_after, unbroken = index_tables(
         lengths, stretch_order, count
     )
     small = (ln1_gain, ln1_bias, b_qkv, b_out, ln2_gain, ln2_bias, b_up, b_down)
     in_parts = (width // devices) % 16 == 0
     groups = groups_of(micro)
     sent = run_send(slot, tokens, 0, micro)
-    moved = to_dp(sent)
     if in_parts:
         place, owner = order_tables()
         first_part, second_part = run_pack(w_qkv, w_out, w_up, w_down, small)
-        halves, _ = gather_halves([after(first_part, sent)])
+        halves, steps = gather_halves(first_part, {1: sent})
+        moved = to_dp(after(sent, steps[0]))
         qkv_all, vectors = run_sort_first(
-            place, owner, *halves[0], [item.shape[0] for item in small]
+            place, owner, *halves, [item.shape[0] for item in small]
         )
+        ready = (qkv_all,)
         second_part = gather_all(second_part)
-        vectors = [
-            vectors[v : v + 1, : devices * item.shape[0]] for v, item in enumerate(small)
-        ]
     else:
-        owner = None
+        owner, ready = None, ()
+        moved = to_dp(sent)
         qkv_all, out_all = gather_all(w_qkv), gather_all(w_out)
         up_all, down_all = gather_all(w_up), gather_all(w_down)
-        vectors = [gather_all(item).astype(f32)[None] for item in small]
-    gain_one, shift_one, bias_qkv, bias_out, gain_two, shift_two, bias_up, bias_down = vectors
+        vectors = [gather_all(item).astype(f32) for item in small]
+        vectors = jnp.stack([jnp.pad(item, (0, ff - item.shape[0])) for item in vectors])
     tables = (placing, restart, opened)
-    vectors = [bias_qkv, gain_one, shift_one, bias_out, gain_two, shift_two, bias_up, bias_down]
-
+
+    sent_grads = run_send(slot, after(cotangent, *ready), 0, micro)
     hops = from_before.shape[1]
-    states = run_state(placing, closing, moved, qkv_all, bias_qkv, gain_one, shift_one)
-    incoming = exchange(states, hops, True)
-    cots = [
-        to_dp(run_send(slot, after(cotangent, states), first, members))
-        for first, members in groups
-    ]
+    states = run_state(placing, closing, moved, qkv_all, vectors)
+    cots = to_dp(after(sent_grads, states))
     if in_parts:
         up_all, down_all, out_all = run_sort_second(after(second_part, states), ff)
-    incoming = joined(incoming, from_before, out_all)
+    incoming = passed_on(states, from_before, unbroken, out_all)
     weights = [qkv_all, out_all, up_all, down_all]
     mids, sums = [], None
     for g, (first, members) in enumerate(groups):
@@ -1231,7 +1262,7 @@
             members,
             target,
             moved,
-            (cots[g], 0),
+            (cots, first),
             incoming,
             weights,
             vectors,
@@ -1245,81 +1276,83 @@
     homes = [to_dp(out[0]) for out in mids]
     sizes = [MODEL, MODEL, 2 * MODEL, MODEL, MODEL, MODEL, MODEL, ff, MODEL]
     widths = [size // devices for size in sizes]
-    last = scatter_stages() - 1
+    last = len(halving_stages()) - 1
     late = len(groups) - 1
     outgoing[0] = joined(outgoing[0], reach[0], *([mids[-1][7]] if late else []))
     if in_parts:
-        done = 0
         keep, send = sums
         if late:
             send = after(send, outgoing[0], homes[0])
-        keep, send = scatter_step(keep, send, done)
+        keep, send = scatter_step(keep, send, 0)
+        done = 0
     vec_mid = [f[7] for f in mids]
     vec_back, total = [], None
-    grad_rows = [blank((dp, members, count // dp, STRETCH, width)) for _, members in groups]
-    for m in range(micro):
-        g, seat = find(groups, m)
+    grad_rows = []
+    for g, (first, members) in enumerate(groups):
+        if g:
+            outgoing[g] = joined(outgoing[g], reach[g], vec_back[0], homes[g])
+            grad_rows[0] = after(grad_rows[0], outgoing[g])
         saved = list(mids[g])
-        if late and g == late:
-            outgoing[g] = joined(outgoing[g], reach[g], vec_back[0])
-
-        def run(m=m, g=g, seat=seat, saved=saved, total=total, vec_back=tuple(vec_back)):
-            return run_back(
-                tables,
-                m,
-                1,
-                (grad_rows[g], seat),
-                moved,
-                (saved, seat),
-                outgoing[g],
-                qkv_all,
-                gain_one,
-                shift_one,
-                total,
-                owner if m == micro - 1 else None,
-                vec_mid + list(vec_back),
-                widths,
-            )
-
-        if in_parts and done < last - 1:
-            done += 1
+        if in_parts:
             saved[2], keep, send = lax.optimization_barrier((saved[2], keep, send))
-            keep, send, out = scatter_step(keep, send, done, run)
-        else:
-            out = run()
-        grad_rows[g] = out[0]
+            got = swap(send, *halving_stages()[done + 1])
+        out = run_back(
+            tables,
+            first,
+            members,
+            (blank((dp, members, count // dp, STRETCH, width)), 0),
+            moved,
+            (saved, 0),
+            outgoing[g],
+            qkv_all,
+            vectors,
+            total,
+            owner if g == late else None,
+            vec_mid + vec_back,
+            widths,
+        )
+        grad_rows.append(out[0])
         vec_back.append(out[1])
         total = out[2]
-        if m == 0 and late:
-            homes[late] = after(homes[late], out[1])
+        if in_parts:
+            done += 1
+            keep, send = scatter_join(keep, after(got, out[1]), done == last)
+            if g == late:
+                grad_rows[g] = after(grad_rows[g], keep)
     narrow = out[2:]
+    grad_homes = [to_dp(group) for group in grad_rows]
     result = blank((micro, count, STRETCH, width))
     input_grad = blank((micro, count, STRETCH, width))
-    for (first, _), home in zip(groups, homes, strict=True):
-        result = run_land(slot, home, result, first)
-    grad_homes = [to_dp(group) for group in grad_rows]
-    for (first, _), home in zip(groups, grad_homes, strict=True):
-        input_grad = run_land(slot, home, input_grad, first)
-    result = result.reshape(micro, rows, width)
-    input_grad = input_grad.reshape(micro, rows, width)
+
+    def land(output, pieces, *others):
+        for (first, _), home in zip(groups, pieces, strict=True):
+            output = run_land(slot, after(home, *others), output, first)
+        return output
+
     if in_parts:
         part = width // devices
         narrow_keep, narrow_send = narrow
         if len(groups) > 1:
-            narrow_send = after(narrow_send, grad_homes[0])
+            narrow_send = after(narrow_send, grad_homes[0], keep, send)
         while done < last:
             done += 1
-            narrow_send = after(narrow_send, keep, send)
             keep, send = scatter_step(keep, send, done)
+        wide = keep
         parts = ff // MODEL
-        grad_up = jnp.concatenate([keep[c * part : (c + 1) * part] for c in range(parts)], axis=1)
-        grad_down = keep[parts * part : 2 * parts * part]
-        grad_out = keep[2 * parts * part :]
+        grad_up = jnp.concatenate([wide[c * part : (c + 1) * part] for c in range(parts)], axis=1)
+        grad_down = wide[parts * part : 2 * parts * part]
+        grad_out = wide[2 * parts * part :]
         keep, send = narrow_keep, narrow_send
-        for step in range(last + 1):
+        for step in range(last):
             keep, send = scatter_step(keep, send, step)
-        grad_qkv = jnp.concatenate([keep[c * part : (c + 1) * part] for c in range(3)], axis=1)
-        owned_vec = [keep[3 * part + v, :size] for v, size in enumerate(widths)]
+            if step == 0:
+                result = land(result, homes, send)
+            if step == 1:
+                send = after(send, result)
+                input_grad = land(input_grad, grad_homes, send)
+        send = after(send, input_grad)
+        grad_qkv, *owned_vec = run_finish(keep, swap(send, *halving_stages()[last]), widths)
+        owned_vec = [item[0] for item in owned_vec]
     else:
         grad_up, grad_down, grad_out = (scatter_all(x) for x in (sums[0], sums[1].T, sums[2]))
         grad_qkv = scatter_all(total)
@@ -1336,6 +1369,9 @@
             mid[1, 3 * MODEL :],
         )
         owned_vec = [scatter_all(item) for item in vec]
+        result, input_grad = land(result, homes), land(input_grad, grad_homes)
+    result = result.reshape(micro, rows, width)
+    input_grad = input_grad.reshape(micro, rows, width)
     g_gain1, g_bias1, g_qk, g_value, g_bout, g_gain2, g_bias2, g_bup, g_bdown = owned_vec
     return (
         result,

time: 427 us -> 384 us (0.90)
  waiting for transfers between devices: 77.2 us -> 61.4 us
  starting transfers between devices: 80.2 us -> 66.6 us
  Pallas kernels: 206 us -> 196 us
  local copies, waits for them, and re-layouts: 17.6 us -> 12.1 us
    ppermute x15, waiting for transfers between devices: 59.7 us -> 39.3 us  [swap(): lax.ppermute(x, axis, [(i, i ^ bit) for i in range(lax.axis_size(axis))])]
    ppermute x0 -> x2, waiting for transfers between devices: none -> 17.9 us  [passed_on(): got = lax.ppermute(own, 'fsdp', [(i, i + step) for i in range(size - step)])]
    ppermute x15, starting transfers between devices: 38.7 us -> 26.6 us  [swap(): lax.ppermute(x, axis, [(i, i ^ bit) for i in range(lax.axis_size(axis))])]
    ppermute x0 -> x2, starting transfers between devices: none -> 9.25 us  [passed_on(): got = lax.ppermute(own, 'fsdp', [(i, i + step) for i in range(size - step)])]
    ppermute x9 -> x6, starting transfers between devices: 16.2 us -> 7.74 us  [exchange(): got.append(lax.ppermute(states, 'fsdp', pairs))]
    ppermute x9 -> x6, waiting for transfers between devices: 8.03 us -> 0.02 us  [exchange(): got.append(lax.ppermute(states, 'fsdp', pairs))]
    pallas_call x3 -> x2, Pallas kernels: 60 us -> 53.6 us  [run_back(): pl.pallas_call(functools.partial(back_kernel, first=first, resumes=resume...]
    add x0 -> x4, other arithmetic: none -> 5.99 us  [the longest x2 3.15 us: scatter_join(): return (keep[:half] + got[:half].astype(f32), send)]
  transfers between devices with their start and end apart: 32 -> 30, of which waited for: 15 -> 12; matrix products, arithmetic and copies ran while one was open for 7% -> 9% of each run, Pallas kernels for 46% -> 33%
where the time goes in v3:
time: 384 us; the launch traced here: 378 us
  Pallas kernels  196 us (51%)
  starting transfers between devices  66.6 us (17%)
  waiting for transfers between devices  61.4 us (16%)
  other arithmetic  27 us (7%)
  between operations  14.9 us (4%)
  local copies, waits for them, and re-layouts  12.1 us (3%)
    pallas_call x2, Pallas kernels, run_mid(): pl.pallas_call(functools.partial(mid_kernel, first=first, resumes=resumes...  96.2 us
    pallas_call x2, Pallas kernels, run_back(): pl.pallas_call(functools.partial(back_kernel, first=first, resumes=resume...  53.6 us
    ppermute x15, waiting for transfers between devices, swap(): lax.ppermute(x, axis, [(i, i ^ bit) for i in range(lax.axis_size(axis))])  39.3 us
    ppermute x15, starting transfers between devices, swap(): lax.ppermute(x, axis, [(i, i ^ bit) for i in range(lax.axis_size(axis))])  26.6 us
    all_to_all x6, starting transfers between devices, to_dp(): return lax.all_to_all(group, 'dp', split_axis=0, concat_axis=0, tiled=True)  22.9 us
    ppermute x2, waiting for transfers between devices, passed_on(): got = lax.ppermute(own, 'fsdp', [(i, i + step) for i in range(size - step)])  17.9 us
    pallas_call x4, Pallas kernels, run_land(): pl.pallas_call(land_kernel, name='land', grid_spec=pltpu.PrefetchScalarGr...  12.5 us
    pallas_call x1, Pallas kernels, run_state(): pl.pallas_call(state_kernel, name='end_state', grid_spec=pltpu.PrefetchSc...  11.5 us
  transfers between devices with their start and end apart: 30, of which 12 were waited for; matrix products, arithmetic and copies ran while one was open for 9% of the time, Pallas kernels for 33%

profile of v3, /device:TPU:0, one launch (start us, length us, event | category | flops | bytes accessed | tf_op | source)
XLA Modules:
  0.0 378.1 jit_solution(658336263500802757)
XLA Ops:
  7.2 1.8 pack.1
  9.0 3.0 collective-permute-start
  13.8 5.3 %send.2 = bf16[4,3,4,64,512]{4,3,2,1,0:T(8,128)(2,1)} custom-call(s32[3,16]{1,0:T(4,128)} %convert_reduce_fusion.1.slot, bf16[3,16,64,512]{3,2,1,0:T(8,128)(2,1)} %bitcast.38), custom_call_target="tpu_custom_call" | custom-call | bytes 6291456 | tf_op jit(solution)/shard_map/send/pallas_call | solution.py:846
  19.2 2.7 collective-permute-start.1
  21.9 3.7 all-to-all-start
  25.6 3.5 collective-permute-done.1
  29.1 1.7 collective-permute-start.2
  31.3 6.7 %collective-permute-done.2 = bf16[4,64,512]{2,1,0:T(8,128)(2,1)S(1)} collective-permute-done((bf16[4,64,512]{2,1,0:T(8,128)(2,1)S(1)}, bf16[4,64,512]{2,1,0:T(8,128)(2,1)S(1)}, u32[]{:S(2)}, u32[]{:S(2)}) %collective-permute-start.2) | collective-permute-done | bytes 262176 | tf_op jit(solution)/shard_map/ppermute | solution.py:1018
  38.1 1.5 collective-permute-start.3
  41.7 11.3 %collective-permute-done.3 = bf16[8,64,512]{2,1,0:T(8,128)(2,1)S(1)} collective-permute-done((bf16[8,64,512]{2,1,0:T(8,128)(2,1)S(1)}, bf16[8,64,512]{2,1,0:T(8,128)(2,1)S(1)}, u32[]{:S(2)}, u32[]{:S(2)}) %collective-permute-start.3) | collective-permute-done | bytes 524320 | tf_op jit(solution)/shard_map/ppermute | solution.py:1018
  56.8 3.5 sort_first.1
  60.3 5.5 %send.3 = bf16[4,3,4,64,512]{4,3,2,1,0:T(8,128)(2,1)} custom-call(s32[3,16]{1,0:T(4,128)} %convert_reduce_fusion.1.slot, bf16[3,16,64,512]{3,2,1,0:T(8,128)(2,1)} %bitcast.39), custom_call_target="tpu_custom_call" | custom-call | bytes 6291456 | tf_op jit(solution)/shard_map/send/pallas_call | solution.py:846
  65.8 4.2 %all-to-all-done.rows.rows_ref = bf16[4,3,4,64,512]{4,3,2,1,0:T(8,128)(2,1)S(1)} async-done(((bf16[4,3,4,64,512]{4,3,2,1,0:T(8,128)(2,1)}), bf16[4,3,4,64,512]{4,3,2,1,0:T(8,128)(2,1)S(1)}, u32[]{:S(2)}, u32[]{:S(2)}) %all-to-all-start) | async-done | bytes 3145760 | tf_op jit(solution)/shard_map/all_to_all | solution.py:1186
  70.1 1.7 copy-done.3
  71.7 11.5 %end_state.1 = f32[3,72,512]{2,1,0:T(8,128)} custom-call(s32[3,16]{1,0:T(4,128)} %get-tuple-element.204.placing, s32[3,16]{1,0:T(4,128)} %get-tuple-element.203.closing, bf16[4,3,4,64,512]{4,3,2,1,0:T(8,128)(2,1)} %copy-done.3, bf16[512,1536]{1,0:T(8,128)(2,1)} %get-tuple-element.91.weight.w_qkv, f32[8,2048]{1,0:T(8,128)} %get-tuple-element.93.vec), custom_call_target="tpu_custom_call" | custom-call | flops 11811160064 | bytes 5242880 | tf_op jit(solution)/shard_map/end_state/pallas_call | solution.py:203
  83.2 3.7 all-to-all-start.1
  87.6 3.5 collective-permute-start.5
  91.4 10.0 %collective-permute-done.5 = f32[3,72,512]{2,1,0:T(8,128)S(1)} collective-permute-done((f32[3,72,512]{2,1,0:T(8,128)}, f32[3,72,512]{2,1,0:T(8,128)S(1)}, u32[]{:S(2)}, u32[]{:S(2)}) %collective-permute-start.5) | collective-permute-done | bytes 442400 | tf_op jit(solution)/shard_map/ppermute | solution.py:969
  102.1 1.9 multiply_add_fusion.1
  104.1 4.7 %sort_second.1 = (bf16[512,2048]{1,0:T(8,128)(2,1)}, bf16[2048,512]{1,0:T(8,128)(2,1)}, bf16[512,512]{1,0:T(8,128)(2,1)}) custom-call(bf16[32,144,512]{2,1,0:T(8,128)(2,1)} %all-gather.2.cloned.1.call-done.gathered), custom_call_target="tpu_custom_call" | custom-call | tf_op jit(solution)/shard_map/sort_second/pallas_call | solution.py:1163
  108.7 5.8 %collective-permute-start.6 = (f32[3,72,512]{2,1,0:T(8,128)}, f32[3,72,512]{2,1,0:T(8,128)S(1)}, u32[]{:S(2)}, u32[]{:S(2)}) collective-permute-start(f32[3,72,512]{2,1,0:T(8,128)} %multiply_add_fusion.1), channel_id=1, source_target_pairs={{0,2},{1,3},{2,4},{3,5},{4,6},{5,7},{8,10},{9,11},{10,12},{11,13},... | collective-permute-start | bytes 1327112 | tf_op jit(solution)/shard_map/ppermute | solution.py:969
  115.7 7.9 %collective-permute-done.6 = f32[3,72,512]{2,1,0:T(8,128)S(1)} collective-permute-done((f32[3,72,512]{2,1,0:T(8,128)}, f32[3,72,512]{2,1,0:T(8,128)S(1)}, u32[]{:S(2)}, u32[]{:S(2)}) %collective-permute-start.6) | collective-permute-done | bytes 442400 | tf_op jit(solution)/shard_map/ppermute | solution.py:969
  126.1 58.7 %middle.2 = (bf16[4,2,4,64,512]{4,3,2,1,0:T(8,128)(2,1)}, bf16[2048,1536]{1,0:T(8,128)(2,1)}, bf16[2048,512]{1,0:T(8,128)(2,1)}, bf16[2048,512]{1,0:T(8,128)(2,1...) custom-call(s32[3,16]{1,0:T(4,128)} %get-tuple-element.204.placing, ...), custom_call_target="tpu_custom_call", output_to_operand_aliasing={{0}: (4, {})} | custom-call | flops 51539607552 | bytes 33554432 | tf_op jit(solution)/shard_map/middle/pallas_call | solution.py:533
  184.8 1.3 collective-permute-start.7
  188.7 3.6 all-to-all-start.2
  192.4 37.5 %middle.3 = (bf16[4,1,4,64,512]{4,3,2,1,0:T(8,128)(2,1)}, bf16[1024,1536]{1,0:T(8,128)(2,1)}, bf16[1024,512]{1,0:T(8,128)(2,1)}, bf16[1024,512]{1,0:T(8,128)(2,1...) custom-call(s32[3,16]{1,0:T(4,128)} %get-tuple-element.204.placing, ...), custom_call_target="tpu_custom_call", output_to_operand_aliasing={{0}: (4, {})} | custom-call | flops 25769803776 | bytes 16777216 | tf_op jit(solution)/shard_map/middle/pallas_call | solution.py:533
  235.9 3.5 all-to-all-start.3
  239.4 5.0 %add_convert_fusion = (bf16[8,144,512]{2,1,0:T(8,128)(2,1)}, f32[8,144,512]{2,1,0:T(8,128)S(1)}) fusion(f32[16,144,512]{2,1,0:T(8,128)} %get-tuple-element.110, bf16[16,144,512]{2,1,0:T(8,128)(2,1)} %collective-permute-done.10), kind=kLoop, calls=%fused_computation | loop fusion | flops 2949120 | bytes 10616832 | tf_op jit(solution)/shard_map/convert_element_type | solution.py:1041
  244.4 3.3 collective-permute-start.11
  248.3 32.7 %back.2 = (bf16[4,2,4,64,512]{4,3,2,1,0:T(8,128)(2,1)}, f32[8,1536]{1,0:T(8,128)}, f32[512,1536]{1,0:T(8,128)}) custom-call(s32[3,16]{1,0:T(4,128)} %get-tuple-element.204.placing, s32[3,17]{1,0:T(4,128)} %convert_select_fusion.restart, s32[8]{0:T(128)} %broadcast_12_owner.2.owner, ...), custom_call_target="tpu_custom_call", output_to_operand_aliasing={{0}: (3, {})} | custom-call | flops 32212254720 | bytes 33554432 | tf_op jit(solution)/shard_map/back/pallas_call | solution.py:780
  281.0 3.6 multiply_add_fusion.3.inc_ref
  284.7 4.7 %all-to-all-start.4 = ((bf16[4,2,4,64,512]{4,3,2,1,0:T(8,128)(2,1)}), bf16[4,2,4,64,512]{4,3,2,1,0:T(8,128)(2,1)}, u32[]{:S(2)}, u32[]{:S(2)}) async-start(bf16[4,2,4,64,512]{4,3,2,1,0:T(8,128)(2,1)} %get-tuple-element.139), calls=%async_computation.4 | async-start | bytes 4194304 | tf_op jit(solution)/shard_map/all_to_all | solution.py:1186
  289.4 2.5 add_convert_fusion.1
  291.9 4.9 %collective-permute-start.15 = (bf16[4,144,512]{2,1,0:T(8,128)(2,1)}, bf16[4,144,512]{2,1,0:T(8,128)(2,1)S(1)}, u32[]{:S(2)}, u32[]{:S(2)}) collective-permute-start(bf16[4,144,512]{2,1,0:T(8,128)(2,1)} %get-tuple-element.141), channel_id=1, source_target_pairs={{0,2},{1,3},{2,0},{3,1},{4,6},{5,7},{6,4},{7,5},{8,10},{9,11},{10,... | collective-permute-start | bytes 1769480 | tf_op jit(solution)/shard_map/ppermute | solution.py:1018
  296.8 20.9 %back.3 = (bf16[4,1,4,64,512]{4,3,2,1,0:T(8,128)(2,1)}, f32[8,1536]{1,0:T(8,128)}, f32[16,64,512]{2,1,0:T(8,128)}, bf16[16,64,512]{2,1,0:T(8,128)(2,1)}) custom-call(s32[3,16]{1,0:T(4,128)} %get-tuple-element.204.placing, s32[3,17]{1,0:T(4,128)} %convert_select_fusion.restart, s32[32]{0:T(128)} %fusion.27.owner, ...), custom_call_target="tpu_custom_call", output_to_operand_aliasing={{0}: (3, {})} | custom-call | flops 16106127360 | bytes 16777216 | tf_op jit(solution)/shard_map/back/pallas_call | solution.py:780
  319.4 5.0 %collective-permute-start.21 = (bf16[2,144,512]{2,1,0:T(8,128)(2,1)}, bf16[2,144,512]{2,1,0:T(8,128)(2,1)S(1)}, u32[]{:S(2)}, u32[]{:S(2)}) collective-permute-start(bf16[2,144,512]{2,1,0:T(8,128)(2,1)} %get-tuple-element.181), channel_id=1, source_target_pairs={{0,4},{1,5},{2,6},{3,7},{4,0},{5,1},{6,2},{7,3},{8,12},{9,13},{10,... | collective-permute-start | bytes 884744 | tf_op jit(solution)/shard_map/ppermute | solution.py:1018
  324.4 2.0 convert_add_fusion.2
  328.1 3.6 all-to-all-start.5
  331.8 6.6 %collective-permute-done.21 = bf16[2,144,512]{2,1,0:T(8,128)(2,1)S(1)} collective-permute-done((bf16[2,144,512]{2,1,0:T(8,128)(2,1)}, bf16[2,144,512]{2,1,0:T(8,128)(2,1)S(1)}, u32[]{:S(2)}, u32[]{:S(2)}) %collective-permute-start.21) | collective-permute-done | bytes 294944 | tf_op jit(solution)/shard_map/ppermute | solution.py:1018
  338.5 1.5 collective-permute-start.22
  340.0 3.3 land.4._
  343.3 2.9 land.5
  347.5 1.9 collective-permute-done.22
  350.1 5.4 %collective-permute-done.18 = bf16[4,64,512]{2,1,0:T(8,128)(2,1)S(1)} collective-permute-done((bf16[4,64,512]{2,1,0:T(8,128)(2,1)S(1)}, bf16[4,64,512]{2,1,0:T(8,128)(2,1)S(1)}, u32[]{:S(2)}, u32[]{:S(2)}) %collective-permute-start.18) | collective-permute-done | bytes 262176 | tf_op jit(solution)/shard_map/ppermute | solution.py:1018
  357.2 3.3 land.6._
  360.5 2.9 land.7
  365.8 2.8 collective-permute-done.20.got
  369.2 1.6 finish.1
  (116 shorter events, 33.1 us)
Async XLA Ops:
  7.2 96.9 %all-gather.2.cloned.1.call-start = ((), (), s32[]{:S(2)}) async-start(), calls=%async_computation.6 | async-start | bytes 4866048 | tf_op jit(solution)/shard_map/all_gather | solution.py:1178
  9.0 10.2 %collective-permute-start = (bf16[1,64,512]{2,1,0:T(8,128)(2,1)}, bf16[1,64,512]{2,1,0:T(8,128)(2,1)S(1)}, u32[]{:S(2)}, u32[]{:S(2)}) collective-permute-start(bf16[1,64,512]{2,1,0:T(8,128)(2,1)} %get-tuple-element.88), channel_id=1, source_target_pairs={{0,16},{8,24},{16,0},{24,8},{1,17},{9,25},{17,1},{25,9},{2,18},{10... | collective-permute-start | bytes 196616 | tf_op jit(solution)/shard_map/ppermute | solution.py:1018
  13.8 5.3 %copy-start.9 = (bf16[1,64,512]{2,1,0:T(8,128)(2,1)S(1)}, bf16[1,64,512]{2,1,0:T(8,128)(2,1)}, u32[]{:S(2)}) copy-start(bf16[1,64,512]{2,1,0:T(8,128)(2,1)} %get-tuple-element.88) | copy-start | bytes 196612
  19.2 9.9 %collective-permute-start.1 = (bf16[2,64,512]{2,1,0:T(8,128)(2,1)S(1)}, bf16[2,64,512]{2,1,0:T(8,128)(2,1)S(1)}, u32[]{:S(2)}, u32[]{:S(2)}) collective-permute-start(bf16[2,64,512]{2,1,0:T(8,128)(2,1)S(1)} %constant_dynamic-update-slice_fusion), channel_id=1, source_target_pairs={{0,4},{1,5},{2,6},{3,7},{4,0},{5,1},{6,2},{7,3},{8,12},{9,13},{10,... | collective-permute-start | bytes 393224 | tf_op jit(solution)/shard_map/ppermute | solution.py:1018
  21.9 48.2 %all-to-all-start = ((bf16[4,3,4,64,512]{4,3,2,1,0:T(8,128)(2,1)}), bf16[4,3,4,64,512]{4,3,2,1,0:T(8,128)(2,1)S(1)}, u32[]{:S(2)}, u32[]{:S(2)}) async-start(bf16[4,3,4,64,512]{4,3,2,1,0:T(8,128)(2,1)} %send.2), calls=%async_computation | async-start | bytes 6291456 | tf_op jit(solution)/shard_map/all_to_all | solution.py:1186
  25.6 29.4 %copy-start.11 = (s32[3,16]{1,0:T(4,128)S(1)}, s32[3,16]{1,0:T(4,128)}, u32[]{:S(2)}) copy-start(s32[3,16]{1,0:T(4,128)} %param.18) | copy-start | bytes 580
  29.1 8.9 %collective-permute-start.2 = (bf16[4,64,512]{2,1,0:T(8,128)(2,1)S(1)}, bf16[4,64,512]{2,1,0:T(8,128)(2,1)S(1)}, u32[]{:S(2)}, u32[]{:S(2)}) collective-permute-start(bf16[4,64,512]{2,1,0:T(8,128)(2,1)S(1)} %pad_maximum_fusion.1), channel_id=1, source_target_pairs={{0,2},{1,3},{2,0},{3,1},{4,6},{5,7},{6,4},{7,5},{8,10},{9,11},{10,... | collective-permute-start | bytes 786440 | tf_op jit(solution)/shard_map/ppermute | solution.py:1018
  38.1 14.9 %collective-permute-start.3 = (bf16[8,64,512]{2,1,0:T(8,128)(2,1)S(1)}, bf16[8,64,512]{2,1,0:T(8,128)(2,1)S(1)}, u32[]{:S(2)}, u32[]{:S(2)}) collective-permute-start(bf16[8,64,512]{2,1,0:T(8,128)(2,1)S(1)} %pad_maximum_fusion), channel_id=1, source_target_pairs={{0,1},{1,0},{2,3},{3,2},{4,5},{5,4},{6,7},{7,6},{8,9},{9,8},{10,11... | collective-permute-start | bytes 1572872 | tf_op jit(solution)/shard_map/ppermute | solution.py:1018
  53.8 3.0 collective-permute-start.4
  70.1 1.7 copy-start.3
  83.2 41.3 %all-to-all-start.1 = ((bf16[4,3,4,64,512]{4,3,2,1,0:T(8,128)(2,1)}), bf16[4,3,4,64,512]{4,3,2,1,0:T(8,128)(2,1)S(1)}, u32[]{:S(2)}, u32[]{:S(2)}) async-start(bf16[4,3,4,64,512]{4,3,2,1,0:T(8,128)(2,1)} %send.3), calls=%async_computation.1 | async-start | bytes 6291456 | tf_op jit(solution)/shard_map/all_to_all | solution.py:1186
  87.6 13.8 %collective-permute-start.5 = (f32[3,72,512]{2,1,0:T(8,128)}, f32[3,72,512]{2,1,0:T(8,128)S(1)}, u32[]{:S(2)}, u32[]{:S(2)}) collective-permute-start(f32[3,72,512]{2,1,0:T(8,128)} %end_state.1), channel_id=1, source_target_pairs={{0,1},{1,2},{2,3},{3,4},{4,5},{5,6},{6,7},{8,9},{9,10},{10,11},{11... | collective-permute-start | bytes 1327112 | tf_op jit(solution)/shard_map/ppermute | solution.py:969
  101.4 0.8 copy-start.6
  104.1 19.5 %copy-start.7 = (f32[3,72,512]{2,1,0:T(8,128)S(1)}, f32[3,72,512]{2,1,0:T(8,128)}, u32[]{:S(2)}) copy-start(f32[3,72,512]{2,1,0:T(8,128)} %copy-done.6) | copy-start | bytes 1327108
  108.7 14.8 %collective-permute-start.6 = (f32[3,72,512]{2,1,0:T(8,128)}, f32[3,72,512]{2,1,0:T(8,128)S(1)}, u32[]{:S(2)}, u32[]{:S(2)}) collective-permute-start(f32[3,72,512]{2,1,0:T(8,128)} %multiply_add_fusion.1), channel_id=1, source_target_pairs={{0,2},{1,3},{2,4},{3,5},{4,6},{5,7},{8,10},{9,11},{10,12},{11,13},... | collective-permute-start | bytes 1327112 | tf_op jit(solution)/shard_map/ppermute | solution.py:969
  124.5 1.7 copy-start.4
  184.8 45.0 %collective-permute-start.7 = (f32[2,72,512]{2,1,0:T(8,128)}, f32[2,72,512]{2,1,0:T(8,128)S(1)}, u32[]{:S(2)}, u32[]{:S(2)}) collective-permute-start(f32[2,72,512]{2,1,0:T(8,128)} %get-tuple-element.112), channel_id=1, source_target_pairs={{1,0},{2,1},{3,2},{4,3},{5,4},{6,5},{7,6},{9,8},{10,9},{11,10},{12... | collective-permute-start | bytes 884744 | tf_op jit(solution)/shard_map/ppermute | solution.py:961
  186.1 43.7 %collective-permute-start.8 = (f32[2,72,512]{2,1,0:T(8,128)}, f32[2,72,512]{2,1,0:T(8,128)S(1)}, u32[]{:S(2)}, u32[]{:S(2)}) collective-permute-start(f32[2,72,512]{2,1,0:T(8,128)} %get-tuple-element.112), channel_id=1, source_target_pairs={{2,0},{3,1},{4,2},{5,3},{6,4},{7,5},{10,8},{11,9},{12,10},{13,11},... | collective-permute-start | bytes 884744 | tf_op jit(solution)/shard_map/ppermute | solution.py:961
  187.4 42.4 %collective-permute-start.9 = (f32[2,72,512]{2,1,0:T(8,128)}, f32[2,72,512]{2,1,0:T(8,128)S(1)}, u32[]{:S(2)}, u32[]{:S(2)}) collective-permute-start(f32[2,72,512]{2,1,0:T(8,128)} %get-tuple-element.112), channel_id=1, source_target_pairs={{3,0},{4,1},{5,2},{6,3},{7,4},{11,8},{12,9},{13,10},{14,11},{15,12... | collective-permute-start | bytes 884744 | tf_op jit(solution)/shard_map/ppermute | solution.py:961
  188.7 42.0 %all-to-all-start.2 = ((bf16[4,2,4,64,512]{4,3,2,1,0:T(8,128)(2,1)}), bf16[4,2,4,64,512]{4,3,2,1,0:T(8,128)(2,1)S(1)}, u32[]{:S(2)}, u32[]{:S(2)}) async-start(bf16[4,2,4,64,512]{4,3,2,1,0:T(8,128)(2,1)} %get-tuple-element.101), calls=%async_computation.2 | async-start | bytes 4194304 | tf_op jit(solution)/shard_map/all_to_all | solution.py:1186
  230.7 5.1 %copy-start = (bf16[4,2,4,64,512]{4,3,2,1,0:T(8,128)(2,1)}, bf16[4,2,4,64,512]{4,3,2,1,0:T(8,128)(2,1)S(1)}, u32[]{:S(2)}) copy-start(bf16[4,2,4,64,512]{4,3,2,1,0:T(8,128)(2,1)S(1)} %all-to-all-done.2.source) | copy-start | bytes 6291460
  230.7 8.6 %collective-permute-start.10 = (bf16[16,144,512]{2,1,0:T(8,128)(2,1)}, bf16[16,144,512]{2,1,0:T(8,128)(2,1)}, u32[]{:S(2)}, u32[]{:S(2)}) collective-permute-start(bf16[16,144,512]{2,1,0:T(8,128)(2,1)} %get-tuple-element.117), channel_id=1, source_target_pairs={{0,8},{8,0},{16,24},{24,16},{1,9},{9,1},{17,25},{25,17},{2,10},{10... | collective-permute-start | bytes 7077896 | tf_op jit(solution)/shard_map/ppermute | solution.py:1018
  232.0 49.0 %collective-permute-start.12 = (f32[1,72,512]{2,1,0:T(8,128)}, f32[1,72,512]{2,1,0:T(8,128)S(1)}, u32[]{:S(2)}, u32[]{:S(2)}) collective-permute-start(f32[1,72,512]{2,1,0:T(8,128)} %get-tuple-element.129), channel_id=1, source_target_pairs={{1,0},{2,1},{3,2},{4,3},{5,4},{6,5},{7,6},{9,8},{10,9},{11,10},{12... | collective-permute-start | bytes 442376 | tf_op jit(solution)/shard_map/ppermute | solution.py:961
  233.2 47.7 %collective-permute-start.13 = (f32[1,72,512]{2,1,0:T(8,128)}, f32[1,72,512]{2,1,0:T(8,128)}, u32[]{:S(2)}, u32[]{:S(2)}) collective-permute-start(f32[1,72,512]{2,1,0:T(8,128)} %get-tuple-element.129), channel_id=1, source_target_pairs={{2,0},{3,1},{4,2},{5,3},{6,4},{7,5},{10,8},{11,9},{12,10},{13,11},... | collective-permute-start | bytes 442376 | tf_op jit(solution)/shard_map/ppermute | solution.py:961
  234.5 46.5 %collective-permute-start.14 = (f32[1,72,512]{2,1,0:T(8,128)}, f32[1,72,512]{2,1,0:T(8,128)}, u32[]{:S(2)}, u32[]{:S(2)}) collective-permute-start(f32[1,72,512]{2,1,0:T(8,128)} %get-tuple-element.129), channel_id=1, source_target_pairs={{3,0},{4,1},{5,2},{6,3},{7,4},{11,8},{12,9},{13,10},{14,11},{15,12... | collective-permute-start | bytes 442376 | tf_op jit(solution)/shard_map/ppermute | solution.py:961
  235.9 45.2 %all-to-all-start.3 = ((bf16[4,1,4,64,512]{4,3,2,1,0:T(8,128)(2,1)}), bf16[4,1,4,64,512]{4,3,2,1,0:T(8,128)(2,1)S(1)}, u32[]{:S(2)}, u32[]{:S(2)}) async-start(bf16[4,1,4,64,512]{4,3,2,1,0:T(8,128)(2,1)} %get-tuple-element.130), calls=%async_computation.3 | async-start | bytes 2097152 | tf_op jit(solution)/shard_map/all_to_all | solution.py:1186
  244.4 45.0 %collective-permute-start.11 = (bf16[8,144,512]{2,1,0:T(8,128)(2,1)}, bf16[8,144,512]{2,1,0:T(8,128)(2,1)}, u32[]{:S(2)}, u32[]{:S(2)}) collective-permute-start(bf16[8,144,512]{2,1,0:T(8,128)(2,1)} %get-tuple-element.119), channel_id=1, source_target_pairs={{0,1},{1,0},{2,3},{3,2},{4,5},{5,4},{6,7},{7,6},{8,9},{9,8},{10,11... | collective-permute-start | bytes 3538952 | tf_op jit(solution)/shard_map/ppermute | solution.py:1018
  281.0 3.6 copy-start.1
  284.7 34.3 %all-to-all-start.4 = ((bf16[4,2,4,64,512]{4,3,2,1,0:T(8,128)(2,1)}), bf16[4,2,4,64,512]{4,3,2,1,0:T(8,128)(2,1)}, u32[]{:S(2)}, u32[]{:S(2)}) async-start(bf16[4,2,4,64,512]{4,3,2,1,0:T(8,128)(2,1)} %get-tuple-element.139), calls=%async_computation.4 | async-start | bytes 4194304 | tf_op jit(solution)/shard_map/all_to_all | solution.py:1186
  291.9 25.8 %collective-permute-start.15 = (bf16[4,144,512]{2,1,0:T(8,128)(2,1)}, bf16[4,144,512]{2,1,0:T(8,128)(2,1)S(1)}, u32[]{:S(2)}, u32[]{:S(2)}) collective-permute-start(bf16[4,144,512]{2,1,0:T(8,128)(2,1)} %get-tuple-element.141), channel_id=1, source_target_pairs={{0,2},{1,3},{2,0},{3,1},{4,6},{5,7},{6,4},{7,5},{8,10},{9,11},{10,... | collective-permute-start | bytes 1769480 | tf_op jit(solution)/shard_map/ppermute | solution.py:1018
  317.7 1.5 copy-start.12
  319.2 5.2 %collective-permute-start.16 = (bf16[16,64,512]{2,1,0:T(8,128)(2,1)S(1)}, bf16[16,64,512]{2,1,0:T(8,128)(2,1)S(1)}, u32[]{:S(2)}, u32[]{:S(2)}) collective-permute-start(bf16[16,64,512]{2,1,0:T(8,128)(2,1)S(1)} %copy-done.12), channel_id=1, source_target_pairs={{0,8},{8,0},{16,24},{24,16},{1,9},{9,1},{17,25},{25,17},{2,10},{10... | collective-permute-start | bytes 3145736 | tf_op jit(solution)/shard_map/ppermute | solution.py:1018
  319.4 19.0 %collective-permute-start.21 = (bf16[2,144,512]{2,1,0:T(8,128)(2,1)}, bf16[2,144,512]{2,1,0:T(8,128)(2,1)S(1)}, u32[]{:S(2)}, u32[]{:S(2)}) collective-permute-start(bf16[2,144,512]{2,1,0:T(8,128)(2,1)} %get-tuple-element.181), channel_id=1, source_target_pairs={{0,4},{1,5},{2,6},{3,7},{4,0},{5,1},{6,2},{7,3},{8,12},{9,13},{10,... | collective-permute-start | bytes 884744 | tf_op jit(solution)/shard_map/ppermute | solution.py:1018
  324.4 2.6 copy-start.10
  326.4 19.8 %collective-permute-start.17 = (bf16[8,64,512]{2,1,0:T(8,128)(2,1)S(1)}, bf16[8,64,512]{2,1,0:T(8,128)(2,1)}, u32[]{:S(2)}, u32[]{:S(2)}) collective-permute-start(bf16[8,64,512]{2,1,0:T(8,128)(2,1)S(1)} %get-tuple-element.180), channel_id=1, source_target_pairs={{0,1},{1,0},{2,3},{3,2},{4,5},{5,4},{6,7},{7,6},{8,9},{9,8},{10,11... | collective-permute-start | bytes 1572872 | tf_op jit(solution)/shard_map/ppermute | solution.py:1018
  328.1 10.3 %copy-start.5 = (f32[2,144,512]{2,1,0:T(8,128)S(1)}, f32[2,144,512]{2,1,0:T(8,128)}, u32[]{:S(2)}) copy-start(f32[2,144,512]{2,1,0:T(8,128)} %get-tuple-element.182) | copy-start | bytes 1769476
  328.1 29.0 %all-to-all-start.5 = ((bf16[4,1,4,64,512]{4,3,2,1,0:T(8,128)(2,1)}), bf16[4,1,4,64,512]{4,3,2,1,0:T(8,128)(2,1)S(1)}, u32[]{:S(2)}, u32[]{:S(2)}) async-start(bf16[4,1,4,64,512]{4,3,2,1,0:T(8,128)(2,1)} %get-tuple-element.148), calls=%async_computation.5 | async-start | bytes 2097152 | tf_op jit(solution)/shard_map/all_to_all | solution.py:1186
  338.5 10.9 %collective-permute-start.22 = (bf16[1,144,512]{2,1,0:T(8,128)(2,1)S(1)}, bf16[1,144,512]{2,1,0:T(8,128)(2,1)S(1)}, u32[]{:S(2)}, u32[]{:S(2)}) collective-permute-start(bf16[1,144,512]{2,1,0:T(8,128)(2,1)S(1)} %fusion.1), channel_id=1, source_target_pairs={{0,16},{8,24},{16,0},{24,8},{1,17},{9,25},{17,1},{25,9},{2,18},{10... | collective-permute-start | bytes 442376 | tf_op jit(solution)/shard_map/ppermute | solution.py:1018
  347.4 8.1 %collective-permute-start.18 = (bf16[4,64,512]{2,1,0:T(8,128)(2,1)S(1)}, bf16[4,64,512]{2,1,0:T(8,128)(2,1)S(1)}, u32[]{:S(2)}, u32[]{:S(2)}) collective-permute-start(bf16[4,64,512]{2,1,0:T(8,128)(2,1)S(1)} %get-tuple-element.145), channel_id=1, source_target_pairs={{0,2},{1,3},{2,0},{3,1},{4,6},{5,7},{6,4},{7,5},{8,10},{9,11},{10,... | collective-permute-start | bytes 786440 | tf_op jit(solution)/shard_map/ppermute | solution.py:1018
  355.5 8.1 %collective-permute-start.19 = (bf16[2,64,512]{2,1,0:T(8,128)(2,1)S(1)}, bf16[2,64,512]{2,1,0:T(8,128)(2,1)S(1)}, u32[]{:S(2)}, u32[]{:S(2)}) collective-permute-start(bf16[2,64,512]{2,1,0:T(8,128)(2,1)S(1)} %get-tuple-element.185), channel_id=1, source_target_pairs={{0,4},{1,5},{2,6},{3,7},{4,0},{5,1},{6,2},{7,3},{8,12},{9,13},{10,... | collective-permute-start | bytes 393224 | tf_op jit(solution)/shard_map/ppermute | solution.py:1018
  357.2 3.3 copy-start.2
  364.4 4.3 %collective-permute-start.20 = (bf16[1,64,512]{2,1,0:T(8,128)(2,1)S(1)}, bf16[1,64,512]{2,1,0:T(8,128)(2,1)S(1)}, u32[]{:S(2)}, u32[]{:S(2)}) collective-permute-start(bf16[1,64,512]{2,1,0:T(8,128)(2,1)S(1)} %get-tuple-element.150), channel_id=1, source_target_pairs={{0,16},{8,24},{16,0},{24,8},{1,17},{9,25},{17,1},{25,9},{2,18},{10... | collective-permute-start | bytes 196616 | tf_op jit(solution)/shard_map/ppermute | solution.py:1018
  368.6 0.6 copy-start.8
Sparse Core Ops, SparseCore 0:
  10.9 72.2 all-gather.1

commit v4 on v3

--- a/solution.py
+++ b/solution.py
@@ -510,7 +510,7 @@
         devices = owner.shape[0]
         half = (devices // 2, (2 * ff + MODEL) // devices, MODEL)
         out_specs += [fixed(half), fixed(half)]
-        out_shape += [jax.ShapeDtypeStruct(half, f32), jax.ShapeDtypeStruct(half, bf16)]
+        out_shape += [jax.ShapeDtypeStruct(half, bf16)] * 2
     else:
         out_specs += [ANYWHERE] * 3
         out_shape += [jax.ShapeDtypeStruct(shape, f32) for shape in f32_sums]
@@ -553,12 +553,13 @@
         cost_estimate=pl.CostEstimate(
             flops=members * (24 << 30), bytes_accessed=members << 24, transcendentals=0
         ),
-    )(*tables, owner, target, rows, cot[0], inc, weights[0], vec, *weights[1:], *(before or ()))
+    )(*tables[:3], owner, target, rows, cot[0], inc, weights[0], vec, *weights[1:], *(before or ()))
 
 
 def back_kernel(
     placing,
     restart,
+    reach,
     owner,
     _,
     rows_ref,
@@ -567,7 +568,6 @@
     gd_ref,
     branch_ref,
     states_ref,
-    inc_ref,
     weight,
     vec,
     owner_col,
@@ -577,7 +577,9 @@
     final,
     widths,
     sums,
+    hops,
 ):
+    incs, refs = refs[:hops], refs[hops:]
     gain, shift = vector(vec, GAIN_ONE), vector(vec, SHIFT_ONE)
     before, refs = (refs[:1], refs[1:]) if resumes else ((), refs)
     vec_others, refs = refs[:sums], refs[sums:]
@@ -610,8 +612,11 @@
     @pl.when(step == 0)
     def _():
         only = jnp.concatenate([jnp.ones((PAIR, PAIR), f32), jnp.where(inner == 0, 1.0, 0.0)], axis=1)
+        inc = jnp.zeros((HEAD_DIM + 8, MODEL), f32)
+        for hop, ref in enumerate(incs):
+            inc = inc + ref[0] * reach[micro, hop]
         for pair in range(PAIRS):
-            carry[pair] = unpack_state(inc_ref[0], pair) * only
+            carry[pair] = unpack_state(inc, pair) * only
 
     block = same_head()
     wide_block = jnp.concatenate([block, block], axis=1)
@@ -741,7 +746,7 @@
                 target[j % half, 3 * less :, :] = block16.astype(target.dtype)
 
 
-def run_back(tables, first, members, target, rows, mid, inc, weight, vec, before, owner, others, widths):
+def run_back(tables, first, members, target, rows, mid, incs, weight, vec, before, owner, others, widths):
     (group, seat), (saved, at) = target, mid
     micro, count = tables[0].shape
     width = rows.shape[-1]
@@ -761,7 +766,7 @@
     scratch = []
     if final:
         out_specs += [fixed(half), fixed(half)]
-        out_shape += [jax.ShapeDtypeStruct(half, f32), jax.ShapeDtypeStruct(half, bf16)]
+        out_shape += [jax.ShapeDtypeStruct(half, bf16)] * 2
         scratch.append(pltpu.VMEM((width, 3 * MODEL), f32))
     else:
         out_specs.append(fixed((width, 3 * MODEL)))
@@ -779,11 +784,17 @@
 
     return pl.pallas_call(
         functools.partial(
-            back_kernel, first=first, resumes=resumes, final=final, widths=widths, sums=len(others)
+            back_kernel,
+            first=first,
+            resumes=resumes,
+            final=final,
+            widths=widths,
+            sums=len(others),
+            hops=len(incs),
         ),
         name="back",
         grid_spec=pltpu.PrefetchScalarGridSpec(
-            num_scalar_prefetch=3,
+            num_scalar_prefetch=4,
             grid=(members, tiles),
             in_specs=[
                 ANYWHERE,
@@ -796,18 +807,18 @@
                     (TILE // CHUNK, MODEL, 3 * PAIR),
                     lambda i, t, *_: ((at + i) * tiles + tiles - 1 - t, 0, 0),
                 ),
-                member_spec(at),
                 fixed(weight.shape),
                 fixed(vec.shape),
                 fixed((owner.shape[0], 1)),
             ]
+            + [member_spec(at)] * len(incs)
             + ([ANYWHERE] if resumes else [])
             + [fixed(item.shape) for item in others],
             out_specs=out_specs,
             scratch_shapes=scratch,
         ),
         out_shape=out_shape,
-        input_output_aliases={3: 0},
+        input_output_aliases={4: 0},
         compiler_params=params(),
         cost_estimate=pl.CostEstimate(
             flops=members * (15 << 30), bytes_accessed=members << 24, transcendentals=0
@@ -815,6 +826,7 @@
     )(
         tables[0],
         tables[1],
+        tables[3],
         owner,
         group,
         rows,
@@ -823,17 +835,17 @@
         saved[4],
         saved[2],
         saved[5],
-        inc,
         weight,
         vec,
         owner[:, None],
+        *incs,
         *(() if before is None else (before,)),
         *others,
     )
 
 
-def send_kernel(slot, source, target):
-    micro = pl.program_id(0)
+def send_kernel(slot, source, target, *, first):
+    micro = first + pl.program_id(0)
     for i in range(source.shape[1]):
         put(target, slot[micro, i], source[0, i])
 
@@ -844,7 +856,7 @@
     groups = lax.axis_size("dp")
     shape = (groups, members, stretches // groups, STRETCH, width)
     return pl.pallas_call(
-        send_kernel,
+        functools.partial(send_kernel, first=first),
         name="send",
         grid_spec=pltpu.PrefetchScalarGridSpec(
             num_scalar_prefetch=1,
@@ -859,11 +871,11 @@
         cost_estimate=pl.CostEstimate(
             flops=0, bytes_accessed=4 * members * count * width, transcendentals=0
         ),
-    )(slot[first : first + members], rows.reshape(micro, stretches, STRETCH, width))
-
-
-def land_kernel(slot, _, source, target):
-    micro = pl.program_id(0)
+    )(slot, rows.reshape(micro, stretches, STRETCH, width))
+
+
+def land_kernel(slot, _, source, target, *, first):
+    micro = first + pl.program_id(0)
     for i in range(target.shape[1]):
         target[0, i] = pick(source, slot[micro, i])
 
@@ -873,7 +885,7 @@
     shape = output.shape
     block = (landed.shape[0], 1) + landed.shape[2:]
     return pl.pallas_call(
-        land_kernel,
+        functools.partial(land_kernel, first=first),
         name="land",
         grid_spec=pltpu.PrefetchScalarGridSpec(
             num_scalar_prefetch=1,
@@ -888,7 +900,7 @@
         input_output_aliases={1: 0},
         compiler_params=pltpu.CompilerParams(vmem_limit_bytes=VMEM_LIMIT),
         cost_estimate=pl.CostEstimate(flops=0, bytes_accessed=4 * landed.size, transcendentals=0),
-    )(slot[first : first + members], output, landed)
+    )(slot, output, landed)
 
 
 def blank(shape):
@@ -967,15 +979,12 @@
     total, own, step = jnp.zeros_like(states), states, 1
     while step <= weights.shape[1] and step < size:
         got = lax.ppermute(own, "fsdp", [(i, i + step) for i in range(size - step)])
+        if step == 1:
+            got = after(got, beside)
         total = total + got * weights[:, step - 1, None, None]
-        own = after(own + got * unbroken[:, step - 1, None, None], beside)
+        own = own + got * unbroken[:, step - 1, None, None]
         step *= 2
     return total
-
-
-def joined(got, weights, *others):
-    got = after(got, *others)
-    return sum(item * weights[:, hop, None, None] for hop, item in enumerate(got))
 
 
 def halving_stages():
@@ -1036,10 +1045,10 @@
 
 def scatter_join(keep, got, last):
     if last:
-        return keep[0] + got[0].astype(f32), None
+        return keep[0].astype(f32) + got[0].astype(f32), None
     half = keep.shape[0] // 2
-    send = (keep[half:] + got[half:].astype(f32)).astype(bf16)
-    return keep[:half] + got[:half].astype(f32), send
+    send = (keep[half:].astype(f32) + got[half:].astype(f32)).astype(bf16)
+    return keep[:half].astype(f32) + got[:half].astype(f32), send
 
 
 def finish_kernel(keep, got, qkv, *vectors):
@@ -1222,6 +1231,7 @@
     slot, placing, restart, opened, closing, from_before, from_after, unbroken = index_tables(
         lengths, stretch_order, count
     )
+    tables = (placing, restart, opened, from_after)
     small = (ln1_gain, ln1_bias, b_qkv, b_out, ln2_gain, ln2_bias, b_up, b_down)
     in_parts = (width // devices) % 16 == 0
     groups = groups_of(micro)
@@ -1229,7 +1239,7 @@
     if in_parts:
         place, owner = order_tables()
         first_part, second_part = run_pack(w_qkv, w_out, w_up, w_down, small)
-        halves, steps = gather_halves(first_part, {1: sent})
+        halves, steps = gather_halves(first_part, {1: sent, 2: tables + (closing, from_before, unbroken)})
         moved = to_dp(after(sent, steps[0]))
         qkv_all, vectors = run_sort_first(
             place, owner, *halves, [item.shape[0] for item in small]
@@ -1243,12 +1253,11 @@
         up_all, down_all = gather_all(w_up), gather_all(w_down)
         vectors = [gather_all(item).astype(f32) for item in small]
         vectors = jnp.stack([jnp.pad(item, (0, ff - item.shape[0])) for item in vectors])
-    tables = (placing, restart, opened)
 
     sent_grads = run_send(slot, after(cotangent, *ready), 0, micro)
     hops = from_before.shape[1]
     states = run_state(placing, closing, moved, qkv_all, vectors)
-    cots = to_dp(after(sent_grads, states))
+    cots = to_dp(sent_grads)
     if in_parts:
         up_all, down_all, out_all = run_sort_second(after(second_part, states), ff)
     incoming = passed_on(states, from_before, unbroken, out_all)
@@ -1272,13 +1281,12 @@
         sums = out[8:]
         mids.append(out)
     outgoing = [exchange(out[6], hops, False) for out in mids]
-    reach = [from_after[first : first + members] for first, members in groups]
     homes = [to_dp(out[0]) for out in mids]
     sizes = [MODEL, MODEL, 2 * MODEL, MODEL, MODEL, MODEL, MODEL, ff, MODEL]
     widths = [size // devices for size in sizes]
     last = len(halving_stages()) - 1
     late = len(groups) - 1
-    outgoing[0] = joined(outgoing[0], reach[0], *([mids[-1][7]] if late else []))
+    outgoing[0] = after(outgoing[0], *([mids[-1][7]] if late else []))
     if in_parts:
         keep, send = sums
         if late:
@@ -1290,7 +1298,7 @@
     grad_rows = []
     for g, (first, members) in enumerate(groups):
         if g:
-            outgoing[g] = joined(outgoing[g], reach[g], vec_back[0], homes[g])
+            outgoing[g] = after(outgoing[g], vec_back[0], homes[g])
             grad_rows[0] = after(grad_rows[0], outgoing[g])
         saved = list(mids[g])
         if in_parts:
@@ -1334,14 +1342,10 @@
         narrow_keep, narrow_send = narrow
         if len(groups) > 1:
             narrow_send = after(narrow_send, grad_homes[0], keep, send)
-        while done < last:
+        wide_keep, wide_send, got = keep, send, None
+        if done < last:
             done += 1
-            keep, send = scatter_step(keep, send, done)
-        wide = keep
-        parts = ff // MODEL
-        grad_up = jnp.concatenate([wide[c * part : (c + 1) * part] for c in range(parts)], axis=1)
-        grad_down = wide[parts * part : 2 * parts * part]
-        grad_out = wide[2 * parts * part :]
+            got = swap(send, *halving_stages()[done])
         keep, send = narrow_keep, narrow_send
         for step in range(last):
             keep, send = scatter_step(keep, send, step)
@@ -1350,7 +1354,18 @@
             if step == 1:
                 send = after(send, result)
                 input_grad = land(input_grad, grad_homes, send)
-        send = after(send, input_grad)
+            if step == 2:
+                send = after(send, input_grad)
+                if got is not None:
+                    wide_keep, wide_send = scatter_join(wide_keep, after(got, send), done == last)
+                while done < last:
+                    done += 1
+                    wide_keep, wide_send = scatter_step(wide_keep, wide_send, done)
+        wide = wide_keep
+        parts = ff // MODEL
+        grad_up = jnp.concatenate([wide[c * part : (c + 1) * part] for c in range(parts)], axis=1)
+        grad_down = wide[parts * part : 2 * parts * part]
+        grad_out = wide[2 * parts * part :]
         grad_qkv, *owned_vec = run_finish(keep, swap(send, *halving_stages()[last]), widths)
         owned_vec = [item[0] for item in owned_vec]
     else:

time: 384 us -> 370 us (0.964)
  other arithmetic: 27 us -> 18.2 us
  local copies, waits for them, and re-layouts: 12.1 us -> 6.06 us
    add x7 -> x4, other arithmetic: 9.63 us -> 1.34 us  [the longest x2 1.16 us: scatter_join(): return (keep[:half].astype(f32) + got[:half].astype(f32), send)]
    ppermute x15, waiting for transfers between devices: 39.3 us -> 43.3 us  [swap(): lax.ppermute(x, axis, [(i, i ^ bit) for i in range(lax.axis_size(axis))])]
  transfers between devices with their start and end apart: 30 -> 30, of which waited for: 12 -> 14; matrix products, arithmetic and copies ran while one was open for 9% -> 6% of each run, Pallas kernels for 33% -> 34%
where the time goes in v4:
time: 370 us; the launch traced here: 364 us
  Pallas kernels  196 us (53%)
  starting transfers between devices  66.3 us (18%)
  waiting for transfers between devices  63.5 us (17%)
  other arithmetic  18.2 us (5%)
  between operations  14.8 us (4%)
  local copies, waits for them, and re-layouts  6.06 us (2%)
    pallas_call x2, Pallas kernels, run_mid(): pl.pallas_call(functools.partial(mid_kernel, first=first, resumes=resumes...  95.8 us
    pallas_call x2, Pallas kernels, run_back(): pl.pallas_call(functools.partial(back_kernel, first=first, resumes=resume...  53.4 us
    ppermute x15, waiting for transfers between devices, swap(): lax.ppermute(x, axis, [(i, i ^ bit) for i in range(lax.axis_size(axis))])  43.3 us
    ppermute x15, starting transfers between devices, swap(): lax.ppermute(x, axis, [(i, i ^ bit) for i in range(lax.axis_size(axis))])  26.1 us
    all_to_all x6, starting transfers between devices, to_dp(): return lax.all_to_all(group, 'dp', split_axis=0, concat_axis=0, tiled=True)  23.7 us
    ppermute x2, waiting for transfers between devices, passed_on(): got = lax.ppermute(own, 'fsdp', [(i, i + step) for i in range(size - step)])  14.1 us
    pallas_call x4, Pallas kernels, run_land(): pl.pallas_call(functools.partial(land_kernel, first=first), name='land',...  12.7 us
    pallas_call x1, Pallas kernels, run_state(): pl.pallas_call(state_kernel, name='end_state', grid_spec=pltpu.PrefetchSc...  11.5 us
  transfers between devices with their start and end apart: 30, of which 14 were waited for; matrix products, arithmetic and copies ran while one was open for 6% of the time, Pallas kernels for 34%

profile of v4, /device:TPU:0, one launch (start us, length us, event | category | flops | bytes accessed | tf_op | source)
XLA Modules:
  0.0 364.4 jit_solution(7754004258066857191)
XLA Ops:
  7.2 1.8 pack.1
  9.0 3.0 collective-permute-start
  13.8 5.3 %send.2 = bf16[4,3,4,64,512]{4,3,2,1,0:T(8,128)(2,1)} custom-call(s32[3,16]{1,0:T(4,128)} %convert_reduce_fusion.1.slot, bf16[3,16,64,512]{3,2,1,0:T(8,128)(2,1)} %bitcast.35), custom_call_target="tpu_custom_call" | custom-call | bytes 6291456 | tf_op jit(solution)/shard_map/send/pallas_call | solution.py:858
  22.0 2.7 collective-permute-start.1
  24.7 3.7 %all-to-all-start = ((bf16[4,3,4,64,512]{4,3,2,1,0:T(8,128)(2,1)}), bf16[4,3,4,64,512]{4,3,2,1,0:T(8,128)(2,1)S(1)}, u32[]{:S(2)}, u32[]{:S(2)}) async-start(bf16[4,3,4,64,512]{4,3,2,1,0:T(8,128)(2,1)} %send.2), calls=%async_computation | async-start | bytes 6291456 | tf_op jit(solution)/shard_map/all_to_all | solution.py:1195
  29.0 4.1 %collective-permute-done.1 = bf16[2,64,512]{2,1,0:T(8,128)(2,1)S(1)} collective-permute-done((bf16[2,64,512]{2,1,0:T(8,128)(2,1)S(1)}, bf16[2,64,512]{2,1,0:T(8,128)(2,1)S(1)}, u32[]{:S(2)}, u32[]{:S(2)}) %collective-permute-start.1) | collective-permute-done | bytes 131104 | tf_op jit(solution)/shard_map/ppermute | solution.py:1027
  33.2 7.4 %collective-permute-done.2 = bf16[4,64,512]{2,1,0:T(8,128)(2,1)S(1)} collective-permute-done((bf16[4,64,512]{2,1,0:T(8,128)(2,1)S(1)}, bf16[4,64,512]{2,1,0:T(8,128)(2,1)S(1)}, u32[]{:S(2)}, u32[]{:S(2)}) %collective-permute-start.2) | collective-permute-done | bytes 262176 | tf_op jit(solution)/shard_map/ppermute | solution.py:1027
  40.7 1.7 collective-permute-start.3
  42.4 12.5 %collective-permute-done.3 = bf16[8,64,512]{2,1,0:T(8,128)(2,1)S(1)} collective-permute-done((bf16[8,64,512]{2,1,0:T(8,128)(2,1)S(1)}, bf16[8,64,512]{2,1,0:T(8,128)(2,1)S(1)}, u32[]{:S(2)}, u32[]{:S(2)}) %collective-permute-start.3) | collective-permute-done | bytes 524320 | tf_op jit(solution)/shard_map/ppermute | solution.py:1027
  57.0 1.6 collective-permute-done.4.got
  58.7 3.5 sort_first.1
  62.2 5.4 %send.3 = bf16[4,3,4,64,512]{4,3,2,1,0:T(8,128)(2,1)} custom-call(s32[3,16]{1,0:T(4,128)} %convert_reduce_fusion.1.slot, bf16[3,16,64,512]{3,2,1,0:T(8,128)(2,1)} %bitcast.36), custom_call_target="tpu_custom_call" | custom-call | bytes 6291456 | tf_op jit(solution)/shard_map/send/pallas_call | solution.py:858
  67.5 6.0 %all-to-all-done.rows.rows_ref = bf16[4,3,4,64,512]{4,3,2,1,0:T(8,128)(2,1)S(1)} async-done(((bf16[4,3,4,64,512]{4,3,2,1,0:T(8,128)(2,1)}), bf16[4,3,4,64,512]{4,3,2,1,0:T(8,128)(2,1)S(1)}, u32[]{:S(2)}, u32[]{:S(2)}) %all-to-all-start) | async-done | bytes 3145760 | tf_op jit(solution)/shard_map/all_to_all | solution.py:1195
  73.6 1.7 copy-done.3
  75.2 4.7 %all-to-all-start.1 = ((bf16[4,3,4,64,512]{4,3,2,1,0:T(8,128)(2,1)}), bf16[4,3,4,64,512]{4,3,2,1,0:T(8,128)(2,1)}, u32[]{:S(2)}, u32[]{:S(2)}) async-start(bf16[4,3,4,64,512]{4,3,2,1,0:T(8,128)(2,1)} %send.3), calls=%async_computation.1 | async-start | bytes 6291456 | tf_op jit(solution)/shard_map/all_to_all | solution.py:1195
  80.0 11.5 %end_state.1 = f32[3,72,512]{2,1,0:T(8,128)} custom-call(s32[3,16]{1,0:T(4,128)} %get-tuple-element.200.placing, s32[3,16]{1,0:T(4,128)} %get-tuple-element.199.closing, bf16[4,3,4,64,512]{4,3,2,1,0:T(8,128)(2,1)} %copy-done.3, bf16[512,1536]{1,0:T(8,128)(2,1)} %get-tuple-element.93.weight.w_qkv, f32[8,2048]{1,0:T(8,128)} %get-tuple-element.95.vec), custom_call_target="tpu_custom_call" | custom-call | flops 11811160064 | bytes 5242880 | tf_op jit(solution)/shard_map/end_state/pallas_call | solution.py:203
  91.4 3.5 collective-permute-start.5
  95.1 4.6 %sort_second.1 = (bf16[512,2048]{1,0:T(8,128)(2,1)}, bf16[2048,512]{1,0:T(8,128)(2,1)}, bf16[512,512]{1,0:T(8,128)(2,1)}) custom-call(bf16[32,144,512]{2,1,0:T(8,128)(2,1)} %all-gather.2.cloned.1.call-done.gathered), custom_call_target="tpu_custom_call" | custom-call | tf_op jit(solution)/shard_map/sort_second/pallas_call | solution.py:1172
  99.7 5.6 %collective-permute-done.5 = f32[3,72,512]{2,1,0:T(8,128)S(1)} collective-permute-done((f32[3,72,512]{2,1,0:T(8,128)}, f32[3,72,512]{2,1,0:T(8,128)S(1)}, u32[]{:S(2)}, u32[]{:S(2)}) %collective-permute-start.5) | collective-permute-done | bytes 442400 | tf_op jit(solution)/shard_map/ppermute | solution.py:981
  105.4 5.3 %collective-permute-start.6 = (f32[3,72,512]{2,1,0:T(8,128)S(1)}, f32[3,72,512]{2,1,0:T(8,128)S(1)}, u32[]{:S(2)}, u32[]{:S(2)}) collective-permute-start(f32[3,72,512]{2,1,0:T(8,128)S(1)} %multiply_add_fusion.1), channel_id=1, source_target_pairs={{0,2},{1,3},{2,4},{3,5},{4,6},{5,7},{8,10},{9,11},{10,12},{11,13},... | collective-permute-start | bytes 1327112 | tf_op jit(solution)/shard_map/ppermute | solution.py:981
  111.4 8.5 %collective-permute-done.6 = f32[3,72,512]{2,1,0:T(8,128)S(1)} collective-permute-done((f32[3,72,512]{2,1,0:T(8,128)S(1)}, f32[3,72,512]{2,1,0:T(8,128)S(1)}, u32[]{:S(2)}, u32[]{:S(2)}) %collective-permute-start.6) | collective-permute-done | bytes 442400 | tf_op jit(solution)/shard_map/ppermute | solution.py:981
  121.4 58.9 %middle.2 = (bf16[4,2,4,64,512]{4,3,2,1,0:T(8,128)(2,1)}, bf16[2048,1536]{1,0:T(8,128)(2,1)}, bf16[2048,512]{1,0:T(8,128)(2,1)}, bf16[2048,512]{1,0:T(8,128)(2,1...) custom-call(s32[3,16]{1,0:T(4,128)} %get-tuple-element.200.placing, ...), custom_call_target="tpu_custom_call", output_to_operand_aliasing={{0}: (4, {})} | custom-call | flops 51539607552 | bytes 33554432 | tf_op jit(solution)/shard_map/middle/pallas_call | solution.py:533
  180.3 1.3 collective-permute-start.7
  181.6 1.3 collective-permute-start.8
  184.2 3.6 all-to-all-start.2
  187.8 36.9 %middle.3 = (bf16[4,1,4,64,512]{4,3,2,1,0:T(8,128)(2,1)}, bf16[1024,1536]{1,0:T(8,128)(2,1)}, bf16[1024,512]{1,0:T(8,128)(2,1)}, bf16[1024,512]{1,0:T(8,128)(2,1...) custom-call(s32[3,16]{1,0:T(4,128)} %get-tuple-element.200.placing, ...), custom_call_target="tpu_custom_call", output_to_operand_aliasing={{0}: (4, {})} | custom-call | flops 25769803776 | bytes 16777216 | tf_op jit(solution)/shard_map/middle/pallas_call | solution.py:533
  229.2 3.5 all-to-all-start.3
  232.7 4.1 %add_convert_fusion = (bf16[8,144,512]{2,1,0:T(8,128)(2,1)}, f32[8,144,512]{2,1,0:T(8,128)S(1)}) fusion(bf16[16,144,512]{2,1,0:T(8,128)(2,1)} %collective-permute-done.10, bf16[16,144,512]{2,1,0:T(8,128)(2,1)} %get-tuple-element.111), kind=kLoop, calls=%fused_computation | loop fusion | flops 4128768 | bytes 8257536 | tf_op jit(solution)/shard_map/convert_element_type | solution.py:1050
  236.8 3.3 collective-permute-start.11
  240.7 32.8 %back.2 = (bf16[4,2,4,64,512]{4,3,2,1,0:T(8,128)(2,1)}, f32[8,1536]{1,0:T(8,128)}, f32[512,1536]{1,0:T(8,128)}) custom-call(s32[3,16]{1,0:T(4,128)} %get-tuple-element.200.placing, s32[3,17]{1,0:T(4,128)} %convert_select_fusion.restart, f32[3,3]{1,0:T(4,128)} %convert_subtract_fusion.3.reach, ...), custom_call_target="tpu_custom_call", output_to_operand_aliasing={{0}: (4, {})} | custom-call | flops 32212254720 | bytes 33554432 | tf_op jit(solution)/shard_map/back/pallas_call | solution.py:785
  273.6 4.6 %all-to-all-start.4 = ((bf16[4,2,4,64,512]{4,3,2,1,0:T(8,128)(2,1)}), bf16[4,2,4,64,512]{4,3,2,1,0:T(8,128)(2,1)}, u32[]{:S(2)}, u32[]{:S(2)}) async-start(bf16[4,2,4,64,512]{4,3,2,1,0:T(8,128)(2,1)} %get-tuple-element.140), calls=%async_computation.4 | async-start | bytes 4194304 | tf_op jit(solution)/shard_map/all_to_all | solution.py:1195
  278.2 2.5 add_convert_fusion.1
  280.7 5.0 %collective-permute-start.15 = (bf16[4,144,512]{2,1,0:T(8,128)(2,1)}, bf16[4,144,512]{2,1,0:T(8,128)(2,1)S(1)}, u32[]{:S(2)}, u32[]{:S(2)}) collective-permute-start(bf16[4,144,512]{2,1,0:T(8,128)(2,1)} %get-tuple-element.142), channel_id=1, source_target_pairs={{0,2},{1,3},{2,0},{3,1},{4,6},{5,7},{6,4},{7,5},{8,10},{9,11},{10,... | collective-permute-start | bytes 1769480 | tf_op jit(solution)/shard_map/ppermute | solution.py:1027
  285.7 20.6 %back.3 = (bf16[4,1,4,64,512]{4,3,2,1,0:T(8,128)(2,1)}, f32[8,1536]{1,0:T(8,128)}, bf16[16,64,512]{2,1,0:T(8,128)(2,1)}, bf16[16,64,512]{2,1,0:T(8,128)(2,1)}) custom-call(s32[3,16]{1,0:T(4,128)} %get-tuple-element.200.placing, s32[3,17]{1,0:T(4,128)} %convert_select_fusion.restart, ...), custom_call_target="tpu_custom_call", output_to_operand_aliasing={{0}: (4, {})} | custom-call | flops 16106127360 | bytes 16777216 | tf_op jit(solution)/shard_map/back/pallas_call | solution.py:785
  307.6 2.7 collective-permute-done.16
  310.7 3.5 all-to-all-start.5
  314.2 3.3 land.4._
  317.5 2.9 land.5
  320.5 4.2 %collective-permute-done.17 = bf16[8,64,512]{2,1,0:T(8,128)(2,1)S(1)} collective-permute-done((bf16[8,64,512]{2,1,0:T(8,128)(2,1)S(1)}, bf16[8,64,512]{2,1,0:T(8,128)(2,1)S(1)}, u32[]{:S(2)}, u32[]{:S(2)}) %collective-permute-start.17) | collective-permute-done | bytes 524320 | tf_op jit(solution)/shard_map/ppermute | solution.py:1027
  325.5 1.5 collective-permute-start.18
  327.0 5.0 %collective-permute-start.21 = (bf16[2,144,512]{2,1,0:T(8,128)(2,1)S(1)}, bf16[2,144,512]{2,1,0:T(8,128)(2,1)S(1)}, u32[]{:S(2)}, u32[]{:S(2)}) collective-permute-start(bf16[2,144,512]{2,1,0:T(8,128)(2,1)S(1)} %copy-done.8), channel_id=1, source_target_pairs={{0,4},{1,5},{2,6},{3,7},{4,0},{5,1},{6,2},{7,3},{8,12},{9,13},{10,... | collective-permute-start | bytes 884744 | tf_op jit(solution)/shard_map/ppermute | solution.py:1027
  332.0 3.3 land.6._
  335.3 3.1 land.7
  339.0 1.7 collective-permute-start.19
  340.7 7.0 %collective-permute-done.21 = bf16[2,144,512]{2,1,0:T(8,128)(2,1)S(1)} collective-permute-done((bf16[2,144,512]{2,1,0:T(8,128)(2,1)S(1)}, bf16[2,144,512]{2,1,0:T(8,128)(2,1)S(1)}, u32[]{:S(2)}, u32[]{:S(2)}) %collective-permute-start.21) | collective-permute-done | bytes 294944 | tf_op jit(solution)/shard_map/ppermute | solution.py:1027
  347.8 2.4 collective-permute-done.19
  350.9 1.4 collective-permute-start.20
  355.8 1.6 finish.1
  (115 shorter events, 23.7 us)
Async XLA Ops:
  7.2 87.9 %all-gather.2.cloned.1.call-start = ((), (), s32[]{:S(2)}) async-start(), calls=%async_computation.6 | async-start | bytes 4866048 | tf_op jit(solution)/shard_map/all_gather | solution.py:1187
  9.0 13.0 %collective-permute-start = (bf16[1,64,512]{2,1,0:T(8,128)(2,1)}, bf16[1,64,512]{2,1,0:T(8,128)(2,1)S(1)}, u32[]{:S(2)}, u32[]{:S(2)}) collective-permute-start(bf16[1,64,512]{2,1,0:T(8,128)(2,1)} %get-tuple-element.89), channel_id=1, source_target_pairs={{0,16},{8,24},{16,0},{24,8},{1,17},{9,25},{17,1},{25,9},{2,18},{10... | collective-permute-start | bytes 196616 | tf_op jit(solution)/shard_map/ppermute | solution.py:1027
  13.8 5.4 %copy-start.11 = (s32[3,16]{1,0:T(4,128)S(1)}, s32[3,16]{1,0:T(4,128)}, u32[]{:S(2)}) copy-start(s32[3,16]{1,0:T(4,128)} %param.18) | copy-start | bytes 580
  13.8 8.2 %copy-start.10 = (bf16[1,64,512]{2,1,0:T(8,128)(2,1)S(1)}, bf16[1,64,512]{2,1,0:T(8,128)(2,1)}, u32[]{:S(2)}) copy-start(bf16[1,64,512]{2,1,0:T(8,128)(2,1)} %get-tuple-element.89) | copy-start | bytes 196612
  22.0 11.1 %collective-permute-start.1 = (bf16[2,64,512]{2,1,0:T(8,128)(2,1)S(1)}, bf16[2,64,512]{2,1,0:T(8,128)(2,1)S(1)}, u32[]{:S(2)}, u32[]{:S(2)}) collective-permute-start(bf16[2,64,512]{2,1,0:T(8,128)(2,1)S(1)} %constant_dynamic-update-slice_fusion), channel_id=1, source_target_pairs={{0,4},{1,5},{2,6},{3,7},{4,0},{5,1},{6,2},{7,3},{8,12},{9,13},{10,... | collective-permute-start | bytes 393224 | tf_op jit(solution)/shard_map/ppermute | solution.py:1027
  24.7 48.9 %all-to-all-start = ((bf16[4,3,4,64,512]{4,3,2,1,0:T(8,128)(2,1)}), bf16[4,3,4,64,512]{4,3,2,1,0:T(8,128)(2,1)S(1)}, u32[]{:S(2)}, u32[]{:S(2)}) async-start(bf16[4,3,4,64,512]{4,3,2,1,0:T(8,128)(2,1)} %send.2), calls=%async_computation | async-start | bytes 6291456 | tf_op jit(solution)/shard_map/all_to_all | solution.py:1195
  33.1 7.5 %collective-permute-start.2 = (bf16[4,64,512]{2,1,0:T(8,128)(2,1)S(1)}, bf16[4,64,512]{2,1,0:T(8,128)(2,1)S(1)}, u32[]{:S(2)}, u32[]{:S(2)}) collective-permute-start(bf16[4,64,512]{2,1,0:T(8,128)(2,1)S(1)} %pad_maximum_fusion.1), channel_id=1, source_target_pairs={{0,2},{1,3},{2,0},{3,1},{4,6},{5,7},{6,4},{7,5},{8,10},{9,11},{10,... | collective-permute-start | bytes 786440 | tf_op jit(solution)/shard_map/ppermute | solution.py:1027
  40.7 14.2 %collective-permute-start.3 = (bf16[8,64,512]{2,1,0:T(8,128)(2,1)S(1)}, bf16[8,64,512]{2,1,0:T(8,128)(2,1)S(1)}, u32[]{:S(2)}, u32[]{:S(2)}) collective-permute-start(bf16[8,64,512]{2,1,0:T(8,128)(2,1)S(1)} %pad_maximum_fusion), channel_id=1, source_target_pairs={{0,1},{1,0},{2,3},{3,2},{4,5},{5,4},{6,7},{7,6},{8,9},{9,8},{10,11... | collective-permute-start | bytes 1572872 | tf_op jit(solution)/shard_map/ppermute | solution.py:1027
  54.9 1.0 copy-start.5
  55.9 2.8 collective-permute-start.4
  73.6 1.7 copy-start.3
  75.2 45.6 %all-to-all-start.1 = ((bf16[4,3,4,64,512]{4,3,2,1,0:T(8,128)(2,1)}), bf16[4,3,4,64,512]{4,3,2,1,0:T(8,128)(2,1)}, u32[]{:S(2)}, u32[]{:S(2)}) async-start(bf16[4,3,4,64,512]{4,3,2,1,0:T(8,128)(2,1)} %send.3), calls=%async_computation.1 | async-start | bytes 6291456 | tf_op jit(solution)/shard_map/all_to_all | solution.py:1195
  91.4 13.9 %collective-permute-start.5 = (f32[3,72,512]{2,1,0:T(8,128)}, f32[3,72,512]{2,1,0:T(8,128)S(1)}, u32[]{:S(2)}, u32[]{:S(2)}) collective-permute-start(f32[3,72,512]{2,1,0:T(8,128)} %end_state.1), channel_id=1, source_target_pairs={{0,1},{1,2},{2,3},{3,4},{4,5},{5,6},{6,7},{8,9},{9,10},{10,11},{11... | collective-permute-start | bytes 1327112 | tf_op jit(solution)/shard_map/ppermute | solution.py:981
  95.0 10.3 %copy-start.7 = (f32[3,72,512]{2,1,0:T(8,128)S(1)}, f32[3,72,512]{2,1,0:T(8,128)}, u32[]{:S(2)}) copy-start(f32[3,72,512]{2,1,0:T(8,128)} %end_state.1) | copy-start | bytes 1327108
  105.4 14.5 %collective-permute-start.6 = (f32[3,72,512]{2,1,0:T(8,128)S(1)}, f32[3,72,512]{2,1,0:T(8,128)S(1)}, u32[]{:S(2)}, u32[]{:S(2)}) collective-permute-start(f32[3,72,512]{2,1,0:T(8,128)S(1)} %multiply_add_fusion.1), channel_id=1, source_target_pairs={{0,2},{1,3},{2,4},{3,5},{4,6},{5,7},{8,10},{9,11},{10,12},{11,13},... | collective-permute-start | bytes 1327112 | tf_op jit(solution)/shard_map/ppermute | solution.py:981
  180.3 44.4 %collective-permute-start.7 = (f32[2,72,512]{2,1,0:T(8,128)}, f32[2,72,512]{2,1,0:T(8,128)S(1)}, u32[]{:S(2)}, u32[]{:S(2)}) collective-permute-start(f32[2,72,512]{2,1,0:T(8,128)} %get-tuple-element.113), channel_id=1, source_target_pairs={{1,0},{2,1},{3,2},{4,3},{5,4},{6,5},{7,6},{9,8},{10,9},{11,10},{12... | collective-permute-start | bytes 884744 | tf_op jit(solution)/shard_map/ppermute | solution.py:973
  181.6 43.1 %collective-permute-start.8 = (f32[2,72,512]{2,1,0:T(8,128)}, f32[2,72,512]{2,1,0:T(8,128)S(1)}, u32[]{:S(2)}, u32[]{:S(2)}) collective-permute-start(f32[2,72,512]{2,1,0:T(8,128)} %get-tuple-element.113), channel_id=1, source_target_pairs={{2,0},{3,1},{4,2},{5,3},{6,4},{7,5},{10,8},{11,9},{12,10},{13,11},... | collective-permute-start | bytes 884744 | tf_op jit(solution)/shard_map/ppermute | solution.py:973
  182.9 41.9 %collective-permute-start.9 = (f32[2,72,512]{2,1,0:T(8,128)}, f32[2,72,512]{2,1,0:T(8,128)S(1)}, u32[]{:S(2)}, u32[]{:S(2)}) collective-permute-start(f32[2,72,512]{2,1,0:T(8,128)} %get-tuple-element.113), channel_id=1, source_target_pairs={{3,0},{4,1},{5,2},{6,3},{7,4},{11,8},{12,9},{13,10},{14,11},{15,12... | collective-permute-start | bytes 884744 | tf_op jit(solution)/shard_map/ppermute | solution.py:973
  184.2 40.6 %all-to-all-start.2 = ((bf16[4,2,4,64,512]{4,3,2,1,0:T(8,128)(2,1)}), bf16[4,2,4,64,512]{4,3,2,1,0:T(8,128)(2,1)S(1)}, u32[]{:S(2)}, u32[]{:S(2)}) async-start(bf16[4,2,4,64,512]{4,3,2,1,0:T(8,128)(2,1)} %get-tuple-element.102), calls=%async_computation.2 | async-start | bytes 4194304 | tf_op jit(solution)/shard_map/all_to_all | solution.py:1195
  224.7 4.5 %copy-start.12 = (f32[2,72,512]{2,1,0:T(8,128)}, f32[2,72,512]{2,1,0:T(8,128)S(1)}, u32[]{:S(2)}) copy-start(f32[2,72,512]{2,1,0:T(8,128)S(1)} %collective-permute-done.7.refs_0_) | copy-start | bytes 884740
  224.7 4.5 %copy-start.13 = (f32[2,72,512]{2,1,0:T(8,128)}, f32[2,72,512]{2,1,0:T(8,128)S(1)}, u32[]{:S(2)}) copy-start(f32[2,72,512]{2,1,0:T(8,128)S(1)} %collective-permute-done.8.refs_1_) | copy-start | bytes 884740
  224.7 4.5 %copy-start.14 = (f32[2,72,512]{2,1,0:T(8,128)}, f32[2,72,512]{2,1,0:T(8,128)S(1)}, u32[]{:S(2)}) copy-start(f32[2,72,512]{2,1,0:T(8,128)S(1)} %collective-permute-done.9.refs_2_) | copy-start | bytes 884740
  224.8 4.4 %copy-start = (bf16[4,2,4,64,512]{4,3,2,1,0:T(8,128)(2,1)}, bf16[4,2,4,64,512]{4,3,2,1,0:T(8,128)(2,1)S(1)}, u32[]{:S(2)}) copy-start(bf16[4,2,4,64,512]{4,3,2,1,0:T(8,128)(2,1)S(1)} %all-to-all-done.2.source) | copy-start | bytes 6291460
  224.8 8.0 %collective-permute-start.10 = (bf16[16,144,512]{2,1,0:T(8,128)(2,1)}, bf16[16,144,512]{2,1,0:T(8,128)(2,1)}, u32[]{:S(2)}, u32[]{:S(2)}) collective-permute-start(bf16[16,144,512]{2,1,0:T(8,128)(2,1)} %get-tuple-element.118), channel_id=1, source_target_pairs={{0,8},{8,0},{16,24},{24,16},{1,9},{9,1},{17,25},{25,17},{2,10},{10... | collective-permute-start | bytes 7077896 | tf_op jit(solution)/shard_map/ppermute | solution.py:1027
  225.3 48.2 %collective-permute-start.12 = (f32[1,72,512]{2,1,0:T(8,128)}, f32[1,72,512]{2,1,0:T(8,128)S(1)}, u32[]{:S(2)}, u32[]{:S(2)}) collective-permute-start(f32[1,72,512]{2,1,0:T(8,128)} %get-tuple-element.130), channel_id=1, source_target_pairs={{1,0},{2,1},{3,2},{4,3},{5,4},{6,5},{7,6},{9,8},{10,9},{11,10},{12... | collective-permute-start | bytes 442376 | tf_op jit(solution)/shard_map/ppermute | solution.py:973
  226.6 47.0 %collective-permute-start.13 = (f32[1,72,512]{2,1,0:T(8,128)}, f32[1,72,512]{2,1,0:T(8,128)}, u32[]{:S(2)}, u32[]{:S(2)}) collective-permute-start(f32[1,72,512]{2,1,0:T(8,128)} %get-tuple-element.130), channel_id=1, source_target_pairs={{2,0},{3,1},{4,2},{5,3},{6,4},{7,5},{10,8},{11,9},{12,10},{13,11},... | collective-permute-start | bytes 442376 | tf_op jit(solution)/shard_map/ppermute | solution.py:973
  227.9 45.7 %collective-permute-start.14 = (f32[1,72,512]{2,1,0:T(8,128)}, f32[1,72,512]{2,1,0:T(8,128)}, u32[]{:S(2)}, u32[]{:S(2)}) collective-permute-start(f32[1,72,512]{2,1,0:T(8,128)} %get-tuple-element.130), channel_id=1, source_target_pairs={{3,0},{4,1},{5,2},{6,3},{7,4},{11,8},{12,9},{13,10},{14,11},{15,12... | collective-permute-start | bytes 442376 | tf_op jit(solution)/shard_map/ppermute | solution.py:973
  229.2 44.4 %all-to-all-start.3 = ((bf16[4,1,4,64,512]{4,3,2,1,0:T(8,128)(2,1)}), bf16[4,1,4,64,512]{4,3,2,1,0:T(8,128)(2,1)S(1)}, u32[]{:S(2)}, u32[]{:S(2)}) async-start(bf16[4,1,4,64,512]{4,3,2,1,0:T(8,128)(2,1)} %get-tuple-element.131), calls=%async_computation.3 | async-start | bytes 2097152 | tf_op jit(solution)/shard_map/all_to_all | solution.py:1195
  236.8 41.4 %collective-permute-start.11 = (bf16[8,144,512]{2,1,0:T(8,128)(2,1)}, bf16[8,144,512]{2,1,0:T(8,128)(2,1)}, u32[]{:S(2)}, u32[]{:S(2)}) collective-permute-start(bf16[8,144,512]{2,1,0:T(8,128)(2,1)} %get-tuple-element.120), channel_id=1, source_target_pairs={{0,1},{1,0},{2,3},{3,2},{4,5},{5,4},{6,7},{7,6},{8,9},{9,8},{10,11... | collective-permute-start | bytes 3538952 | tf_op jit(solution)/shard_map/ppermute | solution.py:1027
  273.5 4.7 %copy-start.15 = (f32[1,72,512]{2,1,0:T(8,128)}, f32[1,72,512]{2,1,0:T(8,128)S(1)}, u32[]{:S(2)}) copy-start(f32[1,72,512]{2,1,0:T(8,128)S(1)} %collective-permute-done.12.refs_0_) | copy-start | bytes 442372
  273.6 4.7 %copy-start.1 = (bf16[4,1,4,64,512]{4,3,2,1,0:T(8,128)(2,1)}, bf16[4,1,4,64,512]{4,3,2,1,0:T(8,128)(2,1)S(1)}, u32[]{:S(2)}) copy-start(bf16[4,1,4,64,512]{4,3,2,1,0:T(8,128)(2,1)S(1)} %all-to-all-done.3.source) | copy-start | bytes 3145732
  273.6 33.8 %all-to-all-start.4 = ((bf16[4,2,4,64,512]{4,3,2,1,0:T(8,128)(2,1)}), bf16[4,2,4,64,512]{4,3,2,1,0:T(8,128)(2,1)}, u32[]{:S(2)}, u32[]{:S(2)}) async-start(bf16[4,2,4,64,512]{4,3,2,1,0:T(8,128)(2,1)} %get-tuple-element.140), calls=%async_computation.4 | async-start | bytes 4194304 | tf_op jit(solution)/shard_map/all_to_all | solution.py:1195
  280.7 25.6 %collective-permute-start.15 = (bf16[4,144,512]{2,1,0:T(8,128)(2,1)}, bf16[4,144,512]{2,1,0:T(8,128)(2,1)S(1)}, u32[]{:S(2)}, u32[]{:S(2)}) collective-permute-start(bf16[4,144,512]{2,1,0:T(8,128)(2,1)} %get-tuple-element.142), channel_id=1, source_target_pairs={{0,2},{1,3},{2,0},{3,1},{4,6},{5,7},{6,4},{7,5},{8,10},{9,11},{10,... | collective-permute-start | bytes 1769480 | tf_op jit(solution)/shard_map/ppermute | solution.py:1027
  306.3 4.0 %copy-start.6 = (bf16[16,64,512]{2,1,0:T(8,128)(2,1)S(1)}, bf16[16,64,512]{2,1,0:T(8,128)(2,1)}, u32[]{:S(2)}) copy-start(bf16[16,64,512]{2,1,0:T(8,128)(2,1)} %get-tuple-element.137) | copy-start | bytes 3145732
  307.4 2.9 collective-permute-start.16
  310.6 14.1 %collective-permute-start.17 = (bf16[8,64,512]{2,1,0:T(8,128)(2,1)S(1)}, bf16[8,64,512]{2,1,0:T(8,128)(2,1)S(1)}, u32[]{:S(2)}, u32[]{:S(2)}) collective-permute-start(bf16[8,64,512]{2,1,0:T(8,128)(2,1)S(1)} %get-tuple-element.179), channel_id=1, source_target_pairs={{0,1},{1,0},{2,3},{3,2},{4,5},{5,4},{6,7},{7,6},{8,9},{9,8},{10,11... | collective-permute-start | bytes 1572872 | tf_op jit(solution)/shard_map/ppermute | solution.py:1027
  310.7 21.3 %all-to-all-start.5 = ((bf16[4,1,4,64,512]{4,3,2,1,0:T(8,128)(2,1)}), bf16[4,1,4,64,512]{4,3,2,1,0:T(8,128)(2,1)S(1)}, u32[]{:S(2)}, u32[]{:S(2)}) async-start(bf16[4,1,4,64,512]{4,3,2,1,0:T(8,128)(2,1)} %get-tuple-element.149), calls=%async_computation.5 | async-start | bytes 2097152 | tf_op jit(solution)/shard_map/all_to_all | solution.py:1195
  320.5 6.5 %copy-start.8 = (bf16[2,144,512]{2,1,0:T(8,128)(2,1)S(1)}, bf16[2,144,512]{2,1,0:T(8,128)(2,1)}, u32[]{:S(2)}) copy-start(bf16[2,144,512]{2,1,0:T(8,128)(2,1)} %get-tuple-element.180) | copy-start | bytes 884740
  325.5 13.4 %collective-permute-start.18 = (bf16[4,64,512]{2,1,0:T(8,128)(2,1)}, bf16[4,64,512]{2,1,0:T(8,128)(2,1)S(1)}, u32[]{:S(2)}, u32[]{:S(2)}) collective-permute-start(bf16[4,64,512]{2,1,0:T(8,128)(2,1)} %get-tuple-element.146), channel_id=1, source_target_pairs={{0,2},{1,3},{2,0},{3,1},{4,6},{5,7},{6,4},{7,5},{8,10},{9,11},{10,... | collective-permute-start | bytes 786440 | tf_op jit(solution)/shard_map/ppermute | solution.py:1027
  327.0 20.7 %collective-permute-start.21 = (bf16[2,144,512]{2,1,0:T(8,128)(2,1)S(1)}, bf16[2,144,512]{2,1,0:T(8,128)(2,1)S(1)}, u32[]{:S(2)}, u32[]{:S(2)}) collective-permute-start(bf16[2,144,512]{2,1,0:T(8,128)(2,1)S(1)} %copy-done.8), channel_id=1, source_target_pairs={{0,4},{1,5},{2,6},{3,7},{4,0},{5,1},{6,2},{7,3},{8,12},{9,13},{10,... | collective-permute-start | bytes 884744 | tf_op jit(solution)/shard_map/ppermute | solution.py:1027
  332.0 3.3 copy-start.2
  335.3 12.4 %copy-start.4 = (f32[2,144,512]{2,1,0:T(8,128)S(1)}, f32[2,144,512]{2,1,0:T(8,128)}, u32[]{:S(2)}) copy-start(f32[2,144,512]{2,1,0:T(8,128)} %get-tuple-element.181) | copy-start | bytes 1769476
  339.0 11.2 %collective-permute-start.19 = (bf16[2,64,512]{2,1,0:T(8,128)(2,1)S(1)}, bf16[2,64,512]{2,1,0:T(8,128)(2,1)S(1)}, u32[]{:S(2)}, u32[]{:S(2)}) collective-permute-start(bf16[2,64,512]{2,1,0:T(8,128)(2,1)S(1)} %get-tuple-element.151), channel_id=1, source_target_pairs={{0,4},{1,5},{2,6},{3,7},{4,0},{5,1},{6,2},{7,3},{8,12},{9,13},{10,... | collective-permute-start | bytes 393224 | tf_op jit(solution)/shard_map/ppermute | solution.py:1027
  347.7 5.2 %collective-permute-start.22 = (bf16[1,144,512]{2,1,0:T(8,128)(2,1)S(1)}, bf16[1,144,512]{2,1,0:T(8,128)(2,1)S(1)}, u32[]{:S(2)}, u32[]{:S(2)}) collective-permute-start(bf16[1,144,512]{2,1,0:T(8,128)(2,1)S(1)} %fusion.1), channel_id=1, source_target_pairs={{0,16},{8,24},{16,0},{24,8},{1,17},{9,25},{17,1},{25,9},{2,18},{10... | collective-permute-start | bytes 442376 | tf_op jit(solution)/shard_map/ppermute | solution.py:1027
  350.9 4.3 %collective-permute-start.20 = (bf16[1,64,512]{2,1,0:T(8,128)(2,1)S(1)}, bf16[1,64,512]{2,1,0:T(8,128)(2,1)S(1)}, u32[]{:S(2)}, u32[]{:S(2)}) collective-permute-start(bf16[1,64,512]{2,1,0:T(8,128)(2,1)S(1)} %get-tuple-element.186), channel_id=1, source_target_pairs={{0,16},{8,24},{16,0},{24,8},{1,17},{9,25},{17,1},{25,9},{2,18},{10... | collective-permute-start | bytes 196616 | tf_op jit(solution)/shard_map/ppermute | solution.py:1027
  355.1 0.6 copy-start.9
Sparse Core Ops, SparseCore 0:
  10.9 75.0 all-gather.1

commit v5 on v4

--- a/solution.py
+++ b/solution.py
@@ -13,6 +13,7 @@
 LONGEST = 48
 CHUNK = 2 * STRETCH
 TILE = 4 * CHUNK
+STATE_TILE = 8 * CHUNK
 PAIRS = HEADS // 2
 PAIR = 2 * HEAD_DIM
 MODEL = HEADS * HEAD_DIM
@@ -136,7 +137,7 @@
 
 
 def states_spec(tiles, reverse=False):
-    block = (TILE // CHUNK, MODEL, 3 * PAIR)
+    block = (TILE // CHUNK, 3 * HEAD_DIM, MODEL)
     if reverse:
         return pl.BlockSpec(block, lambda i, t, *_: (i * tiles + tiles - 1 - t, 0, 0))
     return pl.BlockSpec(block, lambda i, t, *_: (i * tiles + t, 0, 0))
@@ -166,7 +167,7 @@
 def state_kernel(placing, closing, rows, weight, vec, state_out, x_scr, acc, sums):
     gain, shift, bias = vector(vec, GAIN_ONE), vector(vec, SHIFT_ONE), vector(vec, BIAS_QKV)
     micro, step = pl.program_id(0), pl.program_id(1)
-    per = TILE // STRETCH
+    per = STATE_TILE // STRETCH
 
     @pl.when(step == 0)
     def _():
@@ -199,7 +200,7 @@
 def run_state(placing, closing, rows, weight, vec):
     micro, count = placing.shape
     width = rows.shape[-1]
-    tiles = count * STRETCH // TILE
+    tiles = count * STRETCH // STATE_TILE
     return pl.pallas_call(
         state_kernel,
         name="end_state",
@@ -213,7 +214,7 @@
             ],
             out_specs=member_spec(),
             scratch_shapes=[
-                pltpu.VMEM((TILE, width), bf16),
+                pltpu.VMEM((STATE_TILE, width), bf16),
                 pltpu.VMEM((PAIRS, PAIR, PAIR), f32),
                 pltpu.VMEM((1, MODEL), f32),
             ],
@@ -317,6 +318,7 @@
     upper = sublanes(CHUNK, PAIR) < STRETCH
     inner = lanes(PAIR, PAIR) % HEAD_DIM
     zero_s = jnp.zeros((PAIR, PAIR), bf16)
+    low_half = first_head(HEAD_DIM)
     for i in range(per):
         x_scr[i * STRETCH : (i + 1) * STRETCH, :] = pick(rows_ref, placing[micro, step * per + i])
         cot_scr[i * STRETCH : (i + 1) * STRETCH, :] = pick(cot_ref, placing[micro, step * per + i])
@@ -344,16 +346,13 @@
             state = carry[pair] * (1.0 - r0)
             state_b = state.astype(bf16)
             state_low = (state - state_b.astype(f32)).astype(bf16)
-            states_out[chunk, pair * PAIR : (pair + 1) * PAIR, :] = jnp.concatenate(
-                [
-                    state_b[:, :PAIR],
-                    jnp.where(
-                        inner < 2, state_b[:, PAIR:], jnp.where(inner == 2, state_low[:, PAIR:], zero_s)
-                    ),
-                    state_low[:, :PAIR],
-                ],
-                axis=1,
+            marked = jnp.where(
+                inner < 2, state_b[:, PAIR:], jnp.where(inner == 2, state_low[:, PAIR:], zero_s)
             )
+            for n_, item in enumerate((state_b[:, :PAIR], marked, state_low[:, :PAIR])):
+                states_out[chunk, n_ * HEAD_DIM : (n_ + 1) * HEAD_DIM, col(pair)] = jnp.where(
+                    low_half, item[:HEAD_DIM], item[HEAD_DIM:]
+                )
             mixing = nt(q, by_head(k, CHUNK)) * mask
             values = jnp.concatenate([by_head(v, CHUNK), ones_both], axis=1)
             out = nn(mixing.astype(bf16), values)
@@ -502,7 +501,7 @@
         jax.ShapeDtypeStruct((total, width), bf16),
         jax.ShapeDtypeStruct((total, MODEL), bf16),
         jax.ShapeDtypeStruct((total, MODEL), bf16),
-        jax.ShapeDtypeStruct((total // CHUNK, MODEL, 3 * PAIR), bf16),
+        jax.ShapeDtypeStruct((total // CHUNK, 3 * HEAD_DIM, MODEL), bf16),
         jax.ShapeDtypeStruct((members, HEAD_DIM + 8, MODEL), f32),
         jax.ShapeDtypeStruct((8, ff), f32),
     ]
@@ -568,7 +567,7 @@
     gd_ref,
     branch_ref,
     states_ref,
-    weight,
+    weight_far,
     vec,
     owner_col,
     *refs,
@@ -589,10 +588,9 @@
         keep_out, send_out, acc = refs[:3]
         refs = refs[3:]
     else:
-        acc = refs[0]
-        refs = refs[1:]
-    carry, x_scr, mixed_scr = refs[:3]
-    sems = refs[3] if resumes else None
+        far_acc, acc = refs[:2]
+        refs = refs[2:]
+    carry, x_scr, mixed_scr, weight, sems = refs
     member, step = pl.program_id(0), pl.program_id(1)
     micro = first + member
     per = TILE // STRETCH
@@ -601,12 +599,18 @@
     lane = lanes(CHUNK, PAIR)
     inner = lane % HEAD_DIM
 
+    closing = (member == pl.num_programs(0) - 1) & (step == pl.num_programs(1) - 1)
+    arriving = [pltpu.make_async_copy(weight_far, weight, sems.at[0])]
+    if resumes:
+        arriving.append(pltpu.make_async_copy(before[0], acc, sems.at[1]))
+    leaving = [] if final else [pltpu.make_async_copy(acc, far_acc, sems.at[2])]
+
     @pl.when(opening)
     def _():
         vec_out[...] = jnp.zeros_like(vec_out)
-        if resumes:
-            pltpu.make_async_copy(before[0], acc, sems.at[0]).start()
-        else:
+        for copy in arriving:
+            copy.start()
+        if not resumes:
             acc[...] = jnp.zeros_like(acc)
 
     @pl.when(step == 0)
@@ -643,7 +647,10 @@
             v = qkv_ref[rows, 2 * MODEL + pair * PAIR : 2 * MODEL + (pair + 1) * PAIR]
             gn = gn_ref[rows, col(pair)]
             gdx = gd_ref[rows, col(pair)]
-            state = states_ref[chunk, pair * PAIR : (pair + 1) * PAIR, :]
+            state, state_z, state_low = (
+                by_head(states_ref[chunk, n * HEAD_DIM : (n + 1) * HEAD_DIM, col(pair)], HEAD_DIM)
+                for n in range(3)
+            )
             grown = carry[pair] * (1.0 - r2)
             grown_b = grown.astype(bf16)
             rest = grown - grown_b.astype(f32)
@@ -661,7 +668,9 @@
             g_mix = (nt(both, jnp.concatenate([v2, marks_both], axis=1)) * mask).astype(bf16)
             v_marks = jnp.concatenate([v, marks], axis=1)
             g_mix_t = (nt(v_marks, jnp.concatenate([gn2, gd2], axis=1)) * mask_t).astype(bf16)
-            dq = nn(g_mix, k2) + (nt(both, state[:, : 2 * PAIR]) + nt(gn, state[:, 2 * PAIR :])) * keep_low
+            dq = nn(g_mix, k2) + (
+                nt(both, jnp.concatenate([state, state_z], axis=1)) + nt(gn, state_low)
+            ) * keep_low
             dk = nn(g_mix_t, q2) + (nt(v_marks, grown_x) + nt(v, grown_low)) * keep_key
             dv = nn(mixing_t, gn2) + nn(k, grown_b[:, :PAIR]) * keep_key
             q_keep = (q.astype(f32) * keep_low).astype(bf16)
@@ -675,27 +684,34 @@
             ).astype(bf16)
             mixed_scr[rows, 2 * MODEL + pair * PAIR : 2 * MODEL + (pair + 1) * PAIR] = dv.astype(bf16)
 
+    @pl.when(opening)
+    def _():
+        for copy in arriving:
+            copy.wait()
+
     mixed = mixed_scr[...]
     vec_out[0:1, :] += jnp.sum(mixed.astype(f32), axis=0, keepdims=True)
     upstream = nt(mixed, weight[...])
     n, scale = standardize(x_scr[...].astype(f32))
     normed_t = (n * gain + shift).astype(bf16).T
-    if resumes:
-
-        @pl.when(opening)
-        def _():
-            pltpu.make_async_copy(before[0], acc, sems.at[0]).wait()
-
     for part in range(3):
         at = slice(part * MODEL, (part + 1) * MODEL)
         acc[:, at] += nn(normed_t, mixed[:, at])
+    start_all(closing, leaving)
     vec_out[1:2, :MODEL] += jnp.sum(upstream * n, axis=0, keepdims=True)
     vec_out[1:2, MODEL : 2 * MODEL] += jnp.sum(upstream, axis=0, keepdims=True)
     total = (branch_ref[...].astype(f32) + norm_back(upstream, gain, n, scale)).astype(bf16)
     for i in range(per):
         put(grad_rows, placing[micro, tile * per + i], total[i * STRETCH : (i + 1) * STRETCH, :])
 
-    if final:
+    if not final:
+
+        @pl.when(closing)
+        def _():
+            for copy in leaving:
+                copy.wait()
+
+    else:
 
         @pl.when((member == pl.num_programs(0) - 1) & (step == pl.num_programs(1) - 1))
         def _():
@@ -724,7 +740,7 @@
                 mid[0:1, :],
                 mid[1:2, 3 * MODEL : 4 * MODEL],
             )
-            rows16 = sublanes(16, MODEL)
+            rows8 = sublanes(8, MODEL)
             pieces = []
             for source, width in zip(sources, widths, strict=True):
                 size = devices * width
@@ -736,14 +752,16 @@
                 high = picked.astype(bf16)
                 low = (picked - high.astype(f32)).astype(bf16)
                 pieces.append(nn(high, gather) + nn(low, gather))
-            rest = jnp.zeros((1, MODEL - PAIR), f32)
+            rest = jnp.zeros((1, MODEL - 2 * PAIR), f32)
+            blank_row = jnp.zeros((1, PAIR), f32)
             for j in range(devices):
-                block16 = jnp.zeros((16, MODEL), f32)
-                for v, piece in enumerate(pieces):
-                    row = jnp.concatenate([piece[j : j + 1, :], rest], axis=1)
-                    block16 = block16 + jnp.where(rows16 == v, row, 0.0)
+                block8 = jnp.zeros((8, MODEL), f32)
+                for v, piece in enumerate(pieces[:8]):
+                    more = pieces[8 + v][j : j + 1, :] if 8 + v < len(pieces) else blank_row
+                    row = jnp.concatenate([piece[j : j + 1, :], more, rest], axis=1)
+                    block8 = block8 + jnp.where(rows8 == v, row, 0.0)
                 target = keep_out if j < half else send_out
-                target[j % half, 3 * less :, :] = block16.astype(target.dtype)
+                target[j % half, 3 * less :, :] = block8.astype(target.dtype)
 
 
 def run_back(tables, first, members, target, rows, mid, incs, weight, vec, before, owner, others, widths):
@@ -757,7 +775,7 @@
     if not final:
         owner = jnp.zeros((8,), jnp.int32)
         others = []
-    half = (devices // 2, 3 * MODEL // max(devices, 1) + 16, MODEL)
+    half = (devices // 2, 3 * MODEL // max(devices, 1) + 8, MODEL)
     out_specs = [group_spec(group.shape, seat), fixed((8, 3 * MODEL))]
     out_shape = [
         jax.ShapeDtypeStruct(group.shape, bf16),
@@ -767,17 +785,17 @@
     if final:
         out_specs += [fixed(half), fixed(half)]
         out_shape += [jax.ShapeDtypeStruct(half, bf16)] * 2
-        scratch.append(pltpu.VMEM((width, 3 * MODEL), f32))
     else:
-        out_specs.append(fixed((width, 3 * MODEL)))
+        out_specs.append(ANYWHERE)
         out_shape.append(jax.ShapeDtypeStruct((width, 3 * MODEL), f32))
     scratch += [
+        pltpu.VMEM((width, 3 * MODEL), f32),
         pltpu.VMEM((PAIRS, PAIR, 2 * PAIR), f32),
         pltpu.VMEM((TILE, width), bf16),
         pltpu.VMEM((TILE, 3 * MODEL), bf16),
+        pltpu.VMEM(weight.shape, bf16),
+        pltpu.SemaphoreType.DMA((3,)),
     ]
-    if resumes:
-        scratch.append(pltpu.SemaphoreType.DMA((1,)))
 
     def tile(width_):
         return pl.BlockSpec((TILE, width_), lambda i, t, *_: ((at + i) * tiles + tiles - 1 - t, 0))
@@ -804,10 +822,10 @@
                 tile(MODEL),
                 tile(width),
                 pl.BlockSpec(
-                    (TILE // CHUNK, MODEL, 3 * PAIR),
+                    (TILE // CHUNK, 3 * HEAD_DIM, MODEL),
                     lambda i, t, *_: ((at + i) * tiles + tiles - 1 - t, 0, 0),
                 ),
-                fixed(weight.shape),
+                ANYWHERE,
                 fixed(vec.shape),
                 fixed((owner.shape[0], 1)),
             ]
@@ -1057,11 +1075,12 @@
     for part in range(3):
         qkv[:, part * MODEL : (part + 1) * MODEL] = total[part * rows : (part + 1) * rows, :]
     for v, ref in enumerate(vectors):
-        ref[...] = total[3 * rows + v : 3 * rows + v + 1, : ref.shape[1]]
+        row, at = 3 * rows + v % 8, v // 8 * PAIR
+        ref[...] = total[row : row + 1, at : at + ref.shape[1]]
 
 
 def run_finish(keep, got, widths):
-    rows = (keep.shape[1] - 16) // 3
+    rows = (keep.shape[1] - 8) // 3
     return pl.pallas_call(
         finish_kernel,
         name="finish",
@@ -1352,7 +1371,7 @@
             if step == 0:
                 result = land(result, homes, send)
             if step == 1:
-                send = after(send, result)
+                send = after(send, result, *(() if got is None else (got,)))
                 input_grad = land(input_grad, grad_homes, send)
             if step == 2:
                 send = after(send, input_grad)

time: 370 us -> 368 us (level)
  transfers between devices with their start and end apart: 30 -> 30, of which waited for: 14 -> 12; matrix products, arithmetic and copies ran while one was open for 6% -> 6% of each run, Pallas kernels for 34% -> 33%
where the time goes in v5:
time: 368 us; the launch traced here: 362 us
  Pallas kernels  193 us (52%)
  starting transfers between devices  69.7 us (19%)
  waiting for transfers between devices  59.9 us (16%)
  other arithmetic  18.1 us (5%)
  between operations  15 us (4%)
  local copies, waits for them, and re-layouts  6.06 us (2%)
    pallas_call x2, Pallas kernels, run_mid(): pl.pallas_call(functools.partial(mid_kernel, first=first, resumes=resumes...  95.4 us
    pallas_call x2, Pallas kernels, run_back(): pl.pallas_call(functools.partial(back_kernel, first=first, resumes=resume...  52 us
    ppermute x15, waiting for transfers between devices, swap(): lax.ppermute(x, axis, [(i, i ^ bit) for i in range(lax.axis_size(axis))])  39.7 us
    ppermute x15, starting transfers between devices, swap(): lax.ppermute(x, axis, [(i, i ^ bit) for i in range(lax.axis_size(axis))])  29.5 us
    all_to_all x6, starting transfers between devices, to_dp(): return lax.all_to_all(group, 'dp', split_axis=0, concat_axis=0, tiled=True)  23.7 us
    ppermute x2, waiting for transfers between devices, passed_on(): got = lax.ppermute(own, 'fsdp', [(i, i + step) for i in range(size - step)])  14 us
    pallas_call x4, Pallas kernels, run_land(): pl.pallas_call(functools.partial(land_kernel, first=first), name='land',...  12.7 us
    pallas_call x1, Pallas kernels, run_state(): pl.pallas_call(state_kernel, name='end_state', grid_spec=pltpu.PrefetchSc...  10.7 us
  transfers between devices with their start and end apart: 30, of which 12 were waited for; matrix products, arithmetic and copies ran while one was open for 6% of the time, Pallas kernels for 33%

profile of v5, /device:TPU:0, one launch (start us, length us, event | category | flops | bytes accessed | tf_op | source)
XLA Modules:
  0.0 361.7 jit_solution(2126614543591278)
XLA Ops:
  7.2 1.8 pack.1
  9.0 3.0 collective-permute-start
  13.8 5.3 %send.2 = bf16[4,3,4,64,512]{4,3,2,1,0:T(8,128)(2,1)} custom-call(s32[3,16]{1,0:T(4,128)} %convert_reduce_fusion.1.slot, bf16[3,16,64,512]{3,2,1,0:T(8,128)(2,1)} %bitcast.35), custom_call_target="tpu_custom_call" | custom-call | bytes 6291456 | tf_op jit(solution)/shard_map/send/pallas_call | solution.py:876
  22.0 2.7 collective-permute-start.1
  24.7 3.7 %all-to-all-start = ((bf16[4,3,4,64,512]{4,3,2,1,0:T(8,128)(2,1)}), bf16[4,3,4,64,512]{4,3,2,1,0:T(8,128)(2,1)S(1)}, u32[]{:S(2)}, u32[]{:S(2)}) async-start(bf16[4,3,4,64,512]{4,3,2,1,0:T(8,128)(2,1)} %send.2), calls=%async_computation | async-start | bytes 6291456 | tf_op jit(solution)/shard_map/all_to_all | solution.py:1214
  28.9 4.2 %collective-permute-done.1 = bf16[2,64,512]{2,1,0:T(8,128)(2,1)S(1)} collective-permute-done((bf16[2,64,512]{2,1,0:T(8,128)(2,1)S(1)}, bf16[2,64,512]{2,1,0:T(8,128)(2,1)S(1)}, u32[]{:S(2)}, u32[]{:S(2)}) %collective-permute-start.1) | collective-permute-done | bytes 131104 | tf_op jit(solution)/shard_map/ppermute | solution.py:1045
  33.2 7.4 %collective-permute-done.2 = bf16[4,64,512]{2,1,0:T(8,128)(2,1)S(1)} collective-permute-done((bf16[4,64,512]{2,1,0:T(8,128)(2,1)S(1)}, bf16[4,64,512]{2,1,0:T(8,128)(2,1)S(1)}, u32[]{:S(2)}, u32[]{:S(2)}) %collective-permute-start.2) | collective-permute-done | bytes 262176 | tf_op jit(solution)/shard_map/ppermute | solution.py:1045
  40.7 1.7 collective-permute-start.3
  42.4 12.4 %collective-permute-done.3 = bf16[8,64,512]{2,1,0:T(8,128)(2,1)S(1)} collective-permute-done((bf16[8,64,512]{2,1,0:T(8,128)(2,1)S(1)}, bf16[8,64,512]{2,1,0:T(8,128)(2,1)S(1)}, u32[]{:S(2)}, u32[]{:S(2)}) %collective-permute-start.3) | collective-permute-done | bytes 524320 | tf_op jit(solution)/shard_map/ppermute | solution.py:1045
  57.0 1.6 collective-permute-done.4.got
  58.6 3.5 sort_first.1
  62.1 5.3 %send.3 = bf16[4,3,4,64,512]{4,3,2,1,0:T(8,128)(2,1)} custom-call(s32[3,16]{1,0:T(4,128)} %convert_reduce_fusion.1.slot, bf16[3,16,64,512]{3,2,1,0:T(8,128)(2,1)} %bitcast.36), custom_call_target="tpu_custom_call" | custom-call | bytes 6291456 | tf_op jit(solution)/shard_map/send/pallas_call | solution.py:876
  67.4 6.2 %all-to-all-done.rows.rows_ref = bf16[4,3,4,64,512]{4,3,2,1,0:T(8,128)(2,1)S(1)} async-done(((bf16[4,3,4,64,512]{4,3,2,1,0:T(8,128)(2,1)}), bf16[4,3,4,64,512]{4,3,2,1,0:T(8,128)(2,1)S(1)}, u32[]{:S(2)}, u32[]{:S(2)}) %all-to-all-start) | async-done | bytes 3145760 | tf_op jit(solution)/shard_map/all_to_all | solution.py:1214
  73.5 1.7 copy-done.3
  75.2 4.7 %all-to-all-start.1 = ((bf16[4,3,4,64,512]{4,3,2,1,0:T(8,128)(2,1)}), bf16[4,3,4,64,512]{4,3,2,1,0:T(8,128)(2,1)}, u32[]{:S(2)}, u32[]{:S(2)}) async-start(bf16[4,3,4,64,512]{4,3,2,1,0:T(8,128)(2,1)} %send.3), calls=%async_computation.1 | async-start | bytes 6291456 | tf_op jit(solution)/shard_map/all_to_all | solution.py:1214
  79.9 10.7 %end_state.1 = f32[3,72,512]{2,1,0:T(8,128)} custom-call(s32[3,16]{1,0:T(4,128)} %get-tuple-element.200.placing, s32[3,16]{1,0:T(4,128)} %get-tuple-element.199.closing, bf16[4,3,4,64,512]{4,3,2,1,0:T(8,128)(2,1)} %copy-done.3, bf16[512,1536]{1,0:T(8,128)(2,1)} %get-tuple-element.93.weight.w_qkv.weight_far, f32[8,2048]{1,0:T(8,128)} %get-tuple-element.95.vec), custom_call_target="tpu_custom_call" | custom-call | flops 11811160064 | bytes 5242880 | tf_op jit(solution)/shard_map/end_state/pallas_call | solution.py:204
  90.5 3.5 collective-permute-start.5
  94.2 4.7 %sort_second.1 = (bf16[512,2048]{1,0:T(8,128)(2,1)}, bf16[2048,512]{1,0:T(8,128)(2,1)}, bf16[512,512]{1,0:T(8,128)(2,1)}) custom-call(bf16[32,144,512]{2,1,0:T(8,128)(2,1)} %all-gather.2.cloned.1.call-done.gathered), custom_call_target="tpu_custom_call" | custom-call | tf_op jit(solution)/shard_map/sort_second/pallas_call | solution.py:1191
  98.9 5.5 %collective-permute-done.5 = f32[3,72,512]{2,1,0:T(8,128)S(1)} collective-permute-done((f32[3,72,512]{2,1,0:T(8,128)}, f32[3,72,512]{2,1,0:T(8,128)S(1)}, u32[]{:S(2)}, u32[]{:S(2)}) %collective-permute-start.5) | collective-permute-done | bytes 442400 | tf_op jit(solution)/shard_map/ppermute | solution.py:999
  104.5 5.3 %collective-permute-start.6 = (f32[3,72,512]{2,1,0:T(8,128)S(1)}, f32[3,72,512]{2,1,0:T(8,128)S(1)}, u32[]{:S(2)}, u32[]{:S(2)}) collective-permute-start(f32[3,72,512]{2,1,0:T(8,128)S(1)} %multiply_add_fusion.1), channel_id=1, source_target_pairs={{0,2},{1,3},{2,4},{3,5},{4,6},{5,7},{8,10},{9,11},{10,12},{11,13},... | collective-permute-start | bytes 1327112 | tf_op jit(solution)/shard_map/ppermute | solution.py:999
  110.5 8.5 %collective-permute-done.6 = f32[3,72,512]{2,1,0:T(8,128)S(1)} collective-permute-done((f32[3,72,512]{2,1,0:T(8,128)S(1)}, f32[3,72,512]{2,1,0:T(8,128)S(1)}, u32[]{:S(2)}, u32[]{:S(2)}) %collective-permute-start.6) | collective-permute-done | bytes 442400 | tf_op jit(solution)/shard_map/ppermute | solution.py:999
  120.5 58.9 %middle.2 = (bf16[4,2,4,64,512]{4,3,2,1,0:T(8,128)(2,1)}, bf16[2048,1536]{1,0:T(8,128)(2,1)}, bf16[2048,512]{1,0:T(8,128)(2,1)}, bf16[2048,512]{1,0:T(8,128)(2,1...) custom-call(s32[3,16]{1,0:T(4,128)} %get-tuple-element.200.placing, ...), custom_call_target="tpu_custom_call", output_to_operand_aliasing={{0}: (4, {})} | custom-call | flops 51539607552 | bytes 33554432 | tf_op jit(solution)/shard_map/middle/pallas_call | solution.py:532
  179.4 1.3 collective-permute-start.7
  183.3 3.6 %all-to-all-start.2 = ((bf16[4,2,4,64,512]{4,3,2,1,0:T(8,128)(2,1)}), bf16[4,2,4,64,512]{4,3,2,1,0:T(8,128)(2,1)S(1)}, u32[]{:S(2)}, u32[]{:S(2)}) async-start(bf16[4,2,4,64,512]{4,3,2,1,0:T(8,128)(2,1)} %get-tuple-element.102), calls=%async_computation.2 | async-start | bytes 4194304 | tf_op jit(solution)/shard_map/all_to_all | solution.py:1214
  186.9 36.5 %middle.3 = (bf16[4,1,4,64,512]{4,3,2,1,0:T(8,128)(2,1)}, bf16[1024,1536]{1,0:T(8,128)(2,1)}, bf16[1024,512]{1,0:T(8,128)(2,1)}, bf16[1024,512]{1,0:T(8,128)(2,1...) custom-call(s32[3,16]{1,0:T(4,128)} %get-tuple-element.200.placing, ...), custom_call_target="tpu_custom_call", output_to_operand_aliasing={{0}: (4, {})} | custom-call | flops 25769803776 | bytes 16777216 | tf_op jit(solution)/shard_map/middle/pallas_call | solution.py:532
  225.3 1.3 collective-permute-start.13
  226.6 1.3 collective-permute-start.14
  228.0 3.5 all-to-all-start.3
  231.5 4.1 %add_convert_fusion = (bf16[8,144,512]{2,1,0:T(8,128)(2,1)}, f32[8,144,512]{2,1,0:T(8,128)S(1)}) fusion(bf16[16,144,512]{2,1,0:T(8,128)(2,1)} %collective-permute-done.10, bf16[16,144,512]{2,1,0:T(8,128)(2,1)} %get-tuple-element.111), kind=kLoop, calls=%fused_computation | loop fusion | flops 4128768 | bytes 8257536 | tf_op jit(solution)/shard_map/convert_element_type | solution.py:1068
  235.6 3.3 collective-permute-start.11
  239.4 32.8 %back.2 = (bf16[4,2,4,64,512]{4,3,2,1,0:T(8,128)(2,1)}, f32[8,1536]{1,0:T(8,128)}, f32[512,1536]{1,0:T(8,128)}) custom-call(s32[3,16]{1,0:T(4,128)} %get-tuple-element.200.placing, s32[3,17]{1,0:T(4,128)} %convert_select_fusion.restart, f32[3,3]{1,0:T(4,128)} %convert_subtract_fusion.3.reach, ...), custom_call_target="tpu_custom_call", output_to_operand_aliasing={{0}: (4, {})} | custom-call | flops 32212254720 | bytes 33554432 | tf_op jit(solution)/shard_map/back/pallas_call | solution.py:803
  272.3 4.7 %all-to-all-start.4 = ((bf16[4,2,4,64,512]{4,3,2,1,0:T(8,128)(2,1)}), bf16[4,2,4,64,512]{4,3,2,1,0:T(8,128)(2,1)}, u32[]{:S(2)}, u32[]{:S(2)}) async-start(bf16[4,2,4,64,512]{4,3,2,1,0:T(8,128)(2,1)} %get-tuple-element.140), calls=%async_computation.4 | async-start | bytes 4194304 | tf_op jit(solution)/shard_map/all_to_all | solution.py:1214
  277.0 2.4 add_convert_fusion.1
  279.5 5.0 %collective-permute-start.15 = (bf16[4,144,512]{2,1,0:T(8,128)(2,1)}, bf16[4,144,512]{2,1,0:T(8,128)(2,1)S(1)}, u32[]{:S(2)}, u32[]{:S(2)}) collective-permute-start(bf16[4,144,512]{2,1,0:T(8,128)(2,1)} %get-tuple-element.142), channel_id=1, source_target_pairs={{0,2},{1,3},{2,0},{3,1},{4,6},{5,7},{6,4},{7,5},{8,10},{9,11},{10,... | collective-permute-start | bytes 1769480 | tf_op jit(solution)/shard_map/ppermute | solution.py:1045
  284.5 19.3 %back.3 = (bf16[4,1,4,64,512]{4,3,2,1,0:T(8,128)(2,1)}, f32[8,1536]{1,0:T(8,128)}, bf16[16,56,512]{2,1,0:T(8,128)(2,1)}, bf16[16,56,512]{2,1,0:T(8,128)(2,1)}) custom-call(s32[3,16]{1,0:T(4,128)} %get-tuple-element.200.placing, s32[3,17]{1,0:T(4,128)} %convert_select_fusion.restart, ...), custom_call_target="tpu_custom_call", output_to_operand_aliasing={{0}: (4, {})} | custom-call | flops 16106127360 | bytes 16777216 | tf_op jit(solution)/shard_map/back/pallas_call | solution.py:803
  305.1 2.5 collective-permute-done.16
  307.9 3.5 all-to-all-start.5
  311.4 5.8 %collective-permute-start.18 = (bf16[2,144,512]{2,1,0:T(8,128)(2,1)S(1)}, bf16[2,144,512]{2,1,0:T(8,128)(2,1)S(1)}, u32[]{:S(2)}, u32[]{:S(2)}) collective-permute-start(bf16[2,144,512]{2,1,0:T(8,128)(2,1)S(1)} %copy-done.8), channel_id=1, source_target_pairs={{0,4},{1,5},{2,6},{3,7},{4,0},{5,1},{6,2},{7,3},{8,12},{9,13},{10,... | collective-permute-start | bytes 884744 | tf_op jit(solution)/shard_map/ppermute | solution.py:1045
  317.3 3.3 land.4._
  320.6 2.9 land.5
  324.4 6.8 %collective-permute-done.18 = bf16[2,144,512]{2,1,0:T(8,128)(2,1)S(1)} collective-permute-done((bf16[2,144,512]{2,1,0:T(8,128)(2,1)S(1)}, bf16[2,144,512]{2,1,0:T(8,128)(2,1)S(1)}, u32[]{:S(2)}, u32[]{:S(2)}) %collective-permute-start.18) | collective-permute-done | bytes 294944 | tf_op jit(solution)/shard_map/ppermute | solution.py:1045
  331.9 3.3 land.6._
  335.2 3.1 land.7
  338.8 3.1 collective-permute-start.20
  341.9 1.7 collective-permute-start.22
  343.6 3.8 %collective-permute-done.20 = bf16[2,56,512]{2,1,0:T(8,128)(2,1)S(1)} collective-permute-done((bf16[2,56,512]{2,1,0:T(8,128)(2,1)S(1)}, bf16[2,56,512]{2,1,0:T(8,128)(2,1)S(1)}, u32[]{:S(2)}, u32[]{:S(2)}) %collective-permute-start.20) | collective-permute-done | bytes 114720 | tf_op jit(solution)/shard_map/ppermute | solution.py:1045
  348.0 1.6 collective-permute-start.21
  352.8 1.6 finish.1
  (115 shorter events, 22.5 us)
Async XLA Ops:
  7.2 87.0 %all-gather.2.cloned.1.call-start = ((), (), s32[]{:S(2)}) async-start(), calls=%async_computation.6 | async-start | bytes 4866048 | tf_op jit(solution)/shard_map/all_gather | solution.py:1206
  9.0 13.0 %collective-permute-start = (bf16[1,64,512]{2,1,0:T(8,128)(2,1)}, bf16[1,64,512]{2,1,0:T(8,128)(2,1)S(1)}, u32[]{:S(2)}, u32[]{:S(2)}) collective-permute-start(bf16[1,64,512]{2,1,0:T(8,128)(2,1)} %get-tuple-element.89), channel_id=1, source_target_pairs={{0,16},{8,24},{16,0},{24,8},{1,17},{9,25},{17,1},{25,9},{2,18},{10... | collective-permute-start | bytes 196616 | tf_op jit(solution)/shard_map/ppermute | solution.py:1045
  13.8 5.4 %copy-start.11 = (s32[3,16]{1,0:T(4,128)S(1)}, s32[3,16]{1,0:T(4,128)}, u32[]{:S(2)}) copy-start(s32[3,16]{1,0:T(4,128)} %param.18) | copy-start | bytes 580
  13.8 8.1 %copy-start.9 = (bf16[1,64,512]{2,1,0:T(8,128)(2,1)S(1)}, bf16[1,64,512]{2,1,0:T(8,128)(2,1)}, u32[]{:S(2)}) copy-start(bf16[1,64,512]{2,1,0:T(8,128)(2,1)} %get-tuple-element.89) | copy-start | bytes 196612
  22.0 11.1 %collective-permute-start.1 = (bf16[2,64,512]{2,1,0:T(8,128)(2,1)S(1)}, bf16[2,64,512]{2,1,0:T(8,128)(2,1)S(1)}, u32[]{:S(2)}, u32[]{:S(2)}) collective-permute-start(bf16[2,64,512]{2,1,0:T(8,128)(2,1)S(1)} %constant_dynamic-update-slice_fusion), channel_id=1, source_target_pairs={{0,4},{1,5},{2,6},{3,7},{4,0},{5,1},{6,2},{7,3},{8,12},{9,13},{10,... | collective-permute-start | bytes 393224 | tf_op jit(solution)/shard_map/ppermute | solution.py:1045
  24.7 48.9 %all-to-all-start = ((bf16[4,3,4,64,512]{4,3,2,1,0:T(8,128)(2,1)}), bf16[4,3,4,64,512]{4,3,2,1,0:T(8,128)(2,1)S(1)}, u32[]{:S(2)}, u32[]{:S(2)}) async-start(bf16[4,3,4,64,512]{4,3,2,1,0:T(8,128)(2,1)} %send.2), calls=%async_computation | async-start | bytes 6291456 | tf_op jit(solution)/shard_map/all_to_all | solution.py:1214
  33.1 7.5 %collective-permute-start.2 = (bf16[4,64,512]{2,1,0:T(8,128)(2,1)S(1)}, bf16[4,64,512]{2,1,0:T(8,128)(2,1)S(1)}, u32[]{:S(2)}, u32[]{:S(2)}) collective-permute-start(bf16[4,64,512]{2,1,0:T(8,128)(2,1)S(1)} %pad_maximum_fusion.1), channel_id=1, source_target_pairs={{0,2},{1,3},{2,0},{3,1},{4,6},{5,7},{6,4},{7,5},{8,10},{9,11},{10,... | collective-permute-start | bytes 786440 | tf_op jit(solution)/shard_map/ppermute | solution.py:1045
  40.7 14.1 %collective-permute-start.3 = (bf16[8,64,512]{2,1,0:T(8,128)(2,1)S(1)}, bf16[8,64,512]{2,1,0:T(8,128)(2,1)S(1)}, u32[]{:S(2)}, u32[]{:S(2)}) collective-permute-start(bf16[8,64,512]{2,1,0:T(8,128)(2,1)S(1)} %pad_maximum_fusion), channel_id=1, source_target_pairs={{0,1},{1,0},{2,3},{3,2},{4,5},{5,4},{6,7},{7,6},{8,9},{9,8},{10,11... | collective-permute-start | bytes 1572872 | tf_op jit(solution)/shard_map/ppermute | solution.py:1045
  54.8 1.0 copy-start.5
  55.8 2.8 collective-permute-start.4
  73.5 1.7 copy-start.3
  75.2 44.7 %all-to-all-start.1 = ((bf16[4,3,4,64,512]{4,3,2,1,0:T(8,128)(2,1)}), bf16[4,3,4,64,512]{4,3,2,1,0:T(8,128)(2,1)}, u32[]{:S(2)}, u32[]{:S(2)}) async-start(bf16[4,3,4,64,512]{4,3,2,1,0:T(8,128)(2,1)} %send.3), calls=%async_computation.1 | async-start | bytes 6291456 | tf_op jit(solution)/shard_map/all_to_all | solution.py:1214
  90.5 13.8 %collective-permute-start.5 = (f32[3,72,512]{2,1,0:T(8,128)}, f32[3,72,512]{2,1,0:T(8,128)S(1)}, u32[]{:S(2)}, u32[]{:S(2)}) collective-permute-start(f32[3,72,512]{2,1,0:T(8,128)} %end_state.1), channel_id=1, source_target_pairs={{0,1},{1,2},{2,3},{3,4},{4,5},{5,6},{6,7},{8,9},{9,10},{10,11},{11... | collective-permute-start | bytes 1327112 | tf_op jit(solution)/shard_map/ppermute | solution.py:999
  94.1 10.2 %copy-start.7 = (f32[3,72,512]{2,1,0:T(8,128)S(1)}, f32[3,72,512]{2,1,0:T(8,128)}, u32[]{:S(2)}) copy-start(f32[3,72,512]{2,1,0:T(8,128)} %end_state.1) | copy-start | bytes 1327108
  104.5 14.5 %collective-permute-start.6 = (f32[3,72,512]{2,1,0:T(8,128)S(1)}, f32[3,72,512]{2,1,0:T(8,128)S(1)}, u32[]{:S(2)}, u32[]{:S(2)}) collective-permute-start(f32[3,72,512]{2,1,0:T(8,128)S(1)} %multiply_add_fusion.1), channel_id=1, source_target_pairs={{0,2},{1,3},{2,4},{3,5},{4,6},{5,7},{8,10},{9,11},{10,12},{11,13},... | collective-permute-start | bytes 1327112 | tf_op jit(solution)/shard_map/ppermute | solution.py:999
  179.4 44.0 %collective-permute-start.7 = (f32[2,72,512]{2,1,0:T(8,128)}, f32[2,72,512]{2,1,0:T(8,128)S(1)}, u32[]{:S(2)}, u32[]{:S(2)}) collective-permute-start(f32[2,72,512]{2,1,0:T(8,128)} %get-tuple-element.113), channel_id=1, source_target_pairs={{1,0},{2,1},{3,2},{4,3},{5,4},{6,5},{7,6},{9,8},{10,9},{11,10},{12... | collective-permute-start | bytes 884744 | tf_op jit(solution)/shard_map/ppermute | solution.py:991
  180.7 42.7 %collective-permute-start.8 = (f32[2,72,512]{2,1,0:T(8,128)}, f32[2,72,512]{2,1,0:T(8,128)S(1)}, u32[]{:S(2)}, u32[]{:S(2)}) collective-permute-start(f32[2,72,512]{2,1,0:T(8,128)} %get-tuple-element.113), channel_id=1, source_target_pairs={{2,0},{3,1},{4,2},{5,3},{6,4},{7,5},{10,8},{11,9},{12,10},{13,11},... | collective-permute-start | bytes 884744 | tf_op jit(solution)/shard_map/ppermute | solution.py:991
  182.0 41.5 %collective-permute-start.9 = (f32[2,72,512]{2,1,0:T(8,128)}, f32[2,72,512]{2,1,0:T(8,128)S(1)}, u32[]{:S(2)}, u32[]{:S(2)}) collective-permute-start(f32[2,72,512]{2,1,0:T(8,128)} %get-tuple-element.113), channel_id=1, source_target_pairs={{3,0},{4,1},{5,2},{6,3},{7,4},{11,8},{12,9},{13,10},{14,11},{15,12... | collective-permute-start | bytes 884744 | tf_op jit(solution)/shard_map/ppermute | solution.py:991
  183.3 40.2 %all-to-all-start.2 = ((bf16[4,2,4,64,512]{4,3,2,1,0:T(8,128)(2,1)}), bf16[4,2,4,64,512]{4,3,2,1,0:T(8,128)(2,1)S(1)}, u32[]{:S(2)}, u32[]{:S(2)}) async-start(bf16[4,2,4,64,512]{4,3,2,1,0:T(8,128)(2,1)} %get-tuple-element.102), calls=%async_computation.2 | async-start | bytes 4194304 | tf_op jit(solution)/shard_map/all_to_all | solution.py:1214
  223.4 4.5 %copy-start.12 = (f32[2,72,512]{2,1,0:T(8,128)}, f32[2,72,512]{2,1,0:T(8,128)S(1)}, u32[]{:S(2)}) copy-start(f32[2,72,512]{2,1,0:T(8,128)S(1)} %collective-permute-done.7.refs_0_) | copy-start | bytes 884740
  223.5 4.5 %copy-start.13 = (f32[2,72,512]{2,1,0:T(8,128)}, f32[2,72,512]{2,1,0:T(8,128)S(1)}, u32[]{:S(2)}) copy-start(f32[2,72,512]{2,1,0:T(8,128)S(1)} %collective-permute-done.8.refs_1_) | copy-start | bytes 884740
  223.5 4.5 %copy-start.14 = (f32[2,72,512]{2,1,0:T(8,128)}, f32[2,72,512]{2,1,0:T(8,128)S(1)}, u32[]{:S(2)}) copy-start(f32[2,72,512]{2,1,0:T(8,128)S(1)} %collective-permute-done.9.refs_2_) | copy-start | bytes 884740
  223.5 4.4 %copy-start = (bf16[4,2,4,64,512]{4,3,2,1,0:T(8,128)(2,1)}, bf16[4,2,4,64,512]{4,3,2,1,0:T(8,128)(2,1)S(1)}, u32[]{:S(2)}) copy-start(bf16[4,2,4,64,512]{4,3,2,1,0:T(8,128)(2,1)S(1)} %all-to-all-done.2.source) | copy-start | bytes 6291460
  223.5 8.0 %collective-permute-start.10 = (bf16[16,144,512]{2,1,0:T(8,128)(2,1)}, bf16[16,144,512]{2,1,0:T(8,128)(2,1)}, u32[]{:S(2)}, u32[]{:S(2)}) collective-permute-start(bf16[16,144,512]{2,1,0:T(8,128)(2,1)} %get-tuple-element.118), channel_id=1, source_target_pairs={{0,8},{8,0},{16,24},{24,16},{1,9},{9,1},{17,25},{25,17},{2,10},{10... | collective-permute-start | bytes 7077896 | tf_op jit(solution)/shard_map/ppermute | solution.py:1045
  224.0 48.2 %collective-permute-start.12 = (f32[1,72,512]{2,1,0:T(8,128)}, f32[1,72,512]{2,1,0:T(8,128)S(1)}, u32[]{:S(2)}, u32[]{:S(2)}) collective-permute-start(f32[1,72,512]{2,1,0:T(8,128)} %get-tuple-element.130), channel_id=1, source_target_pairs={{1,0},{2,1},{3,2},{4,3},{5,4},{6,5},{7,6},{9,8},{10,9},{11,10},{12... | collective-permute-start | bytes 442376 | tf_op jit(solution)/shard_map/ppermute | solution.py:991
  225.3 46.9 %collective-permute-start.13 = (f32[1,72,512]{2,1,0:T(8,128)}, f32[1,72,512]{2,1,0:T(8,128)}, u32[]{:S(2)}, u32[]{:S(2)}) collective-permute-start(f32[1,72,512]{2,1,0:T(8,128)} %get-tuple-element.130), channel_id=1, source_target_pairs={{2,0},{3,1},{4,2},{5,3},{6,4},{7,5},{10,8},{11,9},{12,10},{13,11},... | collective-permute-start | bytes 442376 | tf_op jit(solution)/shard_map/ppermute | solution.py:991
  226.6 45.6 %collective-permute-start.14 = (f32[1,72,512]{2,1,0:T(8,128)}, f32[1,72,512]{2,1,0:T(8,128)}, u32[]{:S(2)}, u32[]{:S(2)}) collective-permute-start(f32[1,72,512]{2,1,0:T(8,128)} %get-tuple-element.130), channel_id=1, source_target_pairs={{3,0},{4,1},{5,2},{6,3},{7,4},{11,8},{12,9},{13,10},{14,11},{15,12... | collective-permute-start | bytes 442376 | tf_op jit(solution)/shard_map/ppermute | solution.py:991
  228.0 44.3 %all-to-all-start.3 = ((bf16[4,1,4,64,512]{4,3,2,1,0:T(8,128)(2,1)}), bf16[4,1,4,64,512]{4,3,2,1,0:T(8,128)(2,1)S(1)}, u32[]{:S(2)}, u32[]{:S(2)}) async-start(bf16[4,1,4,64,512]{4,3,2,1,0:T(8,128)(2,1)} %get-tuple-element.131), calls=%async_computation.3 | async-start | bytes 2097152 | tf_op jit(solution)/shard_map/all_to_all | solution.py:1214
  235.6 41.4 %collective-permute-start.11 = (bf16[8,144,512]{2,1,0:T(8,128)(2,1)}, bf16[8,144,512]{2,1,0:T(8,128)(2,1)}, u32[]{:S(2)}, u32[]{:S(2)}) collective-permute-start(bf16[8,144,512]{2,1,0:T(8,128)(2,1)} %get-tuple-element.120), channel_id=1, source_target_pairs={{0,1},{1,0},{2,3},{3,2},{4,5},{5,4},{6,7},{7,6},{8,9},{9,8},{10,11... | collective-permute-start | bytes 3538952 | tf_op jit(solution)/shard_map/ppermute | solution.py:1045
  272.2 4.8 %copy-start.15 = (f32[1,72,512]{2,1,0:T(8,128)}, f32[1,72,512]{2,1,0:T(8,128)S(1)}, u32[]{:S(2)}) copy-start(f32[1,72,512]{2,1,0:T(8,128)S(1)} %collective-permute-done.12.refs_0_) | copy-start | bytes 442372
  272.3 4.7 %copy-start.1 = (bf16[4,1,4,64,512]{4,3,2,1,0:T(8,128)(2,1)}, bf16[4,1,4,64,512]{4,3,2,1,0:T(8,128)(2,1)S(1)}, u32[]{:S(2)}) copy-start(bf16[4,1,4,64,512]{4,3,2,1,0:T(8,128)(2,1)S(1)} %all-to-all-done.3.source) | copy-start | bytes 3145732
  272.3 32.6 %all-to-all-start.4 = ((bf16[4,2,4,64,512]{4,3,2,1,0:T(8,128)(2,1)}), bf16[4,2,4,64,512]{4,3,2,1,0:T(8,128)(2,1)}, u32[]{:S(2)}, u32[]{:S(2)}) async-start(bf16[4,2,4,64,512]{4,3,2,1,0:T(8,128)(2,1)} %get-tuple-element.140), calls=%async_computation.4 | async-start | bytes 4194304 | tf_op jit(solution)/shard_map/all_to_all | solution.py:1214
  279.5 24.3 %collective-permute-start.15 = (bf16[4,144,512]{2,1,0:T(8,128)(2,1)}, bf16[4,144,512]{2,1,0:T(8,128)(2,1)S(1)}, u32[]{:S(2)}, u32[]{:S(2)}) collective-permute-start(bf16[4,144,512]{2,1,0:T(8,128)(2,1)} %get-tuple-element.142), channel_id=1, source_target_pairs={{0,2},{1,3},{2,0},{3,1},{4,6},{5,7},{6,4},{7,5},{8,10},{9,11},{10,... | collective-permute-start | bytes 1769480 | tf_op jit(solution)/shard_map/ppermute | solution.py:1045
  303.8 3.8 %copy-start.6 = (bf16[16,56,512]{2,1,0:T(8,128)(2,1)S(1)}, bf16[16,56,512]{2,1,0:T(8,128)(2,1)}, u32[]{:S(2)}) copy-start(bf16[16,56,512]{2,1,0:T(8,128)(2,1)} %get-tuple-element.137) | copy-start | bytes 2752516
  304.9 2.7 collective-permute-start.16
  307.6 3.9 %copy-start.8 = (bf16[2,144,512]{2,1,0:T(8,128)(2,1)S(1)}, bf16[2,144,512]{2,1,0:T(8,128)(2,1)}, u32[]{:S(2)}) copy-start(bf16[2,144,512]{2,1,0:T(8,128)(2,1)} %get-tuple-element.180) | copy-start | bytes 884740
  307.8 15.7 %collective-permute-start.17 = (bf16[8,56,512]{2,1,0:T(8,128)(2,1)S(1)}, bf16[8,56,512]{2,1,0:T(8,128)(2,1)S(1)}, u32[]{:S(2)}, u32[]{:S(2)}) collective-permute-start(bf16[8,56,512]{2,1,0:T(8,128)(2,1)S(1)} %get-tuple-element.179), channel_id=1, source_target_pairs={{0,1},{1,0},{2,3},{3,2},{4,5},{5,4},{6,7},{7,6},{8,9},{9,8},{10,11... | collective-permute-start | bytes 1376264 | tf_op jit(solution)/shard_map/ppermute | solution.py:1045
  307.9 24.0 %all-to-all-start.5 = ((bf16[4,1,4,64,512]{4,3,2,1,0:T(8,128)(2,1)}), bf16[4,1,4,64,512]{4,3,2,1,0:T(8,128)(2,1)S(1)}, u32[]{:S(2)}, u32[]{:S(2)}) async-start(bf16[4,1,4,64,512]{4,3,2,1,0:T(8,128)(2,1)} %get-tuple-element.149), calls=%async_computation.5 | async-start | bytes 2097152 | tf_op jit(solution)/shard_map/all_to_all | solution.py:1214
  311.4 19.7 %collective-permute-start.18 = (bf16[2,144,512]{2,1,0:T(8,128)(2,1)S(1)}, bf16[2,144,512]{2,1,0:T(8,128)(2,1)S(1)}, u32[]{:S(2)}, u32[]{:S(2)}) collective-permute-start(bf16[2,144,512]{2,1,0:T(8,128)(2,1)S(1)} %copy-done.8), channel_id=1, source_target_pairs={{0,4},{1,5},{2,6},{3,7},{4,0},{5,1},{6,2},{7,3},{8,12},{9,13},{10,... | collective-permute-start | bytes 884744 | tf_op jit(solution)/shard_map/ppermute | solution.py:1045
  331.2 7.5 %collective-permute-start.19 = (bf16[4,56,512]{2,1,0:T(8,128)(2,1)}, bf16[4,56,512]{2,1,0:T(8,128)(2,1)S(1)}, u32[]{:S(2)}, u32[]{:S(2)}) collective-permute-start(bf16[4,56,512]{2,1,0:T(8,128)(2,1)} %get-tuple-element.146), channel_id=1, source_target_pairs={{0,2},{1,3},{2,0},{3,1},{4,6},{5,7},{6,4},{7,5},{8,10},{9,11},{10,... | collective-permute-start | bytes 688136 | tf_op jit(solution)/shard_map/ppermute | solution.py:1045
  331.9 3.3 copy-start.2
  335.2 6.6 %copy-start.4 = (f32[2,144,512]{2,1,0:T(8,128)S(1)}, f32[2,144,512]{2,1,0:T(8,128)}, u32[]{:S(2)}) copy-start(f32[2,144,512]{2,1,0:T(8,128)} %get-tuple-element.181) | copy-start | bytes 1769476
  338.8 8.6 %collective-permute-start.20 = (bf16[2,56,512]{2,1,0:T(8,128)(2,1)S(1)}, bf16[2,56,512]{2,1,0:T(8,128)(2,1)S(1)}, u32[]{:S(2)}, u32[]{:S(2)}) collective-permute-start(bf16[2,56,512]{2,1,0:T(8,128)(2,1)S(1)} %get-tuple-element.151), channel_id=1, source_target_pairs={{0,4},{1,5},{2,6},{3,7},{4,0},{5,1},{6,2},{7,3},{8,12},{9,13},{10,... | collective-permute-start | bytes 344072 | tf_op jit(solution)/shard_map/ppermute | solution.py:1045
  341.9 7.8 %collective-permute-start.22 = (bf16[1,144,512]{2,1,0:T(8,128)(2,1)S(1)}, bf16[1,144,512]{2,1,0:T(8,128)(2,1)S(1)}, u32[]{:S(2)}, u32[]{:S(2)}) collective-permute-start(bf16[1,144,512]{2,1,0:T(8,128)(2,1)S(1)} %fusion.1), channel_id=1, source_target_pairs={{0,16},{8,24},{16,0},{24,8},{1,17},{9,25},{17,1},{25,9},{2,18},{10... | collective-permute-start | bytes 442376 | tf_op jit(solution)/shard_map/ppermute | solution.py:1045
  348.0 4.2 %collective-permute-start.21 = (bf16[1,56,512]{2,1,0:T(8,128)(2,1)S(1)}, bf16[1,56,512]{2,1,0:T(8,128)(2,1)S(1)}, u32[]{:S(2)}, u32[]{:S(2)}) collective-permute-start(bf16[1,56,512]{2,1,0:T(8,128)(2,1)S(1)} %get-tuple-element.186), channel_id=1, source_target_pairs={{0,16},{8,24},{16,0},{24,8},{1,17},{9,25},{17,1},{25,9},{2,18},{10... | collective-permute-start | bytes 172040 | tf_op jit(solution)/shard_map/ppermute | solution.py:1045
  352.2 0.6 copy-start.10
Sparse Core Ops, SparseCore 0:
  10.9 75.0 all-gather.1

commit v6 on v5

--- a/solution.py
+++ b/solution.py
@@ -1258,7 +1258,7 @@
     if in_parts:
         place, owner = order_tables()
         first_part, second_part = run_pack(w_qkv, w_out, w_up, w_down, small)
-        halves, steps = gather_halves(first_part, {1: sent, 2: tables + (closing, from_before, unbroken)})
+        halves, steps = gather_halves(first_part, {1: sent, 3: tables + (closing, from_before, unbroken)})
         moved = to_dp(after(sent, steps[0]))
         qkv_all, vectors = run_sort_first(
             place, owner, *halves, [item.shape[0] for item in small]

time: 368 us -> 368 us (level)
  no operation moved by 1% of the time
where the time goes in v6:
time: 368 us; the launch traced here: 361 us
  Pallas kernels  193 us (52%)
  starting transfers between devices  69.9 us (19%)
  waiting for transfers between devices  59.3 us (16%)
  other arithmetic  18.1 us (5%)
  between operations  15 us (4%)
  local copies, waits for them, and re-layouts  6.06 us (2%)
    pallas_call x2, Pallas kernels, run_mid(): pl.pallas_call(functools.partial(mid_kernel, first=first, resumes=resumes...  95.4 us
    pallas_call x2, Pallas kernels, run_back(): pl.pallas_call(functools.partial(back_kernel, first=first, resumes=resume...  52 us
    ppermute x15, waiting for transfers between devices, swap(): lax.ppermute(x, axis, [(i, i ^ bit) for i in range(lax.axis_size(axis))])  38.3 us
    ppermute x15, starting transfers between devices, swap(): lax.ppermute(x, axis, [(i, i ^ bit) for i in range(lax.axis_size(axis))])  29.7 us
    all_to_all x6, starting transfers between devices, to_dp(): return lax.all_to_all(group, 'dp', split_axis=0, concat_axis=0, tiled=True)  23.7 us
    ppermute x2, waiting for transfers between devices, passed_on(): got = lax.ppermute(own, 'fsdp', [(i, i + step) for i in range(size - step)])  14.1 us
    pallas_call x4, Pallas kernels, run_land(): pl.pallas_call(functools.partial(land_kernel, first=first), name='land',...  12.7 us
    pallas_call x1, Pallas kernels, run_state(): pl.pallas_call(state_kernel, name='end_state', grid_spec=pltpu.PrefetchSc...  10.7 us
  transfers between devices with their start and end apart: 30, of which 12 were waited for; matrix products, arithmetic and copies ran while one was open for 6% of the time, Pallas kernels for 33%

profile of v6, /device:TPU:0, one launch (start us, length us, event | category | flops | bytes accessed | tf_op | source)
XLA Modules:
  0.0 361.3 jit_solution(13204404357925976933)
XLA Ops:
  7.2 1.8 pack.1
  9.0 3.0 collective-permute-start
  13.8 5.3 %send.2 = bf16[4,3,4,64,512]{4,3,2,1,0:T(8,128)(2,1)} custom-call(s32[3,16]{1,0:T(4,128)} %convert_reduce_fusion.1.slot, bf16[3,16,64,512]{3,2,1,0:T(8,128)(2,1)} %bitcast.35), custom_call_target="tpu_custom_call" | custom-call | bytes 6291456 | tf_op jit(solution)/shard_map/send/pallas_call | solution.py:876
  21.1 2.7 collective-permute-start.1
  24.1 3.7 %all-to-all-start = ((bf16[4,3,4,64,512]{4,3,2,1,0:T(8,128)(2,1)}), bf16[4,3,4,64,512]{4,3,2,1,0:T(8,128)(2,1)S(1)}, u32[]{:S(2)}, u32[]{:S(2)}) async-start(bf16[4,3,4,64,512]{4,3,2,1,0:T(8,128)(2,1)} %send.2), calls=%async_computation | async-start | bytes 6291456 | tf_op jit(solution)/shard_map/all_to_all | solution.py:1214
  27.8 4.1 %collective-permute-done.1 = bf16[2,64,512]{2,1,0:T(8,128)(2,1)S(1)} collective-permute-done((bf16[2,64,512]{2,1,0:T(8,128)(2,1)S(1)}, bf16[2,64,512]{2,1,0:T(8,128)(2,1)S(1)}, u32[]{:S(2)}, u32[]{:S(2)}) %collective-permute-start.1) | collective-permute-done | bytes 131104 | tf_op jit(solution)/shard_map/ppermute | solution.py:1045
  33.4 6.1 %collective-permute-done.2 = bf16[4,64,512]{2,1,0:T(8,128)(2,1)S(1)} collective-permute-done((bf16[4,64,512]{2,1,0:T(8,128)(2,1)S(1)}, bf16[4,64,512]{2,1,0:T(8,128)(2,1)S(1)}, u32[]{:S(2)}, u32[]{:S(2)}) %collective-permute-start.2) | collective-permute-done | bytes 262176 | tf_op jit(solution)/shard_map/ppermute | solution.py:1045
  39.6 1.6 collective-permute-start.3
  41.2 12.5 %collective-permute-done.3 = bf16[8,64,512]{2,1,0:T(8,128)(2,1)S(1)} collective-permute-done((bf16[8,64,512]{2,1,0:T(8,128)(2,1)S(1)}, bf16[8,64,512]{2,1,0:T(8,128)(2,1)S(1)}, u32[]{:S(2)}, u32[]{:S(2)}) %collective-permute-start.3) | collective-permute-done | bytes 524320 | tf_op jit(solution)/shard_map/ppermute | solution.py:1045
  55.8 1.6 collective-permute-done.4.got
  57.4 3.5 sort_first.1
  60.9 5.2 %send.3 = bf16[4,3,4,64,512]{4,3,2,1,0:T(8,128)(2,1)} custom-call(s32[3,16]{1,0:T(4,128)} %convert_reduce_fusion.1.slot, bf16[3,16,64,512]{3,2,1,0:T(8,128)(2,1)} %bitcast.36), custom_call_target="tpu_custom_call" | custom-call | bytes 6291456 | tf_op jit(solution)/shard_map/send/pallas_call | solution.py:876
  66.2 6.9 %all-to-all-done.rows.rows_ref = bf16[4,3,4,64,512]{4,3,2,1,0:T(8,128)(2,1)S(1)} async-done(((bf16[4,3,4,64,512]{4,3,2,1,0:T(8,128)(2,1)}), bf16[4,3,4,64,512]{4,3,2,1,0:T(8,128)(2,1)S(1)}, u32[]{:S(2)}, u32[]{:S(2)}) %all-to-all-start) | async-done | bytes 3145760 | tf_op jit(solution)/shard_map/all_to_all | solution.py:1214
  73.1 1.7 copy-done.3
  74.7 4.7 %all-to-all-start.1 = ((bf16[4,3,4,64,512]{4,3,2,1,0:T(8,128)(2,1)}), bf16[4,3,4,64,512]{4,3,2,1,0:T(8,128)(2,1)}, u32[]{:S(2)}, u32[]{:S(2)}) async-start(bf16[4,3,4,64,512]{4,3,2,1,0:T(8,128)(2,1)} %send.3), calls=%async_computation.1 | async-start | bytes 6291456 | tf_op jit(solution)/shard_map/all_to_all | solution.py:1214
  79.4 10.7 %end_state.1 = f32[3,72,512]{2,1,0:T(8,128)} custom-call(s32[3,16]{1,0:T(4,128)} %get-tuple-element.200.placing, s32[3,16]{1,0:T(4,128)} %get-tuple-element.199.closing, bf16[4,3,4,64,512]{4,3,2,1,0:T(8,128)(2,1)} %copy-done.3, bf16[512,1536]{1,0:T(8,128)(2,1)} %get-tuple-element.93.weight.w_qkv.weight_far, f32[8,2048]{1,0:T(8,128)} %get-tuple-element.95.vec), custom_call_target="tpu_custom_call" | custom-call | flops 11811160064 | bytes 5242880 | tf_op jit(solution)/shard_map/end_state/pallas_call | solution.py:204
  90.1 3.5 collective-permute-start.5
  93.7 4.7 %sort_second.1 = (bf16[512,2048]{1,0:T(8,128)(2,1)}, bf16[2048,512]{1,0:T(8,128)(2,1)}, bf16[512,512]{1,0:T(8,128)(2,1)}) custom-call(bf16[32,144,512]{2,1,0:T(8,128)(2,1)} %all-gather.2.cloned.1.call-done.gathered), custom_call_target="tpu_custom_call" | custom-call | tf_op jit(solution)/shard_map/sort_second/pallas_call | solution.py:1191
  98.4 5.5 %collective-permute-done.5 = f32[3,72,512]{2,1,0:T(8,128)S(1)} collective-permute-done((f32[3,72,512]{2,1,0:T(8,128)}, f32[3,72,512]{2,1,0:T(8,128)S(1)}, u32[]{:S(2)}, u32[]{:S(2)}) %collective-permute-start.5) | collective-permute-done | bytes 442400 | tf_op jit(solution)/shard_map/ppermute | solution.py:999
  104.1 5.3 %collective-permute-start.6 = (f32[3,72,512]{2,1,0:T(8,128)S(1)}, f32[3,72,512]{2,1,0:T(8,128)S(1)}, u32[]{:S(2)}, u32[]{:S(2)}) collective-permute-start(f32[3,72,512]{2,1,0:T(8,128)S(1)} %multiply_add_fusion.1), channel_id=1, source_target_pairs={{0,2},{1,3},{2,4},{3,5},{4,6},{5,7},{8,10},{9,11},{10,12},{11,13},... | collective-permute-start | bytes 1327112 | tf_op jit(solution)/shard_map/ppermute | solution.py:999
  110.1 8.5 %collective-permute-done.6 = f32[3,72,512]{2,1,0:T(8,128)S(1)} collective-permute-done((f32[3,72,512]{2,1,0:T(8,128)S(1)}, f32[3,72,512]{2,1,0:T(8,128)S(1)}, u32[]{:S(2)}, u32[]{:S(2)}) %collective-permute-start.6) | collective-permute-done | bytes 442400 | tf_op jit(solution)/shard_map/ppermute | solution.py:999
  120.0 58.9 %middle.2 = (bf16[4,2,4,64,512]{4,3,2,1,0:T(8,128)(2,1)}, bf16[2048,1536]{1,0:T(8,128)(2,1)}, bf16[2048,512]{1,0:T(8,128)(2,1)}, bf16[2048,512]{1,0:T(8,128)(2,1...) custom-call(s32[3,16]{1,0:T(4,128)} %get-tuple-element.200.placing, ...), custom_call_target="tpu_custom_call", output_to_operand_aliasing={{0}: (4, {})} | custom-call | flops 51539607552 | bytes 33554432 | tf_op jit(solution)/shard_map/middle/pallas_call | solution.py:532
  179.0 1.3 collective-permute-start.7
  182.9 3.6 %all-to-all-start.2 = ((bf16[4,2,4,64,512]{4,3,2,1,0:T(8,128)(2,1)}), bf16[4,2,4,64,512]{4,3,2,1,0:T(8,128)(2,1)S(1)}, u32[]{:S(2)}, u32[]{:S(2)}) async-start(bf16[4,2,4,64,512]{4,3,2,1,0:T(8,128)(2,1)} %get-tuple-element.102), calls=%async_computation.2 | async-start | bytes 4194304 | tf_op jit(solution)/shard_map/all_to_all | solution.py:1214
  186.5 36.5 %middle.3 = (bf16[4,1,4,64,512]{4,3,2,1,0:T(8,128)(2,1)}, bf16[1024,1536]{1,0:T(8,128)(2,1)}, bf16[1024,512]{1,0:T(8,128)(2,1)}, bf16[1024,512]{1,0:T(8,128)(2,1...) custom-call(s32[3,16]{1,0:T(4,128)} %get-tuple-element.200.placing, ...), custom_call_target="tpu_custom_call", output_to_operand_aliasing={{0}: (4, {})} | custom-call | flops 25769803776 | bytes 16777216 | tf_op jit(solution)/shard_map/middle/pallas_call | solution.py:532
  224.9 1.3 collective-permute-start.13
  226.2 1.3 collective-permute-start.14
  227.5 3.5 all-to-all-start.3
  231.1 4.1 %add_convert_fusion = (bf16[8,144,512]{2,1,0:T(8,128)(2,1)}, f32[8,144,512]{2,1,0:T(8,128)S(1)}) fusion(bf16[16,144,512]{2,1,0:T(8,128)(2,1)} %collective-permute-done.10, bf16[16,144,512]{2,1,0:T(8,128)(2,1)} %get-tuple-element.111), kind=kLoop, calls=%fused_computation | loop fusion | flops 4128768 | bytes 8257536 | tf_op jit(solution)/shard_map/convert_element_type | solution.py:1068
  235.1 3.3 collective-permute-start.11
  239.0 32.8 %back.2 = (bf16[4,2,4,64,512]{4,3,2,1,0:T(8,128)(2,1)}, f32[8,1536]{1,0:T(8,128)}, f32[512,1536]{1,0:T(8,128)}) custom-call(s32[3,16]{1,0:T(4,128)} %get-tuple-element.200.placing, s32[3,17]{1,0:T(4,128)} %convert_select_fusion.restart, f32[3,3]{1,0:T(4,128)} %convert_subtract_fusion.3.reach, ...), custom_call_target="tpu_custom_call", output_to_operand_aliasing={{0}: (4, {})} | custom-call | flops 32212254720 | bytes 33554432 | tf_op jit(solution)/shard_map/back/pallas_call | solution.py:803
  271.8 4.7 %all-to-all-start.4 = ((bf16[4,2,4,64,512]{4,3,2,1,0:T(8,128)(2,1)}), bf16[4,2,4,64,512]{4,3,2,1,0:T(8,128)(2,1)}, u32[]{:S(2)}, u32[]{:S(2)}) async-start(bf16[4,2,4,64,512]{4,3,2,1,0:T(8,128)(2,1)} %get-tuple-element.140), calls=%async_computation.4 | async-start | bytes 4194304 | tf_op jit(solution)/shard_map/all_to_all | solution.py:1214
  276.6 2.4 add_convert_fusion.1
  279.0 5.0 %collective-permute-start.15 = (bf16[4,144,512]{2,1,0:T(8,128)(2,1)}, bf16[4,144,512]{2,1,0:T(8,128)(2,1)S(1)}, u32[]{:S(2)}, u32[]{:S(2)}) collective-permute-start(bf16[4,144,512]{2,1,0:T(8,128)(2,1)} %get-tuple-element.142), channel_id=1, source_target_pairs={{0,2},{1,3},{2,0},{3,1},{4,6},{5,7},{6,4},{7,5},{8,10},{9,11},{10,... | collective-permute-start | bytes 1769480 | tf_op jit(solution)/shard_map/ppermute | solution.py:1045
  284.1 19.3 %back.3 = (bf16[4,1,4,64,512]{4,3,2,1,0:T(8,128)(2,1)}, f32[8,1536]{1,0:T(8,128)}, bf16[16,56,512]{2,1,0:T(8,128)(2,1)}, bf16[16,56,512]{2,1,0:T(8,128)(2,1)}) custom-call(s32[3,16]{1,0:T(4,128)} %get-tuple-element.200.placing, s32[3,17]{1,0:T(4,128)} %convert_select_fusion.restart, ...), custom_call_target="tpu_custom_call", output_to_operand_aliasing={{0}: (4, {})} | custom-call | flops 16106127360 | bytes 16777216 | tf_op jit(solution)/shard_map/back/pallas_call | solution.py:803
  304.6 2.5 collective-permute-done.16
  307.4 3.5 all-to-all-start.5
  311.0 5.8 %collective-permute-start.18 = (bf16[2,144,512]{2,1,0:T(8,128)(2,1)S(1)}, bf16[2,144,512]{2,1,0:T(8,128)(2,1)S(1)}, u32[]{:S(2)}, u32[]{:S(2)}) collective-permute-start(bf16[2,144,512]{2,1,0:T(8,128)(2,1)S(1)} %copy-done.8), channel_id=1, source_target_pairs={{0,4},{1,5},{2,6},{3,7},{4,0},{5,1},{6,2},{7,3},{8,12},{9,13},{10,... | collective-permute-start | bytes 884744 | tf_op jit(solution)/shard_map/ppermute | solution.py:1045
  316.8 3.3 land.4._
  320.1 2.9 land.5
  323.9 6.8 %collective-permute-done.18 = bf16[2,144,512]{2,1,0:T(8,128)(2,1)S(1)} collective-permute-done((bf16[2,144,512]{2,1,0:T(8,128)(2,1)S(1)}, bf16[2,144,512]{2,1,0:T(8,128)(2,1)S(1)}, u32[]{:S(2)}, u32[]{:S(2)}) %collective-permute-start.18) | collective-permute-done | bytes 294944 | tf_op jit(solution)/shard_map/ppermute | solution.py:1045
  331.5 3.3 land.6._
  334.8 3.1 land.7
  338.3 3.1 collective-permute-start.20
  341.4 1.7 collective-permute-start.22
  343.1 3.8 %collective-permute-done.20 = bf16[2,56,512]{2,1,0:T(8,128)(2,1)S(1)} collective-permute-done((bf16[2,56,512]{2,1,0:T(8,128)(2,1)S(1)}, bf16[2,56,512]{2,1,0:T(8,128)(2,1)S(1)}, u32[]{:S(2)}, u32[]{:S(2)}) %collective-permute-start.20) | collective-permute-done | bytes 114720 | tf_op jit(solution)/shard_map/ppermute | solution.py:1045
  347.6 1.6 collective-permute-start.21
  352.4 1.6 finish.1
  (114 shorter events, 22.8 us)
Async XLA Ops:
  7.2 86.5 %all-gather.2.cloned.1.call-start = ((), (), s32[]{:S(2)}) async-start(), calls=%async_computation.6 | async-start | bytes 4866048 | tf_op jit(solution)/shard_map/all_gather | solution.py:1206
  9.0 12.1 %collective-permute-start = (bf16[1,64,512]{2,1,0:T(8,128)(2,1)}, bf16[1,64,512]{2,1,0:T(8,128)(2,1)S(1)}, u32[]{:S(2)}, u32[]{:S(2)}) collective-permute-start(bf16[1,64,512]{2,1,0:T(8,128)(2,1)} %get-tuple-element.89), channel_id=1, source_target_pairs={{0,16},{8,24},{16,0},{24,8},{1,17},{9,25},{17,1},{25,9},{2,18},{10... | collective-permute-start | bytes 196616 | tf_op jit(solution)/shard_map/ppermute | solution.py:1045
  13.8 5.4 %copy-start.11 = (s32[3,16]{1,0:T(4,128)S(1)}, s32[3,16]{1,0:T(4,128)}, u32[]{:S(2)}) copy-start(s32[3,16]{1,0:T(4,128)} %param.18) | copy-start | bytes 580
  13.8 7.3 %copy-start.9 = (bf16[1,64,512]{2,1,0:T(8,128)(2,1)S(1)}, bf16[1,64,512]{2,1,0:T(8,128)(2,1)}, u32[]{:S(2)}) copy-start(bf16[1,64,512]{2,1,0:T(8,128)(2,1)} %get-tuple-element.89) | copy-start | bytes 196612
  21.1 10.7 %collective-permute-start.1 = (bf16[2,64,512]{2,1,0:T(8,128)(2,1)S(1)}, bf16[2,64,512]{2,1,0:T(8,128)(2,1)S(1)}, u32[]{:S(2)}, u32[]{:S(2)}) collective-permute-start(bf16[2,64,512]{2,1,0:T(8,128)(2,1)S(1)} %constant_dynamic-update-slice_fusion), channel_id=1, source_target_pairs={{0,4},{1,5},{2,6},{3,7},{4,0},{5,1},{6,2},{7,3},{8,12},{9,13},{10,... | collective-permute-start | bytes 393224 | tf_op jit(solution)/shard_map/ppermute | solution.py:1045
  24.1 49.0 %all-to-all-start = ((bf16[4,3,4,64,512]{4,3,2,1,0:T(8,128)(2,1)}), bf16[4,3,4,64,512]{4,3,2,1,0:T(8,128)(2,1)S(1)}, u32[]{:S(2)}, u32[]{:S(2)}) async-start(bf16[4,3,4,64,512]{4,3,2,1,0:T(8,128)(2,1)} %send.2), calls=%async_computation | async-start | bytes 6291456 | tf_op jit(solution)/shard_map/all_to_all | solution.py:1214
  31.9 7.6 %collective-permute-start.2 = (bf16[4,64,512]{2,1,0:T(8,128)(2,1)S(1)}, bf16[4,64,512]{2,1,0:T(8,128)(2,1)S(1)}, u32[]{:S(2)}, u32[]{:S(2)}) collective-permute-start(bf16[4,64,512]{2,1,0:T(8,128)(2,1)S(1)} %pad_maximum_fusion.1), channel_id=1, source_target_pairs={{0,2},{1,3},{2,0},{3,1},{4,6},{5,7},{6,4},{7,5},{8,10},{9,11},{10,... | collective-permute-start | bytes 786440 | tf_op jit(solution)/shard_map/ppermute | solution.py:1045
  39.6 14.1 %collective-permute-start.3 = (bf16[8,64,512]{2,1,0:T(8,128)(2,1)S(1)}, bf16[8,64,512]{2,1,0:T(8,128)(2,1)S(1)}, u32[]{:S(2)}, u32[]{:S(2)}) collective-permute-start(bf16[8,64,512]{2,1,0:T(8,128)(2,1)S(1)} %pad_maximum_fusion), channel_id=1, source_target_pairs={{0,1},{1,0},{2,3},{3,2},{4,5},{5,4},{6,7},{7,6},{8,9},{9,8},{10,11... | collective-permute-start | bytes 1572872 | tf_op jit(solution)/shard_map/ppermute | solution.py:1045
  53.7 1.0 copy-start.4
  54.6 2.8 collective-permute-start.4
  73.1 1.7 copy-start.3
  74.7 44.8 %all-to-all-start.1 = ((bf16[4,3,4,64,512]{4,3,2,1,0:T(8,128)(2,1)}), bf16[4,3,4,64,512]{4,3,2,1,0:T(8,128)(2,1)}, u32[]{:S(2)}, u32[]{:S(2)}) async-start(bf16[4,3,4,64,512]{4,3,2,1,0:T(8,128)(2,1)} %send.3), calls=%async_computation.1 | async-start | bytes 6291456 | tf_op jit(solution)/shard_map/all_to_all | solution.py:1214
  90.1 13.9 %collective-permute-start.5 = (f32[3,72,512]{2,1,0:T(8,128)}, f32[3,72,512]{2,1,0:T(8,128)S(1)}, u32[]{:S(2)}, u32[]{:S(2)}) collective-permute-start(f32[3,72,512]{2,1,0:T(8,128)} %end_state.1), channel_id=1, source_target_pairs={{0,1},{1,2},{2,3},{3,4},{4,5},{5,6},{6,7},{8,9},{9,10},{10,11},{11... | collective-permute-start | bytes 1327112 | tf_op jit(solution)/shard_map/ppermute | solution.py:999
  93.7 10.3 %copy-start.7 = (f32[3,72,512]{2,1,0:T(8,128)S(1)}, f32[3,72,512]{2,1,0:T(8,128)}, u32[]{:S(2)}) copy-start(f32[3,72,512]{2,1,0:T(8,128)} %end_state.1) | copy-start | bytes 1327108
  104.1 14.5 %collective-permute-start.6 = (f32[3,72,512]{2,1,0:T(8,128)S(1)}, f32[3,72,512]{2,1,0:T(8,128)S(1)}, u32[]{:S(2)}, u32[]{:S(2)}) collective-permute-start(f32[3,72,512]{2,1,0:T(8,128)S(1)} %multiply_add_fusion.1), channel_id=1, source_target_pairs={{0,2},{1,3},{2,4},{3,5},{4,6},{5,7},{8,10},{9,11},{10,12},{11,13},... | collective-permute-start | bytes 1327112 | tf_op jit(solution)/shard_map/ppermute | solution.py:999
  179.0 44.0 %collective-permute-start.7 = (f32[2,72,512]{2,1,0:T(8,128)}, f32[2,72,512]{2,1,0:T(8,128)S(1)}, u32[]{:S(2)}, u32[]{:S(2)}) collective-permute-start(f32[2,72,512]{2,1,0:T(8,128)} %get-tuple-element.113), channel_id=1, source_target_pairs={{1,0},{2,1},{3,2},{4,3},{5,4},{6,5},{7,6},{9,8},{10,9},{11,10},{12... | collective-permute-start | bytes 884744 | tf_op jit(solution)/shard_map/ppermute | solution.py:991
  180.3 42.7 %collective-permute-start.8 = (f32[2,72,512]{2,1,0:T(8,128)}, f32[2,72,512]{2,1,0:T(8,128)S(1)}, u32[]{:S(2)}, u32[]{:S(2)}) collective-permute-start(f32[2,72,512]{2,1,0:T(8,128)} %get-tuple-element.113), channel_id=1, source_target_pairs={{2,0},{3,1},{4,2},{5,3},{6,4},{7,5},{10,8},{11,9},{12,10},{13,11},... | collective-permute-start | bytes 884744 | tf_op jit(solution)/shard_map/ppermute | solution.py:991
  181.6 41.5 %collective-permute-start.9 = (f32[2,72,512]{2,1,0:T(8,128)}, f32[2,72,512]{2,1,0:T(8,128)S(1)}, u32[]{:S(2)}, u32[]{:S(2)}) collective-permute-start(f32[2,72,512]{2,1,0:T(8,128)} %get-tuple-element.113), channel_id=1, source_target_pairs={{3,0},{4,1},{5,2},{6,3},{7,4},{11,8},{12,9},{13,10},{14,11},{15,12... | collective-permute-start | bytes 884744 | tf_op jit(solution)/shard_map/ppermute | solution.py:991
  182.9 40.2 %all-to-all-start.2 = ((bf16[4,2,4,64,512]{4,3,2,1,0:T(8,128)(2,1)}), bf16[4,2,4,64,512]{4,3,2,1,0:T(8,128)(2,1)S(1)}, u32[]{:S(2)}, u32[]{:S(2)}) async-start(bf16[4,2,4,64,512]{4,3,2,1,0:T(8,128)(2,1)} %get-tuple-element.102), calls=%async_computation.2 | async-start | bytes 4194304 | tf_op jit(solution)/shard_map/all_to_all | solution.py:1214
  223.0 4.5 %copy-start.12 = (f32[2,72,512]{2,1,0:T(8,128)}, f32[2,72,512]{2,1,0:T(8,128)S(1)}, u32[]{:S(2)}) copy-start(f32[2,72,512]{2,1,0:T(8,128)S(1)} %collective-permute-done.7.refs_0_) | copy-start | bytes 884740
  223.0 4.5 %copy-start.13 = (f32[2,72,512]{2,1,0:T(8,128)}, f32[2,72,512]{2,1,0:T(8,128)S(1)}, u32[]{:S(2)}) copy-start(f32[2,72,512]{2,1,0:T(8,128)S(1)} %collective-permute-done.8.refs_1_) | copy-start | bytes 884740
  223.0 4.5 %copy-start.14 = (f32[2,72,512]{2,1,0:T(8,128)}, f32[2,72,512]{2,1,0:T(8,128)S(1)}, u32[]{:S(2)}) copy-start(f32[2,72,512]{2,1,0:T(8,128)S(1)} %collective-permute-done.9.refs_2_) | copy-start | bytes 884740
  223.0 4.4 %copy-start = (bf16[4,2,4,64,512]{4,3,2,1,0:T(8,128)(2,1)}, bf16[4,2,4,64,512]{4,3,2,1,0:T(8,128)(2,1)S(1)}, u32[]{:S(2)}) copy-start(bf16[4,2,4,64,512]{4,3,2,1,0:T(8,128)(2,1)S(1)} %all-to-all-done.2.source) | copy-start | bytes 6291460
  223.1 8.0 %collective-permute-start.10 = (bf16[16,144,512]{2,1,0:T(8,128)(2,1)}, bf16[16,144,512]{2,1,0:T(8,128)(2,1)}, u32[]{:S(2)}, u32[]{:S(2)}) collective-permute-start(bf16[16,144,512]{2,1,0:T(8,128)(2,1)} %get-tuple-element.118), channel_id=1, source_target_pairs={{0,8},{8,0},{16,24},{24,16},{1,9},{9,1},{17,25},{25,17},{2,10},{10... | collective-permute-start | bytes 7077896 | tf_op jit(solution)/shard_map/ppermute | solution.py:1045
  223.6 48.2 %collective-permute-start.12 = (f32[1,72,512]{2,1,0:T(8,128)}, f32[1,72,512]{2,1,0:T(8,128)S(1)}, u32[]{:S(2)}, u32[]{:S(2)}) collective-permute-start(f32[1,72,512]{2,1,0:T(8,128)} %get-tuple-element.130), channel_id=1, source_target_pairs={{1,0},{2,1},{3,2},{4,3},{5,4},{6,5},{7,6},{9,8},{10,9},{11,10},{12... | collective-permute-start | bytes 442376 | tf_op jit(solution)/shard_map/ppermute | solution.py:991
  224.9 46.9 %collective-permute-start.13 = (f32[1,72,512]{2,1,0:T(8,128)}, f32[1,72,512]{2,1,0:T(8,128)}, u32[]{:S(2)}, u32[]{:S(2)}) collective-permute-start(f32[1,72,512]{2,1,0:T(8,128)} %get-tuple-element.130), channel_id=1, source_target_pairs={{2,0},{3,1},{4,2},{5,3},{6,4},{7,5},{10,8},{11,9},{12,10},{13,11},... | collective-permute-start | bytes 442376 | tf_op jit(solution)/shard_map/ppermute | solution.py:991
  226.2 45.6 %collective-permute-start.14 = (f32[1,72,512]{2,1,0:T(8,128)}, f32[1,72,512]{2,1,0:T(8,128)}, u32[]{:S(2)}, u32[]{:S(2)}) collective-permute-start(f32[1,72,512]{2,1,0:T(8,128)} %get-tuple-element.130), channel_id=1, source_target_pairs={{3,0},{4,1},{5,2},{6,3},{7,4},{11,8},{12,9},{13,10},{14,11},{15,12... | collective-permute-start | bytes 442376 | tf_op jit(solution)/shard_map/ppermute | solution.py:991
  227.5 44.3 %all-to-all-start.3 = ((bf16[4,1,4,64,512]{4,3,2,1,0:T(8,128)(2,1)}), bf16[4,1,4,64,512]{4,3,2,1,0:T(8,128)(2,1)S(1)}, u32[]{:S(2)}, u32[]{:S(2)}) async-start(bf16[4,1,4,64,512]{4,3,2,1,0:T(8,128)(2,1)} %get-tuple-element.131), calls=%async_computation.3 | async-start | bytes 2097152 | tf_op jit(solution)/shard_map/all_to_all | solution.py:1214
  235.1 41.4 %collective-permute-start.11 = (bf16[8,144,512]{2,1,0:T(8,128)(2,1)}, bf16[8,144,512]{2,1,0:T(8,128)(2,1)}, u32[]{:S(2)}, u32[]{:S(2)}) collective-permute-start(bf16[8,144,512]{2,1,0:T(8,128)(2,1)} %get-tuple-element.120), channel_id=1, source_target_pairs={{0,1},{1,0},{2,3},{3,2},{4,5},{5,4},{6,7},{7,6},{8,9},{9,8},{10,11... | collective-permute-start | bytes 3538952 | tf_op jit(solution)/shard_map/ppermute | solution.py:1045
  271.8 4.8 %copy-start.15 = (f32[1,72,512]{2,1,0:T(8,128)}, f32[1,72,512]{2,1,0:T(8,128)S(1)}, u32[]{:S(2)}) copy-start(f32[1,72,512]{2,1,0:T(8,128)S(1)} %collective-permute-done.12.refs_0_) | copy-start | bytes 442372
  271.8 4.7 %copy-start.1 = (bf16[4,1,4,64,512]{4,3,2,1,0:T(8,128)(2,1)}, bf16[4,1,4,64,512]{4,3,2,1,0:T(8,128)(2,1)S(1)}, u32[]{:S(2)}) copy-start(bf16[4,1,4,64,512]{4,3,2,1,0:T(8,128)(2,1)S(1)} %all-to-all-done.3.source) | copy-start | bytes 3145732
  271.8 32.6 %all-to-all-start.4 = ((bf16[4,2,4,64,512]{4,3,2,1,0:T(8,128)(2,1)}), bf16[4,2,4,64,512]{4,3,2,1,0:T(8,128)(2,1)}, u32[]{:S(2)}, u32[]{:S(2)}) async-start(bf16[4,2,4,64,512]{4,3,2,1,0:T(8,128)(2,1)} %get-tuple-element.140), calls=%async_computation.4 | async-start | bytes 4194304 | tf_op jit(solution)/shard_map/all_to_all | solution.py:1214
  279.0 24.3 %collective-permute-start.15 = (bf16[4,144,512]{2,1,0:T(8,128)(2,1)}, bf16[4,144,512]{2,1,0:T(8,128)(2,1)S(1)}, u32[]{:S(2)}, u32[]{:S(2)}) collective-permute-start(bf16[4,144,512]{2,1,0:T(8,128)(2,1)} %get-tuple-element.142), channel_id=1, source_target_pairs={{0,2},{1,3},{2,0},{3,1},{4,6},{5,7},{6,4},{7,5},{8,10},{9,11},{10,... | collective-permute-start | bytes 1769480 | tf_op jit(solution)/shard_map/ppermute | solution.py:1045
  303.3 3.8 %copy-start.6 = (bf16[16,56,512]{2,1,0:T(8,128)(2,1)S(1)}, bf16[16,56,512]{2,1,0:T(8,128)(2,1)}, u32[]{:S(2)}) copy-start(bf16[16,56,512]{2,1,0:T(8,128)(2,1)} %get-tuple-element.137) | copy-start | bytes 2752516
  304.4 2.7 collective-permute-start.16
  307.1 3.9 %copy-start.8 = (bf16[2,144,512]{2,1,0:T(8,128)(2,1)S(1)}, bf16[2,144,512]{2,1,0:T(8,128)(2,1)}, u32[]{:S(2)}) copy-start(bf16[2,144,512]{2,1,0:T(8,128)(2,1)} %get-tuple-element.180) | copy-start | bytes 884740
  307.4 15.7 %collective-permute-start.17 = (bf16[8,56,512]{2,1,0:T(8,128)(2,1)S(1)}, bf16[8,56,512]{2,1,0:T(8,128)(2,1)S(1)}, u32[]{:S(2)}, u32[]{:S(2)}) collective-permute-start(bf16[8,56,512]{2,1,0:T(8,128)(2,1)S(1)} %get-tuple-element.179), channel_id=1, source_target_pairs={{0,1},{1,0},{2,3},{3,2},{4,5},{5,4},{6,7},{7,6},{8,9},{9,8},{10,11... | collective-permute-start | bytes 1376264 | tf_op jit(solution)/shard_map/ppermute | solution.py:1045
  307.4 24.0 %all-to-all-start.5 = ((bf16[4,1,4,64,512]{4,3,2,1,0:T(8,128)(2,1)}), bf16[4,1,4,64,512]{4,3,2,1,0:T(8,128)(2,1)S(1)}, u32[]{:S(2)}, u32[]{:S(2)}) async-start(bf16[4,1,4,64,512]{4,3,2,1,0:T(8,128)(2,1)} %get-tuple-element.149), calls=%async_computation.5 | async-start | bytes 2097152 | tf_op jit(solution)/shard_map/all_to_all | solution.py:1214
  311.0 19.7 %collective-permute-start.18 = (bf16[2,144,512]{2,1,0:T(8,128)(2,1)S(1)}, bf16[2,144,512]{2,1,0:T(8,128)(2,1)S(1)}, u32[]{:S(2)}, u32[]{:S(2)}) collective-permute-start(bf16[2,144,512]{2,1,0:T(8,128)(2,1)S(1)} %copy-done.8), channel_id=1, source_target_pairs={{0,4},{1,5},{2,6},{3,7},{4,0},{5,1},{6,2},{7,3},{8,12},{9,13},{10,... | collective-permute-start | bytes 884744 | tf_op jit(solution)/shard_map/ppermute | solution.py:1045
  330.7 7.5 %collective-permute-start.19 = (bf16[4,56,512]{2,1,0:T(8,128)(2,1)}, bf16[4,56,512]{2,1,0:T(8,128)(2,1)S(1)}, u32[]{:S(2)}, u32[]{:S(2)}) collective-permute-start(bf16[4,56,512]{2,1,0:T(8,128)(2,1)} %get-tuple-element.146), channel_id=1, source_target_pairs={{0,2},{1,3},{2,0},{3,1},{4,6},{5,7},{6,4},{7,5},{8,10},{9,11},{10,... | collective-permute-start | bytes 688136 | tf_op jit(solution)/shard_map/ppermute | solution.py:1045
  331.5 3.3 copy-start.2
  334.8 6.6 %copy-start.5 = (f32[2,144,512]{2,1,0:T(8,128)S(1)}, f32[2,144,512]{2,1,0:T(8,128)}, u32[]{:S(2)}) copy-start(f32[2,144,512]{2,1,0:T(8,128)} %get-tuple-element.181) | copy-start | bytes 1769476
  338.3 8.6 %collective-permute-start.20 = (bf16[2,56,512]{2,1,0:T(8,128)(2,1)S(1)}, bf16[2,56,512]{2,1,0:T(8,128)(2,1)S(1)}, u32[]{:S(2)}, u32[]{:S(2)}) collective-permute-start(bf16[2,56,512]{2,1,0:T(8,128)(2,1)S(1)} %get-tuple-element.151), channel_id=1, source_target_pairs={{0,4},{1,5},{2,6},{3,7},{4,0},{5,1},{6,2},{7,3},{8,12},{9,13},{10,... | collective-permute-start | bytes 344072 | tf_op jit(solution)/shard_map/ppermute | solution.py:1045
  341.4 7.8 %collective-permute-start.22 = (bf16[1,144,512]{2,1,0:T(8,128)(2,1)S(1)}, bf16[1,144,512]{2,1,0:T(8,128)(2,1)S(1)}, u32[]{:S(2)}, u32[]{:S(2)}) collective-permute-start(bf16[1,144,512]{2,1,0:T(8,128)(2,1)S(1)} %fusion.1), channel_id=1, source_target_pairs={{0,16},{8,24},{16,0},{24,8},{1,17},{9,25},{17,1},{25,9},{2,18},{10... | collective-permute-start | bytes 442376 | tf_op jit(solution)/shard_map/ppermute | solution.py:1045
  347.6 4.2 %collective-permute-start.21 = (bf16[1,56,512]{2,1,0:T(8,128)(2,1)S(1)}, bf16[1,56,512]{2,1,0:T(8,128)(2,1)S(1)}, u32[]{:S(2)}, u32[]{:S(2)}) collective-permute-start(bf16[1,56,512]{2,1,0:T(8,128)(2,1)S(1)} %get-tuple-element.186), channel_id=1, source_target_pairs={{0,16},{8,24},{16,0},{24,8},{1,17},{9,25},{17,1},{25,9},{2,18},{10... | collective-permute-start | bytes 172040 | tf_op jit(solution)/shard_map/ppermute | solution.py:1045
  351.8 0.6 copy-start.10
Sparse Core Ops, SparseCore 0:
  10.9 74.4 all-gather.1
